TPU v7x, 32 devices: a whole 2x2x4 slice. The times are simulated.
32 devices in a mesh: row: 4 (over y, x), col: 8 (over z, core).
Axes of the slice: x: 2, y: 2, z: 4, core: 2. Of those that a mesh axis runs over, the one named last changes fastest.
Arguments:
- final_sens: float32 [32, 2048, 1024], P(None, 'col', 'row'), may hold values from -6 to 6
- courant: float32 [2, 2, 8, 2048, 1024], P(None, None, None, 'col', 'row'), may hold values from 0.03 to 0.45
- limiter: int32 [2, 4, 2048, 1024], P(None, None, 'col', 'row'), may hold values from 0 to 1
- directions: int32 [2, 2, 2048, 1024], P(None, None, 'col', 'row'), may hold values from 0 to 1
- nest_sens: float32 [32, 768, 96], P(None, 'col', 'row'), may hold values from -6 to 6
- box_lon: int32 [1], replicated, may hold values from 0 to 1792
- box_lat: int32 [1], replicated, may hold values from 0 to 992
- eof: float32 [32, 32], replicated, may hold values from -1.1 to 2.1
- lat_filter: bfloat16 [1024, 1024], replicated, may hold values from -1.1 to 2.1
- lon_filter: bfloat16 [2048, 2048], P('row'), may hold values from -1.1 to 2.1
Outputs:
- gradient: float32 [1024, 32, 2048], P('col', 'row')
All inputs are finite; a program needn't handle non-finite values.
Results may differ from a plain program's by a relative error of at most 0.00065.
The roundings to bfloat16 on the way count: a program that leaves them out, or rounds other values in their place, can miss the bound.
Values may be sent and summed in bfloat16 or wider, within the bound.
No kernel may reach another device: no remote copies, remote signals or barrier semaphores. Data moves between devices by JAX's collectives and lax.ppermute only.
A program may use at most 192 MiB of HBM per device.

v0:
```python
import functools

import jax
import jax.numpy as jnp
from jax import lax
from jax.experimental import pallas as pl
from jax.experimental.pallas import tpu as pltpu
from jax.sharding import PartitionSpec as P


RATIO = 3
BOXX = 256
BOXY = 32
LANES = 128
SUB = 8
BAND = 128
GROUP = 32
F32 = jnp.float32
BF16 = jnp.bfloat16
NT = (((1,), (1,)), ((), ()))
HIGHEST = lax.Precision.HIGHEST


def lanes_of(shape):
    return lax.broadcasted_iota(jnp.int32, shape, len(shape) - 1)


def sublanes_of(shape):
    return lax.broadcasted_iota(jnp.int32, shape, len(shape) - 2)


def split(value):
    return [value[:, k * LANES : (k + 1) * LANES] for k in range(value.shape[1] // LANES)]


def rows_at(start):
    return pl.ds(pl.multiple_of(start, SUB), SUB)


def x_fluxes(mu, coef, damp, east):
    flux = coef * damp * mu
    part = east * flux
    return part, flux - part


def stencil(mu, px, qx, up_x, down_x, coef, damp, north, halo_up, halo_down):
    flux = coef * damp * mu
    py = north * flux
    qy = flux - py
    base = mu - px + qx - py + qy + up_x - down_x
    lane = lanes_of((SUB, LANES))
    last, first = lane == LANES - 1, lane == 0
    py, qy, base = split(py), split(qy), split(base)
    rolled_up = [pltpu.roll(v, LANES - 1, 1) for v in py]
    rolled_down = [pltpu.roll(v, 1, 1) for v in qy]
    count = len(base)
    out = []
    for k in range(count):
        above = rolled_up[k + 1] if k + 1 < count else halo_up
        below = rolled_down[k - 1] if k > 0 else halo_down
        out.append(base[k] + jnp.where(last, above, rolled_up[k]) - jnp.where(first, below, rolled_down[k]))
    return out, py, qy


def shifted(px_here, px_next, qx_prev, qx_here):
    sub = sublanes_of(px_here.shape)
    up = jnp.where(sub == SUB - 1, pltpu.roll(px_next, SUB - 1, 0), pltpu.roll(px_here, SUB - 1, 0))
    down = jnp.where(sub == 0, pltpu.roll(qx_prev, 1, 0), pltpu.roll(qx_here, 1, 0))
    return up, down


def first_step(mu_ref, cour_ref, lim_ref, dir_ref, out_ref, ef_ref, em_ref, ew_ref, xr_ref, xm_ref, xw_ref, damp, east, north, rim):
    level = pl.program_id(0)
    fields, _, rows, width = mu_ref.shape
    tiles = width // LANES
    groups = rows // GROUP
    tall = ef_ref.shape[0]
    lane = lanes_of((SUB, LANES))
    last = lane == LANES - 1
    edge = slice((tiles - 1) * LANES, tiles * LANES)

    @pl.when(level == 0)
    def _():
        for ref in (ef_ref, em_ref, ew_ref, xr_ref):
            ref[...] = jnp.zeros_like(ref)

        def prepare(tile, carry):
            at = rows_at(tile * SUB)
            east[at] = dir_ref[1, 0, at].astype(F32)
            north[at] = dir_ref[1, 1, at].astype(F32)
            side = jnp.where(last, 1 - dir_ref[0, 1, at, edge], dir_ref[0, 1, at, :LANES]).astype(F32)
            for f in range(fields):
                damp[f, at] = 0.5 + 0.5 * lim_ref[1, f, at].astype(F32)
                flag = jnp.where(last, lim_ref[0, f, at, edge], lim_ref[0, f, at, :LANES]).astype(F32)
                rim[f, at] = side * (0.5 + 0.5 * flag)
            return carry

        lax.fori_loop(0, rows // SUB, prepare, 0)

    def group(g, carry):
        base = g * GROUP
        inside = GROUP // SUB
        starts = [jnp.maximum(base - SUB, 0)] + [base + SUB * t for t in range(inside)] + [jnp.minimum(base + GROUP, rows - SUB)]
        keep_low = jnp.where(g > 0, 1.0, 0.0).astype(F32)
        keep_high = jnp.where(g < groups - 1, 1.0, 0.0).astype(F32)
        band = base // tall
        held = [[ref[rows_at(lax.rem(base, tall) + SUB * t)] for t in range(inside)] for ref in (ef_ref, em_ref, ew_ref)]
        for f in range(fields):
            slot = level * fields + f
            turn = lax.rem(2 * slot + 1 + band * 64, LANES)
            mine = (lane // 2) == slot + 32 * band
            mus = [mu_ref[f, 0, rows_at(s)] for s in starts]
            pq = [
                x_fluxes(m, cour_ref[1, 0, 0, rows_at(s)], damp[f, rows_at(s)], east[rows_at(s)])
                for m, s in zip(mus, starts)
            ]
            px = [v[0] for v in pq]
            qx = [v[1] for v in pq]
            qx[0] = qx[0] * keep_low
            px[-1] = px[-1] * keep_high
            for t in range(inside):
                at = rows_at(starts[t + 1])
                up, down = shifted(px[t + 1], px[t + 2], qx[t], qx[t + 1])
                new, py, qy = stencil(
                    mus[t + 1], px[t + 1], qx[t + 1], up, down, cour_ref[1, 1, 0, at], damp[f, at], north[at],
                    jnp.zeros((SUB, LANES), F32), jnp.zeros((SUB, LANES), F32),
                )
                for k in range(tiles):
                    out_ref[f, 0, at, k * LANES : (k + 1) * LANES] = new[k]
                weight = jnp.where(last, cour_ref[0, 1, 0, at, edge], cour_ref[0, 1, 0, at, :LANES]) * rim[f, at]
                for which, value in enumerate((jnp.where(last, qy[-1], py[0]), jnp.where(last, new[-1], new[0]), weight)):
                    held[which][t] = jnp.where(mine, pltpu.roll(value, turn, 1), held[which][t])
        for which, ref in enumerate((ef_ref, em_ref, ew_ref)):
            for t in range(inside):
                ref[rows_at(lax.rem(base, tall) + SUB * t)] = held[which][t]
        return carry

    lax.fori_loop(0, groups, group, 0)

    low, high = slice(0, SUB), slice(rows - SUB, rows)
    for f in range(fields):
        slot = level * fields + f
        turn = 2 * slot + 1
        mine = (lane // 2) == slot
        px, _ = x_fluxes(mu_ref[f, 0, low], cour_ref[1, 0, 0, low], damp[f, low], east[low])
        _, qx = x_fluxes(mu_ref[f, 0, high], cour_ref[1, 0, 0, high], damp[f, high], east[high])
        xr_ref[level, f : f + 1] = px[:1]
        xr_ref[level, fields + f : fields + f + 1] = qx[SUB - 1 :]
        px_edge = pltpu.roll(jnp.where(last, px[:, edge], px[:, :LANES]), turn, 1)
        qx_edge = pltpu.roll(jnp.where(last, qx[:, edge], qx[:, :LANES]), turn, 1)
        corner = xr_ref.shape[0] - 1
        xr_ref[corner, 0:1, :LANES] = jnp.where(mine, px_edge, jnp.broadcast_to(xr_ref[corner, 0:1, :LANES], (SUB, LANES)))[:1]
        xr_ref[corner, 4:5, :LANES] = jnp.where(mine, qx_edge, jnp.broadcast_to(xr_ref[corner, 4:5, :LANES], (SUB, LANES)))[SUB - 1 :]
        xm_ref[level, f : f + 1] = out_ref[f, 0, low][:1]
        xm_ref[level, fields + f : fields + f + 1] = out_ref[f, 0, high][SUB - 1 :]
        for at, part, row in ((low, 0, 0), (high, 1, SUB - 1)):
            way = dir_ref[0, 0, at].astype(F32)
            way = 1.0 - way if part else way
            value = way * (0.5 + 0.5 * lim_ref[0, f, at].astype(F32)) * cour_ref[0, 0, 0, at]
            xw_ref[level, part * fields + f : part * fields + f + 1] = value[row : row + 1]


def pick(first, a, b):
    return jnp.where(first, a, b)


def rims(rows, parts, ids, efa_ref, efb_ref, xra_ref, xrb_ref, em_ref, ew_ref, xm_ref, xw_ref, eof_ref, e2_ref, x2_ref, m1_ref, x1_ref, kh_ref, kl_ref):
    me_row = ids[0]
    even_row, even_col = ids[2] == 0, ids[3] == 0
    levels, twice, width = xm_ref.shape
    fields = twice // 2
    tiles = width // LANES
    tall = em_ref.shape[0]
    top_band = (rows - 1) // tall
    lane = lanes_of((tall, LANES))
    sub = sublanes_of((tall, LANES))
    up = pick(even_row, efa_ref[...], efb_ref[...])
    down = pick(even_row, efb_ref[...], efa_ref[...])
    merged = jnp.where(lane % 2 == 1, up, -pltpu.roll(down, 2, 1))
    m1_ref[...] = merged
    fixed = em_ref[...] + jnp.where(lane % 2 == 0, pltpu.roll(up, LANES - 1, 1), -pltpu.roll(down, 1, 1))
    corner = xra_ref.shape[0] - 1
    ca, cb = xra_ref[corner, :, :LANES], xrb_ref[corner, :, :LANES]
    corner_up = pick(even_col, ca, cb)[0:1]
    corner_down = pick(even_col, cb, ca)[4:5]
    if top_band:
        corner_up = pltpu.roll(jnp.broadcast_to(corner_up, (SUB, LANES)), 64 * top_band, 1)[:1]
    fixed = fixed + jnp.where(sub == tall - 1, corner_up, 0.0) - jnp.where(sub == 0, corner_down, 0.0)
    e2_ref[...] = ew_ref[...] * fixed

    lane8 = lanes_of((twice, LANES))
    sub8 = sublanes_of((twice, LANES))
    ends = jnp.where(sub8 < fields, jnp.broadcast_to(merged[0:1], (twice, LANES)), jnp.broadcast_to(merged[tall - 1 :], (twice, LANES)))
    wide = sublanes_of((twice, width))
    for level in range(levels):
        a, b = xra_ref[level], xrb_ref[level]
        halo = jnp.where(wide < fields, pick(even_col, a, b), -pick(even_col, b, a))
        x1_ref[level] = halo
        target = 2 * (level * fields + sub8 % fields) + 1 + jnp.where(sub8 >= fields, 64 * top_band, 0)
        at_last = jnp.sum(jnp.where(lane8 == target, ends, 0.0), axis=1, keepdims=True)
        at_first = jnp.sum(jnp.where(lane8 == (target + 1) % LANES, ends, 0.0), axis=1, keepdims=True)
        here = split(xm_ref[level] + pltpu.roll(halo, fields, 0))
        here[-1] = here[-1] + jnp.where(lane8 == LANES - 1, at_last, 0.0)
        here[0] = here[0] + jnp.where(lane8 == 0, at_first, 0.0)
        for k in range(tiles):
            at = slice(k * LANES, (k + 1) * LANES)
            x2_ref[level, :, at] = xw_ref[level, :, at] * here[k]

    channels = eof_ref.shape[0]
    size = kh_ref.shape[0]
    share = channels // parts
    i = lax.broadcasted_iota(jnp.int32, (size, channels), 0) // SUB
    chosen = ((i // share) ^ me_row) * share + i % share
    left = (lax.broadcasted_iota(jnp.int32, (size, channels), 1) == chosen).astype(F32)
    j = lax.broadcasted_iota(jnp.int32, (channels, size), 1) // SUB
    right = (lax.broadcasted_iota(jnp.int32, (channels, size), 0) == j).astype(F32)
    mixed = jnp.dot(left, eof_ref[...], precision=HIGHEST, preferred_element_type=F32)
    spread = jnp.dot(mixed, right, precision=HIGHEST, preferred_element_type=F32)
    same = (lax.broadcasted_iota(jnp.int32, (size, size), 0) - lax.broadcasted_iota(jnp.int32, (size, size), 1)) % SUB == 0
    spread = jnp.where(same, spread, 0.0)
    high = spread.astype(BF16)
    kh_ref[...] = high
    kl_ref[...] = (spread - high.astype(F32)).astype(BF16)


def second_step(
    band, parts, ids, mu_ref, mu_low, mu_high, cour_ref, cx_low, cx_high, lim_ref, lim_low, lim_high, dir_ref, dir_low, dir_high,
    m1_ref, x1_ref, e2a_ref, e2b_ref, x2a_ref, x2b_ref, box_ref, kh_ref, kl_ref, *rest,
):
    outs, (damp, east, north, m2_ref, mixed) = rest[:-5], rest[-5:]
    g = pl.program_id(0)
    fields, levels, _, width = mu_ref.shape
    rows = ids[5]
    tall = m1_ref.shape[0]
    even_row, even_col = ids[2] == 0, ids[3] == 0
    tiles = width // LANES
    inside = GROUP // SUB
    lane = lanes_of((SUB, LANES))
    sub = sublanes_of((SUB, width))
    last, first = lane == LANES - 1, lane == 0

    @pl.when(g == 0)
    def _():
        wide = lanes_of((tall, LANES))
        up = pick(even_row, e2a_ref[...], e2b_ref[...])
        down = pick(even_row, e2b_ref[...], e2a_ref[...])
        m2_ref[...] = jnp.where(wide % 2 == 1, up, -pltpu.roll(down, 2, 1))

    lims = [(lim_low, 0)] + [(lim_ref, SUB * t) for t in range(inside)] + [(lim_high, 0)]
    dirs = [(dir_low, 0)] + [(dir_ref, SUB * t) for t in range(inside)] + [(dir_high, 0)]
    mus = [(mu_low, 0)] + [(mu_ref, SUB * t) for t in range(inside)] + [(mu_high, 0)]
    cxs = [(cx_low, 0)] + [(cour_ref, SUB * t) for t in range(inside)] + [(cx_high, 0)]
    for t in range(inside + 2):
        put = slice(SUB * t, SUB * (t + 1))
        ref, r = dirs[t]
        east[put] = ref[0, 0, r : r + SUB].astype(F32)
        if 0 < t <= inside:
            north[SUB * (t - 1) : SUB * t] = ref[0, 1, r : r + SUB].astype(F32)
        ref, r = lims[t]
        for f in range(fields):
            damp[f, put] = 0.5 + 0.5 * ref[0, f, r : r + SUB].astype(F32)

    base = band * tall + g * GROUP
    starts = [jnp.maximum(base - SUB, 0)] + [base + SUB * t for t in range(inside)] + [jnp.minimum(base + GROUP, rows - SUB)]
    bands = [s // tall for s in starts]
    places = [lax.rem(s, tall) for s in starts]
    at_start = base == 0
    at_end = base + GROUP == rows
    lat_at = ids[7]
    box_lats = box_ref.shape[1] // (fields * levels * parts)
    away = (lane - lat_at) & (LANES - 1)
    piece = away // box_lats
    total = parts * box_lats
    span = fields * levels * box_lats // LANES
    inner = [((lane + LANES * k - lat_at) >= 0) & ((lane + LANES * k - lat_at) < total) for k in range(tiles)]

    def channel_group(level, carry):
        for f in range(fields):
            slot = level * fields + f
            vals, px, qx = [], [], []
            for t in range(inside + 2):
                ref, r = mus[t]
                value = ref[f, level, r : r + SUB]
                fix = pltpu.roll(m1_ref[rows_at(places[t])], (126 - 2 * slot - 64 * bands[t]) & (LANES - 1), 1)
                pieces = split(value)
                pieces[-1] = pieces[-1] + jnp.where(last, fix, 0.0)
                pieces[0] = pieces[0] + jnp.where(first, fix, 0.0)
                value = jnp.concatenate(pieces, axis=1)
                if t == 1:
                    value = value + jnp.where((sub == 0) & at_start, x1_ref[level, fields + f : fields + f + 1], 0.0)
                if t == inside:
                    value = value + jnp.where((sub == SUB - 1) & at_end, x1_ref[level, f : f + 1], 0.0)
                ref, r = cxs[t]
                p, q = x_fluxes(value, ref[0, 0, level, r : r + SUB], damp[f, SUB * t : SUB * (t + 1)], east[SUB * t : SUB * (t + 1)])
                vals.append(value)
                px.append(p)
                qx.append(q)
            halo_low = pick(even_col, x2b_ref[level, fields + f : fields + f + 1], x2a_ref[level, fields + f : fields + f + 1])
            halo_high = pick(even_col, x2a_ref[level, f : f + 1], x2b_ref[level, f : f + 1])
            qx[0] = jnp.where(at_start, jnp.broadcast_to(halo_low, (SUB, width)), qx[0])
            px[-1] = jnp.where(at_end, jnp.broadcast_to(halo_high, (SUB, width)), px[-1])
            for t in range(inside):
                here = slice(SUB * (t + 1), SUB * (t + 2))
                mine = slice(SUB * t, SUB * (t + 1))
                up, down = shifted(px[t + 1], px[t + 2], qx[t], qx[t + 1])
                halo = pltpu.roll(m2_ref[rows_at(places[t + 1])], (126 - 2 * slot - 64 * bands[t + 1]) & (LANES - 1), 1)
                new, _, _ = stencil(
                    vals[t + 1], px[t + 1], qx[t + 1], up, down, cour_ref[0, 1, level, mine], damp[f, here], north[mine], halo, -halo
                )
                gathered = jnp.zeros((SUB, LANES), F32)
                for r in range(parts):
                    block = r * span + f * levels * box_lats // LANES
                    begin = (f * levels * box_lats) % LANES + level * box_lats
                    source = box_ref[mine, block * LANES : (block + 1) * LANES]
                    moved = pltpu.roll(source, (lat_at + box_lats * r - begin) & (LANES - 1), 1)
                    gathered = jnp.where(piece == r, moved, gathered)
                put = rows_at((f * levels + level) * SUB)
                for k in range(tiles):
                    mixed[t, put, k * LANES : (k + 1) * LANES] = new[k] + jnp.where(inner[k], gathered, 0.0)
        return carry

    lax.fori_loop(0, levels, channel_group, 0)

    channels = fields * levels
    share = channels // parts
    per = len(outs) // parts
    depth = share // per
    for v in range(inside // 2):
        both = []
        for t in (2 * v, 2 * v + 1):
            full = mixed[t]
            high = full.astype(BF16)
            low = (full - high.astype(F32)).astype(BF16)
            result = jnp.dot(kh_ref[...], high, preferred_element_type=F32)
            result += jnp.dot(kl_ref[...], high, preferred_element_type=F32)
            result += jnp.dot(kh_ref[...], low, preferred_element_type=F32)
            both.append(result)
        for c in range(channels):
            at = slice(c * SUB, (c + 1) * SUB)
            pair = jnp.concatenate([both[0][at], both[1][at]], axis=0).astype(BF16)
            outs[(c // share) * per + (c % share) // depth][c % depth, 2 * SUB * v : 2 * SUB * (v + 1)] = pair


def coarse_sums(ids, nest_ref, out_ref, held):
    channels, fine_lat, fine_lon = nest_ref.shape
    lon = ids[1] * fine_lon + lax.broadcasted_iota(jnp.int32, (fine_lat, fine_lon), 1)
    lat = ids[0] * fine_lat + lax.broadcasted_iota(jnp.int32, (fine_lat, fine_lon), 0)
    edge = (lon < RATIO) | (lon >= RATIO * BOXX - RATIO) | (lat < RATIO) | (lat >= RATIO * BOXY - RATIO)
    weight = jnp.where(edge, 1.0, 1.0 / (RATIO * RATIO)).astype(F32)
    for c in range(channels):
        held[c * fine_lat : (c + 1) * fine_lat] = nest_ref[c] * weight
    count = channels * fine_lat // RATIO
    sums = held[pl.ds(0, count, stride=RATIO)]
    for a in range(1, RATIO):
        sums = sums + held[pl.ds(a, count, stride=RATIO)]
    shape = (fine_lon // RATIO, fine_lon)
    select = (lax.broadcasted_iota(jnp.int32, shape, 1) // RATIO == lax.broadcasted_iota(jnp.int32, shape, 0)).astype(F32)
    out_ref[...] = lax.dot_general(select, sums, NT, precision=HIGHEST, preferred_element_type=F32)


def arrange(masks, ids, near_ref, far_ref, out_ref, box):
    half, slab, wide = near_ref.shape
    rows = out_ref.shape[0]
    for p, (row_mask, col_mask) in enumerate(masks):
        at = pl.multiple_of((ids[1] ^ col_mask) * slab, SUB)
        to = pl.multiple_of((ids[0] ^ row_mask) * wide, LANES)
        box[pl.ds(at, slab), pl.ds(to, wide)] = near_ref[p] if p < half else far_ref[p - half]
    height = box.shape[0]
    away = ids[6]
    row = lax.broadcasted_iota(jnp.int32, (rows, LANES), 0) - away
    inside = (row >= 0) & (row < height)
    turn = lax.rem(lax.rem(away, height) + height, height)
    for k in range(box.shape[1] // LANES):
        at = slice(k * LANES, (k + 1) * LANES)
        out_ref[:, at] = jnp.where(inside, pltpu.roll(box[:, at], turn, 0)[:rows], 0.0)


def lat_filter_part(start, height, count, parts, cols, ids, *refs):
    pieces, filt, outs = refs[:parts], refs[parts], refs[parts + 1 :]
    lat_block = pieces[0].shape[2]
    lon = pieces[0].shape[1]
    lat_part = filt.shape[0] // cols
    step = 2
    for p in range(count // step):
        right = [ref[step * p : step * (p + 1)].reshape(step * lon, lat_block) for ref in pieces]
        for s0 in range(0, cols, 4):
            acc = None
            for r in range(parts):
                at = pl.ds(pl.multiple_of((ids[0] ^ r) * lat_block, LANES), lat_block)
                left = jnp.concatenate(
                    [
                        filt[pl.ds(pl.multiple_of((ids[1] ^ s) * lat_part + start, 16), height), at]
                        for s in range(s0, min(s0 + 4, cols))
                    ],
                    axis=0,
                )
                term = lax.dot_general(left, right[r], NT, preferred_element_type=F32)
                acc = term if acc is None else acc + term
            for s in range(s0, min(s0 + 4, cols)):
                for c in range(step):
                    value = acc[(s - s0) * height : (s - s0 + 1) * height, c * lon : (c + 1) * lon]
                    outs[s][step * p + c] = value.astype(BF16)


def lon_filter_part(half, height, cols, parts, n_first, aliased, ids, *refs):
    firsts = refs[:n_first]
    lasts = refs[n_first : n_first + cols]
    filters = refs[n_first + cols : n_first + cols + 2 * parts]
    rest = refs[n_first + cols + 2 * parts + (1 if aliased else 0) :]
    out, lines, buffer, stage, in_sem, out_sem = rest
    channels, _, lon = lasts[0].shape
    wide = lines.shape[1] // cols
    rows = channels * height
    block = filters[0].shape[0]
    steps = 2 * parts
    strips = block // LANES

    def fetch(j):
        return pltpu.make_async_copy(filters[j], buffer.at[j % 2], in_sem.at[j % 2])

    def owner(j):
        row = ids[0] ^ (j // 2)
        return row * 2 + (ids[8] if j % 2 == 0 else 1 - ids[8])

    def flush(j, k):
        at = pl.ds(pl.multiple_of(owner(j) * block + k * LANES, LANES), LANES)
        return pltpu.make_async_copy(stage.at[j % 2, k], out.at[pl.ds(half * rows, rows), at], out_sem.at[j % 2, k])

    fetch(0).start()
    for s in range(cols):
        base = pl.multiple_of((ids[1] ^ s) * wide, LANES)
        for c in range(channels):
            put = slice(c * height, (c + 1) * height)
            for b in range(wide // lon - 1):
                groups = n_first // cols // (wide // lon - 1)
                each = channels // groups
                ref = firsts[(b * groups + c // each) * cols + s]
                lines[put, pl.ds(base + b * lon, lon)] = ref[c % each, half * height : (half + 1) * height]
            lines[put, pl.ds(base + wide - lon, lon)] = lasts[s][c]
    for j in range(steps):
        if j + 1 < steps:
            fetch(j + 1).start()
        fetch(j).wait()
        if j >= 2:
            for k in range(strips):
                flush(j - 2, k).wait()
        acc = lax.dot_general(lines[...], buffer[j % 2], NT, preferred_element_type=F32)
        for c in range(channels):
            for k in range(strips):
                at = slice(k * LANES, (k + 1) * LANES)
                stage[j % 2, k, pl.ds(c, height, stride=channels), :] = acc[c * height : (c + 1) * height, at]
        for k in range(strips):
            flush(j, k).start()
    for j in (steps - 2, steps - 1):
        for k in range(strips):
            flush(j, k).wait()


def swap(value, axis, mask):
    count = lax.axis_size(axis)
    return lax.ppermute(value, axis, [(i, i ^ mask) for i in range(count)])


def neighbours(value, axis, parity):
    count = lax.axis_size(axis)
    pairs = []
    for i in range(parity, count - 1, 2):
        pairs += [(i, i + 1), (i + 1, i)]
    return lax.ppermute(value, axis, pairs)


def shape_of(shape, dtype=F32):
    return jax.ShapeDtypeStruct(shape, dtype)


def whole(shape):
    return pl.BlockSpec(shape, lambda *_: (0,) * len(shape))


VMEM_SPEC = pl.BlockSpec(memory_space=pltpu.VMEM)
SMEM_SPEC = pl.BlockSpec(memory_space=pltpu.SMEM)
ANY_SPEC = pl.BlockSpec(memory_space=pl.ANY)


def shards(final_sens, courant, limiter, directions, nest_sens, box_lon, box_lat, eof, lat_filter, lon_filter):
    channels, lon_block, lat_block = final_sens.shape
    fields, levels = limiter.shape[1], courant.shape[2]
    rows_count, cols_count = lax.axis_size("row"), lax.axis_size("col")
    me_row, me_col = lax.axis_index("row"), lax.axis_index("col")
    ids = jnp.stack(
        [
            me_row,
            me_col,
            me_row % 2,
            me_col % 2,
            me_row * 0,
            me_row * 0 + lon_block,
            box_lon[0] - me_col * lon_block,
            box_lat[0] - me_row * lat_block,
            me_col % 2,
        ]
    ).astype(jnp.int32)
    lat_part = lat_filter.shape[0] // cols_count
    share = channels // rows_count
    tall = min(BAND, lon_block)
    n_bands = lon_block // tall

    nest = jnp.transpose(nest_sens, (0, 2, 1))
    fine_lat, fine_lon = nest.shape[1:]
    coarse = pl.pallas_call(
        coarse_sums,
        out_shape=shape_of((fine_lon // RATIO, channels * fine_lat // RATIO)),
        in_specs=[SMEM_SPEC, VMEM_SPEC],
        out_specs=VMEM_SPEC,
        scratch_shapes=[pltpu.VMEM((channels * fine_lat, fine_lon), F32)],
        name="coarse",
    )(ids, nest)
    masks = [(0, 0)]
    stages = [("col", m) for m in (2**k for k in range(1, 10)) if m < cols_count]
    stages += [("row", m) for m in (2**k for k in range(10)) if m < rows_count]
    stages += [("col", 1)]

    def spread(held, count, last=False):
        nonlocal stages, masks
        for axis, mask in stages[:count]:
            other = swap(held, axis, mask)
            held = (held, other) if last else jnp.concatenate([held, other], axis=0)
            masks = masks + [(r ^ mask, c) if axis == "row" else (r, c ^ mask) for r, c in masks]
        stages = stages[count:]
        return held

    def after(value, *others):
        return lax.optimization_barrier((value, *others))[0]

    held = spread(coarse[None], 1)

    mu = final_sens.reshape(fields, levels, lon_block, lat_block)
    mu1, ef, em, ew, xr, xm, xw = pl.pallas_call(
        first_step,
        grid=(levels,),
        out_shape=(
            shape_of(mu.shape),
            shape_of((tall, LANES)),
            shape_of((tall, LANES)),
            shape_of((tall, LANES)),
            shape_of((levels + 1, 2 * fields, lat_block)),
            shape_of((levels, 2 * fields, lat_block)),
            shape_of((levels, 2 * fields, lat_block)),
        ),
        in_specs=[
            pl.BlockSpec((fields, 1, lon_block, lat_block), lambda l: (0, l, 0, 0)),
            pl.BlockSpec((2, 2, 1, lon_block, lat_block), lambda l: (0, 0, l, 0, 0)),
            whole(limiter.shape),
            whole(directions.shape),
        ],
        out_specs=(
            pl.BlockSpec((fields, 1, lon_block, lat_block), lambda l: (0, l, 0, 0)),
            whole((tall, LANES)),
            whole((tall, LANES)),
            whole((tall, LANES)),
            whole((levels + 1, 2 * fields, lat_block)),
            whole((levels, 2 * fields, lat_block)),
            whole((levels, 2 * fields, lat_block)),
        ),
        scratch_shapes=[
            pltpu.VMEM((fields, lon_block, lat_block), F32),
            pltpu.VMEM((lon_block, lat_block), F32),
            pltpu.VMEM((lon_block, lat_block), F32),
            pltpu.VMEM((fields, lon_block, LANES), F32),
        ],
        name="first_step",
    )(mu, courant, limiter, directions)
    held = spread(after(held, ef), 1)
    efa, efb = neighbours(ef, "row", 0), neighbours(ef, "row", 1)
    xra, xrb = neighbours(xr, "col", 0), neighbours(xr, "col", 1)
    held = spread(after(held, efb, xrb), 1)
    size = channels * SUB
    e2, x2, m1, x1, kh, kl = pl.pallas_call(
        functools.partial(rims, lon_block, rows_count),
        out_shape=(
            shape_of(ef.shape),
            shape_of(xm.shape),
            shape_of(ef.shape),
            shape_of(xm.shape),
            shape_of((size, size), BF16),
            shape_of((size, size), BF16),
        ),
        in_specs=[SMEM_SPEC] + [VMEM_SPEC] * 9,
        out_specs=(VMEM_SPEC,) * 6,
        name="rims",
    )(ids, efa, efb, xra, xrb, em, ew, xm, xw, eof)
    e2a, e2b = neighbours(e2, "row", 0), neighbours(e2, "row", 1)
    x2a, x2b = neighbours(x2, "col", 0), neighbours(x2, "col", 1)
    held = spread(after(held, e2), len(stages) - 1)
    held = spread(held, 1, True)
    box = pl.pallas_call(
        functools.partial(arrange, masks),
        out_shape=shape_of((lon_block, rows_count * coarse.shape[1])),
        in_specs=[SMEM_SPEC, VMEM_SPEC, VMEM_SPEC],
        out_specs=VMEM_SPEC,
        scratch_shapes=[pltpu.VMEM((cols_count * coarse.shape[0], rows_count * coarse.shape[1]), F32)],
        name="arrange",
    )(ids, *held)

    groups = tall // GROUP
    fine = GROUP // SUB
    top = lon_block // SUB - 1

    def control(band, halves, kl):
        def at(g):
            return band * groups + g

        def low(g):
            return jnp.maximum((band * groups + g) * fine - 1, 0)

        def high(g):
            return jnp.minimum((band * groups + g) * fine + fine, top)

        depth = share // halves
        return pl.pallas_call(
            functools.partial(second_step, band, rows_count),
            grid=(groups,),
            out_shape=(shape_of((depth, tall, lat_block), BF16),) * (rows_count * halves),
            in_specs=[
                SMEM_SPEC,
                pl.BlockSpec((fields, levels, GROUP, lat_block), lambda g: (0, 0, at(g), 0)),
                pl.BlockSpec((fields, levels, SUB, lat_block), lambda g: (0, 0, low(g), 0)),
                pl.BlockSpec((fields, levels, SUB, lat_block), lambda g: (0, 0, high(g), 0)),
                pl.BlockSpec((1, 2, levels, GROUP, lat_block), lambda g: (0, 0, 0, at(g), 0)),
                pl.BlockSpec((1, 1, levels, SUB, lat_block), lambda g: (0, 0, 0, low(g), 0)),
                pl.BlockSpec((1, 1, levels, SUB, lat_block), lambda g: (0, 0, 0, high(g), 0)),
                pl.BlockSpec((1, fields, GROUP, lat_block), lambda g: (0, 0, at(g), 0)),
                pl.BlockSpec((1, fields, SUB, lat_block), lambda g: (0, 0, low(g), 0)),
                pl.BlockSpec((1, fields, SUB, lat_block), lambda g: (0, 0, high(g), 0)),
                pl.BlockSpec((1, 2, GROUP, lat_block), lambda g: (0, 0, at(g), 0)),
                pl.BlockSpec((1, 1, SUB, lat_block), lambda g: (0, 0, low(g), 0)),
                pl.BlockSpec((1, 1, SUB, lat_block), lambda g: (0, 0, high(g), 0)),
                whole(m1.shape),
                whole(x1.shape),
                whole(e2.shape),
                whole(e2.shape),
                whole(x2.shape),
                whole(x2.shape),
                pl.BlockSpec((GROUP, box.shape[1]), lambda g: (at(g), 0)),
                whole(kh.shape),
                whole(kl.shape),
            ],
            out_specs=(pl.BlockSpec((depth, GROUP, lat_block), lambda g: (0, g, 0)),) * (rows_count * halves),
            scratch_shapes=[
                pltpu.VMEM((fields, GROUP + 2 * SUB, lat_block), F32),
                pltpu.VMEM((GROUP + 2 * SUB, lat_block), F32),
                pltpu.VMEM((GROUP, lat_block), F32),
                pltpu.VMEM((tall, LANES), F32),
                pltpu.VMEM((fine, channels * SUB, lat_block), F32),
            ],
            name="second_step",
        )(ids, mu1, mu1, mu1, courant, courant, courant, limiter, limiter, limiter, directions, directions, directions,
          m1, x1, e2a, e2b, x2a, x2b, box, kh, kl)

    def to_rows(pieces):
        return [pieces[0]] + [swap(pieces[s], "row", s) for s in range(1, rows_count)]

    def smooth(pieces, start, height, token):
        count = pieces[0].shape[0]
        filt = lat_filter if token is None else after(lat_filter, token)
        call = pl.pallas_call(
            functools.partial(lat_filter_part, start, height, count, rows_count, cols_count),
            out_shape=(shape_of((count, height, tall), BF16),) * cols_count,
            in_specs=[SMEM_SPEC] + [VMEM_SPEC] * (rows_count + 1),
            out_specs=(VMEM_SPEC,) * cols_count,
            name="lat_filter",
        )
        outs = call(ids, *pieces, filt)
        moved = {s: swap(outs[s], "col", s) for s in range(cols_count - 1, 0, -1)}
        return [outs[0]] + [moved[s] for s in range(1, cols_count)], outs[-1]

    firsts = []
    sent = []
    order = None
    for band in range(n_bands):
        final = band == n_bands - 1
        halves = 1 if final else 2
        kl = kl if order is None else after(kl, order)
        outs = control(band, halves, kl)
        order = outs[-1]
        for h in range(halves):
            sent.append(to_rows([outs[s * halves + h] for s in range(rows_count)]))

    height = lon_filter.shape[0] // 2
    own = lax.dynamic_slice_in_dim(lon_filter, (me_col % 2) * height, height, 0)
    own = after(own, order)
    gathered = [own] + [swap(own, "row", s) for s in range(1, rows_count)]

    token = None
    for pieces in sent[:-1]:
        moved, token = smooth(pieces, 0, lat_part, token)
        firsts += moved
    half_height = lat_part // 2
    lasts = []
    for h in range(2):
        moved, token = smooth(sent[-1], h * half_height, half_height, token)
        lasts.append(moved)
    filters = []
    for piece in gathered:
        filters += [piece, swap(after(piece, token), "col", 1)]

    n_lon = cols_count * lon_block
    rows = share * half_height
    if lon_block % LANES:
        stacked = jnp.stack([jnp.concatenate([lasts[0][s], lasts[1][s]], axis=1) for s in range(cols_count)])
        lines = jnp.take(stacked, me_col ^ jnp.arange(cols_count), axis=0)
        lines = jnp.transpose(lines, (2, 1, 0, 3)).reshape(lat_part, share, n_lon)
        whole_filter = jnp.stack(filters).reshape(rows_count, 2, height, n_lon)
        whole_filter = jnp.take(whole_filter, me_row ^ jnp.arange(rows_count), axis=0)
        whole_filter = jnp.take(whole_filter, me_col % 2 ^ jnp.arange(2), axis=1).reshape(n_lon, n_lon)
        return jnp.einsum("lci,oi->lco", lines, whole_filter, preferred_element_type=F32)
    out = None
    for h in range(2):
        aliased = out is not None
        operands = (ids, *firsts, *lasts[h], *filters) + ((out,) if aliased else ())
        call = pl.pallas_call(
            functools.partial(lon_filter_part, h, half_height, cols_count, rows_count, len(firsts), aliased),
            out_shape=shape_of((2 * rows, n_lon)),
            in_specs=[SMEM_SPEC] + [VMEM_SPEC] * (len(firsts) + cols_count) + [ANY_SPEC] * (2 * rows_count + aliased),
            out_specs=ANY_SPEC,
            scratch_shapes=[
                pltpu.VMEM((rows, n_lon), BF16),
                pltpu.VMEM((2, height, n_lon), BF16),
                pltpu.VMEM((2, height // LANES, rows, LANES), F32),
                pltpu.SemaphoreType.DMA((2,)),
                pltpu.SemaphoreType.DMA((2, height // LANES)),
            ],
            input_output_aliases={len(operands) - 1: 0} if aliased else {},
            name="lon_filter",
        )
        out = call(*operands)
    return out.reshape(lat_part, share, n_lon)


def solution(mesh):
    placed = (
        P(None, "col", "row"),
        P(None, None, None, "col", "row"),
        P(None, None, "col", "row"),
        P(None, None, "col", "row"),
        P(None, "col", "row"),
        P(),
        P(),
        P(),
        P(),
        P("row", None),
    )
    return jax.shard_map(shards, mesh=mesh, in_specs=placed, out_specs=P("col", "row", None), check_vma=False)
```

profile of v0, /device:TPU:0, one launch (start us, length us, event | category | flops | bytes accessed | tf_op | source)
XLA Modules:
  0.0 333.9 jit_solution(293892849660528042)
XLA Ops:
  4.0 3.1 collective-permute-start.8
  7.1 22.6 %first_step.1 = (f32[4,8,256,256]{3,2,1,0:T(8,128)}, f32[128,128]{1,0:T(8,128)}, f32[128,128]{1,0:T(8,128)}, f32[128,128]{1,0:T(8,128)}, f32[9,8,256]{2,1,0:T(8,...) custom-call(f32[4,8,256,256]{3,2,1,0:T(8,128)} %bitcast.14, f32[2,2,8,256,256]{4,3,2,1,0:T(8,128)} %cx_high.3, ...), custom_call_target="tpu_custom_call" | custom-call | tf_op jit(solution)/shard_map/first_step/pallas_call | solution.py:538
  29.7 2.7 collective-permute-start.9
  35.5 5.7 %collective-permute-start.10 = (f32[4,32,256]{2,1,0:T(8,128)S(1)}, f32[4,32,256]{2,1,0:T(8,128)S(1)}, u32[]{:S(2)}, u32[]{:S(2)}) collective-permute-start(f32[4,32,256]{2,1,0:T(8,128)S(1)} %pad_maximum_fusion.1), channel_id=1, source_target_pairs={{0,8},{8,0},{16,24},{24,16},{1,9},{9,1},{17,25},{25,17},{2,10},{10... | collective-permute-start | bytes 393224 | tf_op jit(solution)/shard_map/ppermute | solution.py:461
  42.1 4.8 %collective-permute-done.efa_ref = f32[128,128]{1,0:T(8,128)S(1)} collective-permute-done((f32[128,128]{1,0:T(8,128)}, f32[128,128]{1,0:T(8,128)S(1)}, u32[]{:S(2)}, u32[]{:S(2)}) %collective-permute-start) | collective-permute-done | bytes 65568 | tf_op jit(solution)/shard_map/ppermute | solution.py:469
  47.6 2.6 rims.1
  52.3 6.5 %collective-permute-done.11 = f32[8,32,256]{2,1,0:T(8,128)S(1)} collective-permute-done((f32[8,32,256]{2,1,0:T(8,128)S(1)}, f32[8,32,256]{2,1,0:T(8,128)S(1)}, u32[]{:S(2)}, u32[]{:S(2)}) %collective-permute-start.11) | collective-permute-done | bytes 262176 | tf_op jit(solution)/shard_map/ppermute | solution.py:461
  62.4 4.1 %collective-permute-start.4 = (f32[128,128]{1,0:T(8,128)}, f32[128,128]{1,0:T(8,128)S(1)}, u32[]{:S(2)}, u32[]{:S(2)}) collective-permute-start(f32[128,128]{1,0:T(8,128)} %get-tuple-element.83), channel_id=1, source_target_pairs={{0,8},{8,0},{16,24},{24,16},{1,9},{9,1},{17,25},{25,17},{2,10},{10... | collective-permute-start | bytes 196616 | tf_op jit(solution)/shard_map/ppermute | solution.py:469
  67.3 3.0 arrange.1.box_ref
  71.0 19.2 %second_step.2 = (bf16[4,128,256]{2,1,0:T(8,128)(2,1)}, bf16[4,128,256]{2,1,0:T(8,128)(2,1)}, bf16[4,128,256]{2,1,0:T(8,128)(2,1)}, bf16[4,128,256]{2,1,0:T(8,12...) custom-call(s32[9]{0:T(128)} %stack.28.ids, ...), custom_call_target="tpu_custom_call" | custom-call | tf_op jit(solution)/shard_map/second_step/pallas_call | solution.py:620
  96.0 3.8 %collective-permute-done.13.refs_1_ = bf16[4,128,256]{2,1,0:T(8,128)(2,1)S(1)} collective-permute-done((bf16[4,128,256]{2,1,0:T(8,128)(2,1)}, bf16[4,128,256]{2,1,0:T(8,128)(2,1)S(1)}, u32[]{:S(2)}, u32[]{:S(2)}) %collective-permute-start.13) | collective-permute-done | bytes 262176 | tf_op jit(solution)/shard_map/ppermute | solution.py:461
  101.3 4.6 %collective-permute-done.14.refs_2_ = bf16[4,128,256]{2,1,0:T(8,128)(2,1)S(1)} collective-permute-done((bf16[4,128,256]{2,1,0:T(8,128)(2,1)}, bf16[4,128,256]{2,1,0:T(8,128)(2,1)S(1)}, u32[]{:S(2)}, u32[]{:S(2)}) %collective-permute-start.14) | collective-permute-done | bytes 262176 | tf_op jit(solution)/shard_map/ppermute | solution.py:461
  106.6 4.1 %lat_filter.4 = (bf16[4,128,128]{2,1,0:T(8,128)(2,1)}, bf16[4,128,128]{2,1,0:T(8,128)(2,1)}, bf16[4,128,128]{2,1,0:T(8,128)(2,1)}, bf16[4,128,128]{2,1,0:T(8,128...) custom-call(s32[9]{0:T(128)} %stack.28.ids, ...), custom_call_target="tpu_custom_call" | custom-call | tf_op jit(solution)/shard_map/lat_filter/pallas_call | solution.py:673
  112.8 19.1 %second_step.3 = (bf16[8,128,256]{2,1,0:T(8,128)(2,1)}, bf16[8,128,256]{2,1,0:T(8,128)(2,1)}, bf16[8,128,256]{2,1,0:T(8,128)(2,1)}, bf16[8,128,256]{2,1,0:T(8,128)(2,1)}) custom-call(s32[9]{0:T(128)} %stack.28.ids, f32[4,8,256,256]{3,2,1,0:T(8,128)} %get-tuple-element.74.mu_ref.mu_low.mu_high, f32[4,8,256,256]{3,2,1,0:T(8,128)} %get-tuple-element.74.mu_ref.mu_low.mu_high, ...), custom_call_target="tpu_custom_call" | custom-call | tf_op jit(solution)/shard_map/second_step/pallas_call | solution.py:620
  139.7 12.3 %collective-permute-done.19.refs_4_ = bf16[4,128,128]{2,1,0:T(8,128)(2,1)S(1)} collective-permute-done((bf16[4,128,128]{2,1,0:T(8,128)(2,1)}, bf16[4,128,128]{2,1,0:T(8,128)(2,1)S(1)}, u32[]{:S(2)}, u32[]{:S(2)}) %collective-permute-start.19) | collective-permute-done | bytes 131104 | tf_op jit(solution)/shard_map/ppermute | solution.py:461
  155.6 4.1 %lat_filter.5 = (bf16[4,128,128]{2,1,0:T(8,128)(2,1)}, bf16[4,128,128]{2,1,0:T(8,128)(2,1)}, bf16[4,128,128]{2,1,0:T(8,128)(2,1)}, bf16[4,128,128]{2,1,0:T(8,128...) custom-call(s32[9]{0:T(128)} %stack.28.ids, ...), custom_call_target="tpu_custom_call" | custom-call | tf_op jit(solution)/shard_map/lat_filter/pallas_call | solution.py:673
  161.8 2.9 collective-permute-start.27
  164.7 4.1 %collective-permute-done.27.refs_10_ = bf16[4,128,128]{2,1,0:T(8,128)(2,1)} collective-permute-done((bf16[4,128,128]{2,1,0:T(8,128)(2,1)}, bf16[4,128,128]{2,1,0:T(8,128)(2,1)}, u32[]{:S(2)}, u32[]{:S(2)}) %collective-permute-start.27) | collective-permute-done | bytes 131104 | tf_op jit(solution)/shard_map/ppermute | solution.py:461
  171.7 49.5 %collective-permute-done.34.refs_2_ = bf16[8,128,256]{2,1,0:T(8,128)(2,1)} collective-permute-done((bf16[8,128,256]{2,1,0:T(8,128)(2,1)}, bf16[8,128,256]{2,1,0:T(8,128)(2,1)}, u32[]{:S(2)}, u32[]{:S(2)}) %collective-permute-start.34) | collective-permute-done | bytes 524320 | tf_op jit(solution)/shard_map/ppermute | solution.py:461
  221.2 2.2 collective-permute-start.29
  223.5 4.5 %lat_filter.6 = (bf16[8,64,128]{2,1,0:T(8,128)(2,1)}, bf16[8,64,128]{2,1,0:T(8,128)(2,1)}, bf16[8,64,128]{2,1,0:T(8,128)(2,1)}, bf16[8,64,128]{2,1,0:T(8,128)(2,...) custom-call(s32[9]{0:T(128)} %stack.28.ids, ...), custom_call_target="tpu_custom_call" | custom-call | tf_op jit(solution)/shard_map/lat_filter/pallas_call | solution.py:673
  232.8 4.4 %lat_filter.7 = (bf16[8,64,128]{2,1,0:T(8,128)(2,1)}, bf16[8,64,128]{2,1,0:T(8,128)(2,1)}, bf16[8,64,128]{2,1,0:T(8,128)(2,1)}, bf16[8,64,128]{2,1,0:T(8,128)(2,...) custom-call(s32[9]{0:T(128)} %stack.28.ids, ...), custom_call_target="tpu_custom_call" | custom-call | tf_op jit(solution)/shard_map/lat_filter/pallas_call | solution.py:673
  246.7 3.5 %collective-permute-done.50.refs_17_ = bf16[8,64,128]{2,1,0:T(8,128)(2,1)S(1)} collective-permute-done((bf16[8,64,128]{2,1,0:T(8,128)(2,1)}, bf16[8,64,128]{2,1,0:T(8,128)(2,1)S(1)}, u32[]{:S(2)}, u32[]{:S(2)}) %collective-permute-start.50) | collective-permute-done | bytes 131104 | tf_op jit(solution)/shard_map/ppermute | solution.py:461
  250.2 4.3 %collective-permute-start.51 = (bf16[8,64,128]{2,1,0:T(8,128)(2,1)}, bf16[8,64,128]{2,1,0:T(8,128)(2,1)S(1)}, u32[]{:S(2)}, u32[]{:S(2)}) collective-permute-start(bf16[8,64,128]{2,1,0:T(8,128)(2,1)} %get-tuple-element.138), channel_id=1, source_target_pairs={{0,2},{1,3},{2,0},{3,1},{4,6},{5,7},{6,4},{7,5},{8,10},{9,11},{10,... | collective-permute-start | bytes 393224 | tf_op jit(solution)/shard_map/ppermute | solution.py:461
  254.5 4.0 %collective-permute-done.51.refs_18_ = bf16[8,64,128]{2,1,0:T(8,128)(2,1)S(1)} collective-permute-done((bf16[8,64,128]{2,1,0:T(8,128)(2,1)}, bf16[8,64,128]{2,1,0:T(8,128)(2,1)S(1)}, u32[]{:S(2)}, u32[]{:S(2)}) %collective-permute-start.51) | collective-permute-done | bytes 131104 | tf_op jit(solution)/shard_map/ppermute | solution.py:461
  259.2 5.1 %collective-permute-done.52.refs_19_ = bf16[8,64,128]{2,1,0:T(8,128)(2,1)S(1)} collective-permute-done((bf16[8,64,128]{2,1,0:T(8,128)(2,1)}, bf16[8,64,128]{2,1,0:T(8,128)(2,1)S(1)}, u32[]{:S(2)}, u32[]{:S(2)}) %collective-permute-start.52) | collective-permute-done | bytes 131104 | tf_op jit(solution)/shard_map/ppermute | solution.py:461
  266.2 7.5 %collective-permute-done.53.refs_20_ = bf16[8,64,128]{2,1,0:T(8,128)(2,1)S(1)} collective-permute-done((bf16[8,64,128]{2,1,0:T(8,128)(2,1)}, bf16[8,64,128]{2,1,0:T(8,128)(2,1)S(1)}, u32[]{:S(2)}, u32[]{:S(2)}) %collective-permute-start.53) | collective-permute-done | bytes 131104 | tf_op jit(solution)/shard_map/ppermute | solution.py:461
  273.7 8.4 %collective-permute-done.54.refs_21_ = bf16[8,64,128]{2,1,0:T(8,128)(2,1)S(1)} collective-permute-done((bf16[8,64,128]{2,1,0:T(8,128)(2,1)}, bf16[8,64,128]{2,1,0:T(8,128)(2,1)S(1)}, u32[]{:S(2)}, u32[]{:S(2)}) %collective-permute-start.54) | collective-permute-done | bytes 131104 | tf_op jit(solution)/shard_map/ppermute | solution.py:461
  284.0 5.6 %collective-permute-done.55.refs_22_ = bf16[8,64,128]{2,1,0:T(8,128)(2,1)S(1)} collective-permute-done((bf16[8,64,128]{2,1,0:T(8,128)(2,1)}, bf16[8,64,128]{2,1,0:T(8,128)(2,1)S(1)}, u32[]{:S(2)}, u32[]{:S(2)}) %collective-permute-start.55) | collective-permute-done | bytes 131104 | tf_op jit(solution)/shard_map/ppermute | solution.py:461
  290.3 6.5 %collective-permute-done.56.refs_23_ = bf16[8,64,128]{2,1,0:T(8,128)(2,1)S(1)} collective-permute-done((bf16[8,64,128]{2,1,0:T(8,128)(2,1)}, bf16[8,64,128]{2,1,0:T(8,128)(2,1)S(1)}, u32[]{:S(2)}, u32[]{:S(2)}) %collective-permute-start.56) | collective-permute-done | bytes 131104 | tf_op jit(solution)/shard_map/ppermute | solution.py:461
  304.3 14.6 %lon_filter.2.refs_32_ = f32[1024,2048]{1,0:T(8,128)} custom-call(s32[9]{0:T(128)} %stack.28.ids, bf16[4,128,128]{2,1,0:T(8,128)(2,1)} %get-tuple-element.94.refs_0_, bf16[4,128,128]{2,1,0:T(8,128)(2,1)} %copy-done.4, bf16[4,128,128]{2,1,0:T(8,128)(2,1)} %copy-done.5, bf16[4,128,128]{2,1,0:T(8,128)(2,1)} %copy-done.6, bf16[4,128,128]{2,1,0:T(8,128)(2,1)} %copy-done.7, ...), custom_call_target="tpu_custom_call" | custom-call | tf_op jit(solution)/shard_map/lon_filter/pallas_call | solution.py:736
  319.0 14.8 %lon_filter.3 = f32[1024,2048]{1,0:T(8,128)} custom-call(s32[9]{0:T(128)} %stack.28.ids, bf16[4,128,128]{2,1,0:T(8,128)(2,1)} %get-tuple-element.94.refs_0_, bf16[4,128,128]{2,1,0:T(8,128)(2,1)} %copy-done.4, bf16[4,128,128]{2,1,0:T(8,128)(2,1)} %copy-done.5, bf16[4,128,128]{2,1,0:T(8,128)(2,1)} %copy-done.6, ...), custom_call_target="tpu_custom_call", output_to_operand_aliasing={{}: (33, {})} | custom-call | tf_op jit(solution)/shard_map/lon_filter/pallas_call | solution.py:736
  (171 shorter events, 67.6 us)
Async XLA Ops:
  4.0 25.7 %collective-permute-start.8 = (f32[1,32,256]{2,1,0:T(8,128)}, f32[1,32,256]{2,1,0:T(8,128)S(1)}, u32[]{:S(2)}, u32[]{:S(2)}) collective-permute-start(f32[1,32,256]{2,1,0:T(8,128)} %bitcast.16), channel_id=1, source_target_pairs={{0,2},{1,3},{2,0},{3,1},{4,6},{5,7},{6,4},{7,5},{8,10},{9,11},{10,... | collective-permute-start | bytes 98312 | tf_op jit(solution)/shard_map/ppermute | solution.py:461
  35.5 14.7 %collective-permute-start.10 = (f32[4,32,256]{2,1,0:T(8,128)S(1)}, f32[4,32,256]{2,1,0:T(8,128)S(1)}, u32[]{:S(2)}, u32[]{:S(2)}) collective-permute-start(f32[4,32,256]{2,1,0:T(8,128)S(1)} %pad_maximum_fusion.1), channel_id=1, source_target_pairs={{0,8},{8,0},{16,24},{24,16},{1,9},{9,1},{17,25},{25,17},{2,10},{10... | collective-permute-start | bytes 393224 | tf_op jit(solution)/shard_map/ppermute | solution.py:461
  58.9 11.5 %collective-permute-start.7 = (f32[8,8,256]{2,1,0:T(8,128)}, f32[8,8,256]{2,1,0:T(8,128)S(1)}, u32[]{:S(2)}, u32[]{:S(2)}) collective-permute-start(f32[8,8,256]{2,1,0:T(8,128)} %get-tuple-element.84), channel_id=1, source_target_pairs={{1,2},{2,1},{3,4},{4,3},{5,6},{6,5},{9,10},{10,9},{11,12},{12,11},... | collective-permute-start | bytes 196616 | tf_op jit(solution)/shard_map/ppermute | solution.py:469
  90.9 15.0 %collective-permute-start.14 = (bf16[4,128,256]{2,1,0:T(8,128)(2,1)}, bf16[4,128,256]{2,1,0:T(8,128)(2,1)S(1)}, u32[]{:S(2)}, u32[]{:S(2)}) collective-permute-start(bf16[4,128,256]{2,1,0:T(8,128)(2,1)} %get-tuple-element.92), channel_id=1, source_target_pairs={{0,16},{8,24},{16,0},{24,8},{1,17},{9,25},{17,1},{25,9},{2,18},{10... | collective-permute-start | bytes 786440 | tf_op jit(solution)/shard_map/ppermute | solution.py:461
  92.5 13.5 %collective-permute-start.15 = (bf16[4,128,256]{2,1,0:T(8,128)(2,1)}, bf16[4,128,256]{2,1,0:T(8,128)(2,1)}, u32[]{:S(2)}, u32[]{:S(2)}) collective-permute-start(bf16[4,128,256]{2,1,0:T(8,128)(2,1)} %get-tuple-element.93), channel_id=1, source_target_pairs={{0,24},{8,16},{16,8},{24,0},{1,25},{9,17},{17,9},{25,1},{2,26},{10... | collective-permute-start | bytes 786440 | tf_op jit(solution)/shard_map/ppermute | solution.py:461
  93.8 18.8 %collective-permute-start.23 = (bf16[4,128,256]{2,1,0:T(8,128)(2,1)}, bf16[4,128,256]{2,1,0:T(8,128)(2,1)S(1)}, u32[]{:S(2)}, u32[]{:S(2)}) collective-permute-start(bf16[4,128,256]{2,1,0:T(8,128)(2,1)} %get-tuple-element.103), channel_id=1, source_target_pairs={{0,8},{8,0},{16,24},{24,16},{1,9},{9,1},{17,25},{25,17},{2,10},{10... | collective-permute-start | bytes 786440 | tf_op jit(solution)/shard_map/ppermute | solution.py:461
  94.4 37.5 %collective-permute-start.24 = (bf16[4,128,256]{2,1,0:T(8,128)(2,1)}, bf16[4,128,256]{2,1,0:T(8,128)(2,1)S(1)}, u32[]{:S(2)}, u32[]{:S(2)}) collective-permute-start(bf16[4,128,256]{2,1,0:T(8,128)(2,1)} %get-tuple-element.104), channel_id=1, source_target_pairs={{0,16},{8,24},{16,0},{24,8},{1,17},{9,25},{17,1},{25,9},{2,18},{10... | collective-permute-start | bytes 786440 | tf_op jit(solution)/shard_map/ppermute | solution.py:461
  99.7 33.6 %collective-permute-start.25 = (bf16[4,128,256]{2,1,0:T(8,128)(2,1)}, bf16[4,128,256]{2,1,0:T(8,128)(2,1)S(1)}, u32[]{:S(2)}, u32[]{:S(2)}) collective-permute-start(bf16[4,128,256]{2,1,0:T(8,128)(2,1)} %get-tuple-element.105), channel_id=1, source_target_pairs={{0,24},{8,16},{16,8},{24,0},{1,25},{9,17},{17,9},{25,1},{2,26},{10... | collective-permute-start | bytes 786440 | tf_op jit(solution)/shard_map/ppermute | solution.py:461
  110.8 23.4 %collective-permute-start.16 = (bf16[4,128,128]{2,1,0:T(8,128)(2,1)}, bf16[4,128,128]{2,1,0:T(8,128)(2,1)S(1)}, u32[]{:S(2)}, u32[]{:S(2)}) collective-permute-start(bf16[4,128,128]{2,1,0:T(8,128)(2,1)} %get-tuple-element.95), channel_id=1, source_target_pairs={{0,1},{1,0},{2,3},{3,2},{4,5},{5,4},{6,7},{7,6},{8,9},{9,8},{10,11... | collective-permute-start | bytes 393224 | tf_op jit(solution)/shard_map/ppermute | solution.py:461
  110.8 24.8 %collective-permute-start.17 = (bf16[4,128,128]{2,1,0:T(8,128)(2,1)}, bf16[4,128,128]{2,1,0:T(8,128)(2,1)S(1)}, u32[]{:S(2)}, u32[]{:S(2)}) collective-permute-start(bf16[4,128,128]{2,1,0:T(8,128)(2,1)} %get-tuple-element.96), channel_id=1, source_target_pairs={{0,2},{1,3},{2,0},{3,1},{4,6},{5,7},{6,4},{7,5},{8,10},{9,11},{10,... | collective-permute-start | bytes 393224 | tf_op jit(solution)/shard_map/ppermute | solution.py:461
  112.6 24.9 %collective-permute-start.18 = (bf16[4,128,128]{2,1,0:T(8,128)(2,1)}, bf16[4,128,128]{2,1,0:T(8,128)(2,1)S(1)}, u32[]{:S(2)}, u32[]{:S(2)}) collective-permute-start(bf16[4,128,128]{2,1,0:T(8,128)(2,1)} %get-tuple-element.97), channel_id=1, source_target_pairs={{0,3},{1,2},{2,1},{3,0},{4,7},{5,6},{6,5},{7,4},{8,11},{9,10},{10,... | collective-permute-start | bytes 393224 | tf_op jit(solution)/shard_map/ppermute | solution.py:461
  131.9 38.4 %collective-permute-start.33 = (bf16[8,128,256]{2,1,0:T(8,128)(2,1)}, bf16[8,128,256]{2,1,0:T(8,128)(2,1)}, u32[]{:S(2)}, u32[]{:S(2)}) collective-permute-start(bf16[8,128,256]{2,1,0:T(8,128)(2,1)} %get-tuple-element.117), channel_id=1, source_target_pairs={{0,8},{8,0},{16,24},{24,16},{1,9},{9,1},{17,25},{25,17},{2,10},{10... | collective-permute-start | bytes 1572872 | tf_op jit(solution)/shard_map/ppermute | solution.py:461
  133.3 18.7 %collective-permute-start.19 = (bf16[4,128,128]{2,1,0:T(8,128)(2,1)}, bf16[4,128,128]{2,1,0:T(8,128)(2,1)S(1)}, u32[]{:S(2)}, u32[]{:S(2)}) collective-permute-start(bf16[4,128,128]{2,1,0:T(8,128)(2,1)} %get-tuple-element.98), channel_id=1, source_target_pairs={{0,4},{1,5},{2,6},{3,7},{4,0},{5,1},{6,2},{7,3},{8,12},{9,13},{10,... | collective-permute-start | bytes 393224 | tf_op jit(solution)/shard_map/ppermute | solution.py:461
  134.2 19.4 %collective-permute-start.20 = (bf16[4,128,128]{2,1,0:T(8,128)(2,1)}, bf16[4,128,128]{2,1,0:T(8,128)(2,1)S(1)}, u32[]{:S(2)}, u32[]{:S(2)}) collective-permute-start(bf16[4,128,128]{2,1,0:T(8,128)(2,1)} %get-tuple-element.99), channel_id=1, source_target_pairs={{0,5},{1,4},{2,7},{3,6},{4,1},{5,0},{6,3},{7,2},{8,13},{9,12},{10,... | collective-permute-start | bytes 393224 | tf_op jit(solution)/shard_map/ppermute | solution.py:461
  135.6 18.6 %collective-permute-start.21 = (bf16[4,128,128]{2,1,0:T(8,128)(2,1)}, bf16[4,128,128]{2,1,0:T(8,128)(2,1)S(1)}, u32[]{:S(2)}, u32[]{:S(2)}) collective-permute-start(bf16[4,128,128]{2,1,0:T(8,128)(2,1)} %get-tuple-element.100), channel_id=1, source_target_pairs={{0,6},{1,7},{2,4},{3,5},{4,2},{5,3},{6,0},{7,1},{8,14},{9,15},{10,... | collective-permute-start | bytes 393224 | tf_op jit(solution)/shard_map/ppermute | solution.py:461
  137.5 22.2 %collective-permute-start.22 = (bf16[4,128,128]{2,1,0:T(8,128)(2,1)}, bf16[4,128,128]{2,1,0:T(8,128)(2,1)}, u32[]{:S(2)}, u32[]{:S(2)}) collective-permute-start(bf16[4,128,128]{2,1,0:T(8,128)(2,1)} %get-tuple-element.101), channel_id=1, source_target_pairs={{0,7},{1,6},{2,5},{3,4},{4,3},{5,2},{6,1},{7,0},{8,15},{9,14},{10,... | collective-permute-start | bytes 393224 | tf_op jit(solution)/shard_map/ppermute | solution.py:461
  152.1 85.2 %collective-permute-start.48 = (bf16[256,2048]{1,0:T(8,128)(2,1)S(1)}, bf16[256,2048]{1,0:T(8,128)(2,1)}, u32[]{:S(2)}, u32[]{:S(2)}) collective-permute-start(bf16[256,2048]{1,0:T(8,128)(2,1)S(1)} %constant_dynamic-slice_fusion.refs_24_), channel_id=1, source_target_pairs={{0,24},{8,16},{16,8},{24,0},{1,25},{9,17},{17,9},{25,1},{2,26},{10... | collective-permute-start | bytes 3145736 | tf_op jit(solution)/shard_map/ppermute | solution.py:461
  153.6 83.7 %collective-permute-start.46 = (bf16[256,2048]{1,0:T(8,128)(2,1)S(1)}, bf16[256,2048]{1,0:T(8,128)(2,1)}, u32[]{:S(2)}, u32[]{:S(2)}) collective-permute-start(bf16[256,2048]{1,0:T(8,128)(2,1)S(1)} %constant_dynamic-slice_fusion.refs_24_), channel_id=1, source_target_pairs={{0,16},{8,24},{16,0},{24,8},{1,17},{9,25},{17,1},{25,9},{2,18},{10... | collective-permute-start | bytes 3145736 | tf_op jit(solution)/shard_map/ppermute | solution.py:461
  154.3 85.0 %collective-permute-start.44 = (bf16[256,2048]{1,0:T(8,128)(2,1)S(1)}, bf16[256,2048]{1,0:T(8,128)(2,1)}, u32[]{:S(2)}, u32[]{:S(2)}) collective-permute-start(bf16[256,2048]{1,0:T(8,128)(2,1)S(1)} %constant_dynamic-slice_fusion.refs_24_), channel_id=1, source_target_pairs={{0,8},{8,0},{16,24},{24,16},{1,9},{9,1},{17,25},{25,17},{2,10},{10... | collective-permute-start | bytes 3145736 | tf_op jit(solution)/shard_map/ppermute | solution.py:461
  168.9 52.4 %collective-permute-start.34 = (bf16[8,128,256]{2,1,0:T(8,128)(2,1)}, bf16[8,128,256]{2,1,0:T(8,128)(2,1)}, u32[]{:S(2)}, u32[]{:S(2)}) collective-permute-start(bf16[8,128,256]{2,1,0:T(8,128)(2,1)} %get-tuple-element.118), channel_id=1, source_target_pairs={{0,16},{8,24},{16,0},{24,8},{1,17},{9,25},{17,1},{25,9},{2,18},{10... | collective-permute-start | bytes 1572872 | tf_op jit(solution)/shard_map/ppermute | solution.py:461
  170.3 50.9 %collective-permute-start.35 = (bf16[8,128,256]{2,1,0:T(8,128)(2,1)}, bf16[8,128,256]{2,1,0:T(8,128)(2,1)}, u32[]{:S(2)}, u32[]{:S(2)}) collective-permute-start(bf16[8,128,256]{2,1,0:T(8,128)(2,1)} %get-tuple-element.119), channel_id=1, source_target_pairs={{0,24},{8,16},{16,8},{24,0},{1,25},{9,17},{17,9},{25,1},{2,26},{10... | collective-permute-start | bytes 1572872 | tf_op jit(solution)/shard_map/ppermute | solution.py:461
  229.2 11.9 %collective-permute-start.30 = (bf16[4,128,128]{2,1,0:T(8,128)(2,1)}, bf16[4,128,128]{2,1,0:T(8,128)(2,1)}, u32[]{:S(2)}, u32[]{:S(2)}) collective-permute-start(bf16[4,128,128]{2,1,0:T(8,128)(2,1)} %get-tuple-element.112), channel_id=1, source_target_pairs={{0,5},{1,4},{2,7},{3,6},{4,1},{5,0},{6,3},{7,2},{8,13},{9,12},{10,... | collective-permute-start | bytes 393224 | tf_op jit(solution)/shard_map/ppermute | solution.py:461
  230.8 12.4 %collective-permute-start.31 = (bf16[4,128,128]{2,1,0:T(8,128)(2,1)}, bf16[4,128,128]{2,1,0:T(8,128)(2,1)}, u32[]{:S(2)}, u32[]{:S(2)}) collective-permute-start(bf16[4,128,128]{2,1,0:T(8,128)(2,1)} %get-tuple-element.113), channel_id=1, source_target_pairs={{0,6},{1,7},{2,4},{3,5},{4,2},{5,3},{6,0},{7,1},{8,14},{9,15},{10,... | collective-permute-start | bytes 393224 | tf_op jit(solution)/shard_map/ppermute | solution.py:461
  241.1 55.7 %collective-permute-start.43 = (bf16[256,2048]{1,0:T(8,128)(2,1)S(1)}, bf16[256,2048]{1,0:T(8,128)(2,1)S(1)}, u32[]{:S(2)}, u32[]{:S(2)}) collective-permute-start(bf16[256,2048]{1,0:T(8,128)(2,1)S(1)} %constant_dynamic-slice_fusion.refs_24_), channel_id=1, source_target_pairs={{0,1},{1,0},{2,3},{3,2},{4,5},{5,4},{6,7},{7,6},{8,9},{9,8},{10,11... | collective-permute-start | bytes 3145736 | tf_op jit(solution)/shard_map/ppermute | solution.py:461
  243.3 56.1 %collective-permute-start.49 = (bf16[256,2048]{1,0:T(8,128)(2,1)}, bf16[256,2048]{1,0:T(8,128)(2,1)}, u32[]{:S(2)}, u32[]{:S(2)}) collective-permute-start(bf16[256,2048]{1,0:T(8,128)(2,1)} %collective-permute-done.48.refs_30_), channel_id=1, source_target_pairs={{0,1},{1,0},{2,3},{3,2},{4,5},{5,4},{6,7},{7,6},{8,9},{9,8},{10,11... | collective-permute-start | bytes 3145736 | tf_op jit(solution)/shard_map/ppermute | solution.py:461
  244.6 55.5 %collective-permute-start.47 = (bf16[256,2048]{1,0:T(8,128)(2,1)}, bf16[256,2048]{1,0:T(8,128)(2,1)}, u32[]{:S(2)}, u32[]{:S(2)}) collective-permute-start(bf16[256,2048]{1,0:T(8,128)(2,1)} %collective-permute-done.46.refs_28_), channel_id=1, source_target_pairs={{0,1},{1,0},{2,3},{3,2},{4,5},{5,4},{6,7},{7,6},{8,9},{9,8},{10,11... | collective-permute-start | bytes 3145736 | tf_op jit(solution)/shard_map/ppermute | solution.py:461
  244.6 57.5 %collective-permute-start.45 = (bf16[256,2048]{1,0:T(8,128)(2,1)}, bf16[256,2048]{1,0:T(8,128)(2,1)}, u32[]{:S(2)}, u32[]{:S(2)}) collective-permute-start(bf16[256,2048]{1,0:T(8,128)(2,1)} %collective-permute-done.44.refs_26_), channel_id=1, source_target_pairs={{0,1},{1,0},{2,3},{3,2},{4,5},{5,4},{6,7},{7,6},{8,9},{9,8},{10,11... | collective-permute-start | bytes 3145736 | tf_op jit(solution)/shard_map/ppermute | solution.py:461
  296.8 22.1 %collective-permute-start.38 = (bf16[8,64,128]{2,1,0:T(8,128)(2,1)}, bf16[8,64,128]{2,1,0:T(8,128)(2,1)}, u32[]{:S(2)}, u32[]{:S(2)}) collective-permute-start(bf16[8,64,128]{2,1,0:T(8,128)(2,1)} %get-tuple-element.126), channel_id=1, source_target_pairs={{0,3},{1,2},{2,1},{3,0},{4,7},{5,6},{6,5},{7,4},{8,11},{9,10},{10,... | collective-permute-start | bytes 393224 | tf_op jit(solution)/shard_map/ppermute | solution.py:461
  297.9 21.0 %collective-permute-start.39 = (bf16[8,64,128]{2,1,0:T(8,128)(2,1)}, bf16[8,64,128]{2,1,0:T(8,128)(2,1)}, u32[]{:S(2)}, u32[]{:S(2)}) collective-permute-start(bf16[8,64,128]{2,1,0:T(8,128)(2,1)} %get-tuple-element.127), channel_id=1, source_target_pairs={{0,4},{1,5},{2,6},{3,7},{4,0},{5,1},{6,2},{7,3},{8,12},{9,13},{10,... | collective-permute-start | bytes 393224 | tf_op jit(solution)/shard_map/ppermute | solution.py:461
  299.4 19.5 %collective-permute-start.40 = (bf16[8,64,128]{2,1,0:T(8,128)(2,1)}, bf16[8,64,128]{2,1,0:T(8,128)(2,1)}, u32[]{:S(2)}, u32[]{:S(2)}) collective-permute-start(bf16[8,64,128]{2,1,0:T(8,128)(2,1)} %get-tuple-element.128), channel_id=1, source_target_pairs={{0,5},{1,4},{2,7},{3,6},{4,1},{5,0},{6,3},{7,2},{8,13},{9,12},{10,... | collective-permute-start | bytes 393224 | tf_op jit(solution)/shard_map/ppermute | solution.py:461
  300.1 18.8 %collective-permute-start.41 = (bf16[8,64,128]{2,1,0:T(8,128)(2,1)}, bf16[8,64,128]{2,1,0:T(8,128)(2,1)}, u32[]{:S(2)}, u32[]{:S(2)}) collective-permute-start(bf16[8,64,128]{2,1,0:T(8,128)(2,1)} %get-tuple-element.129), channel_id=1, source_target_pairs={{0,6},{1,7},{2,4},{3,5},{4,2},{5,3},{6,0},{7,1},{8,14},{9,15},{10,... | collective-permute-start | bytes 393224 | tf_op jit(solution)/shard_map/ppermute | solution.py:461
  302.1 16.8 %collective-permute-start.42 = (bf16[8,64,128]{2,1,0:T(8,128)(2,1)}, bf16[8,64,128]{2,1,0:T(8,128)(2,1)}, u32[]{:S(2)}, u32[]{:S(2)}) collective-permute-start(bf16[8,64,128]{2,1,0:T(8,128)(2,1)} %get-tuple-element.130), channel_id=1, source_target_pairs={{0,7},{1,6},{2,5},{3,4},{4,3},{5,2},{6,1},{7,0},{8,15},{9,14},{10,... | collective-permute-start | bytes 393224 | tf_op jit(solution)/shard_map/ppermute | solution.py:461
  (60 other events, 1437.1 us)
where the time goes:
time: 337 us; the launch traced here: 334 us
  waiting for transfers between devices  137 us (41%)
  Pallas kernels  115 us (34%)
  starting transfers between devices  75.1 us (22%)
  local copies, waits for them, and re-layouts  4.82 us (1%)
    ppermute x49, waiting for transfers between devices, swap(): return lax.ppermute(value, axis, [(i, i ^ mask) for i in range(count)])  132 us
    ppermute x49, starting transfers between devices, swap(): return lax.ppermute(value, axis, [(i, i ^ mask) for i in range(count)])  65.2 us
    pallas_call x2, Pallas kernels, control(): pl.pallas_call(functools.partial(second_step, band, rows_count), grid=(gr...  38.3 us
    pallas_call x2, Pallas kernels, shards(): out = call(*operands)  29.3 us
    pallas_call x1, Pallas kernels, shards(): pl.pallas_call(first_step, grid=(levels,), out_shape=(shape_of(mu.shape),...  22.6 us
    pallas_call x4, Pallas kernels, smooth(): outs = call(ids, *pieces, filt)  17.1 us
    ppermute x8, starting transfers between devices, neighbours(): return lax.ppermute(value, axis, pairs)  9.9 us
  transfers between devices with their start and end apart: 57, of which 21 were waited for; matrix products, arithmetic and copies ran while one was open for 0% of the time, Pallas kernels for 24%

commit v1 on v0

--- a/solution.py
+++ b/solution.py
@@ -402,7 +402,7 @@
                     outs[s][step * p + c] = value.astype(BF16)
 
 
-def lon_filter_part(half, height, cols, parts, n_first, aliased, ids, *refs):
+def lon_filter_part(half, height, cols, parts, n_first, aliased, owners, ids, *refs):
     firsts = refs[:n_first]
     lasts = refs[n_first : n_first + cols]
     filters = refs[n_first + cols : n_first + cols + 2 * parts]
@@ -419,8 +419,9 @@
         return pltpu.make_async_copy(filters[j], buffer.at[j % 2], in_sem.at[j % 2])
 
     def owner(j):
-        row = ids[0] ^ (j // 2)
-        return row * 2 + (ids[8] if j % 2 == 0 else 1 - ids[8])
+        side = ids[8] if j % 2 == 0 else 1 - ids[8]
+        even, odd = owners[j // 2]
+        return (ids[0] ^ jnp.where(side == 0, even, odd)) * 2 + side
 
     def flush(j, k):
         at = pl.ds(pl.multiple_of(owner(j) * block + k * LANES, LANES), LANES)
@@ -505,6 +506,22 @@
     tall = min(BAND, lon_block)
     n_bands = lon_block // tall
 
+    height = lon_filter.shape[0] // 2
+    gathered = [lax.dynamic_slice_in_dim(lon_filter, (me_col % 2) * height, height, 0)]
+    orders = [2**k for k in range(10) if 2**k < rows_count]
+    turns = (orders, orders[::-1])
+    owners = [(0, 0)]
+
+    def gather(stage, pieces):
+        pairs = []
+        for i in range(rows_count * cols_count):
+            row, col = divmod(i, cols_count)
+            pairs.append((i, (row ^ turns[col % 2][stage]) * cols_count + col))
+        return [lax.ppermute(piece, ("row", "col"), pairs) for piece in pieces]
+
+    gathered += gather(0, gathered)
+    owners += [(turns[0][0], turns[1][0])]
+
     nest = jnp.transpose(nest_sens, (0, 2, 1))
     fine_lat, fine_lon = nest.shape[1:]
     coarse = pl.pallas_call(
@@ -532,10 +549,10 @@
     def after(value, *others):
         return lax.optimization_barrier((value, *others))[0]
 
-    held = spread(coarse[None], 1)
+    held = spread(coarse[None], 2)
 
     mu = final_sens.reshape(fields, levels, lon_block, lat_block)
-    mu1, ef, em, ew, xr, xm, xw = pl.pallas_call(
+    call = pl.pallas_call(
         first_step,
         grid=(levels,),
         out_shape=(
@@ -569,13 +586,14 @@
             pltpu.VMEM((fields, lon_block, LANES), F32),
         ],
         name="first_step",
-    )(mu, courant, limiter, directions)
+    )
+    mu1, ef, em, ew, xr, xm, xw = call(mu, courant, limiter, directions)
     held = spread(after(held, ef), 1)
     efa, efb = neighbours(ef, "row", 0), neighbours(ef, "row", 1)
     xra, xrb = neighbours(xr, "col", 0), neighbours(xr, "col", 1)
-    held = spread(after(held, efb, xrb), 1)
+    held = spread(after(held, efa, efb, xra, xrb), len(stages) - 1)
     size = channels * SUB
-    e2, x2, m1, x1, kh, kl = pl.pallas_call(
+    call = pl.pallas_call(
         functools.partial(rims, lon_block, rows_count),
         out_shape=(
             shape_of(ef.shape),
@@ -588,10 +606,10 @@
         in_specs=[SMEM_SPEC] + [VMEM_SPEC] * 9,
         out_specs=(VMEM_SPEC,) * 6,
         name="rims",
-    )(ids, efa, efb, xra, xrb, em, ew, xm, xw, eof)
+    )
+    e2, x2, m1, x1, kh, kl = call(ids, efa, efb, xra, xrb, em, ew, xm, xw, eof)
     e2a, e2b = neighbours(e2, "row", 0), neighbours(e2, "row", 1)
     x2a, x2b = neighbours(x2, "col", 0), neighbours(x2, "col", 1)
-    held = spread(after(held, e2), len(stages) - 1)
     held = spread(held, 1, True)
     box = pl.pallas_call(
         functools.partial(arrange, masks),
@@ -686,11 +704,6 @@
         for h in range(halves):
             sent.append(to_rows([outs[s * halves + h] for s in range(rows_count)]))
 
-    height = lon_filter.shape[0] // 2
-    own = lax.dynamic_slice_in_dim(lon_filter, (me_col % 2) * height, height, 0)
-    own = after(own, order)
-    gathered = [own] + [swap(own, "row", s) for s in range(1, rows_count)]
-
     token = None
     for pieces in sent[:-1]:
         moved, token = smooth(pieces, 0, lat_part, token)
@@ -698,8 +711,12 @@
     half_height = lat_part // 2
     lasts = []
     for h in range(2):
+        early = token
         moved, token = smooth(sent[-1], h * half_height, half_height, token)
         lasts.append(moved)
+    for stage in range(1, len(orders)):
+        gathered += gather(stage, [after(piece, early) for piece in gathered])
+        owners += [(a ^ turns[0][stage], b ^ turns[1][stage]) for a, b in owners]
     filters = []
     for piece in gathered:
         filters += [piece, swap(after(piece, token), "col", 1)]
@@ -710,16 +727,18 @@
         stacked = jnp.stack([jnp.concatenate([lasts[0][s], lasts[1][s]], axis=1) for s in range(cols_count)])
         lines = jnp.take(stacked, me_col ^ jnp.arange(cols_count), axis=0)
         lines = jnp.transpose(lines, (2, 1, 0, 3)).reshape(lat_part, share, n_lon)
-        whole_filter = jnp.stack(filters).reshape(rows_count, 2, height, n_lon)
-        whole_filter = jnp.take(whole_filter, me_row ^ jnp.arange(rows_count), axis=0)
-        whole_filter = jnp.take(whole_filter, me_col % 2 ^ jnp.arange(2), axis=1).reshape(n_lon, n_lon)
+        whole_filter = jnp.zeros((n_lon, n_lon), BF16)
+        for j, piece in enumerate(filters):
+            side = me_col % 2 if j % 2 == 0 else 1 - me_col % 2
+            owner = (me_row ^ jnp.where(side == 0, *owners[j // 2])) * 2 + side
+            whole_filter = lax.dynamic_update_slice_in_dim(whole_filter, piece, owner * height, 0)
         return jnp.einsum("lci,oi->lco", lines, whole_filter, preferred_element_type=F32)
     out = None
     for h in range(2):
         aliased = out is not None
         operands = (ids, *firsts, *lasts[h], *filters) + ((out,) if aliased else ())
         call = pl.pallas_call(
-            functools.partial(lon_filter_part, h, half_height, cols_count, rows_count, len(firsts), aliased),
+            functools.partial(lon_filter_part, h, half_height, cols_count, rows_count, len(firsts), aliased, owners),
             out_shape=shape_of((2 * rows, n_lon)),
             in_specs=[SMEM_SPEC] + [VMEM_SPEC] * (len(firsts) + cols_count) + [ANY_SPEC] * (2 * rows_count + aliased),
             out_specs=ANY_SPEC,

time: 337 us -> 303 us (0.90)
  waiting for transfers between devices: 137 us -> 105 us
  starting transfers between devices: 75.1 us -> 70.4 us
    ppermute x49 -> x46, waiting for transfers between devices: 132 us -> 99.4 us  [swap(): return lax.ppermute(value, axis, [(i, i ^ mask) for i in range(count)])]
    ppermute x49 -> x46, starting transfers between devices: 65.2 us -> 53 us  [swap(): return lax.ppermute(value, axis, [(i, i ^ mask) for i in range(count)])]
    ppermute x8, starting transfers between devices: 9.9 us -> 15.3 us  [neighbours(): return lax.ppermute(value, axis, pairs)]
  transfers between devices with their start and end apart: 57 -> 57, of which waited for: 21 -> 21; matrix products, arithmetic and copies ran while one was open for 0% -> 0% of each run, Pallas kernels for 24% -> 33%
where the time goes in v1:
time: 303 us; the launch traced here: 301 us
  Pallas kernels  115 us (38%)
  waiting for transfers between devices  105 us (35%)
  starting transfers between devices  70.4 us (23%)
  local copies, waits for them, and re-layouts  7.17 us (2%)
    ppermute x46, waiting for transfers between devices, swap(): return lax.ppermute(value, axis, [(i, i ^ mask) for i in range(count)])  99.4 us
    ppermute x46, starting transfers between devices, swap(): return lax.ppermute(value, axis, [(i, i ^ mask) for i in range(count)])  53 us
    pallas_call x2, Pallas kernels, control(): pl.pallas_call(functools.partial(second_step, band, rows_count), grid=(gr...  38.3 us
    pallas_call x2, Pallas kernels, shards(): out = call(*operands)  29.3 us
    pallas_call x1, Pallas kernels, shards(): mu1, ef, em, ew, xr, xm, xw = call(mu, courant, limiter, directions)  22.6 us
    pallas_call x4, Pallas kernels, smooth(): outs = call(ids, *pieces, filt)  17.2 us
    ppermute x8, starting transfers between devices, neighbours(): return lax.ppermute(value, axis, pairs)  15.3 us
  transfers between devices with their start and end apart: 57, of which 21 were waited for; matrix products, arithmetic and copies ran while one was open for 0% of the time, Pallas kernels for 33%

profile of v1, /device:TPU:0, one launch (start us, length us, event | category | flops | bytes accessed | tf_op | source)
XLA Modules:
  0.0 301.1 jit_solution(4965090596113948507)
XLA Ops:
  4.0 3.1 %collective-permute-start.8 = (f32[1,32,256]{2,1,0:T(8,128)}, f32[1,32,256]{2,1,0:T(8,128)S(1)}, u32[]{:S(2)}, u32[]{:S(2)}) collective-permute-start(f32[1,32,256]{2,1,0:T(8,128)} %bitcast.16), channel_id=1, source_target_pairs={{0,2},{1,3},{2,0},{3,1},{4,6},{5,7},{6,4},{7,5},{8,10},{9,11},{10,... | collective-permute-start | bytes 98312 | tf_op jit(solution)/shard_map/ppermute | solution.py:462
  9.9 3.0 %collective-permute-start.9 = (f32[2,32,256]{2,1,0:T(8,128)S(1)}, f32[2,32,256]{2,1,0:T(8,128)S(1)}, u32[]{:S(2)}, u32[]{:S(2)}) collective-permute-start(f32[2,32,256]{2,1,0:T(8,128)S(1)} %pad_maximum_fusion.2), channel_id=1, source_target_pairs={{0,4},{1,5},{2,6},{3,7},{4,0},{5,1},{6,2},{7,3},{8,12},{9,13},{10,... | collective-permute-start | bytes 196616 | tf_op jit(solution)/shard_map/ppermute | solution.py:462
  13.0 22.6 %first_step.1 = (f32[4,8,256,256]{3,2,1,0:T(8,128)}, f32[128,128]{1,0:T(8,128)}, f32[128,128]{1,0:T(8,128)}, f32[128,128]{1,0:T(8,128)}, f32[9,8,256]{2,1,0:T(8,...) custom-call(f32[4,8,256,256]{3,2,1,0:T(8,128)} %bitcast.14, f32[2,2,8,256,256]{4,3,2,1,0:T(8,128)} %cx_high.3, ...), custom_call_target="tpu_custom_call" | custom-call | tf_op jit(solution)/shard_map/first_step/pallas_call | solution.py:590
  37.8 4.3 %collective-permute-start = (f32[128,128]{1,0:T(8,128)}, f32[128,128]{1,0:T(8,128)S(1)}, u32[]{:S(2)}, u32[]{:S(2)}) collective-permute-start(f32[128,128]{1,0:T(8,128)} %get-tuple-element.75), channel_id=1, source_target_pairs={{0,8},{8,0},{16,24},{24,16},{1,9},{9,1},{17,25},{25,17},{2,10},{10... | collective-permute-start | bytes 196616 | tf_op jit(solution)/shard_map/ppermute | solution.py:470
  42.8 3.0 collective-permute-start.2
  47.7 8.3 %collective-permute-done.11 = f32[8,32,256]{2,1,0:T(8,128)S(1)} collective-permute-done((f32[8,32,256]{2,1,0:T(8,128)S(1)}, f32[8,32,256]{2,1,0:T(8,128)S(1)}, u32[]{:S(2)}, u32[]{:S(2)}) %collective-permute-start.11) | collective-permute-done | bytes 262176 | tf_op jit(solution)/shard_map/ppermute | solution.py:462
  57.0 2.9 rims.1
  60.6 3.5 %collective-permute-start.4 = (f32[128,128]{1,0:T(8,128)}, f32[128,128]{1,0:T(8,128)S(1)}, u32[]{:S(2)}, u32[]{:S(2)}) collective-permute-start(f32[128,128]{1,0:T(8,128)} %get-tuple-element.83), channel_id=1, source_target_pairs={{0,8},{8,0},{16,24},{24,16},{1,9},{9,1},{17,25},{25,17},{2,10},{10... | collective-permute-start | bytes 196616 | tf_op jit(solution)/shard_map/ppermute | solution.py:470
  66.6 3.0 %arrange.1.box_ref = f32[256,1024]{1,0:T(8,128)} custom-call(s32[9]{0:T(128)} %stack.28.ids, f32[16,32,256]{2,1,0:T(8,128)} %constant_dynamic-update-slice_fusion.near_ref, f32[16,32,256]{2,1,0:T(8,128)} %collective-permute-done.12.far_ref), custom_call_target="tpu_custom_call" | custom-call | tf_op jit(solution)/shard_map/arrange/pallas_call | solution.py:614
  69.7 4.9 %collective-permute-done.4.e2a_ref = f32[128,128]{1,0:T(8,128)S(1)} collective-permute-done((f32[128,128]{1,0:T(8,128)}, f32[128,128]{1,0:T(8,128)S(1)}, u32[]{:S(2)}, u32[]{:S(2)}) %collective-permute-start.4) | collective-permute-done | bytes 65568 | tf_op jit(solution)/shard_map/ppermute | solution.py:470
  75.3 19.2 %second_step.2 = (bf16[4,128,256]{2,1,0:T(8,128)(2,1)}, bf16[4,128,256]{2,1,0:T(8,128)(2,1)}, bf16[4,128,256]{2,1,0:T(8,128)(2,1)}, bf16[4,128,256]{2,1,0:T(8,12...) custom-call(s32[9]{0:T(128)} %stack.28.ids, ...), custom_call_target="tpu_custom_call" | custom-call | tf_op jit(solution)/shard_map/second_step/pallas_call | solution.py:638
  98.1 5.8 %collective-permute-done.13.refs_1_ = bf16[4,128,256]{2,1,0:T(8,128)(2,1)S(1)} collective-permute-done((bf16[4,128,256]{2,1,0:T(8,128)(2,1)}, bf16[4,128,256]{2,1,0:T(8,128)(2,1)S(1)}, u32[]{:S(2)}, u32[]{:S(2)}) %collective-permute-start.13) | collective-permute-done | bytes 262176 | tf_op jit(solution)/shard_map/ppermute | solution.py:462
  104.5 19.1 %second_step.3 = (bf16[8,128,256]{2,1,0:T(8,128)(2,1)}, bf16[8,128,256]{2,1,0:T(8,128)(2,1)}, bf16[8,128,256]{2,1,0:T(8,128)(2,1)}, bf16[8,128,256]{2,1,0:T(8,128)(2,1)}) custom-call(s32[9]{0:T(128)} %stack.28.ids, f32[4,8,256,256]{3,2,1,0:T(8,128)} %get-tuple-element.74.mu_ref.mu_low.mu_high, f32[4,8,256,256]{3,2,1,0:T(8,128)} %get-tuple-element.74.mu_ref.mu_low.mu_high, ...), custom_call_target="tpu_custom_call" | custom-call | tf_op jit(solution)/shard_map/second_step/pallas_call | solution.py:638
  129.5 4.1 %lat_filter.4 = (bf16[4,128,128]{2,1,0:T(8,128)(2,1)}, bf16[4,128,128]{2,1,0:T(8,128)(2,1)}, bf16[4,128,128]{2,1,0:T(8,128)(2,1)}, bf16[4,128,128]{2,1,0:T(8,128...) custom-call(s32[9]{0:T(128)} %stack.28.ids, ...), custom_call_target="tpu_custom_call" | custom-call | tf_op jit(solution)/shard_map/lat_filter/pallas_call | solution.py:691
  133.6 14.7 %collective-permute-done.25.refs_3_ = bf16[4,128,256]{2,1,0:T(8,128)(2,1)} collective-permute-done((bf16[4,128,256]{2,1,0:T(8,128)(2,1)}, bf16[4,128,256]{2,1,0:T(8,128)(2,1)}, u32[]{:S(2)}, u32[]{:S(2)}) %collective-permute-start.25) | collective-permute-done | bytes 262176 | tf_op jit(solution)/shard_map/ppermute | solution.py:462
  148.3 4.1 %lat_filter.5 = (bf16[4,128,128]{2,1,0:T(8,128)(2,1)}, bf16[4,128,128]{2,1,0:T(8,128)(2,1)}, bf16[4,128,128]{2,1,0:T(8,128)(2,1)}, bf16[4,128,128]{2,1,0:T(8,128...) custom-call(s32[9]{0:T(128)} %stack.28.ids, ...), custom_call_target="tpu_custom_call" | custom-call | tf_op jit(solution)/shard_map/lat_filter/pallas_call | solution.py:691
  153.3 4.5 %lat_filter.6 = (bf16[8,64,128]{2,1,0:T(8,128)(2,1)}, bf16[8,64,128]{2,1,0:T(8,128)(2,1)}, bf16[8,64,128]{2,1,0:T(8,128)(2,1)}, bf16[8,64,128]{2,1,0:T(8,128)(2,...) custom-call(s32[9]{0:T(128)} %stack.28.ids, ...), custom_call_target="tpu_custom_call" | custom-call | tf_op jit(solution)/shard_map/lat_filter/pallas_call | solution.py:691
  162.5 6.7 %collective-permute-done.17.refs_2_ = bf16[4,128,128]{2,1,0:T(8,128)(2,1)S(1)} collective-permute-done((bf16[4,128,128]{2,1,0:T(8,128)(2,1)}, bf16[4,128,128]{2,1,0:T(8,128)(2,1)S(1)}, u32[]{:S(2)}, u32[]{:S(2)}) %collective-permute-start.17) | collective-permute-done | bytes 131104 | tf_op jit(solution)/shard_map/ppermute | solution.py:462
  175.0 8.7 %collective-permute-done.20.refs_5_ = bf16[4,128,128]{2,1,0:T(8,128)(2,1)} collective-permute-done((bf16[4,128,128]{2,1,0:T(8,128)(2,1)}, bf16[4,128,128]{2,1,0:T(8,128)(2,1)}, u32[]{:S(2)}, u32[]{:S(2)}) %collective-permute-start.20) | collective-permute-done | bytes 131104 | tf_op jit(solution)/shard_map/ppermute | solution.py:462
  193.0 2.7 collective-permute-start.31
  195.8 4.5 %lat_filter.7 = (bf16[8,64,128]{2,1,0:T(8,128)(2,1)}, bf16[8,64,128]{2,1,0:T(8,128)(2,1)}, bf16[8,64,128]{2,1,0:T(8,128)(2,1)}, bf16[8,64,128]{2,1,0:T(8,128)(2,...) custom-call(s32[9]{0:T(128)} %stack.28.ids, ...), custom_call_target="tpu_custom_call" | custom-call | tf_op jit(solution)/shard_map/lat_filter/pallas_call | solution.py:691
  200.3 4.3 %collective-permute-done.29.refs_12_ = bf16[4,128,128]{2,1,0:T(8,128)(2,1)} collective-permute-done((bf16[4,128,128]{2,1,0:T(8,128)(2,1)}, bf16[4,128,128]{2,1,0:T(8,128)(2,1)}, u32[]{:S(2)}, u32[]{:S(2)}) %collective-permute-start.29) | collective-permute-done | bytes 131104 | tf_op jit(solution)/shard_map/ppermute | solution.py:462
  208.3 4.3 %collective-permute-done.32.refs_15_ = bf16[4,128,128]{2,1,0:T(8,128)(2,1)} collective-permute-done((bf16[4,128,128]{2,1,0:T(8,128)(2,1)}, bf16[4,128,128]{2,1,0:T(8,128)(2,1)}, u32[]{:S(2)}, u32[]{:S(2)}) %collective-permute-start.32) | collective-permute-done | bytes 131104 | tf_op jit(solution)/shard_map/ppermute | solution.py:462
  216.9 3.7 %collective-permute-start.51 = (bf16[8,64,128]{2,1,0:T(8,128)(2,1)}, bf16[8,64,128]{2,1,0:T(8,128)(2,1)S(1)}, u32[]{:S(2)}, u32[]{:S(2)}) collective-permute-start(bf16[8,64,128]{2,1,0:T(8,128)(2,1)} %get-tuple-element.138), channel_id=1, source_target_pairs={{0,2},{1,3},{2,0},{3,1},{4,6},{5,7},{6,4},{7,5},{8,10},{9,11},{10,... | collective-permute-start | bytes 393224 | tf_op jit(solution)/shard_map/ppermute | solution.py:462
  220.6 4.0 %collective-permute-done.51.refs_18_ = bf16[8,64,128]{2,1,0:T(8,128)(2,1)S(1)} collective-permute-done((bf16[8,64,128]{2,1,0:T(8,128)(2,1)}, bf16[8,64,128]{2,1,0:T(8,128)(2,1)S(1)}, u32[]{:S(2)}, u32[]{:S(2)}) %collective-permute-start.51) | collective-permute-done | bytes 131104 | tf_op jit(solution)/shard_map/ppermute | solution.py:462
  225.2 5.1 %collective-permute-done.52.refs_19_ = bf16[8,64,128]{2,1,0:T(8,128)(2,1)S(1)} collective-permute-done((bf16[8,64,128]{2,1,0:T(8,128)(2,1)}, bf16[8,64,128]{2,1,0:T(8,128)(2,1)S(1)}, u32[]{:S(2)}, u32[]{:S(2)}) %collective-permute-start.52) | collective-permute-done | bytes 131104 | tf_op jit(solution)/shard_map/ppermute | solution.py:462
  232.9 6.9 %collective-permute-done.53.refs_20_ = bf16[8,64,128]{2,1,0:T(8,128)(2,1)S(1)} collective-permute-done((bf16[8,64,128]{2,1,0:T(8,128)(2,1)}, bf16[8,64,128]{2,1,0:T(8,128)(2,1)S(1)}, u32[]{:S(2)}, u32[]{:S(2)}) %collective-permute-start.53) | collective-permute-done | bytes 131104 | tf_op jit(solution)/shard_map/ppermute | solution.py:462
  239.8 8.8 %collective-permute-done.54.refs_21_ = bf16[8,64,128]{2,1,0:T(8,128)(2,1)S(1)} collective-permute-done((bf16[8,64,128]{2,1,0:T(8,128)(2,1)}, bf16[8,64,128]{2,1,0:T(8,128)(2,1)S(1)}, u32[]{:S(2)}, u32[]{:S(2)}) %collective-permute-start.54) | collective-permute-done | bytes 131104 | tf_op jit(solution)/shard_map/ppermute | solution.py:462
  250.0 6.1 %collective-permute-done.55.refs_22_ = bf16[8,64,128]{2,1,0:T(8,128)(2,1)S(1)} collective-permute-done((bf16[8,64,128]{2,1,0:T(8,128)(2,1)}, bf16[8,64,128]{2,1,0:T(8,128)(2,1)S(1)}, u32[]{:S(2)}, u32[]{:S(2)}) %collective-permute-start.55) | collective-permute-done | bytes 131104 | tf_op jit(solution)/shard_map/ppermute | solution.py:462
  256.4 6.9 %collective-permute-done.56.refs_23_ = bf16[8,64,128]{2,1,0:T(8,128)(2,1)S(1)} collective-permute-done((bf16[8,64,128]{2,1,0:T(8,128)(2,1)}, bf16[8,64,128]{2,1,0:T(8,128)(2,1)S(1)}, u32[]{:S(2)}, u32[]{:S(2)}) %collective-permute-start.56) | collective-permute-done | bytes 131104 | tf_op jit(solution)/shard_map/ppermute | solution.py:462
  270.8 14.8 %lon_filter.2.refs_32_ = f32[1024,2048]{1,0:T(8,128)} custom-call(s32[9]{0:T(128)} %stack.28.ids, bf16[4,128,128]{2,1,0:T(8,128)(2,1)} %get-tuple-element.93.refs_0_, bf16[4,128,128]{2,1,0:T(8,128)(2,1)} %copy-done.11, bf16[4,128,128]{2,1,0:T(8,128)(2,1)} %copy-done.12, bf16[4,128,128]{2,1,0:T(8,128)(2,1)} %copy-done.13, ...), custom_call_target="tpu_custom_call" | custom-call | tf_op jit(solution)/shard_map/lon_filter/pallas_call | solution.py:755
  286.4 14.5 %lon_filter.3 = f32[1024,2048]{1,0:T(8,128)} custom-call(s32[9]{0:T(128)} %stack.28.ids, bf16[4,128,128]{2,1,0:T(8,128)(2,1)} %get-tuple-element.93.refs_0_, bf16[4,128,128]{2,1,0:T(8,128)(2,1)} %copy-done.11, bf16[4,128,128]{2,1,0:T(8,128)(2,1)} %copy-done.12, bf16[4,128,128]{2,1,0:T(8,128)(2,1)} %copy-done.13, ...), custom_call_target="tpu_custom_call", output_to_operand_aliasing={{}: (33, {})} | custom-call | tf_op jit(solution)/shard_map/lon_filter/pallas_call | solution.py:755
  (179 shorter events, 66.7 us)
Async XLA Ops:
  9.9 25.7 %collective-permute-start.9 = (f32[2,32,256]{2,1,0:T(8,128)S(1)}, f32[2,32,256]{2,1,0:T(8,128)S(1)}, u32[]{:S(2)}, u32[]{:S(2)}) collective-permute-start(f32[2,32,256]{2,1,0:T(8,128)S(1)} %pad_maximum_fusion.2), channel_id=1, source_target_pairs={{0,4},{1,5},{2,6},{3,7},{4,0},{5,1},{6,2},{7,3},{8,12},{9,13},{10,... | collective-permute-start | bytes 196616 | tf_op jit(solution)/shard_map/ppermute | solution.py:462
  35.6 10.2 %collective-permute-start.10 = (f32[4,32,256]{2,1,0:T(8,128)S(1)}, f32[4,32,256]{2,1,0:T(8,128)S(1)}, u32[]{:S(2)}, u32[]{:S(2)}) collective-permute-start(f32[4,32,256]{2,1,0:T(8,128)S(1)} %pad_maximum_fusion.1), channel_id=1, source_target_pairs={{0,8},{8,0},{16,24},{24,16},{1,9},{9,1},{17,25},{25,17},{2,10},{10... | collective-permute-start | bytes 393224 | tf_op jit(solution)/shard_map/ppermute | solution.py:462
  56.9 101.3 %collective-permute-start.44 = (bf16[256,2048]{1,0:T(8,128)(2,1)S(1)}, bf16[256,2048]{1,0:T(8,128)(2,1)S(1)}, u32[]{:S(2)}, u32[]{:S(2)}) collective-permute-start(bf16[256,2048]{1,0:T(8,128)(2,1)S(1)} %constant_dynamic-slice_fusion.refs_24_), channel_id=1, source_target_pairs={{0,8},{1,17},{2,10},{3,19},{4,12},{5,21},{6,14},{7,23},{8,0},{9,25... | collective-permute-start | bytes 3145736 | tf_op jit(solution)/shard_map/ppermute | solution.py:520
  60.6 14.0 %collective-permute-start.4 = (f32[128,128]{1,0:T(8,128)}, f32[128,128]{1,0:T(8,128)S(1)}, u32[]{:S(2)}, u32[]{:S(2)}) collective-permute-start(f32[128,128]{1,0:T(8,128)} %get-tuple-element.83), channel_id=1, source_target_pairs={{0,8},{8,0},{16,24},{24,16},{1,9},{9,1},{17,25},{25,17},{2,10},{10... | collective-permute-start | bytes 196616 | tf_op jit(solution)/shard_map/ppermute | solution.py:470
  64.1 10.5 %collective-permute-start.7 = (f32[8,8,256]{2,1,0:T(8,128)}, f32[8,8,256]{2,1,0:T(8,128)S(1)}, u32[]{:S(2)}, u32[]{:S(2)}) collective-permute-start(f32[8,8,256]{2,1,0:T(8,128)} %get-tuple-element.84), channel_id=1, source_target_pairs={{1,2},{2,1},{3,4},{4,3},{5,6},{6,5},{9,10},{10,9},{11,12},{12,11},... | collective-permute-start | bytes 196616 | tf_op jit(solution)/shard_map/ppermute | solution.py:470
  94.5 29.1 %collective-permute-start.14 = (bf16[4,128,256]{2,1,0:T(8,128)(2,1)}, bf16[4,128,256]{2,1,0:T(8,128)(2,1)S(1)}, u32[]{:S(2)}, u32[]{:S(2)}) collective-permute-start(bf16[4,128,256]{2,1,0:T(8,128)(2,1)} %get-tuple-element.91), channel_id=1, source_target_pairs={{0,16},{8,24},{16,0},{24,8},{1,17},{9,25},{17,1},{25,9},{2,18},{10... | collective-permute-start | bytes 786440 | tf_op jit(solution)/shard_map/ppermute | solution.py:462
  95.6 29.3 %collective-permute-start.15 = (bf16[4,128,256]{2,1,0:T(8,128)(2,1)}, bf16[4,128,256]{2,1,0:T(8,128)(2,1)S(1)}, u32[]{:S(2)}, u32[]{:S(2)}) collective-permute-start(bf16[4,128,256]{2,1,0:T(8,128)(2,1)} %get-tuple-element.92), channel_id=1, source_target_pairs={{0,24},{8,16},{16,8},{24,0},{1,25},{9,17},{17,9},{25,1},{2,26},{10... | collective-permute-start | bytes 786440 | tf_op jit(solution)/shard_map/ppermute | solution.py:462
  98.0 28.5 %collective-permute-start.23 = (bf16[4,128,256]{2,1,0:T(8,128)(2,1)}, bf16[4,128,256]{2,1,0:T(8,128)(2,1)S(1)}, u32[]{:S(2)}, u32[]{:S(2)}) collective-permute-start(bf16[4,128,256]{2,1,0:T(8,128)(2,1)} %get-tuple-element.102), channel_id=1, source_target_pairs={{0,8},{8,0},{16,24},{24,16},{1,9},{9,1},{17,25},{25,17},{2,10},{10... | collective-permute-start | bytes 786440 | tf_op jit(solution)/shard_map/ppermute | solution.py:462
  103.9 24.7 %collective-permute-start.24 = (bf16[4,128,256]{2,1,0:T(8,128)(2,1)}, bf16[4,128,256]{2,1,0:T(8,128)(2,1)}, u32[]{:S(2)}, u32[]{:S(2)}) collective-permute-start(bf16[4,128,256]{2,1,0:T(8,128)(2,1)} %get-tuple-element.103), channel_id=1, source_target_pairs={{0,16},{8,24},{16,0},{24,8},{1,17},{9,25},{17,1},{25,9},{2,18},{10... | collective-permute-start | bytes 786440 | tf_op jit(solution)/shard_map/ppermute | solution.py:462
  124.4 28.0 %collective-permute-start.33 = (bf16[8,128,256]{2,1,0:T(8,128)(2,1)}, bf16[8,128,256]{2,1,0:T(8,128)(2,1)S(1)}, u32[]{:S(2)}, u32[]{:S(2)}) collective-permute-start(bf16[8,128,256]{2,1,0:T(8,128)(2,1)} %get-tuple-element.116), channel_id=1, source_target_pairs={{0,8},{8,0},{16,24},{24,16},{1,9},{9,1},{17,25},{25,17},{2,10},{10... | collective-permute-start | bytes 1572872 | tf_op jit(solution)/shard_map/ppermute | solution.py:462
  125.5 26.8 %collective-permute-start.34 = (bf16[8,128,256]{2,1,0:T(8,128)(2,1)}, bf16[8,128,256]{2,1,0:T(8,128)(2,1)S(1)}, u32[]{:S(2)}, u32[]{:S(2)}) collective-permute-start(bf16[8,128,256]{2,1,0:T(8,128)(2,1)} %get-tuple-element.117), channel_id=1, source_target_pairs={{0,16},{8,24},{16,0},{24,8},{1,17},{9,25},{17,1},{25,9},{2,18},{10... | collective-permute-start | bytes 1572872 | tf_op jit(solution)/shard_map/ppermute | solution.py:462
  126.5 25.9 %collective-permute-start.35 = (bf16[8,128,256]{2,1,0:T(8,128)(2,1)}, bf16[8,128,256]{2,1,0:T(8,128)(2,1)}, u32[]{:S(2)}, u32[]{:S(2)}) collective-permute-start(bf16[8,128,256]{2,1,0:T(8,128)(2,1)} %get-tuple-element.118), channel_id=1, source_target_pairs={{0,24},{8,16},{16,8},{24,0},{1,25},{9,17},{17,9},{25,1},{2,26},{10... | collective-permute-start | bytes 1572872 | tf_op jit(solution)/shard_map/ppermute | solution.py:462
  128.6 19.7 %collective-permute-start.25 = (bf16[4,128,256]{2,1,0:T(8,128)(2,1)}, bf16[4,128,256]{2,1,0:T(8,128)(2,1)}, u32[]{:S(2)}, u32[]{:S(2)}) collective-permute-start(bf16[4,128,256]{2,1,0:T(8,128)(2,1)} %get-tuple-element.104), channel_id=1, source_target_pairs={{0,24},{8,16},{16,8},{24,0},{1,25},{9,17},{17,9},{25,1},{2,26},{10... | collective-permute-start | bytes 786440 | tf_op jit(solution)/shard_map/ppermute | solution.py:462
  157.8 48.6 %collective-permute-start.46 = (bf16[256,2048]{1,0:T(8,128)(2,1)S(1)}, bf16[256,2048]{1,0:T(8,128)(2,1)S(1)}, u32[]{:S(2)}, u32[]{:S(2)}) collective-permute-start(bf16[256,2048]{1,0:T(8,128)(2,1)S(1)} %constant_dynamic-slice_fusion.refs_24_), channel_id=1, source_target_pairs={{0,16},{1,9},{2,18},{3,11},{4,20},{5,13},{6,22},{7,15},{8,24},{9,1... | collective-permute-start | bytes 3145736 | tf_op jit(solution)/shard_map/ppermute | solution.py:520
  158.2 49.5 %collective-permute-start.48 = (bf16[256,2048]{1,0:T(8,128)(2,1)S(1)}, bf16[256,2048]{1,0:T(8,128)(2,1)}, u32[]{:S(2)}, u32[]{:S(2)}) collective-permute-start(bf16[256,2048]{1,0:T(8,128)(2,1)S(1)} %collective-permute-done.44.refs_26_), channel_id=1, source_target_pairs={{0,16},{1,9},{2,18},{3,11},{4,20},{5,13},{6,22},{7,15},{8,24},{9,1... | collective-permute-start | bytes 3145736 | tf_op jit(solution)/shard_map/ppermute | solution.py:520
  160.9 10.3 %collective-permute-start.18 = (bf16[4,128,128]{2,1,0:T(8,128)(2,1)}, bf16[4,128,128]{2,1,0:T(8,128)(2,1)S(1)}, u32[]{:S(2)}, u32[]{:S(2)}) collective-permute-start(bf16[4,128,128]{2,1,0:T(8,128)(2,1)} %get-tuple-element.96), channel_id=1, source_target_pairs={{0,3},{1,2},{2,1},{3,0},{4,7},{5,6},{6,5},{7,4},{8,11},{9,10},{10,... | collective-permute-start | bytes 393224 | tf_op jit(solution)/shard_map/ppermute | solution.py:462
  161.7 10.7 %collective-permute-start.19 = (bf16[4,128,128]{2,1,0:T(8,128)(2,1)}, bf16[4,128,128]{2,1,0:T(8,128)(2,1)}, u32[]{:S(2)}, u32[]{:S(2)}) collective-permute-start(bf16[4,128,128]{2,1,0:T(8,128)(2,1)} %get-tuple-element.97), channel_id=1, source_target_pairs={{0,4},{1,5},{2,6},{3,7},{4,0},{5,1},{6,2},{7,3},{8,12},{9,13},{10,... | collective-permute-start | bytes 393224 | tf_op jit(solution)/shard_map/ppermute | solution.py:462
  169.2 14.4 %collective-permute-start.20 = (bf16[4,128,128]{2,1,0:T(8,128)(2,1)}, bf16[4,128,128]{2,1,0:T(8,128)(2,1)}, u32[]{:S(2)}, u32[]{:S(2)}) collective-permute-start(bf16[4,128,128]{2,1,0:T(8,128)(2,1)} %get-tuple-element.98), channel_id=1, source_target_pairs={{0,5},{1,4},{2,7},{3,6},{4,1},{5,0},{6,3},{7,2},{8,13},{9,12},{10,... | collective-permute-start | bytes 393224 | tf_op jit(solution)/shard_map/ppermute | solution.py:462
  171.2 12.4 %collective-permute-start.21 = (bf16[4,128,128]{2,1,0:T(8,128)(2,1)}, bf16[4,128,128]{2,1,0:T(8,128)(2,1)}, u32[]{:S(2)}, u32[]{:S(2)}) collective-permute-start(bf16[4,128,128]{2,1,0:T(8,128)(2,1)} %get-tuple-element.99), channel_id=1, source_target_pairs={{0,6},{1,7},{2,4},{3,5},{4,2},{5,3},{6,0},{7,1},{8,14},{9,15},{10,... | collective-permute-start | bytes 393224 | tf_op jit(solution)/shard_map/ppermute | solution.py:462
  172.4 13.6 %collective-permute-start.22 = (bf16[4,128,128]{2,1,0:T(8,128)(2,1)}, bf16[4,128,128]{2,1,0:T(8,128)(2,1)}, u32[]{:S(2)}, u32[]{:S(2)}) collective-permute-start(bf16[4,128,128]{2,1,0:T(8,128)(2,1)} %get-tuple-element.100), channel_id=1, source_target_pairs={{0,7},{1,6},{2,5},{3,4},{4,3},{5,2},{6,1},{7,0},{8,15},{9,14},{10,... | collective-permute-start | bytes 393224 | tf_op jit(solution)/shard_map/ppermute | solution.py:462
  188.6 16.1 %collective-permute-start.29 = (bf16[4,128,128]{2,1,0:T(8,128)(2,1)}, bf16[4,128,128]{2,1,0:T(8,128)(2,1)}, u32[]{:S(2)}, u32[]{:S(2)}) collective-permute-start(bf16[4,128,128]{2,1,0:T(8,128)(2,1)} %get-tuple-element.110), channel_id=1, source_target_pairs={{0,4},{1,5},{2,6},{3,7},{4,0},{5,1},{6,2},{7,3},{8,12},{9,13},{10,... | collective-permute-start | bytes 393224 | tf_op jit(solution)/shard_map/ppermute | solution.py:462
  190.6 17.1 %collective-permute-start.30 = (bf16[4,128,128]{2,1,0:T(8,128)(2,1)}, bf16[4,128,128]{2,1,0:T(8,128)(2,1)}, u32[]{:S(2)}, u32[]{:S(2)}) collective-permute-start(bf16[4,128,128]{2,1,0:T(8,128)(2,1)} %get-tuple-element.111), channel_id=1, source_target_pairs={{0,5},{1,4},{2,7},{3,6},{4,1},{5,0},{6,3},{7,2},{8,13},{9,12},{10,... | collective-permute-start | bytes 393224 | tf_op jit(solution)/shard_map/ppermute | solution.py:462
  193.0 14.9 %collective-permute-start.31 = (bf16[4,128,128]{2,1,0:T(8,128)(2,1)}, bf16[4,128,128]{2,1,0:T(8,128)(2,1)}, u32[]{:S(2)}, u32[]{:S(2)}) collective-permute-start(bf16[4,128,128]{2,1,0:T(8,128)(2,1)} %get-tuple-element.112), channel_id=1, source_target_pairs={{0,6},{1,7},{2,4},{3,5},{4,2},{5,3},{6,0},{7,1},{8,14},{9,15},{10,... | collective-permute-start | bytes 393224 | tf_op jit(solution)/shard_map/ppermute | solution.py:462
  207.7 55.6 %collective-permute-start.43 = (bf16[256,2048]{1,0:T(8,128)(2,1)S(1)}, bf16[256,2048]{1,0:T(8,128)(2,1)S(1)}, u32[]{:S(2)}, u32[]{:S(2)}) collective-permute-start(bf16[256,2048]{1,0:T(8,128)(2,1)S(1)} %constant_dynamic-slice_fusion.refs_24_), channel_id=1, source_target_pairs={{0,1},{1,0},{2,3},{3,2},{4,5},{5,4},{6,7},{7,6},{8,9},{9,8},{10,11... | collective-permute-start | bytes 3145736 | tf_op jit(solution)/shard_map/ppermute | solution.py:462
  207.9 56.5 %collective-permute-start.45 = (bf16[256,2048]{1,0:T(8,128)(2,1)S(1)}, bf16[256,2048]{1,0:T(8,128)(2,1)S(1)}, u32[]{:S(2)}, u32[]{:S(2)}) collective-permute-start(bf16[256,2048]{1,0:T(8,128)(2,1)S(1)} %collective-permute-done.44.refs_26_), channel_id=1, source_target_pairs={{0,1},{1,0},{2,3},{3,2},{4,5},{5,4},{6,7},{7,6},{8,9},{9,8},{10,11... | collective-permute-start | bytes 3145736 | tf_op jit(solution)/shard_map/ppermute | solution.py:462
  212.6 52.7 %collective-permute-start.47 = (bf16[256,2048]{1,0:T(8,128)(2,1)S(1)}, bf16[256,2048]{1,0:T(8,128)(2,1)S(1)}, u32[]{:S(2)}, u32[]{:S(2)}) collective-permute-start(bf16[256,2048]{1,0:T(8,128)(2,1)S(1)} %collective-permute-done.46.refs_28_), channel_id=1, source_target_pairs={{0,1},{1,0},{2,3},{3,2},{4,5},{5,4},{6,7},{7,6},{8,9},{9,8},{10,11... | collective-permute-start | bytes 3145736 | tf_op jit(solution)/shard_map/ppermute | solution.py:462
  212.6 55.5 %collective-permute-start.49 = (bf16[256,2048]{1,0:T(8,128)(2,1)}, bf16[256,2048]{1,0:T(8,128)(2,1)S(1)}, u32[]{:S(2)}, u32[]{:S(2)}) collective-permute-start(bf16[256,2048]{1,0:T(8,128)(2,1)} %collective-permute-done.48.refs_30_), channel_id=1, source_target_pairs={{0,1},{1,0},{2,3},{3,2},{4,5},{5,4},{6,7},{7,6},{8,9},{9,8},{10,11... | collective-permute-start | bytes 3145736 | tf_op jit(solution)/shard_map/ppermute | solution.py:462
  263.3 22.3 %collective-permute-start.38 = (bf16[8,64,128]{2,1,0:T(8,128)(2,1)}, bf16[8,64,128]{2,1,0:T(8,128)(2,1)}, u32[]{:S(2)}, u32[]{:S(2)}) collective-permute-start(bf16[8,64,128]{2,1,0:T(8,128)(2,1)} %get-tuple-element.125), channel_id=1, source_target_pairs={{0,3},{1,2},{2,1},{3,0},{4,7},{5,6},{6,5},{7,4},{8,11},{9,10},{10,... | collective-permute-start | bytes 393224 | tf_op jit(solution)/shard_map/ppermute | solution.py:462
  263.3 22.2 %collective-permute-start.39 = (bf16[8,64,128]{2,1,0:T(8,128)(2,1)}, bf16[8,64,128]{2,1,0:T(8,128)(2,1)S(1)}, u32[]{:S(2)}, u32[]{:S(2)}) collective-permute-start(bf16[8,64,128]{2,1,0:T(8,128)(2,1)} %get-tuple-element.126), channel_id=1, source_target_pairs={{0,4},{1,5},{2,6},{3,7},{4,0},{5,1},{6,2},{7,3},{8,12},{9,13},{10,... | collective-permute-start | bytes 393224 | tf_op jit(solution)/shard_map/ppermute | solution.py:462
  264.4 21.2 %collective-permute-start.40 = (bf16[8,64,128]{2,1,0:T(8,128)(2,1)}, bf16[8,64,128]{2,1,0:T(8,128)(2,1)S(1)}, u32[]{:S(2)}, u32[]{:S(2)}) collective-permute-start(bf16[8,64,128]{2,1,0:T(8,128)(2,1)} %get-tuple-element.127), channel_id=1, source_target_pairs={{0,5},{1,4},{2,7},{3,6},{4,1},{5,0},{6,3},{7,2},{8,13},{9,12},{10,... | collective-permute-start | bytes 393224 | tf_op jit(solution)/shard_map/ppermute | solution.py:462
  265.4 20.2 %collective-permute-start.41 = (bf16[8,64,128]{2,1,0:T(8,128)(2,1)}, bf16[8,64,128]{2,1,0:T(8,128)(2,1)S(1)}, u32[]{:S(2)}, u32[]{:S(2)}) collective-permute-start(bf16[8,64,128]{2,1,0:T(8,128)(2,1)} %get-tuple-element.128), channel_id=1, source_target_pairs={{0,6},{1,7},{2,4},{3,5},{4,2},{5,3},{6,0},{7,1},{8,14},{9,15},{10,... | collective-permute-start | bytes 393224 | tf_op jit(solution)/shard_map/ppermute | solution.py:462
  269.1 16.5 %collective-permute-start.42 = (bf16[8,64,128]{2,1,0:T(8,128)(2,1)}, bf16[8,64,128]{2,1,0:T(8,128)(2,1)S(1)}, u32[]{:S(2)}, u32[]{:S(2)}) collective-permute-start(bf16[8,64,128]{2,1,0:T(8,128)(2,1)} %get-tuple-element.129), channel_id=1, source_target_pairs={{0,7},{1,6},{2,5},{3,4},{4,3},{5,2},{6,1},{7,0},{8,15},{9,14},{10,... | collective-permute-start | bytes 393224 | tf_op jit(solution)/shard_map/ppermute | solution.py:462
  (64 other events, 1283.7 us)

commit v2 on v1

--- a/solution.py
+++ b/solution.py
@@ -37,14 +37,14 @@
     return pl.ds(pl.multiple_of(start, SUB), SUB)
 
 
-def x_fluxes(mu, coef, damp, east):
-    flux = coef * damp * mu
+def x_fluxes(damped, coef, east):
+    flux = coef * damped
     part = east * flux
     return part, flux - part
 
 
-def stencil(mu, px, qx, up_x, down_x, coef, damp, north, halo_up, halo_down):
-    flux = coef * damp * mu
+def stencil(mu, px, qx, up_x, down_x, damped, coef, north, halo_up, halo_down):
+    flux = coef * damped
     py = north * flux
     qy = flux - py
     base = mu - px + qx - py + qy + up_x - down_x
@@ -110,10 +110,8 @@
             turn = lax.rem(2 * slot + 1 + band * 64, LANES)
             mine = (lane // 2) == slot + 32 * band
             mus = [mu_ref[f, 0, rows_at(s)] for s in starts]
-            pq = [
-                x_fluxes(m, cour_ref[1, 0, 0, rows_at(s)], damp[f, rows_at(s)], east[rows_at(s)])
-                for m, s in zip(mus, starts)
-            ]
+            damped = [m * damp[f, rows_at(s)] for m, s in zip(mus, starts)]
+            pq = [x_fluxes(m, cour_ref[1, 0, 0, rows_at(s)], east[rows_at(s)]) for m, s in zip(damped, starts)]
             px = [v[0] for v in pq]
             qx = [v[1] for v in pq]
             qx[0] = qx[0] * keep_low
@@ -122,7 +120,7 @@
                 at = rows_at(starts[t + 1])
                 up, down = shifted(px[t + 1], px[t + 2], qx[t], qx[t + 1])
                 new, py, qy = stencil(
-                    mus[t + 1], px[t + 1], qx[t + 1], up, down, cour_ref[1, 1, 0, at], damp[f, at], north[at],
+                    mus[t + 1], px[t + 1], qx[t + 1], up, down, damped[t + 1], cour_ref[1, 1, 0, at], north[at],
                     jnp.zeros((SUB, LANES), F32), jnp.zeros((SUB, LANES), F32),
                 )
                 for k in range(tiles):
@@ -142,8 +140,8 @@
         slot = level * fields + f
         turn = 2 * slot + 1
         mine = (lane // 2) == slot
-        px, _ = x_fluxes(mu_ref[f, 0, low], cour_ref[1, 0, 0, low], damp[f, low], east[low])
-        _, qx = x_fluxes(mu_ref[f, 0, high], cour_ref[1, 0, 0, high], damp[f, high], east[high])
+        px, _ = x_fluxes(mu_ref[f, 0, low] * damp[f, low], cour_ref[1, 0, 0, low], east[low])
+        _, qx = x_fluxes(mu_ref[f, 0, high] * damp[f, high], cour_ref[1, 0, 0, high], east[high])
         xr_ref[level, f : f + 1] = px[:1]
         xr_ref[level, fields + f : fields + f + 1] = qx[SUB - 1 :]
         px_edge = pltpu.roll(jnp.where(last, px[:, edge], px[:, :LANES]), turn, 1)
@@ -277,7 +275,7 @@
     def channel_group(level, carry):
         for f in range(fields):
             slot = level * fields + f
-            vals, px, qx = [], [], []
+            vals, damped, px, qx = [], [], [], []
             for t in range(inside + 2):
                 ref, r = mus[t]
                 value = ref[f, level, r : r + SUB]
@@ -291,8 +289,10 @@
                 if t == inside:
                     value = value + jnp.where((sub == SUB - 1) & at_end, x1_ref[level, f : f + 1], 0.0)
                 ref, r = cxs[t]
-                p, q = x_fluxes(value, ref[0, 0, level, r : r + SUB], damp[f, SUB * t : SUB * (t + 1)], east[SUB * t : SUB * (t + 1)])
+                weighed = value * damp[f, SUB * t : SUB * (t + 1)]
+                p, q = x_fluxes(weighed, ref[0, 0, level, r : r + SUB], east[SUB * t : SUB * (t + 1)])
                 vals.append(value)
+                damped.append(weighed)
                 px.append(p)
                 qx.append(q)
             halo_low = pick(even_col, x2b_ref[level, fields + f : fields + f + 1], x2a_ref[level, fields + f : fields + f + 1])
@@ -300,12 +300,11 @@
             qx[0] = jnp.where(at_start, jnp.broadcast_to(halo_low, (SUB, width)), qx[0])
             px[-1] = jnp.where(at_end, jnp.broadcast_to(halo_high, (SUB, width)), px[-1])
             for t in range(inside):
-                here = slice(SUB * (t + 1), SUB * (t + 2))
                 mine = slice(SUB * t, SUB * (t + 1))
                 up, down = shifted(px[t + 1], px[t + 2], qx[t], qx[t + 1])
                 halo = pltpu.roll(m2_ref[rows_at(places[t + 1])], (126 - 2 * slot - 64 * bands[t + 1]) & (LANES - 1), 1)
                 new, _, _ = stencil(
-                    vals[t + 1], px[t + 1], qx[t + 1], up, down, cour_ref[0, 1, level, mine], damp[f, here], north[mine], halo, -halo
+                    vals[t + 1], px[t + 1], qx[t + 1], up, down, damped[t + 1], cour_ref[0, 1, level, mine], north[mine], halo, -halo
                 )
                 gathered = jnp.zeros((SUB, LANES), F32)
                 for r in range(parts):
@@ -407,27 +406,21 @@
     lasts = refs[n_first : n_first + cols]
     filters = refs[n_first + cols : n_first + cols + 2 * parts]
     rest = refs[n_first + cols + 2 * parts + (1 if aliased else 0) :]
-    out, lines, buffer, stage, in_sem, out_sem = rest
+    out, lines, stage, sem = rest
     channels, _, lon = lasts[0].shape
     wide = lines.shape[1] // cols
     rows = channels * height
     block = filters[0].shape[0]
-    steps = 2 * parts
     strips = block // LANES
 
-    def fetch(j):
-        return pltpu.make_async_copy(filters[j], buffer.at[j % 2], in_sem.at[j % 2])
-
-    def owner(j):
+    def flush(j, k):
         side = ids[8] if j % 2 == 0 else 1 - ids[8]
         even, odd = owners[j // 2]
-        return (ids[0] ^ jnp.where(side == 0, even, odd)) * 2 + side
-
-    def flush(j, k):
-        at = pl.ds(pl.multiple_of(owner(j) * block + k * LANES, LANES), LANES)
-        return pltpu.make_async_copy(stage.at[j % 2, k], out.at[pl.ds(half * rows, rows), at], out_sem.at[j % 2, k])
-
-    fetch(0).start()
+        owner = (ids[0] ^ jnp.where(side == 0, even, odd)) * 2 + side
+        at = pl.ds(pl.multiple_of(owner * block + k * LANES, LANES), LANES)
+        slot = j % 4
+        return pltpu.make_async_copy(stage.at[slot, k], out.at[pl.ds(half * rows, rows), at], sem.at[slot, k])
+
     for s in range(cols):
         base = pl.multiple_of((ids[1] ^ s) * wide, LANES)
         for c in range(channels):
@@ -438,21 +431,18 @@
                 ref = firsts[(b * groups + c // each) * cols + s]
                 lines[put, pl.ds(base + b * lon, lon)] = ref[c % each, half * height : (half + 1) * height]
             lines[put, pl.ds(base + wide - lon, lon)] = lasts[s][c]
-    for j in range(steps):
-        if j + 1 < steps:
-            fetch(j + 1).start()
-        fetch(j).wait()
-        if j >= 2:
+    for p in range(parts):
+        right = jnp.concatenate([filters[2 * p][...], filters[2 * p + 1][...]], axis=0)
+        acc = lax.dot_general(lines[...], right, NT, preferred_element_type=F32)
+        for j in (2 * p, 2 * p + 1):
             for k in range(strips):
-                flush(j - 2, k).wait()
-        acc = lax.dot_general(lines[...], buffer[j % 2], NT, preferred_element_type=F32)
-        for c in range(channels):
-            for k in range(strips):
-                at = slice(k * LANES, (k + 1) * LANES)
-                stage[j % 2, k, pl.ds(c, height, stride=channels), :] = acc[c * height : (c + 1) * height, at]
-        for k in range(strips):
-            flush(j, k).start()
-    for j in (steps - 2, steps - 1):
+                if j >= 4:
+                    flush(j - 4, k).wait()
+                begin = (j % 2) * block + k * LANES
+                for c in range(channels):
+                    stage[j % 4, k, pl.ds(c, height, stride=channels), :] = acc[c * height : (c + 1) * height, begin : begin + LANES]
+                flush(j, k).start()
+    for j in range(max(0, 2 * parts - 4), 2 * parts):
         for k in range(strips):
             flush(j, k).wait()
 
@@ -519,8 +509,9 @@
             pairs.append((i, (row ^ turns[col % 2][stage]) * cols_count + col))
         return [lax.ppermute(piece, ("row", "col"), pairs) for piece in pieces]
 
-    gathered += gather(0, gathered)
-    owners += [(turns[0][0], turns[1][0])]
+    direct = []
+    for stage in range(len(orders)):
+        direct += gather(stage, gathered[:1])
 
     nest = jnp.transpose(nest_sens, (0, 2, 1))
     fine_lat, fine_lon = nest.shape[1:]
@@ -714,8 +705,8 @@
         early = token
         moved, token = smooth(sent[-1], h * half_height, half_height, token)
         lasts.append(moved)
-    for stage in range(1, len(orders)):
-        gathered += gather(stage, [after(piece, early) for piece in gathered])
+    for stage in range(len(orders)):
+        gathered += [direct[stage]] + gather(stage, [after(piece, early) for piece in gathered[1:]])
         owners += [(a ^ turns[0][stage], b ^ turns[1][stage]) for a, b in owners]
     filters = []
     for piece in gathered:
@@ -740,14 +731,12 @@
         call = pl.pallas_call(
             functools.partial(lon_filter_part, h, half_height, cols_count, rows_count, len(firsts), aliased, owners),
             out_shape=shape_of((2 * rows, n_lon)),
-            in_specs=[SMEM_SPEC] + [VMEM_SPEC] * (len(firsts) + cols_count) + [ANY_SPEC] * (2 * rows_count + aliased),
+            in_specs=[SMEM_SPEC] + [VMEM_SPEC] * (len(firsts) + cols_count + 2 * rows_count) + [ANY_SPEC] * aliased,
             out_specs=ANY_SPEC,
             scratch_shapes=[
                 pltpu.VMEM((rows, n_lon), BF16),
-                pltpu.VMEM((2, height, n_lon), BF16),
-                pltpu.VMEM((2, height // LANES, rows, LANES), F32),
-                pltpu.SemaphoreType.DMA((2,)),
-                pltpu.SemaphoreType.DMA((2, height // LANES)),
+                pltpu.VMEM((4, height // LANES, rows, LANES), F32),
+                pltpu.SemaphoreType.DMA((4, height // LANES)),
             ],
             input_output_aliases={len(operands) - 1: 0} if aliased else {},
             name="lon_filter",

time: 303 us -> 301 us (level); the launches traced: 301 us -> 295 us
  starting transfers between devices: 70.4 us -> 88.9 us
  waiting for transfers between devices: 105 us -> 90.5 us
  Pallas kernels: 115 us -> 108 us
    ppermute x46, starting transfers between devices: 53 us -> 70.6 us  [swap(): return lax.ppermute(value, axis, [(i, i ^ mask) for i in range(count)])]
    ppermute x46, waiting for transfers between devices: 99.4 us -> 89.5 us  [swap(): return lax.ppermute(value, axis, [(i, i ^ mask) for i in range(count)])]
    pallas_call x2, Pallas kernels: 29.3 us -> 22.7 us  [shards(): out = call(*operands)]
    ppermute x8, waiting for transfers between devices: 5.98 us -> 1.05 us  [neighbours(): return lax.ppermute(value, axis, pairs)]
  transfers between devices with their start and end apart: 57 -> 57, of which waited for: 21 -> 20; matrix products, arithmetic and copies ran while one was open for 0% -> 0% of each run, Pallas kernels for 33% -> 26%
where the time goes in v2:
time: 301 us; the launch traced here: 295 us
  Pallas kernels  108 us (36%)
  waiting for transfers between devices  90.5 us (30%)
  starting transfers between devices  88.9 us (30%)
  local copies, waits for them, and re-layouts  4.4 us (1%)
    ppermute x46, waiting for transfers between devices, swap(): return lax.ppermute(value, axis, [(i, i ^ mask) for i in range(count)])  89.5 us
    ppermute x46, starting transfers between devices, swap(): return lax.ppermute(value, axis, [(i, i ^ mask) for i in range(count)])  70.6 us
    pallas_call x2, Pallas kernels, control(): pl.pallas_call(functools.partial(second_step, band, rows_count), grid=(gr...  38.5 us
    pallas_call x2, Pallas kernels, shards(): out = call(*operands)  22.7 us
    pallas_call x1, Pallas kernels, shards(): mu1, ef, em, ew, xr, xm, xw = call(mu, courant, limiter, directions)  22.5 us
    pallas_call x4, Pallas kernels, smooth(): outs = call(ids, *pieces, filt)  17.2 us
    ppermute x8, starting transfers between devices, neighbours(): return lax.ppermute(value, axis, pairs)  14.1 us
  transfers between devices with their start and end apart: 57, of which 20 were waited for; matrix products, arithmetic and copies ran while one was open for 0% of the time, Pallas kernels for 26%

profile of v2, /device:TPU:0, one launch (start us, length us, event | category | flops | bytes accessed | tf_op | source)
XLA Modules:
  0.0 295.1 jit_solution(5420459311806366061)
XLA Ops:
  4.0 3.1 %collective-permute-start.8 = (f32[1,32,256]{2,1,0:T(8,128)}, f32[1,32,256]{2,1,0:T(8,128)S(1)}, u32[]{:S(2)}, u32[]{:S(2)}) collective-permute-start(f32[1,32,256]{2,1,0:T(8,128)} %bitcast.16), channel_id=1, source_target_pairs={{0,2},{1,3},{2,0},{3,1},{4,6},{5,7},{6,4},{7,5},{8,10},{9,11},{10,... | collective-permute-start | bytes 98312 | tf_op jit(solution)/shard_map/ppermute | solution.py:452
  9.9 3.0 %collective-permute-start.9 = (f32[2,32,256]{2,1,0:T(8,128)S(1)}, f32[2,32,256]{2,1,0:T(8,128)S(1)}, u32[]{:S(2)}, u32[]{:S(2)}) collective-permute-start(f32[2,32,256]{2,1,0:T(8,128)S(1)} %pad_maximum_fusion.2), channel_id=1, source_target_pairs={{0,4},{1,5},{2,6},{3,7},{4,0},{5,1},{6,2},{7,3},{8,12},{9,13},{10,... | collective-permute-start | bytes 196616 | tf_op jit(solution)/shard_map/ppermute | solution.py:452
  13.0 22.5 %first_step.1 = (f32[4,8,256,256]{3,2,1,0:T(8,128)}, f32[128,128]{1,0:T(8,128)}, f32[128,128]{1,0:T(8,128)}, f32[128,128]{1,0:T(8,128)}, f32[9,8,256]{2,1,0:T(8,...) custom-call(f32[4,8,256,256]{3,2,1,0:T(8,128)} %bitcast.14, f32[2,2,8,256,256]{4,3,2,1,0:T(8,128)} %cx_high.3, ...), custom_call_target="tpu_custom_call" | custom-call | tf_op jit(solution)/shard_map/first_step/pallas_call | solution.py:581
  37.7 4.3 %collective-permute-start = (f32[128,128]{1,0:T(8,128)}, f32[128,128]{1,0:T(8,128)S(1)}, u32[]{:S(2)}, u32[]{:S(2)}) collective-permute-start(f32[128,128]{1,0:T(8,128)} %get-tuple-element.74), channel_id=1, source_target_pairs={{0,8},{8,0},{16,24},{24,16},{1,9},{9,1},{17,25},{25,17},{2,10},{10... | collective-permute-start | bytes 196616 | tf_op jit(solution)/shard_map/ppermute | solution.py:460
  42.6 3.0 %collective-permute-start.2 = (f32[9,8,256]{2,1,0:T(8,128)}, f32[9,8,256]{2,1,0:T(8,128)S(1)}, u32[]{:S(2)}, u32[]{:S(2)}) collective-permute-start(f32[9,8,256]{2,1,0:T(8,128)} %get-tuple-element.75), channel_id=1, source_target_pairs={{0,1},{1,0},{2,3},{3,2},{4,5},{5,4},{6,7},{7,6},{8,9},{9,8},{10,11... | collective-permute-start | bytes 221192 | tf_op jit(solution)/shard_map/ppermute | solution.py:460
  46.8 9.0 %collective-permute-done.11 = f32[8,32,256]{2,1,0:T(8,128)S(1)} collective-permute-done((f32[8,32,256]{2,1,0:T(8,128)S(1)}, f32[8,32,256]{2,1,0:T(8,128)S(1)}, u32[]{:S(2)}, u32[]{:S(2)}) %collective-permute-start.11) | collective-permute-done | bytes 262176 | tf_op jit(solution)/shard_map/ppermute | solution.py:452
  65.0 3.0 %arrange.1.box_ref = f32[256,1024]{1,0:T(8,128)} custom-call(s32[9]{0:T(128)} %stack.28.ids, f32[16,32,256]{2,1,0:T(8,128)} %copy-done.9, f32[16,32,256]{2,1,0:T(8,128)} %copy-done.13), custom_call_target="tpu_custom_call" | custom-call | tf_op jit(solution)/shard_map/arrange/pallas_call | solution.py:605
  68.7 19.3 %second_step.2 = (bf16[4,128,256]{2,1,0:T(8,128)(2,1)}, bf16[4,128,256]{2,1,0:T(8,128)(2,1)}, bf16[4,128,256]{2,1,0:T(8,128)(2,1)}, bf16[4,128,256]{2,1,0:T(8,12...) custom-call(s32[9]{0:T(128)} %stack.28.ids, ...), custom_call_target="tpu_custom_call" | custom-call | tf_op jit(solution)/shard_map/second_step/pallas_call | solution.py:629
  93.8 3.7 %collective-permute-done.13.refs_1_ = bf16[4,128,256]{2,1,0:T(8,128)(2,1)S(1)} collective-permute-done((bf16[4,128,256]{2,1,0:T(8,128)(2,1)}, bf16[4,128,256]{2,1,0:T(8,128)(2,1)S(1)}, u32[]{:S(2)}, u32[]{:S(2)}) %collective-permute-start.13) | collective-permute-done | bytes 262176 | tf_op jit(solution)/shard_map/ppermute | solution.py:452
  97.5 5.0 %collective-permute-done.14.refs_2_ = bf16[4,128,256]{2,1,0:T(8,128)(2,1)S(1)} collective-permute-done((bf16[4,128,256]{2,1,0:T(8,128)(2,1)}, bf16[4,128,256]{2,1,0:T(8,128)(2,1)S(1)}, u32[]{:S(2)}, u32[]{:S(2)}) %collective-permute-start.14) | collective-permute-done | bytes 262176 | tf_op jit(solution)/shard_map/ppermute | solution.py:452
  104.0 19.2 %second_step.3 = (bf16[8,128,256]{2,1,0:T(8,128)(2,1)}, bf16[8,128,256]{2,1,0:T(8,128)(2,1)}, bf16[8,128,256]{2,1,0:T(8,128)(2,1)}, bf16[8,128,256]{2,1,0:T(8,128)(2,1)}) custom-call(s32[9]{0:T(128)} %stack.28.ids, f32[4,8,256,256]{3,2,1,0:T(8,128)} %get-tuple-element.73.mu_ref.mu_low.mu_high, f32[4,8,256,256]{3,2,1,0:T(8,128)} %get-tuple-element.73.mu_ref.mu_low.mu_high, ...), custom_call_target="tpu_custom_call" | custom-call | tf_op jit(solution)/shard_map/second_step/pallas_call | solution.py:629
  127.0 4.1 %lat_filter.4 = (bf16[4,128,128]{2,1,0:T(8,128)(2,1)}, bf16[4,128,128]{2,1,0:T(8,128)(2,1)}, bf16[4,128,128]{2,1,0:T(8,128)(2,1)}, bf16[4,128,128]{2,1,0:T(8,128...) custom-call(s32[9]{0:T(128)} %stack.28.ids, ...), custom_call_target="tpu_custom_call" | custom-call | tf_op jit(solution)/shard_map/lat_filter/pallas_call | solution.py:682
  131.1 4.1 %lat_filter.5 = (bf16[4,128,128]{2,1,0:T(8,128)(2,1)}, bf16[4,128,128]{2,1,0:T(8,128)(2,1)}, bf16[4,128,128]{2,1,0:T(8,128)(2,1)}, bf16[4,128,128]{2,1,0:T(8,128...) custom-call(s32[9]{0:T(128)} %stack.28.ids, ...), custom_call_target="tpu_custom_call" | custom-call | tf_op jit(solution)/shard_map/lat_filter/pallas_call | solution.py:682
  135.2 3.3 %collective-permute-done.34.refs_2_ = bf16[8,128,256]{2,1,0:T(8,128)(2,1)} collective-permute-done((bf16[8,128,256]{2,1,0:T(8,128)(2,1)}, bf16[8,128,256]{2,1,0:T(8,128)(2,1)}, u32[]{:S(2)}, u32[]{:S(2)}) %collective-permute-start.34) | collective-permute-done | bytes 524320 | tf_op jit(solution)/shard_map/ppermute | solution.py:452
  138.5 4.5 %lat_filter.6 = (bf16[8,64,128]{2,1,0:T(8,128)(2,1)}, bf16[8,64,128]{2,1,0:T(8,128)(2,1)}, bf16[8,64,128]{2,1,0:T(8,128)(2,1)}, bf16[8,64,128]{2,1,0:T(8,128)(2,...) custom-call(s32[9]{0:T(128)} %stack.28.ids, ...), custom_call_target="tpu_custom_call" | custom-call | tf_op jit(solution)/shard_map/lat_filter/pallas_call | solution.py:682
  145.1 17.7 %collective-permute-start.16 = (bf16[4,128,128]{2,1,0:T(8,128)(2,1)}, bf16[4,128,128]{2,1,0:T(8,128)(2,1)S(1)}, u32[]{:S(2)}, u32[]{:S(2)}) collective-permute-start(bf16[4,128,128]{2,1,0:T(8,128)(2,1)} %get-tuple-element.93), channel_id=1, source_target_pairs={{0,1},{1,0},{2,3},{3,2},{4,5},{5,4},{6,7},{7,6},{8,9},{9,8},{10,11... | collective-permute-start | bytes 393224 | tf_op jit(solution)/shard_map/ppermute | solution.py:452
  167.2 5.0 %collective-permute-done.17.refs_2_ = bf16[4,128,128]{2,1,0:T(8,128)(2,1)S(1)} collective-permute-done((bf16[4,128,128]{2,1,0:T(8,128)(2,1)}, bf16[4,128,128]{2,1,0:T(8,128)(2,1)S(1)}, u32[]{:S(2)}, u32[]{:S(2)}) %collective-permute-start.17) | collective-permute-done | bytes 131104 | tf_op jit(solution)/shard_map/ppermute | solution.py:452
  172.2 3.1 %collective-permute-start.21 = (bf16[4,128,128]{2,1,0:T(8,128)(2,1)}, bf16[4,128,128]{2,1,0:T(8,128)(2,1)}, u32[]{:S(2)}, u32[]{:S(2)}) collective-permute-start(bf16[4,128,128]{2,1,0:T(8,128)(2,1)} %get-tuple-element.98), channel_id=1, source_target_pairs={{0,6},{1,7},{2,4},{3,5},{4,2},{5,3},{6,0},{7,1},{8,14},{9,15},{10,... | collective-permute-start | bytes 393224 | tf_op jit(solution)/shard_map/ppermute | solution.py:452
  177.3 6.2 %collective-permute-done.19.refs_4_ = bf16[4,128,128]{2,1,0:T(8,128)(2,1)} collective-permute-done((bf16[4,128,128]{2,1,0:T(8,128)(2,1)}, bf16[4,128,128]{2,1,0:T(8,128)(2,1)}, u32[]{:S(2)}, u32[]{:S(2)}) %collective-permute-start.19) | collective-permute-done | bytes 131104 | tf_op jit(solution)/shard_map/ppermute | solution.py:452
  188.1 4.3 %collective-permute-start.29 = (bf16[4,128,128]{2,1,0:T(8,128)(2,1)}, bf16[4,128,128]{2,1,0:T(8,128)(2,1)}, u32[]{:S(2)}, u32[]{:S(2)}) collective-permute-start(bf16[4,128,128]{2,1,0:T(8,128)(2,1)} %get-tuple-element.109), channel_id=1, source_target_pairs={{0,4},{1,5},{2,6},{3,7},{4,0},{5,1},{6,2},{7,3},{8,12},{9,13},{10,... | collective-permute-start | bytes 393224 | tf_op jit(solution)/shard_map/ppermute | solution.py:452
  194.3 4.4 %lat_filter.7 = (bf16[8,64,128]{2,1,0:T(8,128)(2,1)}, bf16[8,64,128]{2,1,0:T(8,128)(2,1)}, bf16[8,64,128]{2,1,0:T(8,128)(2,1)}, bf16[8,64,128]{2,1,0:T(8,128)(2,...) custom-call(s32[9]{0:T(128)} %stack.28.ids, ...), custom_call_target="tpu_custom_call" | custom-call | tf_op jit(solution)/shard_map/lat_filter/pallas_call | solution.py:682
  200.1 8.2 %collective-permute-done.29.refs_12_ = bf16[4,128,128]{2,1,0:T(8,128)(2,1)} collective-permute-done((bf16[4,128,128]{2,1,0:T(8,128)(2,1)}, bf16[4,128,128]{2,1,0:T(8,128)(2,1)}, u32[]{:S(2)}, u32[]{:S(2)}) %collective-permute-start.29) | collective-permute-done | bytes 131104 | tf_op jit(solution)/shard_map/ppermute | solution.py:452
  211.5 2.9 collective-permute-done.37.refs_18_
  214.4 3.5 %collective-permute-done.50.refs_17_ = bf16[8,64,128]{2,1,0:T(8,128)(2,1)S(1)} collective-permute-done((bf16[8,64,128]{2,1,0:T(8,128)(2,1)}, bf16[8,64,128]{2,1,0:T(8,128)(2,1)S(1)}, u32[]{:S(2)}, u32[]{:S(2)}) %collective-permute-start.50) | collective-permute-done | bytes 131104 | tf_op jit(solution)/shard_map/ppermute | solution.py:452
  220.5 4.2 %collective-permute-done.51.refs_18_ = bf16[8,64,128]{2,1,0:T(8,128)(2,1)S(1)} collective-permute-done((bf16[8,64,128]{2,1,0:T(8,128)(2,1)}, bf16[8,64,128]{2,1,0:T(8,128)(2,1)S(1)}, u32[]{:S(2)}, u32[]{:S(2)}) %collective-permute-start.51) | collective-permute-done | bytes 131104 | tf_op jit(solution)/shard_map/ppermute | solution.py:452
  225.6 4.8 %collective-permute-done.52.refs_19_ = bf16[8,64,128]{2,1,0:T(8,128)(2,1)S(1)} collective-permute-done((bf16[8,64,128]{2,1,0:T(8,128)(2,1)}, bf16[8,64,128]{2,1,0:T(8,128)(2,1)S(1)}, u32[]{:S(2)}, u32[]{:S(2)}) %collective-permute-start.52) | collective-permute-done | bytes 131104 | tf_op jit(solution)/shard_map/ppermute | solution.py:452
  232.3 7.6 %collective-permute-done.53.refs_20_ = bf16[8,64,128]{2,1,0:T(8,128)(2,1)S(1)} collective-permute-done((bf16[8,64,128]{2,1,0:T(8,128)(2,1)}, bf16[8,64,128]{2,1,0:T(8,128)(2,1)S(1)}, u32[]{:S(2)}, u32[]{:S(2)}) %collective-permute-start.53) | collective-permute-done | bytes 131104 | tf_op jit(solution)/shard_map/ppermute | solution.py:452
  239.9 8.2 %collective-permute-done.54.refs_21_ = bf16[8,64,128]{2,1,0:T(8,128)(2,1)S(1)} collective-permute-done((bf16[8,64,128]{2,1,0:T(8,128)(2,1)}, bf16[8,64,128]{2,1,0:T(8,128)(2,1)S(1)}, u32[]{:S(2)}, u32[]{:S(2)}) %collective-permute-start.54) | collective-permute-done | bytes 131104 | tf_op jit(solution)/shard_map/ppermute | solution.py:452
  250.2 5.4 %collective-permute-done.55.refs_22_ = bf16[8,64,128]{2,1,0:T(8,128)(2,1)S(1)} collective-permute-done((bf16[8,64,128]{2,1,0:T(8,128)(2,1)}, bf16[8,64,128]{2,1,0:T(8,128)(2,1)S(1)}, u32[]{:S(2)}, u32[]{:S(2)}) %collective-permute-start.55) | collective-permute-done | bytes 131104 | tf_op jit(solution)/shard_map/ppermute | solution.py:452
  256.5 6.2 %collective-permute-done.56.refs_23_ = bf16[8,64,128]{2,1,0:T(8,128)(2,1)S(1)} collective-permute-done((bf16[8,64,128]{2,1,0:T(8,128)(2,1)}, bf16[8,64,128]{2,1,0:T(8,128)(2,1)S(1)}, u32[]{:S(2)}, u32[]{:S(2)}) %collective-permute-start.56) | collective-permute-done | bytes 131104 | tf_op jit(solution)/shard_map/ppermute | solution.py:452
  270.6 11.3 %lon_filter.2.refs_32_ = f32[1024,2048]{1,0:T(8,128)} custom-call(s32[9]{0:T(128)} %stack.28.ids, bf16[4,128,128]{2,1,0:T(8,128)(2,1)} %get-tuple-element.92.refs_0_, bf16[4,128,128]{2,1,0:T(8,128)(2,1)} %copy-done.10, bf16[4,128,128]{2,1,0:T(8,128)(2,1)} %copy-done.11, bf16[4,128,128]{2,1,0:T(8,128)(2,1)} %copy-done.12, ...), custom_call_target="tpu_custom_call" | custom-call | tf_op jit(solution)/shard_map/lon_filter/pallas_call | solution.py:744
  283.5 11.4 %lon_filter.3 = f32[1024,2048]{1,0:T(8,128)} custom-call(s32[9]{0:T(128)} %stack.28.ids, bf16[4,128,128]{2,1,0:T(8,128)(2,1)} %get-tuple-element.92.refs_0_, bf16[4,128,128]{2,1,0:T(8,128)(2,1)} %copy-done.10, bf16[4,128,128]{2,1,0:T(8,128)(2,1)} %copy-done.11, bf16[4,128,128]{2,1,0:T(8,128)(2,1)} %copy-done.12, ...), custom_call_target="tpu_custom_call", output_to_operand_aliasing={{}: (33, {})} | custom-call | tf_op jit(solution)/shard_map/lon_filter/pallas_call | solution.py:744
  (181 shorter events, 67.2 us)
Async XLA Ops:
  9.9 25.5 %collective-permute-start.9 = (f32[2,32,256]{2,1,0:T(8,128)S(1)}, f32[2,32,256]{2,1,0:T(8,128)S(1)}, u32[]{:S(2)}, u32[]{:S(2)}) collective-permute-start(f32[2,32,256]{2,1,0:T(8,128)S(1)} %pad_maximum_fusion.2), channel_id=1, source_target_pairs={{0,4},{1,5},{2,6},{3,7},{4,0},{5,1},{6,2},{7,3},{8,12},{9,13},{10,... | collective-permute-start | bytes 196616 | tf_op jit(solution)/shard_map/ppermute | solution.py:452
  88.2 54.8 %collective-permute-start.44 = (bf16[256,2048]{1,0:T(8,128)(2,1)S(1)}, bf16[256,2048]{1,0:T(8,128)(2,1)S(1)}, u32[]{:S(2)}, u32[]{:S(2)}) collective-permute-start(bf16[256,2048]{1,0:T(8,128)(2,1)S(1)} %constant_dynamic-slice_fusion.refs_24_), channel_id=1, source_target_pairs={{0,8},{1,17},{2,10},{3,19},{4,12},{5,21},{6,14},{7,23},{8,0},{9,25... | collective-permute-start | bytes 3145736 | tf_op jit(solution)/shard_map/ppermute | solution.py:510
  90.3 12.2 %collective-permute-start.14 = (bf16[4,128,256]{2,1,0:T(8,128)(2,1)}, bf16[4,128,256]{2,1,0:T(8,128)(2,1)S(1)}, u32[]{:S(2)}, u32[]{:S(2)}) collective-permute-start(bf16[4,128,256]{2,1,0:T(8,128)(2,1)} %get-tuple-element.90), channel_id=1, source_target_pairs={{0,16},{8,24},{16,0},{24,8},{1,17},{9,25},{17,1},{25,9},{2,18},{10... | collective-permute-start | bytes 786440 | tf_op jit(solution)/shard_map/ppermute | solution.py:452
  90.4 32.8 %collective-permute-start.15 = (bf16[4,128,256]{2,1,0:T(8,128)(2,1)}, bf16[4,128,256]{2,1,0:T(8,128)(2,1)S(1)}, u32[]{:S(2)}, u32[]{:S(2)}) collective-permute-start(bf16[4,128,256]{2,1,0:T(8,128)(2,1)} %get-tuple-element.91), channel_id=1, source_target_pairs={{0,24},{8,16},{16,8},{24,0},{1,25},{9,17},{17,9},{25,1},{2,26},{10... | collective-permute-start | bytes 786440 | tf_op jit(solution)/shard_map/ppermute | solution.py:452
  91.9 31.5 %collective-permute-start.23 = (bf16[4,128,256]{2,1,0:T(8,128)(2,1)}, bf16[4,128,256]{2,1,0:T(8,128)(2,1)S(1)}, u32[]{:S(2)}, u32[]{:S(2)}) collective-permute-start(bf16[4,128,256]{2,1,0:T(8,128)(2,1)} %get-tuple-element.101), channel_id=1, source_target_pairs={{0,8},{8,0},{16,24},{24,16},{1,9},{9,1},{17,25},{25,17},{2,10},{10... | collective-permute-start | bytes 786440 | tf_op jit(solution)/shard_map/ppermute | solution.py:452
  97.5 27.8 %collective-permute-start.24 = (bf16[4,128,256]{2,1,0:T(8,128)(2,1)}, bf16[4,128,256]{2,1,0:T(8,128)(2,1)S(1)}, u32[]{:S(2)}, u32[]{:S(2)}) collective-permute-start(bf16[4,128,256]{2,1,0:T(8,128)(2,1)} %get-tuple-element.102), channel_id=1, source_target_pairs={{0,16},{8,24},{16,0},{24,8},{1,17},{9,25},{17,1},{25,9},{2,18},{10... | collective-permute-start | bytes 786440 | tf_op jit(solution)/shard_map/ppermute | solution.py:452
  102.5 24.3 %collective-permute-start.25 = (bf16[4,128,256]{2,1,0:T(8,128)(2,1)}, bf16[4,128,256]{2,1,0:T(8,128)(2,1)}, u32[]{:S(2)}, u32[]{:S(2)}) collective-permute-start(bf16[4,128,256]{2,1,0:T(8,128)(2,1)} %get-tuple-element.103), channel_id=1, source_target_pairs={{0,24},{8,16},{16,8},{24,0},{1,25},{9,17},{17,9},{25,1},{2,26},{10... | collective-permute-start | bytes 786440 | tf_op jit(solution)/shard_map/ppermute | solution.py:452
  123.3 12.0 %collective-permute-start.33 = (bf16[8,128,256]{2,1,0:T(8,128)(2,1)}, bf16[8,128,256]{2,1,0:T(8,128)(2,1)}, u32[]{:S(2)}, u32[]{:S(2)}) collective-permute-start(bf16[8,128,256]{2,1,0:T(8,128)(2,1)} %get-tuple-element.115), channel_id=1, source_target_pairs={{0,8},{8,0},{16,24},{24,16},{1,9},{9,1},{17,25},{25,17},{2,10},{10... | collective-permute-start | bytes 1572872 | tf_op jit(solution)/shard_map/ppermute | solution.py:452
  123.4 15.2 %collective-permute-start.34 = (bf16[8,128,256]{2,1,0:T(8,128)(2,1)}, bf16[8,128,256]{2,1,0:T(8,128)(2,1)}, u32[]{:S(2)}, u32[]{:S(2)}) collective-permute-start(bf16[8,128,256]{2,1,0:T(8,128)(2,1)} %get-tuple-element.116), channel_id=1, source_target_pairs={{0,16},{8,24},{16,0},{24,8},{1,17},{9,25},{17,1},{25,9},{2,18},{10... | collective-permute-start | bytes 1572872 | tf_op jit(solution)/shard_map/ppermute | solution.py:452
  125.3 13.2 %collective-permute-start.35 = (bf16[8,128,256]{2,1,0:T(8,128)(2,1)}, bf16[8,128,256]{2,1,0:T(8,128)(2,1)}, u32[]{:S(2)}, u32[]{:S(2)}) collective-permute-start(bf16[8,128,256]{2,1,0:T(8,128)(2,1)} %get-tuple-element.117), channel_id=1, source_target_pairs={{0,24},{8,16},{16,8},{24,0},{1,25},{9,17},{17,9},{25,1},{2,26},{10... | collective-permute-start | bytes 1572872 | tf_op jit(solution)/shard_map/ppermute | solution.py:452
  126.8 37.8 %collective-permute-start.46 = (bf16[256,2048]{1,0:T(8,128)(2,1)S(1)}, bf16[256,2048]{1,0:T(8,128)(2,1)S(1)}, u32[]{:S(2)}, u32[]{:S(2)}) collective-permute-start(bf16[256,2048]{1,0:T(8,128)(2,1)S(1)} %constant_dynamic-slice_fusion.refs_24_), channel_id=1, source_target_pairs={{0,16},{1,9},{2,18},{3,11},{4,20},{5,13},{6,22},{7,15},{8,24},{9,1... | collective-permute-start | bytes 3145736 | tf_op jit(solution)/shard_map/ppermute | solution.py:510
  143.1 65.2 %collective-permute-start.48 = (bf16[256,2048]{1,0:T(8,128)(2,1)S(1)}, bf16[256,2048]{1,0:T(8,128)(2,1)}, u32[]{:S(2)}, u32[]{:S(2)}) collective-permute-start(bf16[256,2048]{1,0:T(8,128)(2,1)S(1)} %collective-permute-done.44.refs_26_), channel_id=1, source_target_pairs={{0,16},{1,9},{2,18},{3,11},{4,20},{5,13},{6,22},{7,15},{8,24},{9,1... | collective-permute-start | bytes 3145736 | tf_op jit(solution)/shard_map/ppermute | solution.py:510
  145.1 20.5 %collective-permute-start.16 = (bf16[4,128,128]{2,1,0:T(8,128)(2,1)}, bf16[4,128,128]{2,1,0:T(8,128)(2,1)S(1)}, u32[]{:S(2)}, u32[]{:S(2)}) collective-permute-start(bf16[4,128,128]{2,1,0:T(8,128)(2,1)} %get-tuple-element.93), channel_id=1, source_target_pairs={{0,1},{1,0},{2,3},{3,2},{4,5},{5,4},{6,7},{7,6},{8,9},{9,8},{10,11... | collective-permute-start | bytes 393224 | tf_op jit(solution)/shard_map/ppermute | solution.py:452
  164.6 10.8 %collective-permute-start.18 = (bf16[4,128,128]{2,1,0:T(8,128)(2,1)}, bf16[4,128,128]{2,1,0:T(8,128)(2,1)S(1)}, u32[]{:S(2)}, u32[]{:S(2)}) collective-permute-start(bf16[4,128,128]{2,1,0:T(8,128)(2,1)} %get-tuple-element.95), channel_id=1, source_target_pairs={{0,3},{1,2},{2,1},{3,0},{4,7},{5,6},{6,5},{7,4},{8,11},{9,10},{10,... | collective-permute-start | bytes 393224 | tf_op jit(solution)/shard_map/ppermute | solution.py:452
  164.6 18.9 %collective-permute-start.19 = (bf16[4,128,128]{2,1,0:T(8,128)(2,1)}, bf16[4,128,128]{2,1,0:T(8,128)(2,1)}, u32[]{:S(2)}, u32[]{:S(2)}) collective-permute-start(bf16[4,128,128]{2,1,0:T(8,128)(2,1)} %get-tuple-element.96), channel_id=1, source_target_pairs={{0,4},{1,5},{2,6},{3,7},{4,0},{5,1},{6,2},{7,3},{8,12},{9,13},{10,... | collective-permute-start | bytes 393224 | tf_op jit(solution)/shard_map/ppermute | solution.py:452
  165.6 19.4 %collective-permute-start.20 = (bf16[4,128,128]{2,1,0:T(8,128)(2,1)}, bf16[4,128,128]{2,1,0:T(8,128)(2,1)}, u32[]{:S(2)}, u32[]{:S(2)}) collective-permute-start(bf16[4,128,128]{2,1,0:T(8,128)(2,1)} %get-tuple-element.97), channel_id=1, source_target_pairs={{0,5},{1,4},{2,7},{3,6},{4,1},{5,0},{6,3},{7,2},{8,13},{9,12},{10,... | collective-permute-start | bytes 393224 | tf_op jit(solution)/shard_map/ppermute | solution.py:452
  172.2 13.0 %collective-permute-start.21 = (bf16[4,128,128]{2,1,0:T(8,128)(2,1)}, bf16[4,128,128]{2,1,0:T(8,128)(2,1)}, u32[]{:S(2)}, u32[]{:S(2)}) collective-permute-start(bf16[4,128,128]{2,1,0:T(8,128)(2,1)} %get-tuple-element.98), channel_id=1, source_target_pairs={{0,6},{1,7},{2,4},{3,5},{4,2},{5,3},{6,0},{7,1},{8,14},{9,15},{10,... | collective-permute-start | bytes 393224 | tf_op jit(solution)/shard_map/ppermute | solution.py:452
  175.3 12.7 %collective-permute-start.22 = (bf16[4,128,128]{2,1,0:T(8,128)(2,1)}, bf16[4,128,128]{2,1,0:T(8,128)(2,1)}, u32[]{:S(2)}, u32[]{:S(2)}) collective-permute-start(bf16[4,128,128]{2,1,0:T(8,128)(2,1)} %get-tuple-element.99), channel_id=1, source_target_pairs={{0,7},{1,6},{2,5},{3,4},{4,3},{5,2},{6,1},{7,0},{8,15},{9,14},{10,... | collective-permute-start | bytes 393224 | tf_op jit(solution)/shard_map/ppermute | solution.py:452
  185.2 13.6 %collective-permute-start.28 = (bf16[4,128,128]{2,1,0:T(8,128)(2,1)}, bf16[4,128,128]{2,1,0:T(8,128)(2,1)}, u32[]{:S(2)}, u32[]{:S(2)}) collective-permute-start(bf16[4,128,128]{2,1,0:T(8,128)(2,1)} %get-tuple-element.108), channel_id=1, source_target_pairs={{0,3},{1,2},{2,1},{3,0},{4,7},{5,6},{6,5},{7,4},{8,11},{9,10},{10,... | collective-permute-start | bytes 393224 | tf_op jit(solution)/shard_map/ppermute | solution.py:452
  188.1 20.2 %collective-permute-start.29 = (bf16[4,128,128]{2,1,0:T(8,128)(2,1)}, bf16[4,128,128]{2,1,0:T(8,128)(2,1)}, u32[]{:S(2)}, u32[]{:S(2)}) collective-permute-start(bf16[4,128,128]{2,1,0:T(8,128)(2,1)} %get-tuple-element.109), channel_id=1, source_target_pairs={{0,4},{1,5},{2,6},{3,7},{4,0},{5,1},{6,2},{7,3},{8,12},{9,13},{10,... | collective-permute-start | bytes 393224 | tf_op jit(solution)/shard_map/ppermute | solution.py:452
  192.4 17.6 %collective-permute-start.30 = (bf16[4,128,128]{2,1,0:T(8,128)(2,1)}, bf16[4,128,128]{2,1,0:T(8,128)(2,1)}, u32[]{:S(2)}, u32[]{:S(2)}) collective-permute-start(bf16[4,128,128]{2,1,0:T(8,128)(2,1)} %get-tuple-element.110), channel_id=1, source_target_pairs={{0,5},{1,4},{2,7},{3,6},{4,1},{5,0},{6,3},{7,2},{8,13},{9,12},{10,... | collective-permute-start | bytes 393224 | tf_op jit(solution)/shard_map/ppermute | solution.py:452
  192.4 18.6 %collective-permute-start.31 = (bf16[4,128,128]{2,1,0:T(8,128)(2,1)}, bf16[4,128,128]{2,1,0:T(8,128)(2,1)}, u32[]{:S(2)}, u32[]{:S(2)}) collective-permute-start(bf16[4,128,128]{2,1,0:T(8,128)(2,1)} %get-tuple-element.111), channel_id=1, source_target_pairs={{0,6},{1,7},{2,4},{3,5},{4,2},{5,3},{6,0},{7,1},{8,14},{9,15},{10,... | collective-permute-start | bytes 393224 | tf_op jit(solution)/shard_map/ppermute | solution.py:452
  198.8 12.2 %collective-permute-start.32 = (bf16[4,128,128]{2,1,0:T(8,128)(2,1)}, bf16[4,128,128]{2,1,0:T(8,128)(2,1)}, u32[]{:S(2)}, u32[]{:S(2)}) collective-permute-start(bf16[4,128,128]{2,1,0:T(8,128)(2,1)} %get-tuple-element.112), channel_id=1, source_target_pairs={{0,7},{1,6},{2,5},{3,4},{4,3},{5,2},{6,1},{7,0},{8,15},{9,14},{10,... | collective-permute-start | bytes 393224 | tf_op jit(solution)/shard_map/ppermute | solution.py:452
  210.0 52.8 %collective-permute-start.43 = (bf16[256,2048]{1,0:T(8,128)(2,1)S(1)}, bf16[256,2048]{1,0:T(8,128)(2,1)S(1)}, u32[]{:S(2)}, u32[]{:S(2)}) collective-permute-start(bf16[256,2048]{1,0:T(8,128)(2,1)S(1)} %constant_dynamic-slice_fusion.refs_24_), channel_id=1, source_target_pairs={{0,1},{1,0},{2,3},{3,2},{4,5},{5,4},{6,7},{7,6},{8,9},{9,8},{10,11... | collective-permute-start | bytes 3145736 | tf_op jit(solution)/shard_map/ppermute | solution.py:452
  210.9 53.7 %collective-permute-start.45 = (bf16[256,2048]{1,0:T(8,128)(2,1)S(1)}, bf16[256,2048]{1,0:T(8,128)(2,1)S(1)}, u32[]{:S(2)}, u32[]{:S(2)}) collective-permute-start(bf16[256,2048]{1,0:T(8,128)(2,1)S(1)} %collective-permute-done.44.refs_26_), channel_id=1, source_target_pairs={{0,1},{1,0},{2,3},{3,2},{4,5},{5,4},{6,7},{7,6},{8,9},{9,8},{10,11... | collective-permute-start | bytes 3145736 | tf_op jit(solution)/shard_map/ppermute | solution.py:452
  211.0 54.3 %collective-permute-start.47 = (bf16[256,2048]{1,0:T(8,128)(2,1)S(1)}, bf16[256,2048]{1,0:T(8,128)(2,1)S(1)}, u32[]{:S(2)}, u32[]{:S(2)}) collective-permute-start(bf16[256,2048]{1,0:T(8,128)(2,1)S(1)} %collective-permute-done.46.refs_28_), channel_id=1, source_target_pairs={{0,1},{1,0},{2,3},{3,2},{4,5},{5,4},{6,7},{7,6},{8,9},{9,8},{10,11... | collective-permute-start | bytes 3145736 | tf_op jit(solution)/shard_map/ppermute | solution.py:452
  211.4 55.8 %collective-permute-start.49 = (bf16[256,2048]{1,0:T(8,128)(2,1)}, bf16[256,2048]{1,0:T(8,128)(2,1)S(1)}, u32[]{:S(2)}, u32[]{:S(2)}) collective-permute-start(bf16[256,2048]{1,0:T(8,128)(2,1)} %collective-permute-done.48.refs_30_), channel_id=1, source_target_pairs={{0,1},{1,0},{2,3},{3,2},{4,5},{5,4},{6,7},{7,6},{8,9},{9,8},{10,11... | collective-permute-start | bytes 3145736 | tf_op jit(solution)/shard_map/ppermute | solution.py:452
  262.8 19.0 %collective-permute-start.38 = (bf16[8,64,128]{2,1,0:T(8,128)(2,1)}, bf16[8,64,128]{2,1,0:T(8,128)(2,1)}, u32[]{:S(2)}, u32[]{:S(2)}) collective-permute-start(bf16[8,64,128]{2,1,0:T(8,128)(2,1)} %get-tuple-element.124), channel_id=1, source_target_pairs={{0,3},{1,2},{2,1},{3,0},{4,7},{5,6},{6,5},{7,4},{8,11},{9,10},{10,... | collective-permute-start | bytes 393224 | tf_op jit(solution)/shard_map/ppermute | solution.py:452
  262.8 19.0 %collective-permute-start.39 = (bf16[8,64,128]{2,1,0:T(8,128)(2,1)}, bf16[8,64,128]{2,1,0:T(8,128)(2,1)S(1)}, u32[]{:S(2)}, u32[]{:S(2)}) collective-permute-start(bf16[8,64,128]{2,1,0:T(8,128)(2,1)} %get-tuple-element.125), channel_id=1, source_target_pairs={{0,4},{1,5},{2,6},{3,7},{4,0},{5,1},{6,2},{7,3},{8,12},{9,13},{10,... | collective-permute-start | bytes 393224 | tf_op jit(solution)/shard_map/ppermute | solution.py:452
  264.6 18.1 %collective-permute-start.40 = (bf16[8,64,128]{2,1,0:T(8,128)(2,1)}, bf16[8,64,128]{2,1,0:T(8,128)(2,1)S(1)}, u32[]{:S(2)}, u32[]{:S(2)}) collective-permute-start(bf16[8,64,128]{2,1,0:T(8,128)(2,1)} %get-tuple-element.126), channel_id=1, source_target_pairs={{0,5},{1,4},{2,7},{3,6},{4,1},{5,0},{6,3},{7,2},{8,13},{9,12},{10,... | collective-permute-start | bytes 393224 | tf_op jit(solution)/shard_map/ppermute | solution.py:452
  265.6 17.1 %collective-permute-start.41 = (bf16[8,64,128]{2,1,0:T(8,128)(2,1)}, bf16[8,64,128]{2,1,0:T(8,128)(2,1)S(1)}, u32[]{:S(2)}, u32[]{:S(2)}) collective-permute-start(bf16[8,64,128]{2,1,0:T(8,128)(2,1)} %get-tuple-element.127), channel_id=1, source_target_pairs={{0,6},{1,7},{2,4},{3,5},{4,2},{5,3},{6,0},{7,1},{8,14},{9,15},{10,... | collective-permute-start | bytes 393224 | tf_op jit(solution)/shard_map/ppermute | solution.py:452
  268.2 14.5 %collective-permute-start.42 = (bf16[8,64,128]{2,1,0:T(8,128)(2,1)}, bf16[8,64,128]{2,1,0:T(8,128)(2,1)S(1)}, u32[]{:S(2)}, u32[]{:S(2)}) collective-permute-start(bf16[8,64,128]{2,1,0:T(8,128)(2,1)} %get-tuple-element.128), channel_id=1, source_target_pairs={{0,7},{1,6},{2,5},{3,4},{4,3},{5,2},{6,1},{7,0},{8,15},{9,14},{10,... | collective-permute-start | bytes 393224 | tf_op jit(solution)/shard_map/ppermute | solution.py:452
  (65 other events, 1342.5 us)

commit v3 on v2

--- a/solution.py
+++ b/solution.py
@@ -14,7 +14,10 @@
 LANES = 128
 SUB = 8
 BAND = 128
-GROUP = 32
+GROUP = 128
+GROUP_ONE = 128
+UNROLL_ONE = 2
+UNROLL_TWO = 2
 F32 = jnp.float32
 BF16 = jnp.bfloat16
 NT = (((1,), (1,)), ((), ()))
@@ -73,7 +76,8 @@
     level = pl.program_id(0)
     fields, _, rows, width = mu_ref.shape
     tiles = width // LANES
-    groups = rows // GROUP
+    size = min(GROUP_ONE, rows)
+    groups = rows // size
     tall = ef_ref.shape[0]
     lane = lanes_of((SUB, LANES))
     last = lane == LANES - 1
@@ -97,43 +101,46 @@
 
         lax.fori_loop(0, rows // SUB, prepare, 0)
 
-    def group(g, carry):
-        base = g * GROUP
-        inside = GROUP // SUB
-        starts = [jnp.maximum(base - SUB, 0)] + [base + SUB * t for t in range(inside)] + [jnp.minimum(base + GROUP, rows - SUB)]
+    def group(index, carry):
+        f, g = index // groups, lax.rem(index, groups)
+        base = g * size
+        inside = size // SUB
+        starts = [jnp.maximum(base - SUB, 0)] + [base + SUB * t for t in range(inside)] + [jnp.minimum(base + size, rows - SUB)]
         keep_low = jnp.where(g > 0, 1.0, 0.0).astype(F32)
         keep_high = jnp.where(g < groups - 1, 1.0, 0.0).astype(F32)
-        band = base // tall
-        held = [[ref[rows_at(lax.rem(base, tall) + SUB * t)] for t in range(inside)] for ref in (ef_ref, em_ref, ew_ref)]
-        for f in range(fields):
-            slot = level * fields + f
-            turn = lax.rem(2 * slot + 1 + band * 64, LANES)
+        slot = level * fields + f
+        none = jnp.zeros((SUB, LANES), F32)
+        mus = [mu_ref[f, 0, rows_at(s)] for s in starts]
+        damped = [m * damp[f, rows_at(s)] for m, s in zip(mus, starts)]
+        pq = [x_fluxes(m, cour_ref[1, 0, 0, rows_at(s)], east[rows_at(s)]) for m, s in zip(damped, starts)]
+        px = [v[0] for v in pq]
+        qx = [v[1] for v in pq]
+        qx[0] = qx[0] * keep_low
+        px[-1] = px[-1] * keep_high
+        for t in range(inside):
+            at = rows_at(starts[t + 1])
+            up, down = shifted(px[t + 1], px[t + 2], qx[t], qx[t + 1])
+            new, py, qy = stencil(
+                mus[t + 1], px[t + 1], qx[t + 1], up, down, damped[t + 1], cour_ref[1, 1, 0, at], north[at], none, none
+            )
+            for k in range(tiles):
+                out_ref[f, 0, at, k * LANES : (k + 1) * LANES] = new[k]
+            band = starts[t + 1] // tall
+            turn = (2 * slot + 1 + band * 64) & (LANES - 1)
             mine = (lane // 2) == slot + 32 * band
-            mus = [mu_ref[f, 0, rows_at(s)] for s in starts]
-            damped = [m * damp[f, rows_at(s)] for m, s in zip(mus, starts)]
-            pq = [x_fluxes(m, cour_ref[1, 0, 0, rows_at(s)], east[rows_at(s)]) for m, s in zip(damped, starts)]
-            px = [v[0] for v in pq]
-            qx = [v[1] for v in pq]
-            qx[0] = qx[0] * keep_low
-            px[-1] = px[-1] * keep_high
-            for t in range(inside):
-                at = rows_at(starts[t + 1])
-                up, down = shifted(px[t + 1], px[t + 2], qx[t], qx[t + 1])
-                new, py, qy = stencil(
-                    mus[t + 1], px[t + 1], qx[t + 1], up, down, damped[t + 1], cour_ref[1, 1, 0, at], north[at],
-                    jnp.zeros((SUB, LANES), F32), jnp.zeros((SUB, LANES), F32),
-                )
-                for k in range(tiles):
-                    out_ref[f, 0, at, k * LANES : (k + 1) * LANES] = new[k]
-                weight = jnp.where(last, cour_ref[0, 1, 0, at, edge], cour_ref[0, 1, 0, at, :LANES]) * rim[f, at]
-                for which, value in enumerate((jnp.where(last, qy[-1], py[0]), jnp.where(last, new[-1], new[0]), weight)):
-                    held[which][t] = jnp.where(mine, pltpu.roll(value, turn, 1), held[which][t])
-        for which, ref in enumerate((ef_ref, em_ref, ew_ref)):
-            for t in range(inside):
-                ref[rows_at(lax.rem(base, tall) + SUB * t)] = held[which][t]
+            weight = jnp.where(last, cour_ref[0, 1, 0, at, edge], cour_ref[0, 1, 0, at, :LANES]) * rim[f, at]
+            place = rows_at(lax.rem(starts[t + 1], tall))
+            values = (jnp.where(last, qy[-1], py[0]), jnp.where(last, new[-1], new[0]), weight)
+            for ref, value in zip((ef_ref, em_ref, ew_ref), values):
+                ref[place] = jnp.where(mine, pltpu.roll(value, turn, 1), ref[place])
         return carry
 
-    lax.fori_loop(0, groups, group, 0)
+    def groups_at(index, carry):
+        for u in range(UNROLL_ONE):
+            group(index + u * (fields // UNROLL_ONE) * groups, carry)
+        return carry
+
+    lax.fori_loop(0, fields * groups // UNROLL_ONE, groups_at, 0)
 
     low, high = slice(0, SUB), slice(rows - SUB, rows)
     for f in range(fields):
@@ -232,7 +239,8 @@
     tall = m1_ref.shape[0]
     even_row, even_col = ids[2] == 0, ids[3] == 0
     tiles = width // LANES
-    inside = GROUP // SUB
+    size = mu_ref.shape[2]
+    inside = size // SUB
     lane = lanes_of((SUB, LANES))
     sub = sublanes_of((SUB, width))
     last, first = lane == LANES - 1, lane == 0
@@ -258,67 +266,66 @@
         for f in range(fields):
             damp[f, put] = 0.5 + 0.5 * ref[0, f, r : r + SUB].astype(F32)
 
-    base = band * tall + g * GROUP
-    starts = [jnp.maximum(base - SUB, 0)] + [base + SUB * t for t in range(inside)] + [jnp.minimum(base + GROUP, rows - SUB)]
+    base = band * tall + g * size
+    starts = [jnp.maximum(base - SUB, 0)] + [base + SUB * t for t in range(inside)] + [jnp.minimum(base + size, rows - SUB)]
     bands = [s // tall for s in starts]
     places = [lax.rem(s, tall) for s in starts]
     at_start = base == 0
-    at_end = base + GROUP == rows
+    at_end = base + size == rows
     lat_at = ids[7]
     box_lats = box_ref.shape[1] // (fields * levels * parts)
-    away = (lane - lat_at) & (LANES - 1)
-    piece = away // box_lats
+    per_tile = LANES // box_lats
     total = parts * box_lats
-    span = fields * levels * box_lats // LANES
     inner = [((lane + LANES * k - lat_at) >= 0) & ((lane + LANES * k - lat_at) < total) for k in range(tiles)]
 
-    def channel_group(level, carry):
-        for f in range(fields):
-            slot = level * fields + f
-            vals, damped, px, qx = [], [], [], []
-            for t in range(inside + 2):
-                ref, r = mus[t]
-                value = ref[f, level, r : r + SUB]
-                fix = pltpu.roll(m1_ref[rows_at(places[t])], (126 - 2 * slot - 64 * bands[t]) & (LANES - 1), 1)
-                pieces = split(value)
-                pieces[-1] = pieces[-1] + jnp.where(last, fix, 0.0)
-                pieces[0] = pieces[0] + jnp.where(first, fix, 0.0)
-                value = jnp.concatenate(pieces, axis=1)
-                if t == 1:
-                    value = value + jnp.where((sub == 0) & at_start, x1_ref[level, fields + f : fields + f + 1], 0.0)
-                if t == inside:
-                    value = value + jnp.where((sub == SUB - 1) & at_end, x1_ref[level, f : f + 1], 0.0)
-                ref, r = cxs[t]
-                weighed = value * damp[f, SUB * t : SUB * (t + 1)]
-                p, q = x_fluxes(weighed, ref[0, 0, level, r : r + SUB], east[SUB * t : SUB * (t + 1)])
-                vals.append(value)
-                damped.append(weighed)
-                px.append(p)
-                qx.append(q)
-            halo_low = pick(even_col, x2b_ref[level, fields + f : fields + f + 1], x2a_ref[level, fields + f : fields + f + 1])
-            halo_high = pick(even_col, x2a_ref[level, f : f + 1], x2b_ref[level, f : f + 1])
-            qx[0] = jnp.where(at_start, jnp.broadcast_to(halo_low, (SUB, width)), qx[0])
-            px[-1] = jnp.where(at_end, jnp.broadcast_to(halo_high, (SUB, width)), px[-1])
-            for t in range(inside):
-                mine = slice(SUB * t, SUB * (t + 1))
-                up, down = shifted(px[t + 1], px[t + 2], qx[t], qx[t + 1])
-                halo = pltpu.roll(m2_ref[rows_at(places[t + 1])], (126 - 2 * slot - 64 * bands[t + 1]) & (LANES - 1), 1)
-                new, _, _ = stencil(
-                    vals[t + 1], px[t + 1], qx[t + 1], up, down, damped[t + 1], cour_ref[0, 1, level, mine], north[mine], halo, -halo
-                )
-                gathered = jnp.zeros((SUB, LANES), F32)
-                for r in range(parts):
-                    block = r * span + f * levels * box_lats // LANES
-                    begin = (f * levels * box_lats) % LANES + level * box_lats
-                    source = box_ref[mine, block * LANES : (block + 1) * LANES]
-                    moved = pltpu.roll(source, (lat_at + box_lats * r - begin) & (LANES - 1), 1)
-                    gathered = jnp.where(piece == r, moved, gathered)
-                put = rows_at((f * levels + level) * SUB)
-                for k in range(tiles):
-                    mixed[t, put, k * LANES : (k + 1) * LANES] = new[k] + jnp.where(inner[k], gathered, 0.0)
+    def channel(index, carry):
+        f, level = index // levels, lax.rem(index, levels)
+        slot = level * fields + f
+        vals, damped, px, qx = [], [], [], []
+        for t in range(inside + 2):
+            ref, r = mus[t]
+            value = ref[f, level, r : r + SUB]
+            fix = pltpu.roll(m1_ref[rows_at(places[t])], (126 - 2 * slot - 64 * bands[t]) & (LANES - 1), 1)
+            pieces = split(value)
+            pieces[-1] = pieces[-1] + jnp.where(last, fix, 0.0)
+            pieces[0] = pieces[0] + jnp.where(first, fix, 0.0)
+            value = jnp.concatenate(pieces, axis=1)
+            if t == 1:
+                value = value + jnp.where((sub == 0) & at_start, x1_ref[level, pl.ds(fields + f, 1)], 0.0)
+            if t == inside:
+                value = value + jnp.where((sub == SUB - 1) & at_end, x1_ref[level, pl.ds(f, 1)], 0.0)
+            ref, r = cxs[t]
+            weighed = value * damp[f, SUB * t : SUB * (t + 1)]
+            p, q = x_fluxes(weighed, ref[0, 0, level, r : r + SUB], east[SUB * t : SUB * (t + 1)])
+            vals.append(value)
+            damped.append(weighed)
+            px.append(p)
+            qx.append(q)
+        halo_low = pick(even_col, x2b_ref[level, pl.ds(fields + f, 1)], x2a_ref[level, pl.ds(fields + f, 1)])
+        halo_high = pick(even_col, x2a_ref[level, pl.ds(f, 1)], x2b_ref[level, pl.ds(f, 1)])
+        qx[0] = jnp.where(at_start, jnp.broadcast_to(halo_low, (SUB, width)), qx[0])
+        px[-1] = jnp.where(at_end, jnp.broadcast_to(halo_high, (SUB, width)), px[-1])
+        box_tile = pl.multiple_of((index // per_tile * parts + lax.rem(index, parts)) * LANES, LANES)
+        box_turn = (lat_at - lax.rem(index, per_tile) * box_lats) & (LANES - 1)
+        put = rows_at(index * SUB)
+        for t in range(inside):
+            mine = slice(SUB * t, SUB * (t + 1))
+            up, down = shifted(px[t + 1], px[t + 2], qx[t], qx[t + 1])
+            halo = pltpu.roll(m2_ref[rows_at(places[t + 1])], (126 - 2 * slot - 64 * bands[t + 1]) & (LANES - 1), 1)
+            new, _, _ = stencil(
+                vals[t + 1], px[t + 1], qx[t + 1], up, down, damped[t + 1], cour_ref[0, 1, level, mine], north[mine], halo, -halo
+            )
+            moved = pltpu.roll(box_ref[mine, pl.ds(box_tile, LANES)], box_turn, 1)
+            for k in range(tiles):
+                mixed[t, put, k * LANES : (k + 1) * LANES] = new[k] + jnp.where(inner[k], moved, 0.0)
         return carry
 
-    lax.fori_loop(0, levels, channel_group, 0)
+    def channels_at(index, carry):
+        for u in range(UNROLL_TWO):
+            channel(index * UNROLL_TWO + u, carry)
+        return carry
+
+    lax.fori_loop(0, fields * levels // UNROLL_TWO, channels_at, 0)
 
     channels = fields * levels
     share = channels // parts
@@ -354,10 +361,12 @@
         sums = sums + held[pl.ds(a, count, stride=RATIO)]
     shape = (fine_lon // RATIO, fine_lon)
     select = (lax.broadcasted_iota(jnp.int32, shape, 1) // RATIO == lax.broadcasted_iota(jnp.int32, shape, 0)).astype(F32)
-    out_ref[...] = lax.dot_general(select, sums, NT, precision=HIGHEST, preferred_element_type=F32)
-
-
-def arrange(masks, ids, near_ref, far_ref, out_ref, box):
+    result = lax.dot_general(select, sums, NT, precision=HIGHEST, preferred_element_type=F32)
+    for k, piece in enumerate(split(result)):
+        out_ref[:, k * LANES : (k + 1) * LANES] = pltpu.roll(piece, (ids[0] * (fine_lat // RATIO)) & (LANES - 1), 1)
+
+
+def arrange(masks, lats, ids, near_ref, far_ref, out_ref, box):
     half, slab, wide = near_ref.shape
     rows = out_ref.shape[0]
     for p, (row_mask, col_mask) in enumerate(masks):
@@ -369,9 +378,16 @@
     row = lax.broadcasted_iota(jnp.int32, (rows, LANES), 0) - away
     inside = (row >= 0) & (row < height)
     turn = lax.rem(lax.rem(away, height) + height, height)
-    for k in range(box.shape[1] // LANES):
-        at = slice(k * LANES, (k + 1) * LANES)
-        out_ref[:, at] = jnp.where(inside, pltpu.roll(box[:, at], turn, 0)[:rows], 0.0)
+    parts = box.shape[1] // wide
+    slot = lanes_of((height, LANES)) // lats
+    for k in range(wide // LANES):
+        pieces = [box[:, r * wide + k * LANES : r * wide + (k + 1) * LANES] for r in range(parts)]
+        for m in range(parts):
+            value = pieces[0]
+            for r in range(1, parts):
+                value = jnp.where((slot - m) % parts == r, pieces[r], value)
+            at = (k * parts + m) * LANES
+            out_ref[:, at : at + LANES] = jnp.where(inside, pltpu.roll(value, turn, 0)[:rows], 0.0)
 
 
 def lat_filter_part(start, height, count, parts, cols, ids, *refs):
@@ -603,7 +619,7 @@
     x2a, x2b = neighbours(x2, "col", 0), neighbours(x2, "col", 1)
     held = spread(held, 1, True)
     box = pl.pallas_call(
-        functools.partial(arrange, masks),
+        functools.partial(arrange, masks, fine_lat // RATIO),
         out_shape=shape_of((lon_block, rows_count * coarse.shape[1])),
         in_specs=[SMEM_SPEC, VMEM_SPEC, VMEM_SPEC],
         out_specs=VMEM_SPEC,
@@ -611,8 +627,9 @@
         name="arrange",
     )(ids, *held)
 
-    groups = tall // GROUP
-    fine = GROUP // SUB
+    size_two = min(GROUP, tall)
+    groups = tall // size_two
+    fine = size_two // SUB
     top = lon_block // SUB - 1
 
     def control(band, halves, kl):
@@ -632,16 +649,16 @@
             out_shape=(shape_of((depth, tall, lat_block), BF16),) * (rows_count * halves),
             in_specs=[
                 SMEM_SPEC,
-                pl.BlockSpec((fields, levels, GROUP, lat_block), lambda g: (0, 0, at(g), 0)),
+                pl.BlockSpec((fields, levels, size_two, lat_block), lambda g: (0, 0, at(g), 0)),
                 pl.BlockSpec((fields, levels, SUB, lat_block), lambda g: (0, 0, low(g), 0)),
                 pl.BlockSpec((fields, levels, SUB, lat_block), lambda g: (0, 0, high(g), 0)),
-                pl.BlockSpec((1, 2, levels, GROUP, lat_block), lambda g: (0, 0, 0, at(g), 0)),
+                pl.BlockSpec((1, 2, levels, size_two, lat_block), lambda g: (0, 0, 0, at(g), 0)),
                 pl.BlockSpec((1, 1, levels, SUB, lat_block), lambda g: (0, 0, 0, low(g), 0)),
                 pl.BlockSpec((1, 1, levels, SUB, lat_block), lambda g: (0, 0, 0, high(g), 0)),
-                pl.BlockSpec((1, fields, GROUP, lat_block), lambda g: (0, 0, at(g), 0)),
+                pl.BlockSpec((1, fields, size_two, lat_block), lambda g: (0, 0, at(g), 0)),
                 pl.BlockSpec((1, fields, SUB, lat_block), lambda g: (0, 0, low(g), 0)),
                 pl.BlockSpec((1, fields, SUB, lat_block), lambda g: (0, 0, high(g), 0)),
-                pl.BlockSpec((1, 2, GROUP, lat_block), lambda g: (0, 0, at(g), 0)),
+                pl.BlockSpec((1, 2, size_two, lat_block), lambda g: (0, 0, at(g), 0)),
                 pl.BlockSpec((1, 1, SUB, lat_block), lambda g: (0, 0, low(g), 0)),
                 pl.BlockSpec((1, 1, SUB, lat_block), lambda g: (0, 0, high(g), 0)),
                 whole(m1.shape),
@@ -650,15 +667,15 @@
                 whole(e2.shape),
                 whole(x2.shape),
                 whole(x2.shape),
-                pl.BlockSpec((GROUP, box.shape[1]), lambda g: (at(g), 0)),
+                pl.BlockSpec((size_two, box.shape[1]), lambda g: (at(g), 0)),
                 whole(kh.shape),
                 whole(kl.shape),
             ],
-            out_specs=(pl.BlockSpec((depth, GROUP, lat_block), lambda g: (0, g, 0)),) * (rows_count * halves),
+            out_specs=(pl.BlockSpec((depth, size_two, lat_block), lambda g: (0, g, 0)),) * (rows_count * halves),
             scratch_shapes=[
-                pltpu.VMEM((fields, GROUP + 2 * SUB, lat_block), F32),
-                pltpu.VMEM((GROUP + 2 * SUB, lat_block), F32),
-                pltpu.VMEM((GROUP, lat_block), F32),
+                pltpu.VMEM((fields, size_two + 2 * SUB, lat_block), F32),
+                pltpu.VMEM((size_two + 2 * SUB, lat_block), F32),
+                pltpu.VMEM((size_two, lat_block), F32),
                 pltpu.VMEM((tall, LANES), F32),
                 pltpu.VMEM((fine, channels * SUB, lat_block), F32),
             ],

time: 301 us -> 289 us (0.960)
  Pallas kernels: 108 us -> 96.3 us
    pallas_call x2, Pallas kernels: 38.5 us -> 27.4 us  [control(): pl.pallas_call(functools.partial(second_step, band, rows_count), grid=(gr...]
    ppermute x46, starting transfers between devices: 70.6 us -> 66.6 us  [swap(): return lax.ppermute(value, axis, [(i, i ^ mask) for i in range(count)])]
  transfers between devices with their start and end apart: 57 -> 57, of which waited for: 20 -> 23; matrix products, arithmetic and copies ran while one was open for 0% -> 0% of each run, Pallas kernels for 26% -> 24%
where the time goes in v3:
time: 289 us; the launch traced here: 284 us
  Pallas kernels  96.3 us (33%)
  waiting for transfers between devices  93.3 us (32%)
  starting transfers between devices  87.6 us (30%)
  local copies, waits for them, and re-layouts  4.4 us (2%)
    ppermute x46, waiting for transfers between devices, swap(): return lax.ppermute(value, axis, [(i, i ^ mask) for i in range(count)])  92.3 us
    ppermute x46, starting transfers between devices, swap(): return lax.ppermute(value, axis, [(i, i ^ mask) for i in range(count)])  66.6 us
    pallas_call x2, Pallas kernels, control(): pl.pallas_call(functools.partial(second_step, band, rows_count), grid=(gr...  27.4 us
    pallas_call x2, Pallas kernels, shards(): out = call(*operands)  22.7 us
    pallas_call x1, Pallas kernels, shards(): mu1, ef, em, ew, xr, xm, xw = call(mu, courant, limiter, directions)  21.1 us
    pallas_call x4, Pallas kernels, smooth(): outs = call(ids, *pieces, filt)  17.2 us
    ppermute x8, starting transfers between devices, neighbours(): return lax.ppermute(value, axis, pairs)  14.1 us
    ppermute x3, starting transfers between devices, gather(): return [lax.ppermute(piece, ('row', 'col'), pairs) for piece in pieces]  6.78 us
  transfers between devices with their start and end apart: 57, of which 23 were waited for; matrix products, arithmetic and copies ran while one was open for 0% of the time, Pallas kernels for 24%

profile of v3, /device:TPU:0, one launch (start us, length us, event | category | flops | bytes accessed | tf_op | source)
XLA Modules:
  0.0 284.5 jit_solution(8321501419564709712)
XLA Ops:
  4.1 3.1 %collective-permute-start.8 = (f32[1,32,256]{2,1,0:T(8,128)}, f32[1,32,256]{2,1,0:T(8,128)S(1)}, u32[]{:S(2)}, u32[]{:S(2)}) collective-permute-start(f32[1,32,256]{2,1,0:T(8,128)} %bitcast.16), channel_id=1, source_target_pairs={{0,2},{1,3},{2,0},{3,1},{4,6},{5,7},{6,4},{7,5},{8,10},{9,11},{10,... | collective-permute-start | bytes 98312 | tf_op jit(solution)/shard_map/ppermute | solution.py:468
  10.0 3.0 %collective-permute-start.9 = (f32[2,32,256]{2,1,0:T(8,128)S(1)}, f32[2,32,256]{2,1,0:T(8,128)S(1)}, u32[]{:S(2)}, u32[]{:S(2)}) collective-permute-start(f32[2,32,256]{2,1,0:T(8,128)S(1)} %pad_maximum_fusion.2), channel_id=1, source_target_pairs={{0,4},{1,5},{2,6},{3,7},{4,0},{5,1},{6,2},{7,3},{8,12},{9,13},{10,... | collective-permute-start | bytes 196616 | tf_op jit(solution)/shard_map/ppermute | solution.py:468
  13.0 21.1 %first_step.1 = (f32[4,8,256,256]{3,2,1,0:T(8,128)}, f32[128,128]{1,0:T(8,128)}, f32[128,128]{1,0:T(8,128)}, f32[128,128]{1,0:T(8,128)}, f32[9,8,256]{2,1,0:T(8,...) custom-call(f32[4,8,256,256]{3,2,1,0:T(8,128)} %bitcast.14, f32[2,2,8,256,256]{4,3,2,1,0:T(8,128)} %cx_high.3, ...), custom_call_target="tpu_custom_call" | custom-call | tf_op jit(solution)/shard_map/first_step/pallas_call | solution.py:597
  36.4 4.3 %collective-permute-start = (f32[128,128]{1,0:T(8,128)}, f32[128,128]{1,0:T(8,128)S(1)}, u32[]{:S(2)}, u32[]{:S(2)}) collective-permute-start(f32[128,128]{1,0:T(8,128)} %get-tuple-element.74), channel_id=1, source_target_pairs={{0,8},{8,0},{16,24},{24,16},{1,9},{9,1},{17,25},{25,17},{2,10},{10... | collective-permute-start | bytes 196616 | tf_op jit(solution)/shard_map/ppermute | solution.py:476
  45.5 9.0 %collective-permute-done.11 = f32[8,32,256]{2,1,0:T(8,128)S(1)} collective-permute-done((f32[8,32,256]{2,1,0:T(8,128)S(1)}, f32[8,32,256]{2,1,0:T(8,128)S(1)}, u32[]{:S(2)}, u32[]{:S(2)}) %collective-permute-start.11) | collective-permute-done | bytes 262176 | tf_op jit(solution)/shard_map/ppermute | solution.py:468
  63.7 3.3 %arrange.1.box_ref = f32[256,1024]{1,0:T(8,128)} custom-call(s32[9]{0:T(128)} %stack.28.ids, f32[16,32,256]{2,1,0:T(8,128)} %copy-done.9, f32[16,32,256]{2,1,0:T(8,128)} %copy-done.13), custom_call_target="tpu_custom_call" | custom-call | tf_op jit(solution)/shard_map/arrange/pallas_call | solution.py:621
  67.8 13.6 %second_step.2 = (bf16[4,128,256]{2,1,0:T(8,128)(2,1)}, bf16[4,128,256]{2,1,0:T(8,128)(2,1)}, bf16[4,128,256]{2,1,0:T(8,128)(2,1)}, bf16[4,128,256]{2,1,0:T(8,12...) custom-call(s32[9]{0:T(128)} %stack.28.ids, ...), custom_call_target="tpu_custom_call" | custom-call | tf_op jit(solution)/shard_map/second_step/pallas_call | solution.py:646
  87.2 3.7 %collective-permute-done.13.refs_1_ = bf16[4,128,256]{2,1,0:T(8,128)(2,1)S(1)} collective-permute-done((bf16[4,128,256]{2,1,0:T(8,128)(2,1)}, bf16[4,128,256]{2,1,0:T(8,128)(2,1)S(1)}, u32[]{:S(2)}, u32[]{:S(2)}) %collective-permute-start.13) | collective-permute-done | bytes 262176 | tf_op jit(solution)/shard_map/ppermute | solution.py:468
  90.9 5.0 %collective-permute-done.14.refs_2_ = bf16[4,128,256]{2,1,0:T(8,128)(2,1)S(1)} collective-permute-done((bf16[4,128,256]{2,1,0:T(8,128)(2,1)}, bf16[4,128,256]{2,1,0:T(8,128)(2,1)S(1)}, u32[]{:S(2)}, u32[]{:S(2)}) %collective-permute-start.14) | collective-permute-done | bytes 262176 | tf_op jit(solution)/shard_map/ppermute | solution.py:468
  97.3 13.8 %second_step.3 = (bf16[8,128,256]{2,1,0:T(8,128)(2,1)}, bf16[8,128,256]{2,1,0:T(8,128)(2,1)}, bf16[8,128,256]{2,1,0:T(8,128)(2,1)}, bf16[8,128,256]{2,1,0:T(8,128)(2,1)}) custom-call(s32[9]{0:T(128)} %stack.28.ids, f32[4,8,256,256]{3,2,1,0:T(8,128)} %get-tuple-element.73.mu_ref.mu_low.mu_high, f32[4,8,256,256]{3,2,1,0:T(8,128)} %get-tuple-element.73.mu_ref.mu_low.mu_high, ...), custom_call_target="tpu_custom_call" | custom-call | tf_op jit(solution)/shard_map/second_step/pallas_call | solution.py:646
  118.5 4.1 %lat_filter.4 = (bf16[4,128,128]{2,1,0:T(8,128)(2,1)}, bf16[4,128,128]{2,1,0:T(8,128)(2,1)}, bf16[4,128,128]{2,1,0:T(8,128)(2,1)}, bf16[4,128,128]{2,1,0:T(8,128...) custom-call(s32[9]{0:T(128)} %stack.28.ids, ...), custom_call_target="tpu_custom_call" | custom-call | tf_op jit(solution)/shard_map/lat_filter/pallas_call | solution.py:699
  122.6 4.1 %lat_filter.5 = (bf16[4,128,128]{2,1,0:T(8,128)(2,1)}, bf16[4,128,128]{2,1,0:T(8,128)(2,1)}, bf16[4,128,128]{2,1,0:T(8,128)(2,1)}, bf16[4,128,128]{2,1,0:T(8,128...) custom-call(s32[9]{0:T(128)} %stack.28.ids, ...), custom_call_target="tpu_custom_call" | custom-call | tf_op jit(solution)/shard_map/lat_filter/pallas_call | solution.py:699
  129.6 4.5 %lat_filter.6 = (bf16[8,64,128]{2,1,0:T(8,128)(2,1)}, bf16[8,64,128]{2,1,0:T(8,128)(2,1)}, bf16[8,64,128]{2,1,0:T(8,128)(2,1)}, bf16[8,64,128]{2,1,0:T(8,128)(2,...) custom-call(s32[9]{0:T(128)} %stack.28.ids, ...), custom_call_target="tpu_custom_call" | custom-call | tf_op jit(solution)/shard_map/lat_filter/pallas_call | solution.py:699
  134.2 3.2 %collective-permute-start.48 = (bf16[256,2048]{1,0:T(8,128)(2,1)S(1)}, bf16[256,2048]{1,0:T(8,128)(2,1)}, u32[]{:S(2)}, u32[]{:S(2)}) collective-permute-start(bf16[256,2048]{1,0:T(8,128)(2,1)S(1)} %collective-permute-done.44.refs_26_), channel_id=1, source_target_pairs={{0,16},{1,9},{2,18},{3,11},{4,20},{5,13},{6,22},{7,15},{8,24},{9,1... | collective-permute-start | bytes 3145736 | tf_op jit(solution)/shard_map/ppermute | solution.py:526
  137.4 14.9 %collective-permute-start.16 = (bf16[4,128,128]{2,1,0:T(8,128)(2,1)}, bf16[4,128,128]{2,1,0:T(8,128)(2,1)S(1)}, u32[]{:S(2)}, u32[]{:S(2)}) collective-permute-start(bf16[4,128,128]{2,1,0:T(8,128)(2,1)} %get-tuple-element.93), channel_id=1, source_target_pairs={{0,1},{1,0},{2,3},{3,2},{4,5},{5,4},{6,7},{7,6},{8,9},{9,8},{10,11... | collective-permute-start | bytes 393224 | tf_op jit(solution)/shard_map/ppermute | solution.py:468
  156.8 4.5 %collective-permute-done.17.refs_2_ = bf16[4,128,128]{2,1,0:T(8,128)(2,1)S(1)} collective-permute-done((bf16[4,128,128]{2,1,0:T(8,128)(2,1)}, bf16[4,128,128]{2,1,0:T(8,128)(2,1)S(1)}, u32[]{:S(2)}, u32[]{:S(2)}) %collective-permute-start.17) | collective-permute-done | bytes 131104 | tf_op jit(solution)/shard_map/ppermute | solution.py:468
  161.3 3.5 %collective-permute-start.21 = (bf16[4,128,128]{2,1,0:T(8,128)(2,1)}, bf16[4,128,128]{2,1,0:T(8,128)(2,1)}, u32[]{:S(2)}, u32[]{:S(2)}) collective-permute-start(bf16[4,128,128]{2,1,0:T(8,128)(2,1)} %get-tuple-element.98), channel_id=1, source_target_pairs={{0,6},{1,7},{2,4},{3,5},{4,2},{5,3},{6,0},{7,1},{8,14},{9,15},{10,... | collective-permute-start | bytes 393224 | tf_op jit(solution)/shard_map/ppermute | solution.py:468
  166.8 6.3 %collective-permute-done.19.refs_4_ = bf16[4,128,128]{2,1,0:T(8,128)(2,1)} collective-permute-done((bf16[4,128,128]{2,1,0:T(8,128)(2,1)}, bf16[4,128,128]{2,1,0:T(8,128)(2,1)}, u32[]{:S(2)}, u32[]{:S(2)}) %collective-permute-start.19) | collective-permute-done | bytes 131104 | tf_op jit(solution)/shard_map/ppermute | solution.py:468
  174.6 3.1 %collective-permute-start.28 = (bf16[4,128,128]{2,1,0:T(8,128)(2,1)}, bf16[4,128,128]{2,1,0:T(8,128)(2,1)}, u32[]{:S(2)}, u32[]{:S(2)}) collective-permute-start(bf16[4,128,128]{2,1,0:T(8,128)(2,1)} %get-tuple-element.108), channel_id=1, source_target_pairs={{0,3},{1,2},{2,1},{3,0},{4,7},{5,6},{6,5},{7,4},{8,11},{9,10},{10,... | collective-permute-start | bytes 393224 | tf_op jit(solution)/shard_map/ppermute | solution.py:468
  177.7 4.0 %collective-permute-start.29 = (bf16[4,128,128]{2,1,0:T(8,128)(2,1)}, bf16[4,128,128]{2,1,0:T(8,128)(2,1)}, u32[]{:S(2)}, u32[]{:S(2)}) collective-permute-start(bf16[4,128,128]{2,1,0:T(8,128)(2,1)} %get-tuple-element.109), channel_id=1, source_target_pairs={{0,4},{1,5},{2,6},{3,7},{4,0},{5,1},{6,2},{7,3},{8,12},{9,13},{10,... | collective-permute-start | bytes 393224 | tf_op jit(solution)/shard_map/ppermute | solution.py:468
  183.7 4.4 %lat_filter.7 = (bf16[8,64,128]{2,1,0:T(8,128)(2,1)}, bf16[8,64,128]{2,1,0:T(8,128)(2,1)}, bf16[8,64,128]{2,1,0:T(8,128)(2,1)}, bf16[8,64,128]{2,1,0:T(8,128)(2,...) custom-call(s32[9]{0:T(128)} %stack.28.ids, ...), custom_call_target="tpu_custom_call" | custom-call | tf_op jit(solution)/shard_map/lat_filter/pallas_call | solution.py:699
  189.5 8.2 %collective-permute-done.29.refs_12_ = bf16[4,128,128]{2,1,0:T(8,128)(2,1)} collective-permute-done((bf16[4,128,128]{2,1,0:T(8,128)(2,1)}, bf16[4,128,128]{2,1,0:T(8,128)(2,1)}, u32[]{:S(2)}, u32[]{:S(2)}) %collective-permute-start.29) | collective-permute-done | bytes 131104 | tf_op jit(solution)/shard_map/ppermute | solution.py:468
  203.8 3.5 %collective-permute-done.50.refs_17_ = bf16[8,64,128]{2,1,0:T(8,128)(2,1)S(1)} collective-permute-done((bf16[8,64,128]{2,1,0:T(8,128)(2,1)}, bf16[8,64,128]{2,1,0:T(8,128)(2,1)S(1)}, u32[]{:S(2)}, u32[]{:S(2)}) %collective-permute-start.50) | collective-permute-done | bytes 131104 | tf_op jit(solution)/shard_map/ppermute | solution.py:468
  207.2 3.0 %collective-permute-start.51 = (bf16[8,64,128]{2,1,0:T(8,128)(2,1)}, bf16[8,64,128]{2,1,0:T(8,128)(2,1)S(1)}, u32[]{:S(2)}, u32[]{:S(2)}) collective-permute-start(bf16[8,64,128]{2,1,0:T(8,128)(2,1)} %get-tuple-element.136), channel_id=1, source_target_pairs={{0,2},{1,3},{2,0},{3,1},{4,6},{5,7},{6,4},{7,5},{8,10},{9,11},{10,... | collective-permute-start | bytes 393224 | tf_op jit(solution)/shard_map/ppermute | solution.py:468
  210.2 4.1 %collective-permute-done.51.refs_18_ = bf16[8,64,128]{2,1,0:T(8,128)(2,1)S(1)} collective-permute-done((bf16[8,64,128]{2,1,0:T(8,128)(2,1)}, bf16[8,64,128]{2,1,0:T(8,128)(2,1)S(1)}, u32[]{:S(2)}, u32[]{:S(2)}) %collective-permute-start.51) | collective-permute-done | bytes 131104 | tf_op jit(solution)/shard_map/ppermute | solution.py:468
  215.0 5.0 %collective-permute-done.52.refs_19_ = bf16[8,64,128]{2,1,0:T(8,128)(2,1)S(1)} collective-permute-done((bf16[8,64,128]{2,1,0:T(8,128)(2,1)}, bf16[8,64,128]{2,1,0:T(8,128)(2,1)S(1)}, u32[]{:S(2)}, u32[]{:S(2)}) %collective-permute-start.52) | collective-permute-done | bytes 131104 | tf_op jit(solution)/shard_map/ppermute | solution.py:468
  221.7 7.7 %collective-permute-done.53.refs_20_ = bf16[8,64,128]{2,1,0:T(8,128)(2,1)S(1)} collective-permute-done((bf16[8,64,128]{2,1,0:T(8,128)(2,1)}, bf16[8,64,128]{2,1,0:T(8,128)(2,1)S(1)}, u32[]{:S(2)}, u32[]{:S(2)}) %collective-permute-start.53) | collective-permute-done | bytes 131104 | tf_op jit(solution)/shard_map/ppermute | solution.py:468
  229.5 8.1 %collective-permute-done.54.refs_21_ = bf16[8,64,128]{2,1,0:T(8,128)(2,1)S(1)} collective-permute-done((bf16[8,64,128]{2,1,0:T(8,128)(2,1)}, bf16[8,64,128]{2,1,0:T(8,128)(2,1)S(1)}, u32[]{:S(2)}, u32[]{:S(2)}) %collective-permute-start.54) | collective-permute-done | bytes 131104 | tf_op jit(solution)/shard_map/ppermute | solution.py:468
  239.7 5.4 %collective-permute-done.55.refs_22_ = bf16[8,64,128]{2,1,0:T(8,128)(2,1)S(1)} collective-permute-done((bf16[8,64,128]{2,1,0:T(8,128)(2,1)}, bf16[8,64,128]{2,1,0:T(8,128)(2,1)S(1)}, u32[]{:S(2)}, u32[]{:S(2)}) %collective-permute-start.55) | collective-permute-done | bytes 131104 | tf_op jit(solution)/shard_map/ppermute | solution.py:468
  246.1 6.2 %collective-permute-done.56.refs_23_ = bf16[8,64,128]{2,1,0:T(8,128)(2,1)S(1)} collective-permute-done((bf16[8,64,128]{2,1,0:T(8,128)(2,1)}, bf16[8,64,128]{2,1,0:T(8,128)(2,1)S(1)}, u32[]{:S(2)}, u32[]{:S(2)}) %collective-permute-start.56) | collective-permute-done | bytes 131104 | tf_op jit(solution)/shard_map/ppermute | solution.py:468
  260.1 11.5 %lon_filter.2.refs_32_ = f32[1024,2048]{1,0:T(8,128)} custom-call(s32[9]{0:T(128)} %stack.28.ids, bf16[4,128,128]{2,1,0:T(8,128)(2,1)} %get-tuple-element.92.refs_0_, bf16[4,128,128]{2,1,0:T(8,128)(2,1)} %copy-done.10, bf16[4,128,128]{2,1,0:T(8,128)(2,1)} %copy-done.11, bf16[4,128,128]{2,1,0:T(8,128)(2,1)} %copy-done.12, ...), custom_call_target="tpu_custom_call" | custom-call | tf_op jit(solution)/shard_map/lon_filter/pallas_call | solution.py:761
  273.0 11.2 %lon_filter.3 = f32[1024,2048]{1,0:T(8,128)} custom-call(s32[9]{0:T(128)} %stack.28.ids, bf16[4,128,128]{2,1,0:T(8,128)(2,1)} %get-tuple-element.92.refs_0_, bf16[4,128,128]{2,1,0:T(8,128)(2,1)} %copy-done.10, bf16[4,128,128]{2,1,0:T(8,128)(2,1)} %copy-done.11, bf16[4,128,128]{2,1,0:T(8,128)(2,1)} %copy-done.12, ...), custom_call_target="tpu_custom_call", output_to_operand_aliasing={{}: (33, {})} | custom-call | tf_op jit(solution)/shard_map/lon_filter/pallas_call | solution.py:761
  (181 shorter events, 71.8 us)
Async XLA Ops:
  10.0 24.1 %collective-permute-start.9 = (f32[2,32,256]{2,1,0:T(8,128)S(1)}, f32[2,32,256]{2,1,0:T(8,128)S(1)}, u32[]{:S(2)}, u32[]{:S(2)}) collective-permute-start(f32[2,32,256]{2,1,0:T(8,128)S(1)} %pad_maximum_fusion.2), channel_id=1, source_target_pairs={{0,4},{1,5},{2,6},{3,7},{4,0},{5,1},{6,2},{7,3},{8,12},{9,13},{10,... | collective-permute-start | bytes 196616 | tf_op jit(solution)/shard_map/ppermute | solution.py:468
  81.6 52.6 %collective-permute-start.44 = (bf16[256,2048]{1,0:T(8,128)(2,1)S(1)}, bf16[256,2048]{1,0:T(8,128)(2,1)S(1)}, u32[]{:S(2)}, u32[]{:S(2)}) collective-permute-start(bf16[256,2048]{1,0:T(8,128)(2,1)S(1)} %constant_dynamic-slice_fusion.refs_24_), channel_id=1, source_target_pairs={{0,8},{1,17},{2,10},{3,19},{4,12},{5,21},{6,14},{7,23},{8,0},{9,25... | collective-permute-start | bytes 3145736 | tf_op jit(solution)/shard_map/ppermute | solution.py:526
  83.7 12.2 %collective-permute-start.14 = (bf16[4,128,256]{2,1,0:T(8,128)(2,1)}, bf16[4,128,256]{2,1,0:T(8,128)(2,1)S(1)}, u32[]{:S(2)}, u32[]{:S(2)}) collective-permute-start(bf16[4,128,256]{2,1,0:T(8,128)(2,1)} %get-tuple-element.90), channel_id=1, source_target_pairs={{0,16},{8,24},{16,0},{24,8},{1,17},{9,25},{17,1},{25,9},{2,18},{10... | collective-permute-start | bytes 786440 | tf_op jit(solution)/shard_map/ppermute | solution.py:468
  83.8 27.4 %collective-permute-start.15 = (bf16[4,128,256]{2,1,0:T(8,128)(2,1)}, bf16[4,128,256]{2,1,0:T(8,128)(2,1)S(1)}, u32[]{:S(2)}, u32[]{:S(2)}) collective-permute-start(bf16[4,128,256]{2,1,0:T(8,128)(2,1)} %get-tuple-element.91), channel_id=1, source_target_pairs={{0,24},{8,16},{16,8},{24,0},{1,25},{9,17},{17,9},{25,1},{2,26},{10... | collective-permute-start | bytes 786440 | tf_op jit(solution)/shard_map/ppermute | solution.py:468
  85.2 27.2 %collective-permute-start.23 = (bf16[4,128,256]{2,1,0:T(8,128)(2,1)}, bf16[4,128,256]{2,1,0:T(8,128)(2,1)S(1)}, u32[]{:S(2)}, u32[]{:S(2)}) collective-permute-start(bf16[4,128,256]{2,1,0:T(8,128)(2,1)} %get-tuple-element.101), channel_id=1, source_target_pairs={{0,8},{8,0},{16,24},{24,16},{1,9},{9,1},{17,25},{25,17},{2,10},{10... | collective-permute-start | bytes 786440 | tf_op jit(solution)/shard_map/ppermute | solution.py:468
  90.8 22.4 %collective-permute-start.24 = (bf16[4,128,256]{2,1,0:T(8,128)(2,1)}, bf16[4,128,256]{2,1,0:T(8,128)(2,1)S(1)}, u32[]{:S(2)}, u32[]{:S(2)}) collective-permute-start(bf16[4,128,256]{2,1,0:T(8,128)(2,1)} %get-tuple-element.102), channel_id=1, source_target_pairs={{0,16},{8,24},{16,0},{24,8},{1,17},{9,25},{17,1},{25,9},{2,18},{10... | collective-permute-start | bytes 786440 | tf_op jit(solution)/shard_map/ppermute | solution.py:468
  95.9 21.2 %collective-permute-start.25 = (bf16[4,128,256]{2,1,0:T(8,128)(2,1)}, bf16[4,128,256]{2,1,0:T(8,128)(2,1)}, u32[]{:S(2)}, u32[]{:S(2)}) collective-permute-start(bf16[4,128,256]{2,1,0:T(8,128)(2,1)} %get-tuple-element.103), channel_id=1, source_target_pairs={{0,24},{8,16},{16,8},{24,0},{1,25},{9,17},{17,9},{25,1},{2,26},{10... | collective-permute-start | bytes 786440 | tf_op jit(solution)/shard_map/ppermute | solution.py:468
  111.1 15.6 %collective-permute-start.33 = (bf16[8,128,256]{2,1,0:T(8,128)(2,1)}, bf16[8,128,256]{2,1,0:T(8,128)(2,1)}, u32[]{:S(2)}, u32[]{:S(2)}) collective-permute-start(bf16[8,128,256]{2,1,0:T(8,128)(2,1)} %get-tuple-element.115), channel_id=1, source_target_pairs={{0,8},{8,0},{16,24},{24,16},{1,9},{9,1},{17,25},{25,17},{2,10},{10... | collective-permute-start | bytes 1572872 | tf_op jit(solution)/shard_map/ppermute | solution.py:468
  112.4 16.6 %collective-permute-start.34 = (bf16[8,128,256]{2,1,0:T(8,128)(2,1)}, bf16[8,128,256]{2,1,0:T(8,128)(2,1)}, u32[]{:S(2)}, u32[]{:S(2)}) collective-permute-start(bf16[8,128,256]{2,1,0:T(8,128)(2,1)} %get-tuple-element.116), channel_id=1, source_target_pairs={{0,16},{8,24},{16,0},{24,8},{1,17},{9,25},{17,1},{25,9},{2,18},{10... | collective-permute-start | bytes 1572872 | tf_op jit(solution)/shard_map/ppermute | solution.py:468
  113.2 16.4 %collective-permute-start.35 = (bf16[8,128,256]{2,1,0:T(8,128)(2,1)}, bf16[8,128,256]{2,1,0:T(8,128)(2,1)}, u32[]{:S(2)}, u32[]{:S(2)}) collective-permute-start(bf16[8,128,256]{2,1,0:T(8,128)(2,1)} %get-tuple-element.117), channel_id=1, source_target_pairs={{0,24},{8,16},{16,8},{24,0},{1,25},{9,17},{17,9},{25,1},{2,26},{10... | collective-permute-start | bytes 1572872 | tf_op jit(solution)/shard_map/ppermute | solution.py:468
  117.0 37.1 %collective-permute-start.46 = (bf16[256,2048]{1,0:T(8,128)(2,1)S(1)}, bf16[256,2048]{1,0:T(8,128)(2,1)S(1)}, u32[]{:S(2)}, u32[]{:S(2)}) collective-permute-start(bf16[256,2048]{1,0:T(8,128)(2,1)S(1)} %constant_dynamic-slice_fusion.refs_24_), channel_id=1, source_target_pairs={{0,16},{1,9},{2,18},{3,11},{4,20},{5,13},{6,22},{7,15},{8,24},{9,1... | collective-permute-start | bytes 3145736 | tf_op jit(solution)/shard_map/ppermute | solution.py:526
  134.2 63.5 %collective-permute-start.48 = (bf16[256,2048]{1,0:T(8,128)(2,1)S(1)}, bf16[256,2048]{1,0:T(8,128)(2,1)}, u32[]{:S(2)}, u32[]{:S(2)}) collective-permute-start(bf16[256,2048]{1,0:T(8,128)(2,1)S(1)} %collective-permute-done.44.refs_26_), channel_id=1, source_target_pairs={{0,16},{1,9},{2,18},{3,11},{4,20},{5,13},{6,22},{7,15},{8,24},{9,1... | collective-permute-start | bytes 3145736 | tf_op jit(solution)/shard_map/ppermute | solution.py:526
  137.4 17.5 %collective-permute-start.16 = (bf16[4,128,128]{2,1,0:T(8,128)(2,1)}, bf16[4,128,128]{2,1,0:T(8,128)(2,1)S(1)}, u32[]{:S(2)}, u32[]{:S(2)}) collective-permute-start(bf16[4,128,128]{2,1,0:T(8,128)(2,1)} %get-tuple-element.93), channel_id=1, source_target_pairs={{0,1},{1,0},{2,3},{3,2},{4,5},{5,4},{6,7},{7,6},{8,9},{9,8},{10,11... | collective-permute-start | bytes 393224 | tf_op jit(solution)/shard_map/ppermute | solution.py:468
  154.1 10.6 %collective-permute-start.18 = (bf16[4,128,128]{2,1,0:T(8,128)(2,1)}, bf16[4,128,128]{2,1,0:T(8,128)(2,1)S(1)}, u32[]{:S(2)}, u32[]{:S(2)}) collective-permute-start(bf16[4,128,128]{2,1,0:T(8,128)(2,1)} %get-tuple-element.95), channel_id=1, source_target_pairs={{0,3},{1,2},{2,1},{3,0},{4,7},{5,6},{6,5},{7,4},{8,11},{9,10},{10,... | collective-permute-start | bytes 393224 | tf_op jit(solution)/shard_map/ppermute | solution.py:468
  154.1 18.9 %collective-permute-start.19 = (bf16[4,128,128]{2,1,0:T(8,128)(2,1)}, bf16[4,128,128]{2,1,0:T(8,128)(2,1)}, u32[]{:S(2)}, u32[]{:S(2)}) collective-permute-start(bf16[4,128,128]{2,1,0:T(8,128)(2,1)} %get-tuple-element.96), channel_id=1, source_target_pairs={{0,4},{1,5},{2,6},{3,7},{4,0},{5,1},{6,2},{7,3},{8,12},{9,13},{10,... | collective-permute-start | bytes 393224 | tf_op jit(solution)/shard_map/ppermute | solution.py:468
  155.0 19.6 %collective-permute-start.20 = (bf16[4,128,128]{2,1,0:T(8,128)(2,1)}, bf16[4,128,128]{2,1,0:T(8,128)(2,1)}, u32[]{:S(2)}, u32[]{:S(2)}) collective-permute-start(bf16[4,128,128]{2,1,0:T(8,128)(2,1)} %get-tuple-element.97), channel_id=1, source_target_pairs={{0,5},{1,4},{2,7},{3,6},{4,1},{5,0},{6,3},{7,2},{8,13},{9,12},{10,... | collective-permute-start | bytes 393224 | tf_op jit(solution)/shard_map/ppermute | solution.py:468
  161.3 13.3 %collective-permute-start.21 = (bf16[4,128,128]{2,1,0:T(8,128)(2,1)}, bf16[4,128,128]{2,1,0:T(8,128)(2,1)}, u32[]{:S(2)}, u32[]{:S(2)}) collective-permute-start(bf16[4,128,128]{2,1,0:T(8,128)(2,1)} %get-tuple-element.98), channel_id=1, source_target_pairs={{0,6},{1,7},{2,4},{3,5},{4,2},{5,3},{6,0},{7,1},{8,14},{9,15},{10,... | collective-permute-start | bytes 393224 | tf_op jit(solution)/shard_map/ppermute | solution.py:468
  164.8 12.9 %collective-permute-start.22 = (bf16[4,128,128]{2,1,0:T(8,128)(2,1)}, bf16[4,128,128]{2,1,0:T(8,128)(2,1)}, u32[]{:S(2)}, u32[]{:S(2)}) collective-permute-start(bf16[4,128,128]{2,1,0:T(8,128)(2,1)} %get-tuple-element.99), channel_id=1, source_target_pairs={{0,7},{1,6},{2,5},{3,4},{4,3},{5,2},{6,1},{7,0},{8,15},{9,14},{10,... | collective-permute-start | bytes 393224 | tf_op jit(solution)/shard_map/ppermute | solution.py:468
  174.6 13.5 %collective-permute-start.28 = (bf16[4,128,128]{2,1,0:T(8,128)(2,1)}, bf16[4,128,128]{2,1,0:T(8,128)(2,1)}, u32[]{:S(2)}, u32[]{:S(2)}) collective-permute-start(bf16[4,128,128]{2,1,0:T(8,128)(2,1)} %get-tuple-element.108), channel_id=1, source_target_pairs={{0,3},{1,2},{2,1},{3,0},{4,7},{5,6},{6,5},{7,4},{8,11},{9,10},{10,... | collective-permute-start | bytes 393224 | tf_op jit(solution)/shard_map/ppermute | solution.py:468
  177.7 20.0 %collective-permute-start.29 = (bf16[4,128,128]{2,1,0:T(8,128)(2,1)}, bf16[4,128,128]{2,1,0:T(8,128)(2,1)}, u32[]{:S(2)}, u32[]{:S(2)}) collective-permute-start(bf16[4,128,128]{2,1,0:T(8,128)(2,1)} %get-tuple-element.109), channel_id=1, source_target_pairs={{0,4},{1,5},{2,6},{3,7},{4,0},{5,1},{6,2},{7,3},{8,12},{9,13},{10,... | collective-permute-start | bytes 393224 | tf_op jit(solution)/shard_map/ppermute | solution.py:468
  181.7 18.0 %collective-permute-start.30 = (bf16[4,128,128]{2,1,0:T(8,128)(2,1)}, bf16[4,128,128]{2,1,0:T(8,128)(2,1)}, u32[]{:S(2)}, u32[]{:S(2)}) collective-permute-start(bf16[4,128,128]{2,1,0:T(8,128)(2,1)} %get-tuple-element.110), channel_id=1, source_target_pairs={{0,5},{1,4},{2,7},{3,6},{4,1},{5,0},{6,3},{7,2},{8,13},{9,12},{10,... | collective-permute-start | bytes 393224 | tf_op jit(solution)/shard_map/ppermute | solution.py:468
  181.7 18.6 %collective-permute-start.31 = (bf16[4,128,128]{2,1,0:T(8,128)(2,1)}, bf16[4,128,128]{2,1,0:T(8,128)(2,1)}, u32[]{:S(2)}, u32[]{:S(2)}) collective-permute-start(bf16[4,128,128]{2,1,0:T(8,128)(2,1)} %get-tuple-element.111), channel_id=1, source_target_pairs={{0,6},{1,7},{2,4},{3,5},{4,2},{5,3},{6,0},{7,1},{8,14},{9,15},{10,... | collective-permute-start | bytes 393224 | tf_op jit(solution)/shard_map/ppermute | solution.py:468
  188.1 12.2 %collective-permute-start.32 = (bf16[4,128,128]{2,1,0:T(8,128)(2,1)}, bf16[4,128,128]{2,1,0:T(8,128)(2,1)}, u32[]{:S(2)}, u32[]{:S(2)}) collective-permute-start(bf16[4,128,128]{2,1,0:T(8,128)(2,1)} %get-tuple-element.112), channel_id=1, source_target_pairs={{0,7},{1,6},{2,5},{3,4},{4,3},{5,2},{6,1},{7,0},{8,15},{9,14},{10,... | collective-permute-start | bytes 393224 | tf_op jit(solution)/shard_map/ppermute | solution.py:468
  199.7 52.6 %collective-permute-start.43 = (bf16[256,2048]{1,0:T(8,128)(2,1)S(1)}, bf16[256,2048]{1,0:T(8,128)(2,1)S(1)}, u32[]{:S(2)}, u32[]{:S(2)}) collective-permute-start(bf16[256,2048]{1,0:T(8,128)(2,1)S(1)} %constant_dynamic-slice_fusion.refs_24_), channel_id=1, source_target_pairs={{0,1},{1,0},{2,3},{3,2},{4,5},{5,4},{6,7},{7,6},{8,9},{9,8},{10,11... | collective-permute-start | bytes 3145736 | tf_op jit(solution)/shard_map/ppermute | solution.py:468
  200.3 53.9 %collective-permute-start.45 = (bf16[256,2048]{1,0:T(8,128)(2,1)S(1)}, bf16[256,2048]{1,0:T(8,128)(2,1)S(1)}, u32[]{:S(2)}, u32[]{:S(2)}) collective-permute-start(bf16[256,2048]{1,0:T(8,128)(2,1)S(1)} %collective-permute-done.44.refs_26_), channel_id=1, source_target_pairs={{0,1},{1,0},{2,3},{3,2},{4,5},{5,4},{6,7},{7,6},{8,9},{9,8},{10,11... | collective-permute-start | bytes 3145736 | tf_op jit(solution)/shard_map/ppermute | solution.py:468
  200.3 54.5 %collective-permute-start.47 = (bf16[256,2048]{1,0:T(8,128)(2,1)S(1)}, bf16[256,2048]{1,0:T(8,128)(2,1)S(1)}, u32[]{:S(2)}, u32[]{:S(2)}) collective-permute-start(bf16[256,2048]{1,0:T(8,128)(2,1)S(1)} %collective-permute-done.46.refs_28_), channel_id=1, source_target_pairs={{0,1},{1,0},{2,3},{3,2},{4,5},{5,4},{6,7},{7,6},{8,9},{9,8},{10,11... | collective-permute-start | bytes 3145736 | tf_op jit(solution)/shard_map/ppermute | solution.py:468
  200.8 56.0 %collective-permute-start.49 = (bf16[256,2048]{1,0:T(8,128)(2,1)}, bf16[256,2048]{1,0:T(8,128)(2,1)S(1)}, u32[]{:S(2)}, u32[]{:S(2)}) collective-permute-start(bf16[256,2048]{1,0:T(8,128)(2,1)} %collective-permute-done.48.refs_30_), channel_id=1, source_target_pairs={{0,1},{1,0},{2,3},{3,2},{4,5},{5,4},{6,7},{7,6},{8,9},{9,8},{10,11... | collective-permute-start | bytes 3145736 | tf_op jit(solution)/shard_map/ppermute | solution.py:468
  252.3 19.3 %collective-permute-start.38 = (bf16[8,64,128]{2,1,0:T(8,128)(2,1)}, bf16[8,64,128]{2,1,0:T(8,128)(2,1)}, u32[]{:S(2)}, u32[]{:S(2)}) collective-permute-start(bf16[8,64,128]{2,1,0:T(8,128)(2,1)} %get-tuple-element.124), channel_id=1, source_target_pairs={{0,3},{1,2},{2,1},{3,0},{4,7},{5,6},{6,5},{7,4},{8,11},{9,10},{10,... | collective-permute-start | bytes 393224 | tf_op jit(solution)/shard_map/ppermute | solution.py:468
  252.3 19.3 %collective-permute-start.39 = (bf16[8,64,128]{2,1,0:T(8,128)(2,1)}, bf16[8,64,128]{2,1,0:T(8,128)(2,1)S(1)}, u32[]{:S(2)}, u32[]{:S(2)}) collective-permute-start(bf16[8,64,128]{2,1,0:T(8,128)(2,1)} %get-tuple-element.125), channel_id=1, source_target_pairs={{0,4},{1,5},{2,6},{3,7},{4,0},{5,1},{6,2},{7,3},{8,12},{9,13},{10,... | collective-permute-start | bytes 393224 | tf_op jit(solution)/shard_map/ppermute | solution.py:468
  254.1 18.1 %collective-permute-start.40 = (bf16[8,64,128]{2,1,0:T(8,128)(2,1)}, bf16[8,64,128]{2,1,0:T(8,128)(2,1)S(1)}, u32[]{:S(2)}, u32[]{:S(2)}) collective-permute-start(bf16[8,64,128]{2,1,0:T(8,128)(2,1)} %get-tuple-element.126), channel_id=1, source_target_pairs={{0,5},{1,4},{2,7},{3,6},{4,1},{5,0},{6,3},{7,2},{8,13},{9,12},{10,... | collective-permute-start | bytes 393224 | tf_op jit(solution)/shard_map/ppermute | solution.py:468
  255.1 17.2 %collective-permute-start.41 = (bf16[8,64,128]{2,1,0:T(8,128)(2,1)}, bf16[8,64,128]{2,1,0:T(8,128)(2,1)S(1)}, u32[]{:S(2)}, u32[]{:S(2)}) collective-permute-start(bf16[8,64,128]{2,1,0:T(8,128)(2,1)} %get-tuple-element.127), channel_id=1, source_target_pairs={{0,6},{1,7},{2,4},{3,5},{4,2},{5,3},{6,0},{7,1},{8,14},{9,15},{10,... | collective-permute-start | bytes 393224 | tf_op jit(solution)/shard_map/ppermute | solution.py:468
  257.8 14.5 %collective-permute-start.42 = (bf16[8,64,128]{2,1,0:T(8,128)(2,1)}, bf16[8,64,128]{2,1,0:T(8,128)(2,1)S(1)}, u32[]{:S(2)}, u32[]{:S(2)}) collective-permute-start(bf16[8,64,128]{2,1,0:T(8,128)(2,1)} %get-tuple-element.128), channel_id=1, source_target_pairs={{0,7},{1,6},{2,5},{3,4},{4,3},{5,2},{6,1},{7,0},{8,15},{9,14},{10,... | collective-permute-start | bytes 393224 | tf_op jit(solution)/shard_map/ppermute | solution.py:468
  (65 other events, 1318.7 us)

commit v4 on v3

--- a/solution.py
+++ b/solution.py
@@ -229,10 +229,10 @@
 
 
 def second_step(
-    band, parts, ids, mu_ref, mu_low, mu_high, cour_ref, cx_low, cx_high, lim_ref, lim_low, lim_high, dir_ref, dir_low, dir_high,
+    offset, parts, n_held, ids, mu_ref, mu_low, mu_high, cour_ref, cx_low, cx_high, lim_ref, lim_low, lim_high, dir_ref, dir_low, dir_high,
     m1_ref, x1_ref, e2a_ref, e2b_ref, x2a_ref, x2b_ref, box_ref, kh_ref, kl_ref, *rest,
 ):
-    outs, (damp, east, north, m2_ref, mixed) = rest[:-5], rest[-5:]
+    outs, (damp, east, north, m2_ref, mixed) = rest[n_held:-5], rest[-5:]
     g = pl.program_id(0)
     fields, levels, _, width = mu_ref.shape
     rows = ids[5]
@@ -266,7 +266,7 @@
         for f in range(fields):
             damp[f, put] = 0.5 + 0.5 * ref[0, f, r : r + SUB].astype(F32)
 
-    base = band * tall + g * size
+    base = offset + g * size
     starts = [jnp.maximum(base - SUB, 0)] + [base + SUB * t for t in range(inside)] + [jnp.minimum(base + size, rows - SUB)]
     bands = [s // tall for s in starts]
     places = [lax.rem(s, tall) for s in starts]
@@ -627,24 +627,25 @@
         name="arrange",
     )(ids, *held)
 
-    size_two = min(GROUP, tall)
-    groups = tall // size_two
-    fine = size_two // SUB
     top = lon_block // SUB - 1
 
-    def control(band, halves, kl):
+    def control(band, halves, kl, cut=1, part=0, held=()):
+        size_two = min(GROUP, tall) // cut
+        groups = tall // size_two // cut
+        fine = size_two // SUB
+
         def at(g):
-            return band * groups + g
+            return (band * cut + part) * groups + g
 
         def low(g):
-            return jnp.maximum((band * groups + g) * fine - 1, 0)
+            return jnp.maximum(at(g) * fine - 1, 0)
 
         def high(g):
-            return jnp.minimum((band * groups + g) * fine + fine, top)
+            return jnp.minimum(at(g) * fine + fine, top)
 
         depth = share // halves
         return pl.pallas_call(
-            functools.partial(second_step, band, rows_count),
+            functools.partial(second_step, band * tall + part * (tall // cut), rows_count, len(held)),
             grid=(groups,),
             out_shape=(shape_of((depth, tall, lat_block), BF16),) * (rows_count * halves),
             in_specs=[
@@ -670,8 +671,10 @@
                 pl.BlockSpec((size_two, box.shape[1]), lambda g: (at(g), 0)),
                 whole(kh.shape),
                 whole(kl.shape),
-            ],
-            out_specs=(pl.BlockSpec((depth, size_two, lat_block), lambda g: (0, g, 0)),) * (rows_count * halves),
+            ]
+            + [ANY_SPEC] * len(held),
+            out_specs=(pl.BlockSpec((depth, size_two, lat_block), lambda g: (0, part * groups + g, 0)),) * (rows_count * halves),
+            input_output_aliases={22 + i: i for i in range(len(held))},
             scratch_shapes=[
                 pltpu.VMEM((fields, size_two + 2 * SUB, lat_block), F32),
                 pltpu.VMEM((size_two + 2 * SUB, lat_block), F32),
@@ -681,10 +684,13 @@
             ],
             name="second_step",
         )(ids, mu1, mu1, mu1, courant, courant, courant, limiter, limiter, limiter, directions, directions, directions,
-          m1, x1, e2a, e2b, x2a, x2b, box, kh, kl)
+          m1, x1, e2a, e2b, x2a, x2b, box, kh, kl, *held)
 
     def to_rows(pieces):
-        return [pieces[0]] + [swap(pieces[s], "row", s) for s in range(1, rows_count)]
+        moved = [pieces[0]]
+        for s in range(1, rows_count):
+            moved.append(swap(pieces[s], "row", s))
+        return moved
 
     def smooth(pieces, start, height, token):
         count = pieces[0].shape[0]
@@ -697,22 +703,29 @@
             name="lat_filter",
         )
         outs = call(ids, *pieces, filt)
-        moved = {s: swap(outs[s], "col", s) for s in range(cols_count - 1, 0, -1)}
+        moved = {}
+        for s in range(cols_count - 1, 0, -1):
+            moved[s] = swap(outs[s], "col", s)
         return [outs[0]] + [moved[s] for s in range(1, cols_count)], outs[-1]
 
     firsts = []
     sent = []
     order = None
+    token = None
     for band in range(n_bands):
         final = band == n_bands - 1
         halves = 1 if final else 2
-        kl = kl if order is None else after(kl, order)
-        outs = control(band, halves, kl)
+        if band:
+            kl = after(kl, order)
+            outs = control(band, halves, kl, 2)
+            token = outs[0]
+            outs = control(band, halves, kl, 2, 1, outs)
+        else:
+            outs = control(band, halves, kl)
         order = outs[-1]
         for h in range(halves):
             sent.append(to_rows([outs[s * halves + h] for s in range(rows_count)]))
 
-    token = None
     for pieces in sent[:-1]:
         moved, token = smooth(pieces, 0, lat_part, token)
         firsts += moved
@@ -726,8 +739,9 @@
         gathered += [direct[stage]] + gather(stage, [after(piece, early) for piece in gathered[1:]])
         owners += [(a ^ turns[0][stage], b ^ turns[1][stage]) for a, b in owners]
     filters = []
-    for piece in gathered:
-        filters += [piece, swap(after(piece, token), "col", 1)]
+    for j, piece in enumerate(gathered):
+        late = j and j == len(gathered) - 1
+        filters += [piece, swap(after(piece, token if late else early), "col", 1)]
 
     n_lon = cols_count * lon_block
     rows = share * half_height

time: 289 us -> 292 us (1.010)
  Pallas kernels: 96.3 us -> 99.7 us
  waiting for transfers between devices: 93.3 us -> 90.2 us
    ppermute x46, starting transfers between devices: 66.6 us -> 70.5 us  [swap(): return lax.ppermute(value, axis, [(i, i ^ mask) for i in range(count)])]
    pallas_call x2 -> x3, Pallas kernels: 27.4 us -> 30.9 us  [control(): pl.pallas_call(functools.partial(second_step, band * tall + part * (tall...]
    ppermute x46, waiting for transfers between devices: 92.3 us -> 89.2 us  [swap(): return lax.ppermute(value, axis, [(i, i ^ mask) for i in range(count)])]
  transfers between devices with their start and end apart: 57 -> 57, of which waited for: 23 -> 20; matrix products, arithmetic and copies ran while one was open for 0% -> 0% of each run, Pallas kernels for 24% -> 25%
where the time goes in v4:
time: 292 us; the launch traced here: 286 us
  Pallas kernels  99.7 us (34%)
  waiting for transfers between devices  90.2 us (31%)
  starting transfers between devices  89 us (30%)
  local copies, waits for them, and re-layouts  4.3 us (1%)
    ppermute x46, waiting for transfers between devices, swap(): return lax.ppermute(value, axis, [(i, i ^ mask) for i in range(count)])  89.2 us
    ppermute x46, starting transfers between devices, swap(): return lax.ppermute(value, axis, [(i, i ^ mask) for i in range(count)])  70.5 us
    pallas_call x3, Pallas kernels, control(): pl.pallas_call(functools.partial(second_step, band * tall + part * (tall...  30.9 us
    pallas_call x2, Pallas kernels, shards(): out = call(*operands)  22.7 us
    pallas_call x1, Pallas kernels, shards(): mu1, ef, em, ew, xr, xm, xw = call(mu, courant, limiter, directions)  21.1 us
    pallas_call x4, Pallas kernels, smooth(): outs = call(ids, *pieces, filt)  17.2 us
    ppermute x8, starting transfers between devices, neighbours(): return lax.ppermute(value, axis, pairs)  14.1 us
  transfers between devices with their start and end apart: 57, of which 20 were waited for; matrix products, arithmetic and copies ran while one was open for 0% of the time, Pallas kernels for 25%

profile of v4, /device:TPU:0, one launch (start us, length us, event | category | flops | bytes accessed | tf_op | source)
XLA Modules:
  0.0 286.1 jit_solution(15318338933495654128)
XLA Ops:
  4.1 3.1 %collective-permute-start.8 = (f32[1,32,256]{2,1,0:T(8,128)}, f32[1,32,256]{2,1,0:T(8,128)S(1)}, u32[]{:S(2)}, u32[]{:S(2)}) collective-permute-start(f32[1,32,256]{2,1,0:T(8,128)} %bitcast.16), channel_id=1, source_target_pairs={{0,2},{1,3},{2,0},{3,1},{4,6},{5,7},{6,4},{7,5},{8,10},{9,11},{10,... | collective-permute-start | bytes 98312 | tf_op jit(solution)/shard_map/ppermute | solution.py:468
  10.0 3.0 %collective-permute-start.9 = (f32[2,32,256]{2,1,0:T(8,128)S(1)}, f32[2,32,256]{2,1,0:T(8,128)S(1)}, u32[]{:S(2)}, u32[]{:S(2)}) collective-permute-start(f32[2,32,256]{2,1,0:T(8,128)S(1)} %pad_maximum_fusion.2), channel_id=1, source_target_pairs={{0,4},{1,5},{2,6},{3,7},{4,0},{5,1},{6,2},{7,3},{8,12},{9,13},{10,... | collective-permute-start | bytes 196616 | tf_op jit(solution)/shard_map/ppermute | solution.py:468
  13.0 21.1 %first_step.1 = (f32[4,8,256,256]{3,2,1,0:T(8,128)}, f32[128,128]{1,0:T(8,128)}, f32[128,128]{1,0:T(8,128)}, f32[128,128]{1,0:T(8,128)}, f32[9,8,256]{2,1,0:T(8,...) custom-call(f32[4,8,256,256]{3,2,1,0:T(8,128)} %bitcast.14, f32[2,2,8,256,256]{4,3,2,1,0:T(8,128)} %cx_high.5, ...), custom_call_target="tpu_custom_call" | custom-call | tf_op jit(solution)/shard_map/first_step/pallas_call | solution.py:597
  36.4 4.3 %collective-permute-start = (f32[128,128]{1,0:T(8,128)}, f32[128,128]{1,0:T(8,128)S(1)}, u32[]{:S(2)}, u32[]{:S(2)}) collective-permute-start(f32[128,128]{1,0:T(8,128)} %get-tuple-element.78), channel_id=1, source_target_pairs={{0,8},{8,0},{16,24},{24,16},{1,9},{9,1},{17,25},{25,17},{2,10},{10... | collective-permute-start | bytes 196616 | tf_op jit(solution)/shard_map/ppermute | solution.py:476
  41.3 3.0 %collective-permute-start.2 = (f32[9,8,256]{2,1,0:T(8,128)}, f32[9,8,256]{2,1,0:T(8,128)S(1)}, u32[]{:S(2)}, u32[]{:S(2)}) collective-permute-start(f32[9,8,256]{2,1,0:T(8,128)} %get-tuple-element.79), channel_id=1, source_target_pairs={{0,1},{1,0},{2,3},{3,2},{4,5},{5,4},{6,7},{7,6},{8,9},{9,8},{10,11... | collective-permute-start | bytes 221192 | tf_op jit(solution)/shard_map/ppermute | solution.py:476
  45.5 9.0 %collective-permute-done.11 = f32[8,32,256]{2,1,0:T(8,128)S(1)} collective-permute-done((f32[8,32,256]{2,1,0:T(8,128)S(1)}, f32[8,32,256]{2,1,0:T(8,128)S(1)}, u32[]{:S(2)}, u32[]{:S(2)}) %collective-permute-start.11) | collective-permute-done | bytes 262176 | tf_op jit(solution)/shard_map/ppermute | solution.py:468
  63.7 3.4 %arrange.1.box_ref = f32[256,1024]{1,0:T(8,128)} custom-call(s32[9]{0:T(128)} %stack.28.ids, f32[16,32,256]{2,1,0:T(8,128)} %copy-done.9, f32[16,32,256]{2,1,0:T(8,128)} %copy-done.17), custom_call_target="tpu_custom_call" | custom-call | tf_op jit(solution)/shard_map/arrange/pallas_call | solution.py:621
  67.7 13.6 %second_step.3 = (bf16[4,128,256]{2,1,0:T(8,128)(2,1)}, bf16[4,128,256]{2,1,0:T(8,128)(2,1)}, bf16[4,128,256]{2,1,0:T(8,128)(2,1)}, bf16[4,128,256]{2,1,0:T(8,12...) custom-call(s32[9]{0:T(128)} %stack.28.ids, ...), custom_call_target="tpu_custom_call" | custom-call | tf_op jit(solution)/shard_map/second_step/pallas_call | solution.py:647
  87.0 3.7 %collective-permute-done.13.refs_1_ = bf16[4,128,256]{2,1,0:T(8,128)(2,1)S(1)} collective-permute-done((bf16[4,128,256]{2,1,0:T(8,128)(2,1)}, bf16[4,128,256]{2,1,0:T(8,128)(2,1)S(1)}, u32[]{:S(2)}, u32[]{:S(2)}) %collective-permute-start.13) | collective-permute-done | bytes 262176 | tf_op jit(solution)/shard_map/ppermute | solution.py:468
  90.8 4.9 %collective-permute-done.14.refs_2_ = bf16[4,128,256]{2,1,0:T(8,128)(2,1)S(1)} collective-permute-done((bf16[4,128,256]{2,1,0:T(8,128)(2,1)}, bf16[4,128,256]{2,1,0:T(8,128)(2,1)S(1)}, u32[]{:S(2)}, u32[]{:S(2)}) %collective-permute-start.14) | collective-permute-done | bytes 262176 | tf_op jit(solution)/shard_map/ppermute | solution.py:468
  97.2 8.5 %second_step.4 = (bf16[8,128,256]{2,1,0:T(8,128)(2,1)}, bf16[8,128,256]{2,1,0:T(8,128)(2,1)}, bf16[8,128,256]{2,1,0:T(8,128)(2,1)}, bf16[8,128,256]{2,1,0:T(8,128)(2,1)}) custom-call(s32[9]{0:T(128)} %stack.28.ids, f32[4,8,256,256]{3,2,1,0:T(8,128)} %get-tuple-element.77.mu_ref.mu_low.mu_high, f32[4,8,256,256]{3,2,1,0:T(8,128)} %get-tuple-element.77.mu_ref.mu_low.mu_high, ...), custom_call_target="tpu_custom_call" | custom-call | tf_op jit(solution)/shard_map/second_step/pallas_call | solution.py:647
  105.8 8.7 %second_step.5 = (bf16[8,128,256]{2,1,0:T(8,128)(2,1)}, bf16[8,128,256]{2,1,0:T(8,128)(2,1)}, bf16[8,128,256]{2,1,0:T(8,128)(2,1)}, bf16[8,128,256]{2,1,0:T(8,128)(2,1)}) custom-call(s32[9]{0:T(128)} %stack.28.ids, ...), custom_call_target="tpu_custom_call", output_to_operand_aliasing={{0}: (22, {}), {1}: (23, {}), {2}: (24, {}), {3}: (25, {})} | custom-call | tf_op jit(solution)/shard_map/second_step/pallas_call | solution.py:647
  118.5 4.2 %lat_filter.4 = (bf16[4,128,128]{2,1,0:T(8,128)(2,1)}, bf16[4,128,128]{2,1,0:T(8,128)(2,1)}, bf16[4,128,128]{2,1,0:T(8,128)(2,1)}, bf16[4,128,128]{2,1,0:T(8,128...) custom-call(s32[9]{0:T(128)} %stack.28.ids, ...), custom_call_target="tpu_custom_call" | custom-call | tf_op jit(solution)/shard_map/lat_filter/pallas_call | solution.py:705
  122.6 4.1 %lat_filter.5 = (bf16[4,128,128]{2,1,0:T(8,128)(2,1)}, bf16[4,128,128]{2,1,0:T(8,128)(2,1)}, bf16[4,128,128]{2,1,0:T(8,128)(2,1)}, bf16[4,128,128]{2,1,0:T(8,128...) custom-call(s32[9]{0:T(128)} %stack.28.ids, ...), custom_call_target="tpu_custom_call" | custom-call | tf_op jit(solution)/shard_map/lat_filter/pallas_call | solution.py:705
  126.7 3.1 %collective-permute-done.34.refs_2_ = bf16[8,128,256]{2,1,0:T(8,128)(2,1)} collective-permute-done((bf16[8,128,256]{2,1,0:T(8,128)(2,1)}, bf16[8,128,256]{2,1,0:T(8,128)(2,1)}, u32[]{:S(2)}, u32[]{:S(2)}) %collective-permute-start.34) | collective-permute-done | bytes 524320 | tf_op jit(solution)/shard_map/ppermute | solution.py:468
  129.8 4.5 %lat_filter.6 = (bf16[8,64,128]{2,1,0:T(8,128)(2,1)}, bf16[8,64,128]{2,1,0:T(8,128)(2,1)}, bf16[8,64,128]{2,1,0:T(8,128)(2,1)}, bf16[8,64,128]{2,1,0:T(8,128)(2,...) custom-call(s32[9]{0:T(128)} %stack.28.ids, ...), custom_call_target="tpu_custom_call" | custom-call | tf_op jit(solution)/shard_map/lat_filter/pallas_call | solution.py:705
  136.4 17.7 %collective-permute-start.26 = (bf16[4,128,128]{2,1,0:T(8,128)(2,1)}, bf16[4,128,128]{2,1,0:T(8,128)(2,1)S(1)}, u32[]{:S(2)}, u32[]{:S(2)}) collective-permute-start(bf16[4,128,128]{2,1,0:T(8,128)(2,1)} %get-tuple-element.113), channel_id=1, source_target_pairs={{0,1},{1,0},{2,3},{3,2},{4,5},{5,4},{6,7},{7,6},{8,9},{9,8},{10,11... | collective-permute-start | bytes 393224 | tf_op jit(solution)/shard_map/ppermute | solution.py:468
  158.5 5.1 %collective-permute-done.27.refs_10_ = bf16[4,128,128]{2,1,0:T(8,128)(2,1)S(1)} collective-permute-done((bf16[4,128,128]{2,1,0:T(8,128)(2,1)}, bf16[4,128,128]{2,1,0:T(8,128)(2,1)S(1)}, u32[]{:S(2)}, u32[]{:S(2)}) %collective-permute-start.27) | collective-permute-done | bytes 131104 | tf_op jit(solution)/shard_map/ppermute | solution.py:468
  163.5 3.1 %collective-permute-start.31 = (bf16[4,128,128]{2,1,0:T(8,128)(2,1)}, bf16[4,128,128]{2,1,0:T(8,128)(2,1)}, u32[]{:S(2)}, u32[]{:S(2)}) collective-permute-start(bf16[4,128,128]{2,1,0:T(8,128)(2,1)} %get-tuple-element.118), channel_id=1, source_target_pairs={{0,6},{1,7},{2,4},{3,5},{4,2},{5,3},{6,0},{7,1},{8,14},{9,15},{10,... | collective-permute-start | bytes 393224 | tf_op jit(solution)/shard_map/ppermute | solution.py:468
  168.6 6.2 %collective-permute-done.29.refs_12_ = bf16[4,128,128]{2,1,0:T(8,128)(2,1)} collective-permute-done((bf16[4,128,128]{2,1,0:T(8,128)(2,1)}, bf16[4,128,128]{2,1,0:T(8,128)(2,1)}, u32[]{:S(2)}, u32[]{:S(2)}) %collective-permute-start.29) | collective-permute-done | bytes 131104 | tf_op jit(solution)/shard_map/ppermute | solution.py:468
  179.3 4.3 %collective-permute-start.19 = (bf16[4,128,128]{2,1,0:T(8,128)(2,1)}, bf16[4,128,128]{2,1,0:T(8,128)(2,1)}, u32[]{:S(2)}, u32[]{:S(2)}) collective-permute-start(bf16[4,128,128]{2,1,0:T(8,128)(2,1)} %get-tuple-element.104), channel_id=1, source_target_pairs={{0,4},{1,5},{2,6},{3,7},{4,0},{5,1},{6,2},{7,3},{8,12},{9,13},{10,... | collective-permute-start | bytes 393224 | tf_op jit(solution)/shard_map/ppermute | solution.py:468
  183.6 4.4 %lat_filter.7 = (bf16[8,64,128]{2,1,0:T(8,128)(2,1)}, bf16[8,64,128]{2,1,0:T(8,128)(2,1)}, bf16[8,64,128]{2,1,0:T(8,128)(2,1)}, bf16[8,64,128]{2,1,0:T(8,128)(2,...) custom-call(s32[9]{0:T(128)} %stack.28.ids, ...), custom_call_target="tpu_custom_call" | custom-call | tf_op jit(solution)/shard_map/lat_filter/pallas_call | solution.py:705
  191.4 8.2 %collective-permute-done.19.refs_4_ = bf16[4,128,128]{2,1,0:T(8,128)(2,1)} collective-permute-done((bf16[4,128,128]{2,1,0:T(8,128)(2,1)}, bf16[4,128,128]{2,1,0:T(8,128)(2,1)}, u32[]{:S(2)}, u32[]{:S(2)}) %collective-permute-start.19) | collective-permute-done | bytes 131104 | tf_op jit(solution)/shard_map/ppermute | solution.py:468
  205.7 3.5 %collective-permute-done.50.refs_17_ = bf16[8,64,128]{2,1,0:T(8,128)(2,1)S(1)} collective-permute-done((bf16[8,64,128]{2,1,0:T(8,128)(2,1)}, bf16[8,64,128]{2,1,0:T(8,128)(2,1)S(1)}, u32[]{:S(2)}, u32[]{:S(2)}) %collective-permute-start.50) | collective-permute-done | bytes 131104 | tf_op jit(solution)/shard_map/ppermute | solution.py:468
  211.8 4.2 %collective-permute-done.51.refs_18_ = bf16[8,64,128]{2,1,0:T(8,128)(2,1)S(1)} collective-permute-done((bf16[8,64,128]{2,1,0:T(8,128)(2,1)}, bf16[8,64,128]{2,1,0:T(8,128)(2,1)S(1)}, u32[]{:S(2)}, u32[]{:S(2)}) %collective-permute-start.51) | collective-permute-done | bytes 131104 | tf_op jit(solution)/shard_map/ppermute | solution.py:468
  216.9 4.8 %collective-permute-done.52.refs_19_ = bf16[8,64,128]{2,1,0:T(8,128)(2,1)S(1)} collective-permute-done((bf16[8,64,128]{2,1,0:T(8,128)(2,1)}, bf16[8,64,128]{2,1,0:T(8,128)(2,1)S(1)}, u32[]{:S(2)}, u32[]{:S(2)}) %collective-permute-start.52) | collective-permute-done | bytes 131104 | tf_op jit(solution)/shard_map/ppermute | solution.py:468
  223.5 7.6 %collective-permute-done.53.refs_20_ = bf16[8,64,128]{2,1,0:T(8,128)(2,1)S(1)} collective-permute-done((bf16[8,64,128]{2,1,0:T(8,128)(2,1)}, bf16[8,64,128]{2,1,0:T(8,128)(2,1)S(1)}, u32[]{:S(2)}, u32[]{:S(2)}) %collective-permute-start.53) | collective-permute-done | bytes 131104 | tf_op jit(solution)/shard_map/ppermute | solution.py:468
  231.2 8.2 %collective-permute-done.54.refs_21_ = bf16[8,64,128]{2,1,0:T(8,128)(2,1)S(1)} collective-permute-done((bf16[8,64,128]{2,1,0:T(8,128)(2,1)}, bf16[8,64,128]{2,1,0:T(8,128)(2,1)S(1)}, u32[]{:S(2)}, u32[]{:S(2)}) %collective-permute-start.54) | collective-permute-done | bytes 131104 | tf_op jit(solution)/shard_map/ppermute | solution.py:468
  241.4 5.4 %collective-permute-done.55.refs_22_ = bf16[8,64,128]{2,1,0:T(8,128)(2,1)S(1)} collective-permute-done((bf16[8,64,128]{2,1,0:T(8,128)(2,1)}, bf16[8,64,128]{2,1,0:T(8,128)(2,1)S(1)}, u32[]{:S(2)}, u32[]{:S(2)}) %collective-permute-start.55) | collective-permute-done | bytes 131104 | tf_op jit(solution)/shard_map/ppermute | solution.py:468
  247.8 6.2 %collective-permute-done.56.refs_23_ = bf16[8,64,128]{2,1,0:T(8,128)(2,1)S(1)} collective-permute-done((bf16[8,64,128]{2,1,0:T(8,128)(2,1)}, bf16[8,64,128]{2,1,0:T(8,128)(2,1)S(1)}, u32[]{:S(2)}, u32[]{:S(2)}) %collective-permute-start.56) | collective-permute-done | bytes 131104 | tf_op jit(solution)/shard_map/ppermute | solution.py:468
  261.8 11.4 %lon_filter.2.refs_32_ = f32[1024,2048]{1,0:T(8,128)} custom-call(s32[9]{0:T(128)} %stack.28.ids, bf16[4,128,128]{2,1,0:T(8,128)(2,1)} %get-tuple-element.100.refs_0_, bf16[4,128,128]{2,1,0:T(8,128)(2,1)} %collective-permute-done.16.refs_1_, bf16[4,128,128]{2,1,0:T(8,128)(2,1)} %collective-permute-done.17.refs_2_, ...), custom_call_target="tpu_custom_call" | custom-call | tf_op jit(solution)/shard_map/lon_filter/pallas_call | solution.py:775
  274.7 11.2 %lon_filter.3 = f32[1024,2048]{1,0:T(8,128)} custom-call(s32[9]{0:T(128)} %stack.28.ids, bf16[4,128,128]{2,1,0:T(8,128)(2,1)} %get-tuple-element.100.refs_0_, bf16[4,128,128]{2,1,0:T(8,128)(2,1)} %collective-permute-done.16.refs_1_, bf16[4,128,128]{2,1,0:T(8,128)(2,1)} %collective-permute-done.17.refs_2_, ...), custom_call_target="tpu_custom_call", output_to_operand_aliasing={{}: (33, {})} | custom-call | tf_op jit(solution)/shard_map/lon_filter/pallas_call | solution.py:775
  (182 shorter events, 70.1 us)
Async XLA Ops:
  10.0 24.1 %collective-permute-start.9 = (f32[2,32,256]{2,1,0:T(8,128)S(1)}, f32[2,32,256]{2,1,0:T(8,128)S(1)}, u32[]{:S(2)}, u32[]{:S(2)}) collective-permute-start(f32[2,32,256]{2,1,0:T(8,128)S(1)} %pad_maximum_fusion.2), channel_id=1, source_target_pairs={{0,4},{1,5},{2,6},{3,7},{4,0},{5,1},{6,2},{7,3},{8,12},{9,13},{10,... | collective-permute-start | bytes 196616 | tf_op jit(solution)/shard_map/ppermute | solution.py:468
  81.5 52.8 %collective-permute-start.44 = (bf16[256,2048]{1,0:T(8,128)(2,1)S(1)}, bf16[256,2048]{1,0:T(8,128)(2,1)S(1)}, u32[]{:S(2)}, u32[]{:S(2)}) collective-permute-start(bf16[256,2048]{1,0:T(8,128)(2,1)S(1)} %constant_dynamic-slice_fusion.refs_24_), channel_id=1, source_target_pairs={{0,8},{1,17},{2,10},{3,19},{4,12},{5,21},{6,14},{7,23},{8,0},{9,25... | collective-permute-start | bytes 3145736 | tf_op jit(solution)/shard_map/ppermute | solution.py:526
  83.6 12.2 %collective-permute-start.14 = (bf16[4,128,256]{2,1,0:T(8,128)(2,1)}, bf16[4,128,256]{2,1,0:T(8,128)(2,1)S(1)}, u32[]{:S(2)}, u32[]{:S(2)}) collective-permute-start(bf16[4,128,256]{2,1,0:T(8,128)(2,1)} %get-tuple-element.94), channel_id=1, source_target_pairs={{0,16},{8,24},{16,0},{24,8},{1,17},{9,25},{17,1},{25,9},{2,18},{10... | collective-permute-start | bytes 786440 | tf_op jit(solution)/shard_map/ppermute | solution.py:468
  83.7 30.9 %collective-permute-start.15 = (bf16[4,128,256]{2,1,0:T(8,128)(2,1)}, bf16[4,128,256]{2,1,0:T(8,128)(2,1)S(1)}, u32[]{:S(2)}, u32[]{:S(2)}) collective-permute-start(bf16[4,128,256]{2,1,0:T(8,128)(2,1)} %get-tuple-element.95), channel_id=1, source_target_pairs={{0,24},{8,16},{16,8},{24,0},{1,25},{9,17},{17,9},{25,1},{2,26},{10... | collective-permute-start | bytes 786440 | tf_op jit(solution)/shard_map/ppermute | solution.py:468
  85.1 29.5 %collective-permute-start.23 = (bf16[4,128,256]{2,1,0:T(8,128)(2,1)}, bf16[4,128,256]{2,1,0:T(8,128)(2,1)S(1)}, u32[]{:S(2)}, u32[]{:S(2)}) collective-permute-start(bf16[4,128,256]{2,1,0:T(8,128)(2,1)} %get-tuple-element.109), channel_id=1, source_target_pairs={{0,8},{8,0},{16,24},{24,16},{1,9},{9,1},{17,25},{25,17},{2,10},{10... | collective-permute-start | bytes 786440 | tf_op jit(solution)/shard_map/ppermute | solution.py:468
  90.8 25.9 %collective-permute-start.24 = (bf16[4,128,256]{2,1,0:T(8,128)(2,1)}, bf16[4,128,256]{2,1,0:T(8,128)(2,1)S(1)}, u32[]{:S(2)}, u32[]{:S(2)}) collective-permute-start(bf16[4,128,256]{2,1,0:T(8,128)(2,1)} %get-tuple-element.110), channel_id=1, source_target_pairs={{0,16},{8,24},{16,0},{24,8},{1,17},{9,25},{17,1},{25,9},{2,18},{10... | collective-permute-start | bytes 786440 | tf_op jit(solution)/shard_map/ppermute | solution.py:468
  95.8 22.4 %collective-permute-start.25 = (bf16[4,128,256]{2,1,0:T(8,128)(2,1)}, bf16[4,128,256]{2,1,0:T(8,128)(2,1)}, u32[]{:S(2)}, u32[]{:S(2)}) collective-permute-start(bf16[4,128,256]{2,1,0:T(8,128)(2,1)} %get-tuple-element.96), channel_id=1, source_target_pairs={{0,24},{8,16},{16,8},{24,0},{1,25},{9,17},{17,9},{25,1},{2,26},{10... | collective-permute-start | bytes 786440 | tf_op jit(solution)/shard_map/ppermute | solution.py:468
  114.6 12.2 %collective-permute-start.33 = (bf16[8,128,256]{2,1,0:T(8,128)(2,1)}, bf16[8,128,256]{2,1,0:T(8,128)(2,1)}, u32[]{:S(2)}, u32[]{:S(2)}) collective-permute-start(bf16[8,128,256]{2,1,0:T(8,128)(2,1)} %get-tuple-element.124), channel_id=1, source_target_pairs={{0,8},{8,0},{16,24},{24,16},{1,9},{9,1},{17,25},{25,17},{2,10},{10... | collective-permute-start | bytes 1572872 | tf_op jit(solution)/shard_map/ppermute | solution.py:468
  114.7 15.2 %collective-permute-start.34 = (bf16[8,128,256]{2,1,0:T(8,128)(2,1)}, bf16[8,128,256]{2,1,0:T(8,128)(2,1)}, u32[]{:S(2)}, u32[]{:S(2)}) collective-permute-start(bf16[8,128,256]{2,1,0:T(8,128)(2,1)} %get-tuple-element.125), channel_id=1, source_target_pairs={{0,16},{8,24},{16,0},{24,8},{1,17},{9,25},{17,1},{25,9},{2,18},{10... | collective-permute-start | bytes 1572872 | tf_op jit(solution)/shard_map/ppermute | solution.py:468
  116.6 13.2 %collective-permute-start.35 = (bf16[8,128,256]{2,1,0:T(8,128)(2,1)}, bf16[8,128,256]{2,1,0:T(8,128)(2,1)}, u32[]{:S(2)}, u32[]{:S(2)}) collective-permute-start(bf16[8,128,256]{2,1,0:T(8,128)(2,1)} %get-tuple-element.126), channel_id=1, source_target_pairs={{0,24},{8,16},{16,8},{24,0},{1,25},{9,17},{17,9},{25,1},{2,26},{10... | collective-permute-start | bytes 1572872 | tf_op jit(solution)/shard_map/ppermute | solution.py:468
  118.1 37.7 %collective-permute-start.46 = (bf16[256,2048]{1,0:T(8,128)(2,1)S(1)}, bf16[256,2048]{1,0:T(8,128)(2,1)S(1)}, u32[]{:S(2)}, u32[]{:S(2)}) collective-permute-start(bf16[256,2048]{1,0:T(8,128)(2,1)S(1)} %constant_dynamic-slice_fusion.refs_24_), channel_id=1, source_target_pairs={{0,16},{1,9},{2,18},{3,11},{4,20},{5,13},{6,22},{7,15},{8,24},{9,1... | collective-permute-start | bytes 3145736 | tf_op jit(solution)/shard_map/ppermute | solution.py:526
  134.4 65.2 %collective-permute-start.48 = (bf16[256,2048]{1,0:T(8,128)(2,1)S(1)}, bf16[256,2048]{1,0:T(8,128)(2,1)}, u32[]{:S(2)}, u32[]{:S(2)}) collective-permute-start(bf16[256,2048]{1,0:T(8,128)(2,1)S(1)} %collective-permute-done.44.refs_26_), channel_id=1, source_target_pairs={{0,16},{1,9},{2,18},{3,11},{4,20},{5,13},{6,22},{7,15},{8,24},{9,1... | collective-permute-start | bytes 3145736 | tf_op jit(solution)/shard_map/ppermute | solution.py:526
  136.4 20.5 %collective-permute-start.26 = (bf16[4,128,128]{2,1,0:T(8,128)(2,1)}, bf16[4,128,128]{2,1,0:T(8,128)(2,1)S(1)}, u32[]{:S(2)}, u32[]{:S(2)}) collective-permute-start(bf16[4,128,128]{2,1,0:T(8,128)(2,1)} %get-tuple-element.113), channel_id=1, source_target_pairs={{0,1},{1,0},{2,3},{3,2},{4,5},{5,4},{6,7},{7,6},{8,9},{9,8},{10,11... | collective-permute-start | bytes 393224 | tf_op jit(solution)/shard_map/ppermute | solution.py:468
  155.9 18.9 %collective-permute-start.29 = (bf16[4,128,128]{2,1,0:T(8,128)(2,1)}, bf16[4,128,128]{2,1,0:T(8,128)(2,1)}, u32[]{:S(2)}, u32[]{:S(2)}) collective-permute-start(bf16[4,128,128]{2,1,0:T(8,128)(2,1)} %get-tuple-element.116), channel_id=1, source_target_pairs={{0,4},{1,5},{2,6},{3,7},{4,0},{5,1},{6,2},{7,3},{8,12},{9,13},{10,... | collective-permute-start | bytes 393224 | tf_op jit(solution)/shard_map/ppermute | solution.py:468
  156.9 19.4 %collective-permute-start.30 = (bf16[4,128,128]{2,1,0:T(8,128)(2,1)}, bf16[4,128,128]{2,1,0:T(8,128)(2,1)}, u32[]{:S(2)}, u32[]{:S(2)}) collective-permute-start(bf16[4,128,128]{2,1,0:T(8,128)(2,1)} %get-tuple-element.117), channel_id=1, source_target_pairs={{0,5},{1,4},{2,7},{3,6},{4,1},{5,0},{6,3},{7,2},{8,13},{9,12},{10,... | collective-permute-start | bytes 393224 | tf_op jit(solution)/shard_map/ppermute | solution.py:468
  163.5 12.9 %collective-permute-start.31 = (bf16[4,128,128]{2,1,0:T(8,128)(2,1)}, bf16[4,128,128]{2,1,0:T(8,128)(2,1)}, u32[]{:S(2)}, u32[]{:S(2)}) collective-permute-start(bf16[4,128,128]{2,1,0:T(8,128)(2,1)} %get-tuple-element.118), channel_id=1, source_target_pairs={{0,6},{1,7},{2,4},{3,5},{4,2},{5,3},{6,0},{7,1},{8,14},{9,15},{10,... | collective-permute-start | bytes 393224 | tf_op jit(solution)/shard_map/ppermute | solution.py:468
  166.6 12.7 %collective-permute-start.32 = (bf16[4,128,128]{2,1,0:T(8,128)(2,1)}, bf16[4,128,128]{2,1,0:T(8,128)(2,1)}, u32[]{:S(2)}, u32[]{:S(2)}) collective-permute-start(bf16[4,128,128]{2,1,0:T(8,128)(2,1)} %get-tuple-element.119), channel_id=1, source_target_pairs={{0,7},{1,6},{2,5},{3,4},{4,3},{5,2},{6,1},{7,0},{8,15},{9,14},{10,... | collective-permute-start | bytes 393224 | tf_op jit(solution)/shard_map/ppermute | solution.py:468
  176.2 11.8 %collective-permute-start.17 = (bf16[4,128,128]{2,1,0:T(8,128)(2,1)}, bf16[4,128,128]{2,1,0:T(8,128)(2,1)}, u32[]{:S(2)}, u32[]{:S(2)}) collective-permute-start(bf16[4,128,128]{2,1,0:T(8,128)(2,1)} %get-tuple-element.102), channel_id=1, source_target_pairs={{0,2},{1,3},{2,0},{3,1},{4,6},{5,7},{6,4},{7,5},{8,10},{9,11},{10,... | collective-permute-start | bytes 393224 | tf_op jit(solution)/shard_map/ppermute | solution.py:468
  176.4 13.1 %collective-permute-start.18 = (bf16[4,128,128]{2,1,0:T(8,128)(2,1)}, bf16[4,128,128]{2,1,0:T(8,128)(2,1)}, u32[]{:S(2)}, u32[]{:S(2)}) collective-permute-start(bf16[4,128,128]{2,1,0:T(8,128)(2,1)} %get-tuple-element.103), channel_id=1, source_target_pairs={{0,3},{1,2},{2,1},{3,0},{4,7},{5,6},{6,5},{7,4},{8,11},{9,10},{10,... | collective-permute-start | bytes 393224 | tf_op jit(solution)/shard_map/ppermute | solution.py:468
  179.3 20.2 %collective-permute-start.19 = (bf16[4,128,128]{2,1,0:T(8,128)(2,1)}, bf16[4,128,128]{2,1,0:T(8,128)(2,1)}, u32[]{:S(2)}, u32[]{:S(2)}) collective-permute-start(bf16[4,128,128]{2,1,0:T(8,128)(2,1)} %get-tuple-element.104), channel_id=1, source_target_pairs={{0,4},{1,5},{2,6},{3,7},{4,0},{5,1},{6,2},{7,3},{8,12},{9,13},{10,... | collective-permute-start | bytes 393224 | tf_op jit(solution)/shard_map/ppermute | solution.py:468
  183.6 17.6 %collective-permute-start.20 = (bf16[4,128,128]{2,1,0:T(8,128)(2,1)}, bf16[4,128,128]{2,1,0:T(8,128)(2,1)}, u32[]{:S(2)}, u32[]{:S(2)}) collective-permute-start(bf16[4,128,128]{2,1,0:T(8,128)(2,1)} %get-tuple-element.105), channel_id=1, source_target_pairs={{0,5},{1,4},{2,7},{3,6},{4,1},{5,0},{6,3},{7,2},{8,13},{9,12},{10,... | collective-permute-start | bytes 393224 | tf_op jit(solution)/shard_map/ppermute | solution.py:468
  188.1 14.1 %collective-permute-start.21 = (bf16[4,128,128]{2,1,0:T(8,128)(2,1)}, bf16[4,128,128]{2,1,0:T(8,128)(2,1)}, u32[]{:S(2)}, u32[]{:S(2)}) collective-permute-start(bf16[4,128,128]{2,1,0:T(8,128)(2,1)} %get-tuple-element.106), channel_id=1, source_target_pairs={{0,6},{1,7},{2,4},{3,5},{4,2},{5,3},{6,0},{7,1},{8,14},{9,15},{10,... | collective-permute-start | bytes 393224 | tf_op jit(solution)/shard_map/ppermute | solution.py:468
  189.5 12.8 %collective-permute-start.22 = (bf16[4,128,128]{2,1,0:T(8,128)(2,1)}, bf16[4,128,128]{2,1,0:T(8,128)(2,1)}, u32[]{:S(2)}, u32[]{:S(2)}) collective-permute-start(bf16[4,128,128]{2,1,0:T(8,128)(2,1)} %get-tuple-element.107), channel_id=1, source_target_pairs={{0,7},{1,6},{2,5},{3,4},{4,3},{5,2},{6,1},{7,0},{8,15},{9,14},{10,... | collective-permute-start | bytes 393224 | tf_op jit(solution)/shard_map/ppermute | solution.py:468
  201.2 52.8 %collective-permute-start.43 = (bf16[256,2048]{1,0:T(8,128)(2,1)S(1)}, bf16[256,2048]{1,0:T(8,128)(2,1)S(1)}, u32[]{:S(2)}, u32[]{:S(2)}) collective-permute-start(bf16[256,2048]{1,0:T(8,128)(2,1)S(1)} %constant_dynamic-slice_fusion.refs_24_), channel_id=1, source_target_pairs={{0,1},{1,0},{2,3},{3,2},{4,5},{5,4},{6,7},{7,6},{8,9},{9,8},{10,11... | collective-permute-start | bytes 3145736 | tf_op jit(solution)/shard_map/ppermute | solution.py:468
  202.2 53.7 %collective-permute-start.45 = (bf16[256,2048]{1,0:T(8,128)(2,1)S(1)}, bf16[256,2048]{1,0:T(8,128)(2,1)S(1)}, u32[]{:S(2)}, u32[]{:S(2)}) collective-permute-start(bf16[256,2048]{1,0:T(8,128)(2,1)S(1)} %collective-permute-done.44.refs_26_), channel_id=1, source_target_pairs={{0,1},{1,0},{2,3},{3,2},{4,5},{5,4},{6,7},{7,6},{8,9},{9,8},{10,11... | collective-permute-start | bytes 3145736 | tf_op jit(solution)/shard_map/ppermute | solution.py:468
  202.3 54.3 %collective-permute-start.47 = (bf16[256,2048]{1,0:T(8,128)(2,1)S(1)}, bf16[256,2048]{1,0:T(8,128)(2,1)S(1)}, u32[]{:S(2)}, u32[]{:S(2)}) collective-permute-start(bf16[256,2048]{1,0:T(8,128)(2,1)S(1)} %collective-permute-done.46.refs_28_), channel_id=1, source_target_pairs={{0,1},{1,0},{2,3},{3,2},{4,5},{5,4},{6,7},{7,6},{8,9},{9,8},{10,11... | collective-permute-start | bytes 3145736 | tf_op jit(solution)/shard_map/ppermute | solution.py:468
  202.7 55.8 %collective-permute-start.49 = (bf16[256,2048]{1,0:T(8,128)(2,1)}, bf16[256,2048]{1,0:T(8,128)(2,1)S(1)}, u32[]{:S(2)}, u32[]{:S(2)}) collective-permute-start(bf16[256,2048]{1,0:T(8,128)(2,1)} %collective-permute-done.48.refs_30_), channel_id=1, source_target_pairs={{0,1},{1,0},{2,3},{3,2},{4,5},{5,4},{6,7},{7,6},{8,9},{9,8},{10,11... | collective-permute-start | bytes 3145736 | tf_op jit(solution)/shard_map/ppermute | solution.py:468
  254.1 19.2 %collective-permute-start.38 = (bf16[8,64,128]{2,1,0:T(8,128)(2,1)}, bf16[8,64,128]{2,1,0:T(8,128)(2,1)}, u32[]{:S(2)}, u32[]{:S(2)}) collective-permute-start(bf16[8,64,128]{2,1,0:T(8,128)(2,1)} %get-tuple-element.133), channel_id=1, source_target_pairs={{0,3},{1,2},{2,1},{3,0},{4,7},{5,6},{6,5},{7,4},{8,11},{9,10},{10,... | collective-permute-start | bytes 393224 | tf_op jit(solution)/shard_map/ppermute | solution.py:468
  254.1 19.2 %collective-permute-start.39 = (bf16[8,64,128]{2,1,0:T(8,128)(2,1)}, bf16[8,64,128]{2,1,0:T(8,128)(2,1)S(1)}, u32[]{:S(2)}, u32[]{:S(2)}) collective-permute-start(bf16[8,64,128]{2,1,0:T(8,128)(2,1)} %get-tuple-element.134), channel_id=1, source_target_pairs={{0,4},{1,5},{2,6},{3,7},{4,0},{5,1},{6,2},{7,3},{8,12},{9,13},{10,... | collective-permute-start | bytes 393224 | tf_op jit(solution)/shard_map/ppermute | solution.py:468
  255.9 18.1 %collective-permute-start.40 = (bf16[8,64,128]{2,1,0:T(8,128)(2,1)}, bf16[8,64,128]{2,1,0:T(8,128)(2,1)S(1)}, u32[]{:S(2)}, u32[]{:S(2)}) collective-permute-start(bf16[8,64,128]{2,1,0:T(8,128)(2,1)} %get-tuple-element.135), channel_id=1, source_target_pairs={{0,5},{1,4},{2,7},{3,6},{4,1},{5,0},{6,3},{7,2},{8,13},{9,12},{10,... | collective-permute-start | bytes 393224 | tf_op jit(solution)/shard_map/ppermute | solution.py:468
  256.8 17.1 %collective-permute-start.41 = (bf16[8,64,128]{2,1,0:T(8,128)(2,1)}, bf16[8,64,128]{2,1,0:T(8,128)(2,1)S(1)}, u32[]{:S(2)}, u32[]{:S(2)}) collective-permute-start(bf16[8,64,128]{2,1,0:T(8,128)(2,1)} %get-tuple-element.136), channel_id=1, source_target_pairs={{0,6},{1,7},{2,4},{3,5},{4,2},{5,3},{6,0},{7,1},{8,14},{9,15},{10,... | collective-permute-start | bytes 393224 | tf_op jit(solution)/shard_map/ppermute | solution.py:468
  259.5 14.5 %collective-permute-start.42 = (bf16[8,64,128]{2,1,0:T(8,128)(2,1)}, bf16[8,64,128]{2,1,0:T(8,128)(2,1)S(1)}, u32[]{:S(2)}, u32[]{:S(2)}) collective-permute-start(bf16[8,64,128]{2,1,0:T(8,128)(2,1)} %get-tuple-element.137), channel_id=1, source_target_pairs={{0,7},{1,6},{2,5},{3,4},{4,3},{5,2},{6,1},{7,0},{8,15},{9,14},{10,... | collective-permute-start | bytes 393224 | tf_op jit(solution)/shard_map/ppermute | solution.py:468
  (65 other events, 1314.9 us)

commit v5 on v4

--- a/solution.py
+++ b/solution.py
@@ -417,16 +417,54 @@
                     outs[s][step * p + c] = value.astype(BF16)
 
 
-def lon_filter_part(half, height, cols, parts, n_first, aliased, owners, ids, *refs):
-    firsts = refs[:n_first]
-    lasts = refs[n_first : n_first + cols]
-    filters = refs[n_first + cols : n_first + cols + 2 * parts]
-    rest = refs[n_first + cols + 2 * parts + (1 if aliased else 0) :]
-    out, lines, stage, sem = rest
+def columns(ref, cols, wide, begin, end):
+    return jnp.concatenate([ref[:, k * wide + begin : k * wide + end] for k in range(cols)], axis=1)
+
+
+def lon_first_part(cols, parts, groups, ids, *refs):
+    n_first = len(refs) - 2 * parts - 5
+    firsts, filters = refs[:n_first], refs[n_first : n_first + 2 * parts]
+    outs, (lines, stage, sem) = refs[n_first + 2 * parts : -3], refs[-3:]
+    each, height, lon = firsts[0].shape
+    half = height // 2
+    bands = n_first // cols // groups
+    rows = lines.shape[0] // 2
+    wide = filters[0].shape[1] // cols
+
+    def flush(p, h):
+        return pltpu.make_async_copy(stage.at[p % 2, h], outs[h].at[p], sem.at[p % 2, h])
+
+    for s in range(cols):
+        for b in range(bands):
+            at = pl.ds(pl.multiple_of(((ids[1] ^ s) * bands + b) * lon, LANES), lon)
+            for c in range(each * groups):
+                ref = firsts[(b * groups + c // each) * cols + s]
+                for h in range(2):
+                    put = h * rows + c * half
+                    lines[put : put + half, at] = ref[c % each, h * half : (h + 1) * half]
+    for p in range(parts):
+        right = jnp.concatenate([columns(filters[2 * p + j], cols, wide, 0, bands * lon) for j in range(2)], axis=0)
+        acc = lax.dot_general(lines[...], right, NT, preferred_element_type=F32)
+        for h in range(2):
+            if p >= 2:
+                flush(p - 2, h).wait()
+            stage[p % 2, h] = acc[h * rows : (h + 1) * rows]
+            flush(p, h).start()
+    for p in range(max(0, parts - 2), parts):
+        for h in range(2):
+            flush(p, h).wait()
+
+
+def lon_filter_part(half, height, cols, parts, n_partial, aliased, owners, ids, *refs):
+    partial = refs[:n_partial]
+    lasts = refs[n_partial : n_partial + cols]
+    filters = refs[n_partial + cols : n_partial + cols + 2 * parts]
+    rest = refs[n_partial + cols + 2 * parts + (1 if aliased else 0) :]
+    out, lines, stage, sem, earlier, in_sem = rest
     channels, _, lon = lasts[0].shape
-    wide = lines.shape[1] // cols
     rows = channels * height
-    block = filters[0].shape[0]
+    block, total = filters[0].shape
+    wide = total // cols
     strips = block // LANES
 
     def flush(j, k):
@@ -437,19 +475,22 @@
         slot = j % 4
         return pltpu.make_async_copy(stage.at[slot, k], out.at[pl.ds(half * rows, rows), at], sem.at[slot, k])
 
+    def fetch(p):
+        return pltpu.make_async_copy(partial[0].at[p], earlier.at[p % 2], in_sem.at[p % 2])
+
+    if n_partial:
+        for p in range(min(2, parts)):
+            fetch(p).start()
     for s in range(cols):
-        base = pl.multiple_of((ids[1] ^ s) * wide, LANES)
+        at = pl.ds(pl.multiple_of((ids[1] ^ s) * lon, LANES), lon)
         for c in range(channels):
-            put = slice(c * height, (c + 1) * height)
-            for b in range(wide // lon - 1):
-                groups = n_first // cols // (wide // lon - 1)
-                each = channels // groups
-                ref = firsts[(b * groups + c // each) * cols + s]
-                lines[put, pl.ds(base + b * lon, lon)] = ref[c % each, half * height : (half + 1) * height]
-            lines[put, pl.ds(base + wide - lon, lon)] = lasts[s][c]
+            lines[c * height : (c + 1) * height, at] = lasts[s][c]
     for p in range(parts):
-        right = jnp.concatenate([filters[2 * p][...], filters[2 * p + 1][...]], axis=0)
+        right = jnp.concatenate([columns(filters[2 * p + j], cols, wide, wide - lon, wide) for j in range(2)], axis=0)
         acc = lax.dot_general(lines[...], right, NT, preferred_element_type=F32)
+        if n_partial:
+            fetch(p).wait()
+            acc = acc + earlier[p % 2]
         for j in (2 * p, 2 * p + 1):
             for k in range(strips):
                 if j >= 4:
@@ -458,6 +499,8 @@
                 for c in range(channels):
                     stage[j % 4, k, pl.ds(c, height, stride=channels), :] = acc[c * height : (c + 1) * height, begin : begin + LANES]
                 flush(j, k).start()
+        if n_partial and p + 2 < parts:
+            fetch(p + 2).start()
     for j in range(max(0, 2 * parts - 4), 2 * parts):
         for k in range(strips):
             flush(j, k).wait()
@@ -736,12 +779,11 @@
         moved, token = smooth(sent[-1], h * half_height, half_height, token)
         lasts.append(moved)
     for stage in range(len(orders)):
-        gathered += [direct[stage]] + gather(stage, [after(piece, early) for piece in gathered[1:]])
+        gathered += [direct[stage]] + gather(stage, [after(piece, sent[-1][-1]) for piece in gathered[1:]])
         owners += [(a ^ turns[0][stage], b ^ turns[1][stage]) for a, b in owners]
     filters = []
-    for j, piece in enumerate(gathered):
-        late = j and j == len(gathered) - 1
-        filters += [piece, swap(after(piece, token if late else early), "col", 1)]
+    for piece in gathered:
+        filters += [piece, swap(after(piece, early), "col", 1)]
 
     n_lon = cols_count * lon_block
     rows = share * half_height
@@ -755,19 +797,37 @@
             owner = (me_row ^ jnp.where(side == 0, *owners[j // 2])) * 2 + side
             whole_filter = lax.dynamic_update_slice_in_dim(whole_filter, piece, owner * height, 0)
         return jnp.einsum("lci,oi->lco", lines, whole_filter, preferred_element_type=F32)
+    partial = ()
+    if firsts:
+        call = pl.pallas_call(
+            functools.partial(lon_first_part, cols_count, rows_count, 2),
+            out_shape=(shape_of((rows_count, rows, 2 * height)),) * 2,
+            in_specs=[SMEM_SPEC] + [VMEM_SPEC] * (len(firsts) + 2 * rows_count),
+            out_specs=(ANY_SPEC,) * 2,
+            scratch_shapes=[
+                pltpu.VMEM((2 * rows, n_lon - cols_count * tall), BF16),
+                pltpu.VMEM((2, 2, rows, 2 * height), F32),
+                pltpu.SemaphoreType.DMA((2, 2)),
+            ],
+            name="lon_first",
+        )
+        partial = call(ids, *firsts, *filters)
     out = None
     for h in range(2):
         aliased = out is not None
-        operands = (ids, *firsts, *lasts[h], *filters) + ((out,) if aliased else ())
+        held = partial[h : h + 1]
+        operands = (ids, *held, *lasts[h], *filters) + ((out,) if aliased else ())
         call = pl.pallas_call(
-            functools.partial(lon_filter_part, h, half_height, cols_count, rows_count, len(firsts), aliased, owners),
+            functools.partial(lon_filter_part, h, half_height, cols_count, rows_count, len(held), aliased, owners),
             out_shape=shape_of((2 * rows, n_lon)),
-            in_specs=[SMEM_SPEC] + [VMEM_SPEC] * (len(firsts) + cols_count + 2 * rows_count) + [ANY_SPEC] * aliased,
+            in_specs=[SMEM_SPEC] + [ANY_SPEC] * len(held) + [VMEM_SPEC] * (cols_count + 2 * rows_count) + [ANY_SPEC] * aliased,
             out_specs=ANY_SPEC,
             scratch_shapes=[
-                pltpu.VMEM((rows, n_lon), BF16),
+                pltpu.VMEM((rows, cols_count * tall), BF16),
                 pltpu.VMEM((4, height // LANES, rows, LANES), F32),
                 pltpu.SemaphoreType.DMA((4, height // LANES)),
+                pltpu.VMEM((2, rows, 2 * height), F32),
+                pltpu.SemaphoreType.DMA((2,)),
             ],
             input_output_aliases={len(operands) - 1: 0} if aliased else {},
             name="lon_filter",

time: 292 us -> 307 us (1.051); the launches traced: 286 us -> 307 us
  waiting for transfers between devices: 90.2 us -> 110 us
  starting transfers between devices: 89 us -> 78.8 us
  Pallas kernels: 99.7 us -> 109 us
    ppermute x46, waiting for transfers between devices: 89.2 us -> 109 us  [swap(): return lax.ppermute(value, axis, [(i, i ^ mask) for i in range(count)])]
    pallas_call x0 -> x1, Pallas kernels: none -> 11 us  [shards(): partial = call(ids, *firsts, *filters)]
    ppermute x46, starting transfers between devices: 70.5 us -> 60.9 us  [swap(): return lax.ppermute(value, axis, [(i, i ^ mask) for i in range(count)])]
  transfers between devices with their start and end apart: 57 -> 57, of which waited for: 20 -> 23; matrix products, arithmetic and copies ran while one was open for 0% -> 1% of each run, Pallas kernels for 25% -> 32%
where the time goes in v5:
time: 307 us
  waiting for transfers between devices  110 us (36%)
  Pallas kernels  109 us (36%)
  starting transfers between devices  78.8 us (26%)
  local copies, waits for them, and re-layouts  5.66 us (2%)
    ppermute x46, waiting for transfers between devices, swap(): return lax.ppermute(value, axis, [(i, i ^ mask) for i in range(count)])  109 us
    ppermute x46, starting transfers between devices, swap(): return lax.ppermute(value, axis, [(i, i ^ mask) for i in range(count)])  60.9 us
    pallas_call x3, Pallas kernels, control(): pl.pallas_call(functools.partial(second_step, band * tall + part * (tall...  31 us
    pallas_call x2, Pallas kernels, shards(): out = call(*operands)  21.2 us
    pallas_call x1, Pallas kernels, shards(): mu1, ef, em, ew, xr, xm, xw = call(mu, courant, limiter, directions)  21.1 us
    pallas_call x4, Pallas kernels, smooth(): outs = call(ids, *pieces, filt)  17.2 us
    ppermute x8, starting transfers between devices, neighbours(): return lax.ppermute(value, axis, pairs)  14 us
    pallas_call x1, Pallas kernels, shards(): partial = call(ids, *firsts, *filters)  11 us
  transfers between devices with their start and end apart: 57, of which 23 were waited for; matrix products, arithmetic and copies ran while one was open for 1% of the time, Pallas kernels for 32%

profile of v5, /device:TPU:0, one launch (start us, length us, event | category | flops | bytes accessed | tf_op | source)
XLA Modules:
  0.0 306.7 jit_solution(12321197298528256657)
XLA Ops:
  13.0 21.1 %first_step.1 = (f32[4,8,256,256]{3,2,1,0:T(8,128)}, f32[128,128]{1,0:T(8,128)}, f32[128,128]{1,0:T(8,128)}, f32[128,128]{1,0:T(8,128)}, f32[9,8,256]{2,1,0:T(8,...) custom-call(f32[4,8,256,256]{3,2,1,0:T(8,128)} %bitcast.14, f32[2,2,8,256,256]{4,3,2,1,0:T(8,128)} %cx_high.5, ...), custom_call_target="tpu_custom_call" | custom-call | tf_op jit(solution)/shard_map/first_step/pallas_call | solution.py:640
  36.4 4.3 %collective-permute-start = (f32[128,128]{1,0:T(8,128)}, f32[128,128]{1,0:T(8,128)S(1)}, u32[]{:S(2)}, u32[]{:S(2)}) collective-permute-start(f32[128,128]{1,0:T(8,128)} %get-tuple-element.81), channel_id=1, source_target_pairs={{0,8},{8,0},{16,24},{24,16},{1,9},{9,1},{17,25},{25,17},{2,10},{10... | collective-permute-start | bytes 196616 | tf_op jit(solution)/shard_map/ppermute | solution.py:519
  47.4 7.1 %collective-permute-done.11 = f32[8,32,256]{2,1,0:T(8,128)S(1)} collective-permute-done((f32[8,32,256]{2,1,0:T(8,128)S(1)}, f32[8,32,256]{2,1,0:T(8,128)S(1)}, u32[]{:S(2)}, u32[]{:S(2)}) %collective-permute-start.11) | collective-permute-done | bytes 262176 | tf_op jit(solution)/shard_map/ppermute | solution.py:511
  62.3 4.1 %collective-permute-start.6 = (f32[8,8,256]{2,1,0:T(8,128)}, f32[8,8,256]{2,1,0:T(8,128)S(1)}, u32[]{:S(2)}, u32[]{:S(2)}) collective-permute-start(f32[8,8,256]{2,1,0:T(8,128)} %get-tuple-element.90), channel_id=1, source_target_pairs={{0,1},{1,0},{2,3},{3,2},{4,5},{5,4},{6,7},{7,6},{8,9},{9,8},{10,11... | collective-permute-start | bytes 196616 | tf_op jit(solution)/shard_map/ppermute | solution.py:519
  66.4 3.3 %arrange.1.box_ref = f32[256,1024]{1,0:T(8,128)} custom-call(s32[9]{0:T(128)} %stack.28.ids, f32[16,32,256]{2,1,0:T(8,128)} %constant_dynamic-update-slice_fusion.near_ref, f32[16,32,256]{2,1,0:T(8,128)} %collective-permute-done.12.far_ref), custom_call_target="tpu_custom_call" | custom-call | tf_op jit(solution)/shard_map/arrange/pallas_call | solution.py:664
  70.4 13.6 %second_step.3 = (bf16[4,128,256]{2,1,0:T(8,128)(2,1)}, bf16[4,128,256]{2,1,0:T(8,128)(2,1)}, bf16[4,128,256]{2,1,0:T(8,128)(2,1)}, bf16[4,128,256]{2,1,0:T(8,12...) custom-call(s32[9]{0:T(128)} %stack.28.ids, ...), custom_call_target="tpu_custom_call" | custom-call | tf_op jit(solution)/shard_map/second_step/pallas_call | solution.py:690
  84.0 8.6 %second_step.4 = (bf16[8,128,256]{2,1,0:T(8,128)(2,1)}, bf16[8,128,256]{2,1,0:T(8,128)(2,1)}, bf16[8,128,256]{2,1,0:T(8,128)(2,1)}, bf16[8,128,256]{2,1,0:T(8,128)(2,1)}) custom-call(s32[9]{0:T(128)} %stack.28.ids, f32[4,8,256,256]{3,2,1,0:T(8,128)} %get-tuple-element.80.mu_ref.mu_low.mu_high, f32[4,8,256,256]{3,2,1,0:T(8,128)} %get-tuple-element.80.mu_ref.mu_low.mu_high, ...), custom_call_target="tpu_custom_call" | custom-call | tf_op jit(solution)/shard_map/second_step/pallas_call | solution.py:690
  92.6 8.8 %second_step.5 = (bf16[8,128,256]{2,1,0:T(8,128)(2,1)}, bf16[8,128,256]{2,1,0:T(8,128)(2,1)}, bf16[8,128,256]{2,1,0:T(8,128)(2,1)}, bf16[8,128,256]{2,1,0:T(8,128)(2,1)}) custom-call(s32[9]{0:T(128)} %stack.28.ids, ...), custom_call_target="tpu_custom_call", output_to_operand_aliasing={{0}: (22, {}), {1}: (23, {}), {2}: (24, {}), {3}: (25, {})} | custom-call | tf_op jit(solution)/shard_map/second_step/pallas_call | solution.py:690
  102.9 4.4 %collective-permute-start.13 = (bf16[4,128,256]{2,1,0:T(8,128)(2,1)}, bf16[4,128,256]{2,1,0:T(8,128)(2,1)S(1)}, u32[]{:S(2)}, u32[]{:S(2)}) collective-permute-start(bf16[4,128,256]{2,1,0:T(8,128)(2,1)} %get-tuple-element.96), channel_id=1, source_target_pairs={{0,8},{8,0},{16,24},{24,16},{1,9},{9,1},{17,25},{25,17},{2,10},{10... | collective-permute-start | bytes 786440 | tf_op jit(solution)/shard_map/ppermute | solution.py:511
  111.8 8.6 %collective-permute-start.23 = (bf16[4,128,256]{2,1,0:T(8,128)(2,1)}, bf16[4,128,256]{2,1,0:T(8,128)(2,1)S(1)}, u32[]{:S(2)}, u32[]{:S(2)}) collective-permute-start(bf16[4,128,256]{2,1,0:T(8,128)(2,1)} %get-tuple-element.112), channel_id=1, source_target_pairs={{0,8},{8,0},{16,24},{24,16},{1,9},{9,1},{17,25},{25,17},{2,10},{10... | collective-permute-start | bytes 786440 | tf_op jit(solution)/shard_map/ppermute | solution.py:511
  120.4 3.8 %collective-permute-done.13.refs_1_ = bf16[4,128,256]{2,1,0:T(8,128)(2,1)S(1)} collective-permute-done((bf16[4,128,256]{2,1,0:T(8,128)(2,1)}, bf16[4,128,256]{2,1,0:T(8,128)(2,1)S(1)}, u32[]{:S(2)}, u32[]{:S(2)}) %collective-permute-start.13) | collective-permute-done | bytes 262176 | tf_op jit(solution)/shard_map/ppermute | solution.py:511
  130.3 4.1 %lat_filter.4 = (bf16[4,128,128]{2,1,0:T(8,128)(2,1)}, bf16[4,128,128]{2,1,0:T(8,128)(2,1)}, bf16[4,128,128]{2,1,0:T(8,128)(2,1)}, bf16[4,128,128]{2,1,0:T(8,128...) custom-call(s32[9]{0:T(128)} %stack.28.ids, ...), custom_call_target="tpu_custom_call" | custom-call | tf_op jit(solution)/shard_map/lat_filter/pallas_call | solution.py:748
  135.5 18.2 %collective-permute-done.24.refs_2_ = bf16[4,128,256]{2,1,0:T(8,128)(2,1)} collective-permute-done((bf16[4,128,256]{2,1,0:T(8,128)(2,1)}, bf16[4,128,256]{2,1,0:T(8,128)(2,1)}, u32[]{:S(2)}, u32[]{:S(2)}) %collective-permute-start.24) | collective-permute-done | bytes 262176 | tf_op jit(solution)/shard_map/ppermute | solution.py:511
  153.7 4.1 %lat_filter.5 = (bf16[4,128,128]{2,1,0:T(8,128)(2,1)}, bf16[4,128,128]{2,1,0:T(8,128)(2,1)}, bf16[4,128,128]{2,1,0:T(8,128)(2,1)}, bf16[4,128,128]{2,1,0:T(8,128...) custom-call(s32[9]{0:T(128)} %stack.28.ids, ...), custom_call_target="tpu_custom_call" | custom-call | tf_op jit(solution)/shard_map/lat_filter/pallas_call | solution.py:748
  161.2 5.3 %collective-permute-done.27.refs_10_ = bf16[4,128,128]{2,1,0:T(8,128)(2,1)S(1)} collective-permute-done((bf16[4,128,128]{2,1,0:T(8,128)(2,1)}, bf16[4,128,128]{2,1,0:T(8,128)(2,1)S(1)}, u32[]{:S(2)}, u32[]{:S(2)}) %collective-permute-start.27) | collective-permute-done | bytes 131104 | tf_op jit(solution)/shard_map/ppermute | solution.py:511
  168.0 9.6 %collective-permute-done.29.refs_12_ = bf16[4,128,128]{2,1,0:T(8,128)(2,1)} collective-permute-done((bf16[4,128,128]{2,1,0:T(8,128)(2,1)}, bf16[4,128,128]{2,1,0:T(8,128)(2,1)}, u32[]{:S(2)}, u32[]{:S(2)}) %collective-permute-start.29) | collective-permute-done | bytes 131104 | tf_op jit(solution)/shard_map/ppermute | solution.py:511
  180.2 5.6 %collective-permute-done.31.refs_14_ = bf16[4,128,128]{2,1,0:T(8,128)(2,1)} collective-permute-done((bf16[4,128,128]{2,1,0:T(8,128)(2,1)}, bf16[4,128,128]{2,1,0:T(8,128)(2,1)}, u32[]{:S(2)}, u32[]{:S(2)}) %collective-permute-start.31) | collective-permute-done | bytes 131104 | tf_op jit(solution)/shard_map/ppermute | solution.py:511
  186.7 3.8 %collective-permute-start.17 = (bf16[4,128,128]{2,1,0:T(8,128)(2,1)}, bf16[4,128,128]{2,1,0:T(8,128)(2,1)}, u32[]{:S(2)}, u32[]{:S(2)}) collective-permute-start(bf16[4,128,128]{2,1,0:T(8,128)(2,1)} %get-tuple-element.105), channel_id=1, source_target_pairs={{0,2},{1,3},{2,0},{3,1},{4,6},{5,7},{6,4},{7,5},{8,10},{9,11},{10,... | collective-permute-start | bytes 393224 | tf_op jit(solution)/shard_map/ppermute | solution.py:511
  191.6 4.5 %lat_filter.6 = (bf16[8,64,128]{2,1,0:T(8,128)(2,1)}, bf16[8,64,128]{2,1,0:T(8,128)(2,1)}, bf16[8,64,128]{2,1,0:T(8,128)(2,1)}, bf16[8,64,128]{2,1,0:T(8,128)(2,...) custom-call(s32[9]{0:T(128)} %stack.28.ids, ...), custom_call_target="tpu_custom_call" | custom-call | tf_op jit(solution)/shard_map/lat_filter/pallas_call | solution.py:748
  199.5 4.5 %lat_filter.7 = (bf16[8,64,128]{2,1,0:T(8,128)(2,1)}, bf16[8,64,128]{2,1,0:T(8,128)(2,1)}, bf16[8,64,128]{2,1,0:T(8,128)(2,1)}, bf16[8,64,128]{2,1,0:T(8,128)(2,...) custom-call(s32[9]{0:T(128)} %stack.28.ids, ...), custom_call_target="tpu_custom_call" | custom-call | tf_op jit(solution)/shard_map/lat_filter/pallas_call | solution.py:748
  206.3 5.9 %collective-permute-done.20.refs_5_ = bf16[4,128,128]{2,1,0:T(8,128)(2,1)} collective-permute-done((bf16[4,128,128]{2,1,0:T(8,128)(2,1)}, bf16[4,128,128]{2,1,0:T(8,128)(2,1)}, u32[]{:S(2)}, u32[]{:S(2)}) %collective-permute-start.20) | collective-permute-done | bytes 131104 | tf_op jit(solution)/shard_map/ppermute | solution.py:511
  215.0 4.6 %collective-permute-done.50.refs_2_ = bf16[8,64,128]{2,1,0:T(8,128)(2,1)S(1)} collective-permute-done((bf16[8,64,128]{2,1,0:T(8,128)(2,1)}, bf16[8,64,128]{2,1,0:T(8,128)(2,1)S(1)}, u32[]{:S(2)}, u32[]{:S(2)}) %collective-permute-start.50) | collective-permute-done | bytes 131104 | tf_op jit(solution)/shard_map/ppermute | solution.py:511
  222.8 4.0 %collective-permute-done.51.refs_3_ = bf16[8,64,128]{2,1,0:T(8,128)(2,1)S(1)} collective-permute-done((bf16[8,64,128]{2,1,0:T(8,128)(2,1)}, bf16[8,64,128]{2,1,0:T(8,128)(2,1)S(1)}, u32[]{:S(2)}, u32[]{:S(2)}) %collective-permute-start.51) | collective-permute-done | bytes 131104 | tf_op jit(solution)/shard_map/ppermute | solution.py:511
  227.4 5.1 %collective-permute-done.52.refs_4_ = bf16[8,64,128]{2,1,0:T(8,128)(2,1)S(1)} collective-permute-done((bf16[8,64,128]{2,1,0:T(8,128)(2,1)}, bf16[8,64,128]{2,1,0:T(8,128)(2,1)S(1)}, u32[]{:S(2)}, u32[]{:S(2)}) %collective-permute-start.52) | collective-permute-done | bytes 131104 | tf_op jit(solution)/shard_map/ppermute | solution.py:511
  232.5 3.3 %collective-permute-start.53 = (bf16[8,64,128]{2,1,0:T(8,128)(2,1)}, bf16[8,64,128]{2,1,0:T(8,128)(2,1)S(1)}, u32[]{:S(2)}, u32[]{:S(2)}) collective-permute-start(bf16[8,64,128]{2,1,0:T(8,128)(2,1)} %get-tuple-element.152), channel_id=1, source_target_pairs={{0,4},{1,5},{2,6},{3,7},{4,0},{5,1},{6,2},{7,3},{8,12},{9,13},{10,... | collective-permute-start | bytes 393224 | tf_op jit(solution)/shard_map/ppermute | solution.py:511
  235.8 6.3 %collective-permute-done.53.refs_5_ = bf16[8,64,128]{2,1,0:T(8,128)(2,1)S(1)} collective-permute-done((bf16[8,64,128]{2,1,0:T(8,128)(2,1)}, bf16[8,64,128]{2,1,0:T(8,128)(2,1)S(1)}, u32[]{:S(2)}, u32[]{:S(2)}) %collective-permute-start.53) | collective-permute-done | bytes 131104 | tf_op jit(solution)/shard_map/ppermute | solution.py:511
  242.1 9.4 %collective-permute-done.54.refs_6_ = bf16[8,64,128]{2,1,0:T(8,128)(2,1)S(1)} collective-permute-done((bf16[8,64,128]{2,1,0:T(8,128)(2,1)}, bf16[8,64,128]{2,1,0:T(8,128)(2,1)S(1)}, u32[]{:S(2)}, u32[]{:S(2)}) %collective-permute-start.54) | collective-permute-done | bytes 131104 | tf_op jit(solution)/shard_map/ppermute | solution.py:511
  252.6 6.1 %collective-permute-done.55.refs_7_ = bf16[8,64,128]{2,1,0:T(8,128)(2,1)S(1)} collective-permute-done((bf16[8,64,128]{2,1,0:T(8,128)(2,1)}, bf16[8,64,128]{2,1,0:T(8,128)(2,1)S(1)}, u32[]{:S(2)}, u32[]{:S(2)}) %collective-permute-start.55) | collective-permute-done | bytes 131104 | tf_op jit(solution)/shard_map/ppermute | solution.py:511
  259.0 6.7 %collective-permute-done.56.refs_8_ = bf16[8,64,128]{2,1,0:T(8,128)(2,1)S(1)} collective-permute-done((bf16[8,64,128]{2,1,0:T(8,128)(2,1)}, bf16[8,64,128]{2,1,0:T(8,128)(2,1)S(1)}, u32[]{:S(2)}, u32[]{:S(2)}) %collective-permute-start.56) | collective-permute-done | bytes 131104 | tf_op jit(solution)/shard_map/ppermute | solution.py:511
  273.4 11.0 %lon_first.1 = (f32[4,512,512]{2,1,0:T(8,128)}, f32[4,512,512]{2,1,0:T(8,128)}) custom-call(s32[9]{0:T(128)} %stack.28.ids, bf16[4,128,128]{2,1,0:T(8,128)(2,1)} %get-tuple-element.103.refs_0_, bf16[4,128,128]{2,1,0:T(8,128)(2,1)} %collective-permute-done.16.refs_1_, bf16[4,128,128]{2,1,0:T(8,128)(2,1)} %collective-permute-done.17.refs_2_, ...), custom_call_target="tpu_custom_call" | custom-call | tf_op jit(solution)/shard_map/lon_first/pallas_call | solution.py:814
  284.5 10.6 %lon_filter.2.refs_17_ = f32[1024,2048]{1,0:T(8,128)} custom-call(s32[9]{0:T(128)} %stack.28.ids, f32[4,512,512]{2,1,0:T(8,128)} %get-tuple-element.147.refs_0_, bf16[8,64,128]{2,1,0:T(8,128)(2,1)} %get-tuple-element.148.refs_1_, bf16[8,64,128]{2,1,0:T(8,128)(2,1)} %copy-done.23, bf16[8,64,128]{2,1,0:T(8,128)(2,1)} %copy-done.24, ...), custom_call_target="tpu_custom_call" | custom-call | tf_op jit(solution)/shard_map/lon_filter/pallas_call | solution.py:835
  295.9 10.7 %lon_filter.3 = f32[1024,2048]{1,0:T(8,128)} custom-call(s32[9]{0:T(128)} %stack.28.ids, f32[4,512,512]{2,1,0:T(8,128)} %get-tuple-element.137.refs_0_, bf16[8,64,128]{2,1,0:T(8,128)(2,1)} %get-tuple-element.139.refs_1_, bf16[8,64,128]{2,1,0:T(8,128)(2,1)} %copy-done.20, bf16[8,64,128]{2,1,0:T(8,128)(2,1)} %copy-done.21, ...), custom_call_target="tpu_custom_call", output_to_operand_aliasing={{}: (18, {})} | custom-call | tf_op jit(solution)/shard_map/lon_filter/pallas_call | solution.py:835
  (179 shorter events, 73.6 us)
Async XLA Ops:
  10.0 24.1 %collective-permute-start.9 = (f32[2,32,256]{2,1,0:T(8,128)S(1)}, f32[2,32,256]{2,1,0:T(8,128)S(1)}, u32[]{:S(2)}, u32[]{:S(2)}) collective-permute-start(f32[2,32,256]{2,1,0:T(8,128)S(1)} %pad_maximum_fusion.2), channel_id=1, source_target_pairs={{0,4},{1,5},{2,6},{3,7},{4,0},{5,1},{6,2},{7,3},{8,12},{9,13},{10,... | collective-permute-start | bytes 196616 | tf_op jit(solution)/shard_map/ppermute | solution.py:511
  34.2 10.2 %collective-permute-start.10 = (f32[4,32,256]{2,1,0:T(8,128)S(1)}, f32[4,32,256]{2,1,0:T(8,128)S(1)}, u32[]{:S(2)}, u32[]{:S(2)}) collective-permute-start(f32[4,32,256]{2,1,0:T(8,128)S(1)} %pad_maximum_fusion.1), channel_id=1, source_target_pairs={{0,8},{8,0},{16,24},{24,16},{1,9},{9,1},{17,25},{25,17},{2,10},{10... | collective-permute-start | bytes 393224 | tf_op jit(solution)/shard_map/ppermute | solution.py:511
  45.6 61.8 %collective-permute-start.37 = (bf16[256,2048]{1,0:T(8,128)(2,1)S(1)}, bf16[256,2048]{1,0:T(8,128)(2,1)S(1)}, u32[]{:S(2)}, u32[]{:S(2)}) collective-permute-start(bf16[256,2048]{1,0:T(8,128)(2,1)S(1)} %constant_dynamic-slice_fusion.refs_16_.refs_9_), channel_id=1, source_target_pairs={{0,8},{1,17},{2,10},{3,19},{4,12},{5,21},{6,14},{7,23},{8,0},{9,25... | collective-permute-start | bytes 3145736 | tf_op jit(solution)/shard_map/ppermute | solution.py:569
  58.8 101.2 %collective-permute-start.39 = (bf16[256,2048]{1,0:T(8,128)(2,1)S(1)}, bf16[256,2048]{1,0:T(8,128)(2,1)S(1)}, u32[]{:S(2)}, u32[]{:S(2)}) collective-permute-start(bf16[256,2048]{1,0:T(8,128)(2,1)S(1)} %constant_dynamic-slice_fusion.refs_16_.refs_9_), channel_id=1, source_target_pairs={{0,16},{1,9},{2,18},{3,11},{4,20},{5,13},{6,22},{7,15},{8,24},{9,1... | collective-permute-start | bytes 3145736 | tf_op jit(solution)/shard_map/ppermute | solution.py:569
  101.4 10.4 %collective-permute-start.35 = (bf16[8,128,256]{2,1,0:T(8,128)(2,1)}, bf16[8,128,256]{2,1,0:T(8,128)(2,1)S(1)}, u32[]{:S(2)}, u32[]{:S(2)}) collective-permute-start(bf16[8,128,256]{2,1,0:T(8,128)(2,1)} %get-tuple-element.129), channel_id=1, source_target_pairs={{0,24},{8,16},{16,8},{24,0},{1,25},{9,17},{17,9},{25,1},{2,26},{10... | collective-permute-start | bytes 1572872 | tf_op jit(solution)/shard_map/ppermute | solution.py:511
  102.9 21.3 %collective-permute-start.13 = (bf16[4,128,256]{2,1,0:T(8,128)(2,1)}, bf16[4,128,256]{2,1,0:T(8,128)(2,1)S(1)}, u32[]{:S(2)}, u32[]{:S(2)}) collective-permute-start(bf16[4,128,256]{2,1,0:T(8,128)(2,1)} %get-tuple-element.96), channel_id=1, source_target_pairs={{0,8},{8,0},{16,24},{24,16},{1,9},{9,1},{17,25},{25,17},{2,10},{10... | collective-permute-start | bytes 786440 | tf_op jit(solution)/shard_map/ppermute | solution.py:511
  107.4 18.7 %collective-permute-start.14 = (bf16[4,128,256]{2,1,0:T(8,128)(2,1)}, bf16[4,128,256]{2,1,0:T(8,128)(2,1)}, u32[]{:S(2)}, u32[]{:S(2)}) collective-permute-start(bf16[4,128,256]{2,1,0:T(8,128)(2,1)} %get-tuple-element.97), channel_id=1, source_target_pairs={{0,16},{8,24},{16,0},{24,8},{1,17},{9,25},{17,1},{25,9},{2,18},{10... | collective-permute-start | bytes 786440 | tf_op jit(solution)/shard_map/ppermute | solution.py:511
  107.4 21.7 %collective-permute-start.15 = (bf16[4,128,256]{2,1,0:T(8,128)(2,1)}, bf16[4,128,256]{2,1,0:T(8,128)(2,1)}, u32[]{:S(2)}, u32[]{:S(2)}) collective-permute-start(bf16[4,128,256]{2,1,0:T(8,128)(2,1)} %get-tuple-element.98), channel_id=1, source_target_pairs={{0,24},{8,16},{16,8},{24,0},{1,25},{9,17},{17,9},{25,1},{2,26},{10... | collective-permute-start | bytes 786440 | tf_op jit(solution)/shard_map/ppermute | solution.py:511
  111.8 23.7 %collective-permute-start.23 = (bf16[4,128,256]{2,1,0:T(8,128)(2,1)}, bf16[4,128,256]{2,1,0:T(8,128)(2,1)S(1)}, u32[]{:S(2)}, u32[]{:S(2)}) collective-permute-start(bf16[4,128,256]{2,1,0:T(8,128)(2,1)} %get-tuple-element.112), channel_id=1, source_target_pairs={{0,8},{8,0},{16,24},{24,16},{1,9},{9,1},{17,25},{25,17},{2,10},{10... | collective-permute-start | bytes 786440 | tf_op jit(solution)/shard_map/ppermute | solution.py:511
  124.9 81.4 %collective-permute-start.41 = (bf16[256,2048]{1,0:T(8,128)(2,1)S(1)}, bf16[256,2048]{1,0:T(8,128)(2,1)}, u32[]{:S(2)}, u32[]{:S(2)}) collective-permute-start(bf16[256,2048]{1,0:T(8,128)(2,1)S(1)} %collective-permute-done.37.refs_18_.refs_11_), channel_id=1, source_target_pairs={{0,16},{1,9},{2,18},{3,11},{4,20},{5,13},{6,22},{7,15},{8,24},{9,1... | collective-permute-start | bytes 3145736 | tf_op jit(solution)/shard_map/ppermute | solution.py:569
  126.1 27.7 %collective-permute-start.24 = (bf16[4,128,256]{2,1,0:T(8,128)(2,1)}, bf16[4,128,256]{2,1,0:T(8,128)(2,1)}, u32[]{:S(2)}, u32[]{:S(2)}) collective-permute-start(bf16[4,128,256]{2,1,0:T(8,128)(2,1)} %get-tuple-element.113), channel_id=1, source_target_pairs={{0,16},{8,24},{16,0},{24,8},{1,17},{9,25},{17,1},{25,9},{2,18},{10... | collective-permute-start | bytes 786440 | tf_op jit(solution)/shard_map/ppermute | solution.py:511
  129.0 24.7 %collective-permute-start.25 = (bf16[4,128,256]{2,1,0:T(8,128)(2,1)}, bf16[4,128,256]{2,1,0:T(8,128)(2,1)}, u32[]{:S(2)}, u32[]{:S(2)}) collective-permute-start(bf16[4,128,256]{2,1,0:T(8,128)(2,1)} %get-tuple-element.99), channel_id=1, source_target_pairs={{0,24},{8,16},{16,8},{24,0},{1,25},{9,17},{17,9},{25,1},{2,26},{10... | collective-permute-start | bytes 786440 | tf_op jit(solution)/shard_map/ppermute | solution.py:511
  157.8 32.6 %collective-permute-start.33 = (bf16[8,128,256]{2,1,0:T(8,128)(2,1)}, bf16[8,128,256]{2,1,0:T(8,128)(2,1)}, u32[]{:S(2)}, u32[]{:S(2)}) collective-permute-start(bf16[8,128,256]{2,1,0:T(8,128)(2,1)} %get-tuple-element.127), channel_id=1, source_target_pairs={{0,8},{8,0},{16,24},{24,16},{1,9},{9,1},{17,25},{25,17},{2,10},{10... | collective-permute-start | bytes 1572872 | tf_op jit(solution)/shard_map/ppermute | solution.py:511
  159.6 31.2 %collective-permute-start.34 = (bf16[8,128,256]{2,1,0:T(8,128)(2,1)}, bf16[8,128,256]{2,1,0:T(8,128)(2,1)}, u32[]{:S(2)}, u32[]{:S(2)}) collective-permute-start(bf16[8,128,256]{2,1,0:T(8,128)(2,1)} %get-tuple-element.128), channel_id=1, source_target_pairs={{0,16},{8,24},{16,0},{24,8},{1,17},{9,25},{17,1},{25,9},{2,18},{10... | collective-permute-start | bytes 1572872 | tf_op jit(solution)/shard_map/ppermute | solution.py:511
  166.5 11.1 %collective-permute-start.29 = (bf16[4,128,128]{2,1,0:T(8,128)(2,1)}, bf16[4,128,128]{2,1,0:T(8,128)(2,1)}, u32[]{:S(2)}, u32[]{:S(2)}) collective-permute-start(bf16[4,128,128]{2,1,0:T(8,128)(2,1)} %get-tuple-element.119), channel_id=1, source_target_pairs={{0,4},{1,5},{2,6},{3,7},{4,0},{5,1},{6,2},{7,3},{8,12},{9,13},{10,... | collective-permute-start | bytes 393224 | tf_op jit(solution)/shard_map/ppermute | solution.py:511
  167.2 11.5 %collective-permute-start.30 = (bf16[4,128,128]{2,1,0:T(8,128)(2,1)}, bf16[4,128,128]{2,1,0:T(8,128)(2,1)}, u32[]{:S(2)}, u32[]{:S(2)}) collective-permute-start(bf16[4,128,128]{2,1,0:T(8,128)(2,1)} %get-tuple-element.120), channel_id=1, source_target_pairs={{0,5},{1,4},{2,7},{3,6},{4,1},{5,0},{6,3},{7,2},{8,13},{9,12},{10,... | collective-permute-start | bytes 393224 | tf_op jit(solution)/shard_map/ppermute | solution.py:511
  185.7 10.3 %collective-permute-start.16 = (bf16[4,128,128]{2,1,0:T(8,128)(2,1)}, bf16[4,128,128]{2,1,0:T(8,128)(2,1)}, u32[]{:S(2)}, u32[]{:S(2)}) collective-permute-start(bf16[4,128,128]{2,1,0:T(8,128)(2,1)} %get-tuple-element.104), channel_id=1, source_target_pairs={{0,1},{1,0},{2,3},{3,2},{4,5},{5,4},{6,7},{7,6},{8,9},{9,8},{10,11... | collective-permute-start | bytes 393224 | tf_op jit(solution)/shard_map/ppermute | solution.py:511
  186.7 11.1 %collective-permute-start.17 = (bf16[4,128,128]{2,1,0:T(8,128)(2,1)}, bf16[4,128,128]{2,1,0:T(8,128)(2,1)}, u32[]{:S(2)}, u32[]{:S(2)}) collective-permute-start(bf16[4,128,128]{2,1,0:T(8,128)(2,1)} %get-tuple-element.105), channel_id=1, source_target_pairs={{0,2},{1,3},{2,0},{3,1},{4,6},{5,7},{6,4},{7,5},{8,10},{9,11},{10,... | collective-permute-start | bytes 393224 | tf_op jit(solution)/shard_map/ppermute | solution.py:511
  190.5 13.6 %collective-permute-start.18 = (bf16[4,128,128]{2,1,0:T(8,128)(2,1)}, bf16[4,128,128]{2,1,0:T(8,128)(2,1)}, u32[]{:S(2)}, u32[]{:S(2)}) collective-permute-start(bf16[4,128,128]{2,1,0:T(8,128)(2,1)} %get-tuple-element.106), channel_id=1, source_target_pairs={{0,3},{1,2},{2,1},{3,0},{4,7},{5,6},{6,5},{7,4},{8,11},{9,10},{10,... | collective-permute-start | bytes 393224 | tf_op jit(solution)/shard_map/ppermute | solution.py:511
  190.8 15.3 %collective-permute-start.19 = (bf16[4,128,128]{2,1,0:T(8,128)(2,1)}, bf16[4,128,128]{2,1,0:T(8,128)(2,1)}, u32[]{:S(2)}, u32[]{:S(2)}) collective-permute-start(bf16[4,128,128]{2,1,0:T(8,128)(2,1)} %get-tuple-element.107), channel_id=1, source_target_pairs={{0,4},{1,5},{2,6},{3,7},{4,0},{5,1},{6,2},{7,3},{8,12},{9,13},{10,... | collective-permute-start | bytes 393224 | tf_op jit(solution)/shard_map/ppermute | solution.py:511
  196.0 16.2 %collective-permute-start.20 = (bf16[4,128,128]{2,1,0:T(8,128)(2,1)}, bf16[4,128,128]{2,1,0:T(8,128)(2,1)}, u32[]{:S(2)}, u32[]{:S(2)}) collective-permute-start(bf16[4,128,128]{2,1,0:T(8,128)(2,1)} %get-tuple-element.108), channel_id=1, source_target_pairs={{0,5},{1,4},{2,7},{3,6},{4,1},{5,0},{6,3},{7,2},{8,13},{9,12},{10,... | collective-permute-start | bytes 393224 | tf_op jit(solution)/shard_map/ppermute | solution.py:511
  197.8 14.5 %collective-permute-start.21 = (bf16[4,128,128]{2,1,0:T(8,128)(2,1)}, bf16[4,128,128]{2,1,0:T(8,128)(2,1)}, u32[]{:S(2)}, u32[]{:S(2)}) collective-permute-start(bf16[4,128,128]{2,1,0:T(8,128)(2,1)} %get-tuple-element.109), channel_id=1, source_target_pairs={{0,6},{1,7},{2,4},{3,5},{4,2},{5,3},{6,0},{7,1},{8,14},{9,15},{10,... | collective-permute-start | bytes 393224 | tf_op jit(solution)/shard_map/ppermute | solution.py:511
  212.2 53.9 %collective-permute-start.36 = (bf16[256,2048]{1,0:T(8,128)(2,1)S(1)}, bf16[256,2048]{1,0:T(8,128)(2,1)S(1)}, u32[]{:S(2)}, u32[]{:S(2)}) collective-permute-start(bf16[256,2048]{1,0:T(8,128)(2,1)S(1)} %constant_dynamic-slice_fusion.refs_16_.refs_9_), channel_id=1, source_target_pairs={{0,1},{1,0},{2,3},{3,2},{4,5},{5,4},{6,7},{7,6},{8,9},{9,8},{10,11... | collective-permute-start | bytes 3145736 | tf_op jit(solution)/shard_map/ppermute | solution.py:511
  212.3 54.9 %collective-permute-start.38 = (bf16[256,2048]{1,0:T(8,128)(2,1)S(1)}, bf16[256,2048]{1,0:T(8,128)(2,1)S(1)}, u32[]{:S(2)}, u32[]{:S(2)}) collective-permute-start(bf16[256,2048]{1,0:T(8,128)(2,1)S(1)} %collective-permute-done.37.refs_18_.refs_11_), channel_id=1, source_target_pairs={{0,1},{1,0},{2,3},{3,2},{4,5},{5,4},{6,7},{7,6},{8,9},{9,8},{10,11... | collective-permute-start | bytes 3145736 | tf_op jit(solution)/shard_map/ppermute | solution.py:511
  212.8 55.1 %collective-permute-start.40 = (bf16[256,2048]{1,0:T(8,128)(2,1)S(1)}, bf16[256,2048]{1,0:T(8,128)(2,1)S(1)}, u32[]{:S(2)}, u32[]{:S(2)}) collective-permute-start(bf16[256,2048]{1,0:T(8,128)(2,1)S(1)} %collective-permute-done.39.refs_20_.refs_13_), channel_id=1, source_target_pairs={{0,1},{1,0},{2,3},{3,2},{4,5},{5,4},{6,7},{7,6},{8,9},{9,8},{10,11... | collective-permute-start | bytes 3145736 | tf_op jit(solution)/shard_map/ppermute | solution.py:511
  212.9 58.1 %collective-permute-start.42 = (bf16[256,2048]{1,0:T(8,128)(2,1)}, bf16[256,2048]{1,0:T(8,128)(2,1)S(1)}, u32[]{:S(2)}, u32[]{:S(2)}) collective-permute-start(bf16[256,2048]{1,0:T(8,128)(2,1)} %collective-permute-done.41.refs_22_.refs_15_), channel_id=1, source_target_pairs={{0,1},{1,0},{2,3},{3,2},{4,5},{5,4},{6,7},{7,6},{8,9},{9,8},{10,11... | collective-permute-start | bytes 3145736 | tf_op jit(solution)/shard_map/ppermute | solution.py:511
  232.5 9.6 %collective-permute-start.53 = (bf16[8,64,128]{2,1,0:T(8,128)(2,1)}, bf16[8,64,128]{2,1,0:T(8,128)(2,1)S(1)}, u32[]{:S(2)}, u32[]{:S(2)}) collective-permute-start(bf16[8,64,128]{2,1,0:T(8,128)(2,1)} %get-tuple-element.152), channel_id=1, source_target_pairs={{0,4},{1,5},{2,6},{3,7},{4,0},{5,1},{6,2},{7,3},{8,12},{9,13},{10,... | collective-permute-start | bytes 393224 | tf_op jit(solution)/shard_map/ppermute | solution.py:511
  265.8 29.3 %collective-permute-start.45 = (bf16[8,64,128]{2,1,0:T(8,128)(2,1)}, bf16[8,64,128]{2,1,0:T(8,128)(2,1)}, u32[]{:S(2)}, u32[]{:S(2)}) collective-permute-start(bf16[8,64,128]{2,1,0:T(8,128)(2,1)} %get-tuple-element.142), channel_id=1, source_target_pairs={{0,3},{1,2},{2,1},{3,0},{4,7},{5,6},{6,5},{7,4},{8,11},{9,10},{10,... | collective-permute-start | bytes 393224 | tf_op jit(solution)/shard_map/ppermute | solution.py:511
  266.1 28.9 %collective-permute-start.46 = (bf16[8,64,128]{2,1,0:T(8,128)(2,1)}, bf16[8,64,128]{2,1,0:T(8,128)(2,1)S(1)}, u32[]{:S(2)}, u32[]{:S(2)}) collective-permute-start(bf16[8,64,128]{2,1,0:T(8,128)(2,1)} %get-tuple-element.143), channel_id=1, source_target_pairs={{0,4},{1,5},{2,6},{3,7},{4,0},{5,1},{6,2},{7,3},{8,12},{9,13},{10,... | collective-permute-start | bytes 393224 | tf_op jit(solution)/shard_map/ppermute | solution.py:511
  267.2 27.9 %collective-permute-start.47 = (bf16[8,64,128]{2,1,0:T(8,128)(2,1)}, bf16[8,64,128]{2,1,0:T(8,128)(2,1)S(1)}, u32[]{:S(2)}, u32[]{:S(2)}) collective-permute-start(bf16[8,64,128]{2,1,0:T(8,128)(2,1)} %get-tuple-element.144), channel_id=1, source_target_pairs={{0,5},{1,4},{2,7},{3,6},{4,1},{5,0},{6,3},{7,2},{8,13},{9,12},{10,... | collective-permute-start | bytes 393224 | tf_op jit(solution)/shard_map/ppermute | solution.py:511
  268.1 27.0 %collective-permute-start.48 = (bf16[8,64,128]{2,1,0:T(8,128)(2,1)}, bf16[8,64,128]{2,1,0:T(8,128)(2,1)S(1)}, u32[]{:S(2)}, u32[]{:S(2)}) collective-permute-start(bf16[8,64,128]{2,1,0:T(8,128)(2,1)} %get-tuple-element.145), channel_id=1, source_target_pairs={{0,6},{1,7},{2,4},{3,5},{4,2},{5,3},{6,0},{7,1},{8,14},{9,15},{10,... | collective-permute-start | bytes 393224 | tf_op jit(solution)/shard_map/ppermute | solution.py:511
  272.0 23.2 %collective-permute-start.49 = (bf16[8,64,128]{2,1,0:T(8,128)(2,1)}, bf16[8,64,128]{2,1,0:T(8,128)(2,1)S(1)}, u32[]{:S(2)}, u32[]{:S(2)}) collective-permute-start(bf16[8,64,128]{2,1,0:T(8,128)(2,1)} %get-tuple-element.146), channel_id=1, source_target_pairs={{0,7},{1,6},{2,5},{3,4},{4,3},{5,2},{6,1},{7,0},{8,15},{9,14},{10,... | collective-permute-start | bytes 393224 | tf_op jit(solution)/shard_map/ppermute | solution.py:511
  (63 other events, 1219.2 us)

commit v6 on v4

--- a/solution.py
+++ b/solution.py
@@ -422,7 +422,7 @@
     lasts = refs[n_first : n_first + cols]
     filters = refs[n_first + cols : n_first + cols + 2 * parts]
     rest = refs[n_first + cols + 2 * parts + (1 if aliased else 0) :]
-    out, lines, stage, sem = rest
+    out, lines, stage, sem, held, in_sem = rest
     channels, _, lon = lasts[0].shape
     wide = lines.shape[1] // cols
     rows = channels * height
@@ -437,6 +437,11 @@
         slot = j % 4
         return pltpu.make_async_copy(stage.at[slot, k], out.at[pl.ds(half * rows, rows), at], sem.at[slot, k])
 
+    def fetch(j):
+        return pltpu.make_async_copy(filters[j], held.at[pl.ds(j * block, block)], in_sem.at[j])
+
+    for j in range(2 * parts):
+        fetch(j).start()
     for s in range(cols):
         base = pl.multiple_of((ids[1] ^ s) * wide, LANES)
         for c in range(channels):
@@ -448,7 +453,9 @@
                 lines[put, pl.ds(base + b * lon, lon)] = ref[c % each, half * height : (half + 1) * height]
             lines[put, pl.ds(base + wide - lon, lon)] = lasts[s][c]
     for p in range(parts):
-        right = jnp.concatenate([filters[2 * p][...], filters[2 * p + 1][...]], axis=0)
+        fetch(2 * p).wait()
+        fetch(2 * p + 1).wait()
+        right = held[2 * p * block : (2 * p + 2) * block]
         acc = lax.dot_general(lines[...], right, NT, preferred_element_type=F32)
         for j in (2 * p, 2 * p + 1):
             for k in range(strips):
@@ -762,12 +769,14 @@
         call = pl.pallas_call(
             functools.partial(lon_filter_part, h, half_height, cols_count, rows_count, len(firsts), aliased, owners),
             out_shape=shape_of((2 * rows, n_lon)),
-            in_specs=[SMEM_SPEC] + [VMEM_SPEC] * (len(firsts) + cols_count + 2 * rows_count) + [ANY_SPEC] * aliased,
+            in_specs=[SMEM_SPEC] + [VMEM_SPEC] * (len(firsts) + cols_count) + [ANY_SPEC] * (2 * rows_count + aliased),
             out_specs=ANY_SPEC,
             scratch_shapes=[
                 pltpu.VMEM((rows, n_lon), BF16),
                 pltpu.VMEM((4, height // LANES, rows, LANES), F32),
                 pltpu.SemaphoreType.DMA((4, height // LANES)),
+                pltpu.VMEM((2 * rows_count * height, n_lon), BF16),
+                pltpu.SemaphoreType.DMA((2 * rows_count,)),
             ],
             input_output_aliases={len(operands) - 1: 0} if aliased else {},
             name="lon_filter",

time: 292 us -> 291 us (level)
  transfers between devices with their start and end apart: 57 -> 57, of which waited for: 20 -> 21; matrix products, arithmetic and copies ran while one was open for 0% -> 0% of each run, Pallas kernels for 25% -> 25%
where the time goes in v6:
time: 291 us; the launch traced here: 286 us
  Pallas kernels  98.7 us (34%)
  waiting for transfers between devices  90.7 us (31%)
  starting transfers between devices  89 us (31%)
  local copies, waits for them, and re-layouts  4.3 us (1%)
    ppermute x46, waiting for transfers between devices, swap(): return lax.ppermute(value, axis, [(i, i ^ mask) for i in range(count)])  89.6 us
    ppermute x46, starting transfers between devices, swap(): return lax.ppermute(value, axis, [(i, i ^ mask) for i in range(count)])  70.5 us
    pallas_call x3, Pallas kernels, control(): pl.pallas_call(functools.partial(second_step, band * tall + part * (tall...  30.9 us
    pallas_call x2, Pallas kernels, shards(): out = call(*operands)  21.7 us
    pallas_call x1, Pallas kernels, shards(): mu1, ef, em, ew, xr, xm, xw = call(mu, courant, limiter, directions)  21.1 us
    pallas_call x4, Pallas kernels, smooth(): outs = call(ids, *pieces, filt)  17.2 us
    ppermute x8, starting transfers between devices, neighbours(): return lax.ppermute(value, axis, pairs)  14.1 us
  transfers between devices with their start and end apart: 57, of which 21 were waited for; matrix products, arithmetic and copies ran while one was open for 0% of the time, Pallas kernels for 25%

profile of v6, /device:TPU:0, one launch (start us, length us, event | category | flops | bytes accessed | tf_op | source)
XLA Modules:
  0.0 285.6 jit_solution(3360277878586393768)
XLA Ops:
  4.1 3.1 %collective-permute-start.8 = (f32[1,32,256]{2,1,0:T(8,128)}, f32[1,32,256]{2,1,0:T(8,128)S(1)}, u32[]{:S(2)}, u32[]{:S(2)}) collective-permute-start(f32[1,32,256]{2,1,0:T(8,128)} %bitcast.16), channel_id=1, source_target_pairs={{0,2},{1,3},{2,0},{3,1},{4,6},{5,7},{6,4},{7,5},{8,10},{9,11},{10,... | collective-permute-start | bytes 98312 | tf_op jit(solution)/shard_map/ppermute | solution.py:475
  10.0 3.0 %collective-permute-start.9 = (f32[2,32,256]{2,1,0:T(8,128)S(1)}, f32[2,32,256]{2,1,0:T(8,128)S(1)}, u32[]{:S(2)}, u32[]{:S(2)}) collective-permute-start(f32[2,32,256]{2,1,0:T(8,128)S(1)} %pad_maximum_fusion.2), channel_id=1, source_target_pairs={{0,4},{1,5},{2,6},{3,7},{4,0},{5,1},{6,2},{7,3},{8,12},{9,13},{10,... | collective-permute-start | bytes 196616 | tf_op jit(solution)/shard_map/ppermute | solution.py:475
  13.0 21.1 %first_step.1 = (f32[4,8,256,256]{3,2,1,0:T(8,128)}, f32[128,128]{1,0:T(8,128)}, f32[128,128]{1,0:T(8,128)}, f32[128,128]{1,0:T(8,128)}, f32[9,8,256]{2,1,0:T(8,...) custom-call(f32[4,8,256,256]{3,2,1,0:T(8,128)} %bitcast.14, f32[2,2,8,256,256]{4,3,2,1,0:T(8,128)} %cx_high.5, ...), custom_call_target="tpu_custom_call" | custom-call | tf_op jit(solution)/shard_map/first_step/pallas_call | solution.py:604
  36.4 4.3 %collective-permute-start = (f32[128,128]{1,0:T(8,128)}, f32[128,128]{1,0:T(8,128)S(1)}, u32[]{:S(2)}, u32[]{:S(2)}) collective-permute-start(f32[128,128]{1,0:T(8,128)} %get-tuple-element.78), channel_id=1, source_target_pairs={{0,8},{8,0},{16,24},{24,16},{1,9},{9,1},{17,25},{25,17},{2,10},{10... | collective-permute-start | bytes 196616 | tf_op jit(solution)/shard_map/ppermute | solution.py:483
  41.3 3.0 %collective-permute-start.2 = (f32[9,8,256]{2,1,0:T(8,128)}, f32[9,8,256]{2,1,0:T(8,128)S(1)}, u32[]{:S(2)}, u32[]{:S(2)}) collective-permute-start(f32[9,8,256]{2,1,0:T(8,128)} %get-tuple-element.79), channel_id=1, source_target_pairs={{0,1},{1,0},{2,3},{3,2},{4,5},{5,4},{6,7},{7,6},{8,9},{9,8},{10,11... | collective-permute-start | bytes 221192 | tf_op jit(solution)/shard_map/ppermute | solution.py:483
  45.5 9.0 %collective-permute-done.11 = f32[8,32,256]{2,1,0:T(8,128)S(1)} collective-permute-done((f32[8,32,256]{2,1,0:T(8,128)S(1)}, f32[8,32,256]{2,1,0:T(8,128)S(1)}, u32[]{:S(2)}, u32[]{:S(2)}) %collective-permute-start.11) | collective-permute-done | bytes 262176 | tf_op jit(solution)/shard_map/ppermute | solution.py:475
  63.7 3.4 %arrange.1.box_ref = f32[256,1024]{1,0:T(8,128)} custom-call(s32[9]{0:T(128)} %stack.28.ids, f32[16,32,256]{2,1,0:T(8,128)} %copy-done.9, f32[16,32,256]{2,1,0:T(8,128)} %copy-done.17), custom_call_target="tpu_custom_call" | custom-call | tf_op jit(solution)/shard_map/arrange/pallas_call | solution.py:628
  67.7 13.6 %second_step.3 = (bf16[4,128,256]{2,1,0:T(8,128)(2,1)}, bf16[4,128,256]{2,1,0:T(8,128)(2,1)}, bf16[4,128,256]{2,1,0:T(8,128)(2,1)}, bf16[4,128,256]{2,1,0:T(8,12...) custom-call(s32[9]{0:T(128)} %stack.28.ids, ...), custom_call_target="tpu_custom_call" | custom-call | tf_op jit(solution)/shard_map/second_step/pallas_call | solution.py:654
  87.0 3.7 %collective-permute-done.13.refs_1_ = bf16[4,128,256]{2,1,0:T(8,128)(2,1)S(1)} collective-permute-done((bf16[4,128,256]{2,1,0:T(8,128)(2,1)}, bf16[4,128,256]{2,1,0:T(8,128)(2,1)S(1)}, u32[]{:S(2)}, u32[]{:S(2)}) %collective-permute-start.13) | collective-permute-done | bytes 262176 | tf_op jit(solution)/shard_map/ppermute | solution.py:475
  90.8 4.9 %collective-permute-done.14.refs_2_ = bf16[4,128,256]{2,1,0:T(8,128)(2,1)S(1)} collective-permute-done((bf16[4,128,256]{2,1,0:T(8,128)(2,1)}, bf16[4,128,256]{2,1,0:T(8,128)(2,1)S(1)}, u32[]{:S(2)}, u32[]{:S(2)}) %collective-permute-start.14) | collective-permute-done | bytes 262176 | tf_op jit(solution)/shard_map/ppermute | solution.py:475
  97.2 8.5 %second_step.4 = (bf16[8,128,256]{2,1,0:T(8,128)(2,1)}, bf16[8,128,256]{2,1,0:T(8,128)(2,1)}, bf16[8,128,256]{2,1,0:T(8,128)(2,1)}, bf16[8,128,256]{2,1,0:T(8,128)(2,1)}) custom-call(s32[9]{0:T(128)} %stack.28.ids, f32[4,8,256,256]{3,2,1,0:T(8,128)} %get-tuple-element.77.mu_ref.mu_low.mu_high, f32[4,8,256,256]{3,2,1,0:T(8,128)} %get-tuple-element.77.mu_ref.mu_low.mu_high, ...), custom_call_target="tpu_custom_call" | custom-call | tf_op jit(solution)/shard_map/second_step/pallas_call | solution.py:654
  105.8 8.7 %second_step.5 = (bf16[8,128,256]{2,1,0:T(8,128)(2,1)}, bf16[8,128,256]{2,1,0:T(8,128)(2,1)}, bf16[8,128,256]{2,1,0:T(8,128)(2,1)}, bf16[8,128,256]{2,1,0:T(8,128)(2,1)}) custom-call(s32[9]{0:T(128)} %stack.28.ids, ...), custom_call_target="tpu_custom_call", output_to_operand_aliasing={{0}: (22, {}), {1}: (23, {}), {2}: (24, {}), {3}: (25, {})} | custom-call | tf_op jit(solution)/shard_map/second_step/pallas_call | solution.py:654
  118.5 4.2 %lat_filter.4 = (bf16[4,128,128]{2,1,0:T(8,128)(2,1)}, bf16[4,128,128]{2,1,0:T(8,128)(2,1)}, bf16[4,128,128]{2,1,0:T(8,128)(2,1)}, bf16[4,128,128]{2,1,0:T(8,128...) custom-call(s32[9]{0:T(128)} %stack.28.ids, ...), custom_call_target="tpu_custom_call" | custom-call | tf_op jit(solution)/shard_map/lat_filter/pallas_call | solution.py:712
  122.6 4.1 %lat_filter.5 = (bf16[4,128,128]{2,1,0:T(8,128)(2,1)}, bf16[4,128,128]{2,1,0:T(8,128)(2,1)}, bf16[4,128,128]{2,1,0:T(8,128)(2,1)}, bf16[4,128,128]{2,1,0:T(8,128...) custom-call(s32[9]{0:T(128)} %stack.28.ids, ...), custom_call_target="tpu_custom_call" | custom-call | tf_op jit(solution)/shard_map/lat_filter/pallas_call | solution.py:712
  126.7 3.1 %collective-permute-done.34.refs_2_ = bf16[8,128,256]{2,1,0:T(8,128)(2,1)} collective-permute-done((bf16[8,128,256]{2,1,0:T(8,128)(2,1)}, bf16[8,128,256]{2,1,0:T(8,128)(2,1)}, u32[]{:S(2)}, u32[]{:S(2)}) %collective-permute-start.34) | collective-permute-done | bytes 524320 | tf_op jit(solution)/shard_map/ppermute | solution.py:475
  129.8 4.5 %lat_filter.6 = (bf16[8,64,128]{2,1,0:T(8,128)(2,1)}, bf16[8,64,128]{2,1,0:T(8,128)(2,1)}, bf16[8,64,128]{2,1,0:T(8,128)(2,1)}, bf16[8,64,128]{2,1,0:T(8,128)(2,...) custom-call(s32[9]{0:T(128)} %stack.28.ids, ...), custom_call_target="tpu_custom_call" | custom-call | tf_op jit(solution)/shard_map/lat_filter/pallas_call | solution.py:712
  136.4 17.7 %collective-permute-start.26 = (bf16[4,128,128]{2,1,0:T(8,128)(2,1)}, bf16[4,128,128]{2,1,0:T(8,128)(2,1)S(1)}, u32[]{:S(2)}, u32[]{:S(2)}) collective-permute-start(bf16[4,128,128]{2,1,0:T(8,128)(2,1)} %get-tuple-element.113), channel_id=1, source_target_pairs={{0,1},{1,0},{2,3},{3,2},{4,5},{5,4},{6,7},{7,6},{8,9},{9,8},{10,11... | collective-permute-start | bytes 393224 | tf_op jit(solution)/shard_map/ppermute | solution.py:475
  158.5 5.1 %collective-permute-done.27.refs_10_ = bf16[4,128,128]{2,1,0:T(8,128)(2,1)S(1)} collective-permute-done((bf16[4,128,128]{2,1,0:T(8,128)(2,1)}, bf16[4,128,128]{2,1,0:T(8,128)(2,1)S(1)}, u32[]{:S(2)}, u32[]{:S(2)}) %collective-permute-start.27) | collective-permute-done | bytes 131104 | tf_op jit(solution)/shard_map/ppermute | solution.py:475
  163.5 3.1 %collective-permute-start.31 = (bf16[4,128,128]{2,1,0:T(8,128)(2,1)}, bf16[4,128,128]{2,1,0:T(8,128)(2,1)}, u32[]{:S(2)}, u32[]{:S(2)}) collective-permute-start(bf16[4,128,128]{2,1,0:T(8,128)(2,1)} %get-tuple-element.118), channel_id=1, source_target_pairs={{0,6},{1,7},{2,4},{3,5},{4,2},{5,3},{6,0},{7,1},{8,14},{9,15},{10,... | collective-permute-start | bytes 393224 | tf_op jit(solution)/shard_map/ppermute | solution.py:475
  168.6 6.2 %collective-permute-done.29.refs_12_ = bf16[4,128,128]{2,1,0:T(8,128)(2,1)} collective-permute-done((bf16[4,128,128]{2,1,0:T(8,128)(2,1)}, bf16[4,128,128]{2,1,0:T(8,128)(2,1)}, u32[]{:S(2)}, u32[]{:S(2)}) %collective-permute-start.29) | collective-permute-done | bytes 131104 | tf_op jit(solution)/shard_map/ppermute | solution.py:475
  179.3 4.3 %collective-permute-start.19 = (bf16[4,128,128]{2,1,0:T(8,128)(2,1)}, bf16[4,128,128]{2,1,0:T(8,128)(2,1)}, u32[]{:S(2)}, u32[]{:S(2)}) collective-permute-start(bf16[4,128,128]{2,1,0:T(8,128)(2,1)} %get-tuple-element.104), channel_id=1, source_target_pairs={{0,4},{1,5},{2,6},{3,7},{4,0},{5,1},{6,2},{7,3},{8,12},{9,13},{10,... | collective-permute-start | bytes 393224 | tf_op jit(solution)/shard_map/ppermute | solution.py:475
  183.6 4.4 %lat_filter.7 = (bf16[8,64,128]{2,1,0:T(8,128)(2,1)}, bf16[8,64,128]{2,1,0:T(8,128)(2,1)}, bf16[8,64,128]{2,1,0:T(8,128)(2,1)}, bf16[8,64,128]{2,1,0:T(8,128)(2,...) custom-call(s32[9]{0:T(128)} %stack.28.ids, ...), custom_call_target="tpu_custom_call" | custom-call | tf_op jit(solution)/shard_map/lat_filter/pallas_call | solution.py:712
  191.4 8.2 %collective-permute-done.19.refs_4_ = bf16[4,128,128]{2,1,0:T(8,128)(2,1)} collective-permute-done((bf16[4,128,128]{2,1,0:T(8,128)(2,1)}, bf16[4,128,128]{2,1,0:T(8,128)(2,1)}, u32[]{:S(2)}, u32[]{:S(2)}) %collective-permute-start.19) | collective-permute-done | bytes 131104 | tf_op jit(solution)/shard_map/ppermute | solution.py:475
  205.7 3.5 %collective-permute-done.50.refs_17_ = bf16[8,64,128]{2,1,0:T(8,128)(2,1)S(1)} collective-permute-done((bf16[8,64,128]{2,1,0:T(8,128)(2,1)}, bf16[8,64,128]{2,1,0:T(8,128)(2,1)S(1)}, u32[]{:S(2)}, u32[]{:S(2)}) %collective-permute-start.50) | collective-permute-done | bytes 131104 | tf_op jit(solution)/shard_map/ppermute | solution.py:475
  211.8 4.2 %collective-permute-done.51.refs_18_ = bf16[8,64,128]{2,1,0:T(8,128)(2,1)S(1)} collective-permute-done((bf16[8,64,128]{2,1,0:T(8,128)(2,1)}, bf16[8,64,128]{2,1,0:T(8,128)(2,1)S(1)}, u32[]{:S(2)}, u32[]{:S(2)}) %collective-permute-start.51) | collective-permute-done | bytes 131104 | tf_op jit(solution)/shard_map/ppermute | solution.py:475
  216.9 4.8 %collective-permute-done.52.refs_19_ = bf16[8,64,128]{2,1,0:T(8,128)(2,1)S(1)} collective-permute-done((bf16[8,64,128]{2,1,0:T(8,128)(2,1)}, bf16[8,64,128]{2,1,0:T(8,128)(2,1)S(1)}, u32[]{:S(2)}, u32[]{:S(2)}) %collective-permute-start.52) | collective-permute-done | bytes 131104 | tf_op jit(solution)/shard_map/ppermute | solution.py:475
  223.5 7.6 %collective-permute-done.53.refs_20_ = bf16[8,64,128]{2,1,0:T(8,128)(2,1)S(1)} collective-permute-done((bf16[8,64,128]{2,1,0:T(8,128)(2,1)}, bf16[8,64,128]{2,1,0:T(8,128)(2,1)S(1)}, u32[]{:S(2)}, u32[]{:S(2)}) %collective-permute-start.53) | collective-permute-done | bytes 131104 | tf_op jit(solution)/shard_map/ppermute | solution.py:475
  231.2 8.2 %collective-permute-done.54.refs_21_ = bf16[8,64,128]{2,1,0:T(8,128)(2,1)S(1)} collective-permute-done((bf16[8,64,128]{2,1,0:T(8,128)(2,1)}, bf16[8,64,128]{2,1,0:T(8,128)(2,1)S(1)}, u32[]{:S(2)}, u32[]{:S(2)}) %collective-permute-start.54) | collective-permute-done | bytes 131104 | tf_op jit(solution)/shard_map/ppermute | solution.py:475
  241.4 5.4 %collective-permute-done.55.refs_22_ = bf16[8,64,128]{2,1,0:T(8,128)(2,1)S(1)} collective-permute-done((bf16[8,64,128]{2,1,0:T(8,128)(2,1)}, bf16[8,64,128]{2,1,0:T(8,128)(2,1)S(1)}, u32[]{:S(2)}, u32[]{:S(2)}) %collective-permute-start.55) | collective-permute-done | bytes 131104 | tf_op jit(solution)/shard_map/ppermute | solution.py:475
  247.8 6.2 %collective-permute-done.56.refs_23_ = bf16[8,64,128]{2,1,0:T(8,128)(2,1)S(1)} collective-permute-done((bf16[8,64,128]{2,1,0:T(8,128)(2,1)}, bf16[8,64,128]{2,1,0:T(8,128)(2,1)S(1)}, u32[]{:S(2)}, u32[]{:S(2)}) %collective-permute-start.56) | collective-permute-done | bytes 131104 | tf_op jit(solution)/shard_map/ppermute | solution.py:475
  261.8 11.0 %lon_filter.2.refs_32_ = f32[1024,2048]{1,0:T(8,128)} custom-call(s32[9]{0:T(128)} %stack.28.ids, bf16[4,128,128]{2,1,0:T(8,128)(2,1)} %get-tuple-element.100.refs_0_, bf16[4,128,128]{2,1,0:T(8,128)(2,1)} %collective-permute-done.16.refs_1_, bf16[4,128,128]{2,1,0:T(8,128)(2,1)} %collective-permute-done.17.refs_2_, ...), custom_call_target="tpu_custom_call" | custom-call | tf_op jit(solution)/shard_map/lon_filter/pallas_call | solution.py:784
  274.7 10.7 %lon_filter.3 = f32[1024,2048]{1,0:T(8,128)} custom-call(s32[9]{0:T(128)} %stack.28.ids, bf16[4,128,128]{2,1,0:T(8,128)(2,1)} %get-tuple-element.100.refs_0_, bf16[4,128,128]{2,1,0:T(8,128)(2,1)} %collective-permute-done.16.refs_1_, bf16[4,128,128]{2,1,0:T(8,128)(2,1)} %collective-permute-done.17.refs_2_, ...), custom_call_target="tpu_custom_call", output_to_operand_aliasing={{}: (33, {})} | custom-call | tf_op jit(solution)/shard_map/lon_filter/pallas_call | solution.py:784
  (182 shorter events, 70.6 us)
Async XLA Ops:
  10.0 24.1 %collective-permute-start.9 = (f32[2,32,256]{2,1,0:T(8,128)S(1)}, f32[2,32,256]{2,1,0:T(8,128)S(1)}, u32[]{:S(2)}, u32[]{:S(2)}) collective-permute-start(f32[2,32,256]{2,1,0:T(8,128)S(1)} %pad_maximum_fusion.2), channel_id=1, source_target_pairs={{0,4},{1,5},{2,6},{3,7},{4,0},{5,1},{6,2},{7,3},{8,12},{9,13},{10,... | collective-permute-start | bytes 196616 | tf_op jit(solution)/shard_map/ppermute | solution.py:475
  81.5 52.8 %collective-permute-start.44 = (bf16[256,2048]{1,0:T(8,128)(2,1)S(1)}, bf16[256,2048]{1,0:T(8,128)(2,1)S(1)}, u32[]{:S(2)}, u32[]{:S(2)}) collective-permute-start(bf16[256,2048]{1,0:T(8,128)(2,1)S(1)} %constant_dynamic-slice_fusion.refs_24_), channel_id=1, source_target_pairs={{0,8},{1,17},{2,10},{3,19},{4,12},{5,21},{6,14},{7,23},{8,0},{9,25... | collective-permute-start | bytes 3145736 | tf_op jit(solution)/shard_map/ppermute | solution.py:533
  83.6 12.2 %collective-permute-start.14 = (bf16[4,128,256]{2,1,0:T(8,128)(2,1)}, bf16[4,128,256]{2,1,0:T(8,128)(2,1)S(1)}, u32[]{:S(2)}, u32[]{:S(2)}) collective-permute-start(bf16[4,128,256]{2,1,0:T(8,128)(2,1)} %get-tuple-element.94), channel_id=1, source_target_pairs={{0,16},{8,24},{16,0},{24,8},{1,17},{9,25},{17,1},{25,9},{2,18},{10... | collective-permute-start | bytes 786440 | tf_op jit(solution)/shard_map/ppermute | solution.py:475
  83.7 30.9 %collective-permute-start.15 = (bf16[4,128,256]{2,1,0:T(8,128)(2,1)}, bf16[4,128,256]{2,1,0:T(8,128)(2,1)S(1)}, u32[]{:S(2)}, u32[]{:S(2)}) collective-permute-start(bf16[4,128,256]{2,1,0:T(8,128)(2,1)} %get-tuple-element.95), channel_id=1, source_target_pairs={{0,24},{8,16},{16,8},{24,0},{1,25},{9,17},{17,9},{25,1},{2,26},{10... | collective-permute-start | bytes 786440 | tf_op jit(solution)/shard_map/ppermute | solution.py:475
  85.1 29.5 %collective-permute-start.23 = (bf16[4,128,256]{2,1,0:T(8,128)(2,1)}, bf16[4,128,256]{2,1,0:T(8,128)(2,1)S(1)}, u32[]{:S(2)}, u32[]{:S(2)}) collective-permute-start(bf16[4,128,256]{2,1,0:T(8,128)(2,1)} %get-tuple-element.109), channel_id=1, source_target_pairs={{0,8},{8,0},{16,24},{24,16},{1,9},{9,1},{17,25},{25,17},{2,10},{10... | collective-permute-start | bytes 786440 | tf_op jit(solution)/shard_map/ppermute | solution.py:475
  90.8 25.9 %collective-permute-start.24 = (bf16[4,128,256]{2,1,0:T(8,128)(2,1)}, bf16[4,128,256]{2,1,0:T(8,128)(2,1)S(1)}, u32[]{:S(2)}, u32[]{:S(2)}) collective-permute-start(bf16[4,128,256]{2,1,0:T(8,128)(2,1)} %get-tuple-element.110), channel_id=1, source_target_pairs={{0,16},{8,24},{16,0},{24,8},{1,17},{9,25},{17,1},{25,9},{2,18},{10... | collective-permute-start | bytes 786440 | tf_op jit(solution)/shard_map/ppermute | solution.py:475
  95.8 22.4 %collective-permute-start.25 = (bf16[4,128,256]{2,1,0:T(8,128)(2,1)}, bf16[4,128,256]{2,1,0:T(8,128)(2,1)}, u32[]{:S(2)}, u32[]{:S(2)}) collective-permute-start(bf16[4,128,256]{2,1,0:T(8,128)(2,1)} %get-tuple-element.96), channel_id=1, source_target_pairs={{0,24},{8,16},{16,8},{24,0},{1,25},{9,17},{17,9},{25,1},{2,26},{10... | collective-permute-start | bytes 786440 | tf_op jit(solution)/shard_map/ppermute | solution.py:475
  114.6 12.2 %collective-permute-start.33 = (bf16[8,128,256]{2,1,0:T(8,128)(2,1)}, bf16[8,128,256]{2,1,0:T(8,128)(2,1)}, u32[]{:S(2)}, u32[]{:S(2)}) collective-permute-start(bf16[8,128,256]{2,1,0:T(8,128)(2,1)} %get-tuple-element.124), channel_id=1, source_target_pairs={{0,8},{8,0},{16,24},{24,16},{1,9},{9,1},{17,25},{25,17},{2,10},{10... | collective-permute-start | bytes 1572872 | tf_op jit(solution)/shard_map/ppermute | solution.py:475
  114.7 15.2 %collective-permute-start.34 = (bf16[8,128,256]{2,1,0:T(8,128)(2,1)}, bf16[8,128,256]{2,1,0:T(8,128)(2,1)}, u32[]{:S(2)}, u32[]{:S(2)}) collective-permute-start(bf16[8,128,256]{2,1,0:T(8,128)(2,1)} %get-tuple-element.125), channel_id=1, source_target_pairs={{0,16},{8,24},{16,0},{24,8},{1,17},{9,25},{17,1},{25,9},{2,18},{10... | collective-permute-start | bytes 1572872 | tf_op jit(solution)/shard_map/ppermute | solution.py:475
  116.6 13.2 %collective-permute-start.35 = (bf16[8,128,256]{2,1,0:T(8,128)(2,1)}, bf16[8,128,256]{2,1,0:T(8,128)(2,1)}, u32[]{:S(2)}, u32[]{:S(2)}) collective-permute-start(bf16[8,128,256]{2,1,0:T(8,128)(2,1)} %get-tuple-element.126), channel_id=1, source_target_pairs={{0,24},{8,16},{16,8},{24,0},{1,25},{9,17},{17,9},{25,1},{2,26},{10... | collective-permute-start | bytes 1572872 | tf_op jit(solution)/shard_map/ppermute | solution.py:475
  118.1 37.7 %collective-permute-start.46 = (bf16[256,2048]{1,0:T(8,128)(2,1)S(1)}, bf16[256,2048]{1,0:T(8,128)(2,1)S(1)}, u32[]{:S(2)}, u32[]{:S(2)}) collective-permute-start(bf16[256,2048]{1,0:T(8,128)(2,1)S(1)} %constant_dynamic-slice_fusion.refs_24_), channel_id=1, source_target_pairs={{0,16},{1,9},{2,18},{3,11},{4,20},{5,13},{6,22},{7,15},{8,24},{9,1... | collective-permute-start | bytes 3145736 | tf_op jit(solution)/shard_map/ppermute | solution.py:533
  134.4 65.2 %collective-permute-start.48 = (bf16[256,2048]{1,0:T(8,128)(2,1)S(1)}, bf16[256,2048]{1,0:T(8,128)(2,1)}, u32[]{:S(2)}, u32[]{:S(2)}) collective-permute-start(bf16[256,2048]{1,0:T(8,128)(2,1)S(1)} %collective-permute-done.44.refs_26_), channel_id=1, source_target_pairs={{0,16},{1,9},{2,18},{3,11},{4,20},{5,13},{6,22},{7,15},{8,24},{9,1... | collective-permute-start | bytes 3145736 | tf_op jit(solution)/shard_map/ppermute | solution.py:533
  136.4 20.5 %collective-permute-start.26 = (bf16[4,128,128]{2,1,0:T(8,128)(2,1)}, bf16[4,128,128]{2,1,0:T(8,128)(2,1)S(1)}, u32[]{:S(2)}, u32[]{:S(2)}) collective-permute-start(bf16[4,128,128]{2,1,0:T(8,128)(2,1)} %get-tuple-element.113), channel_id=1, source_target_pairs={{0,1},{1,0},{2,3},{3,2},{4,5},{5,4},{6,7},{7,6},{8,9},{9,8},{10,11... | collective-permute-start | bytes 393224 | tf_op jit(solution)/shard_map/ppermute | solution.py:475
  155.9 18.9 %collective-permute-start.29 = (bf16[4,128,128]{2,1,0:T(8,128)(2,1)}, bf16[4,128,128]{2,1,0:T(8,128)(2,1)}, u32[]{:S(2)}, u32[]{:S(2)}) collective-permute-start(bf16[4,128,128]{2,1,0:T(8,128)(2,1)} %get-tuple-element.116), channel_id=1, source_target_pairs={{0,4},{1,5},{2,6},{3,7},{4,0},{5,1},{6,2},{7,3},{8,12},{9,13},{10,... | collective-permute-start | bytes 393224 | tf_op jit(solution)/shard_map/ppermute | solution.py:475
  156.9 19.4 %collective-permute-start.30 = (bf16[4,128,128]{2,1,0:T(8,128)(2,1)}, bf16[4,128,128]{2,1,0:T(8,128)(2,1)}, u32[]{:S(2)}, u32[]{:S(2)}) collective-permute-start(bf16[4,128,128]{2,1,0:T(8,128)(2,1)} %get-tuple-element.117), channel_id=1, source_target_pairs={{0,5},{1,4},{2,7},{3,6},{4,1},{5,0},{6,3},{7,2},{8,13},{9,12},{10,... | collective-permute-start | bytes 393224 | tf_op jit(solution)/shard_map/ppermute | solution.py:475
  163.5 12.9 %collective-permute-start.31 = (bf16[4,128,128]{2,1,0:T(8,128)(2,1)}, bf16[4,128,128]{2,1,0:T(8,128)(2,1)}, u32[]{:S(2)}, u32[]{:S(2)}) collective-permute-start(bf16[4,128,128]{2,1,0:T(8,128)(2,1)} %get-tuple-element.118), channel_id=1, source_target_pairs={{0,6},{1,7},{2,4},{3,5},{4,2},{5,3},{6,0},{7,1},{8,14},{9,15},{10,... | collective-permute-start | bytes 393224 | tf_op jit(solution)/shard_map/ppermute | solution.py:475
  166.6 12.7 %collective-permute-start.32 = (bf16[4,128,128]{2,1,0:T(8,128)(2,1)}, bf16[4,128,128]{2,1,0:T(8,128)(2,1)}, u32[]{:S(2)}, u32[]{:S(2)}) collective-permute-start(bf16[4,128,128]{2,1,0:T(8,128)(2,1)} %get-tuple-element.119), channel_id=1, source_target_pairs={{0,7},{1,6},{2,5},{3,4},{4,3},{5,2},{6,1},{7,0},{8,15},{9,14},{10,... | collective-permute-start | bytes 393224 | tf_op jit(solution)/shard_map/ppermute | solution.py:475
  176.2 11.8 %collective-permute-start.17 = (bf16[4,128,128]{2,1,0:T(8,128)(2,1)}, bf16[4,128,128]{2,1,0:T(8,128)(2,1)}, u32[]{:S(2)}, u32[]{:S(2)}) collective-permute-start(bf16[4,128,128]{2,1,0:T(8,128)(2,1)} %get-tuple-element.102), channel_id=1, source_target_pairs={{0,2},{1,3},{2,0},{3,1},{4,6},{5,7},{6,4},{7,5},{8,10},{9,11},{10,... | collective-permute-start | bytes 393224 | tf_op jit(solution)/shard_map/ppermute | solution.py:475
  176.4 13.1 %collective-permute-start.18 = (bf16[4,128,128]{2,1,0:T(8,128)(2,1)}, bf16[4,128,128]{2,1,0:T(8,128)(2,1)}, u32[]{:S(2)}, u32[]{:S(2)}) collective-permute-start(bf16[4,128,128]{2,1,0:T(8,128)(2,1)} %get-tuple-element.103), channel_id=1, source_target_pairs={{0,3},{1,2},{2,1},{3,0},{4,7},{5,6},{6,5},{7,4},{8,11},{9,10},{10,... | collective-permute-start | bytes 393224 | tf_op jit(solution)/shard_map/ppermute | solution.py:475
  179.3 20.2 %collective-permute-start.19 = (bf16[4,128,128]{2,1,0:T(8,128)(2,1)}, bf16[4,128,128]{2,1,0:T(8,128)(2,1)}, u32[]{:S(2)}, u32[]{:S(2)}) collective-permute-start(bf16[4,128,128]{2,1,0:T(8,128)(2,1)} %get-tuple-element.104), channel_id=1, source_target_pairs={{0,4},{1,5},{2,6},{3,7},{4,0},{5,1},{6,2},{7,3},{8,12},{9,13},{10,... | collective-permute-start | bytes 393224 | tf_op jit(solution)/shard_map/ppermute | solution.py:475
  183.6 17.6 %collective-permute-start.20 = (bf16[4,128,128]{2,1,0:T(8,128)(2,1)}, bf16[4,128,128]{2,1,0:T(8,128)(2,1)}, u32[]{:S(2)}, u32[]{:S(2)}) collective-permute-start(bf16[4,128,128]{2,1,0:T(8,128)(2,1)} %get-tuple-element.105), channel_id=1, source_target_pairs={{0,5},{1,4},{2,7},{3,6},{4,1},{5,0},{6,3},{7,2},{8,13},{9,12},{10,... | collective-permute-start | bytes 393224 | tf_op jit(solution)/shard_map/ppermute | solution.py:475
  188.1 14.1 %collective-permute-start.21 = (bf16[4,128,128]{2,1,0:T(8,128)(2,1)}, bf16[4,128,128]{2,1,0:T(8,128)(2,1)}, u32[]{:S(2)}, u32[]{:S(2)}) collective-permute-start(bf16[4,128,128]{2,1,0:T(8,128)(2,1)} %get-tuple-element.106), channel_id=1, source_target_pairs={{0,6},{1,7},{2,4},{3,5},{4,2},{5,3},{6,0},{7,1},{8,14},{9,15},{10,... | collective-permute-start | bytes 393224 | tf_op jit(solution)/shard_map/ppermute | solution.py:475
  189.5 12.8 %collective-permute-start.22 = (bf16[4,128,128]{2,1,0:T(8,128)(2,1)}, bf16[4,128,128]{2,1,0:T(8,128)(2,1)}, u32[]{:S(2)}, u32[]{:S(2)}) collective-permute-start(bf16[4,128,128]{2,1,0:T(8,128)(2,1)} %get-tuple-element.107), channel_id=1, source_target_pairs={{0,7},{1,6},{2,5},{3,4},{4,3},{5,2},{6,1},{7,0},{8,15},{9,14},{10,... | collective-permute-start | bytes 393224 | tf_op jit(solution)/shard_map/ppermute | solution.py:475
  201.2 52.8 %collective-permute-start.43 = (bf16[256,2048]{1,0:T(8,128)(2,1)S(1)}, bf16[256,2048]{1,0:T(8,128)(2,1)S(1)}, u32[]{:S(2)}, u32[]{:S(2)}) collective-permute-start(bf16[256,2048]{1,0:T(8,128)(2,1)S(1)} %constant_dynamic-slice_fusion.refs_24_), channel_id=1, source_target_pairs={{0,1},{1,0},{2,3},{3,2},{4,5},{5,4},{6,7},{7,6},{8,9},{9,8},{10,11... | collective-permute-start | bytes 3145736 | tf_op jit(solution)/shard_map/ppermute | solution.py:475
  202.2 53.7 %collective-permute-start.45 = (bf16[256,2048]{1,0:T(8,128)(2,1)S(1)}, bf16[256,2048]{1,0:T(8,128)(2,1)S(1)}, u32[]{:S(2)}, u32[]{:S(2)}) collective-permute-start(bf16[256,2048]{1,0:T(8,128)(2,1)S(1)} %collective-permute-done.44.refs_26_), channel_id=1, source_target_pairs={{0,1},{1,0},{2,3},{3,2},{4,5},{5,4},{6,7},{7,6},{8,9},{9,8},{10,11... | collective-permute-start | bytes 3145736 | tf_op jit(solution)/shard_map/ppermute | solution.py:475
  202.3 54.3 %collective-permute-start.47 = (bf16[256,2048]{1,0:T(8,128)(2,1)S(1)}, bf16[256,2048]{1,0:T(8,128)(2,1)S(1)}, u32[]{:S(2)}, u32[]{:S(2)}) collective-permute-start(bf16[256,2048]{1,0:T(8,128)(2,1)S(1)} %collective-permute-done.46.refs_28_), channel_id=1, source_target_pairs={{0,1},{1,0},{2,3},{3,2},{4,5},{5,4},{6,7},{7,6},{8,9},{9,8},{10,11... | collective-permute-start | bytes 3145736 | tf_op jit(solution)/shard_map/ppermute | solution.py:475
  202.7 55.8 %collective-permute-start.49 = (bf16[256,2048]{1,0:T(8,128)(2,1)}, bf16[256,2048]{1,0:T(8,128)(2,1)S(1)}, u32[]{:S(2)}, u32[]{:S(2)}) collective-permute-start(bf16[256,2048]{1,0:T(8,128)(2,1)} %collective-permute-done.48.refs_30_), channel_id=1, source_target_pairs={{0,1},{1,0},{2,3},{3,2},{4,5},{5,4},{6,7},{7,6},{8,9},{9,8},{10,11... | collective-permute-start | bytes 3145736 | tf_op jit(solution)/shard_map/ppermute | solution.py:475
  254.1 18.7 %collective-permute-start.38 = (bf16[8,64,128]{2,1,0:T(8,128)(2,1)}, bf16[8,64,128]{2,1,0:T(8,128)(2,1)}, u32[]{:S(2)}, u32[]{:S(2)}) collective-permute-start(bf16[8,64,128]{2,1,0:T(8,128)(2,1)} %get-tuple-element.133), channel_id=1, source_target_pairs={{0,3},{1,2},{2,1},{3,0},{4,7},{5,6},{6,5},{7,4},{8,11},{9,10},{10,... | collective-permute-start | bytes 393224 | tf_op jit(solution)/shard_map/ppermute | solution.py:475
  254.1 18.8 %collective-permute-start.39 = (bf16[8,64,128]{2,1,0:T(8,128)(2,1)}, bf16[8,64,128]{2,1,0:T(8,128)(2,1)S(1)}, u32[]{:S(2)}, u32[]{:S(2)}) collective-permute-start(bf16[8,64,128]{2,1,0:T(8,128)(2,1)} %get-tuple-element.134), channel_id=1, source_target_pairs={{0,4},{1,5},{2,6},{3,7},{4,0},{5,1},{6,2},{7,3},{8,12},{9,13},{10,... | collective-permute-start | bytes 393224 | tf_op jit(solution)/shard_map/ppermute | solution.py:475
  255.9 18.1 %collective-permute-start.40 = (bf16[8,64,128]{2,1,0:T(8,128)(2,1)}, bf16[8,64,128]{2,1,0:T(8,128)(2,1)S(1)}, u32[]{:S(2)}, u32[]{:S(2)}) collective-permute-start(bf16[8,64,128]{2,1,0:T(8,128)(2,1)} %get-tuple-element.135), channel_id=1, source_target_pairs={{0,5},{1,4},{2,7},{3,6},{4,1},{5,0},{6,3},{7,2},{8,13},{9,12},{10,... | collective-permute-start | bytes 393224 | tf_op jit(solution)/shard_map/ppermute | solution.py:475
  256.8 17.1 %collective-permute-start.41 = (bf16[8,64,128]{2,1,0:T(8,128)(2,1)}, bf16[8,64,128]{2,1,0:T(8,128)(2,1)S(1)}, u32[]{:S(2)}, u32[]{:S(2)}) collective-permute-start(bf16[8,64,128]{2,1,0:T(8,128)(2,1)} %get-tuple-element.136), channel_id=1, source_target_pairs={{0,6},{1,7},{2,4},{3,5},{4,2},{5,3},{6,0},{7,1},{8,14},{9,15},{10,... | collective-permute-start | bytes 393224 | tf_op jit(solution)/shard_map/ppermute | solution.py:475
  259.5 14.5 %collective-permute-start.42 = (bf16[8,64,128]{2,1,0:T(8,128)(2,1)}, bf16[8,64,128]{2,1,0:T(8,128)(2,1)S(1)}, u32[]{:S(2)}, u32[]{:S(2)}) collective-permute-start(bf16[8,64,128]{2,1,0:T(8,128)(2,1)} %get-tuple-element.137), channel_id=1, source_target_pairs={{0,7},{1,6},{2,5},{3,4},{4,3},{5,2},{6,1},{7,0},{8,15},{9,14},{10,... | collective-permute-start | bytes 393224 | tf_op jit(solution)/shard_map/ppermute | solution.py:475
  (65 other events, 1314.7 us)

commit v7 on v6

--- a/solution.py
+++ b/solution.py
@@ -440,8 +440,8 @@
     def fetch(j):
         return pltpu.make_async_copy(filters[j], held.at[pl.ds(j * block, block)], in_sem.at[j])
 
-    for j in range(2 * parts):
-        fetch(j).start()
+    fetch(0).start()
+    fetch(1).start()
     for s in range(cols):
         base = pl.multiple_of((ids[1] ^ s) * wide, LANES)
         for c in range(channels):
@@ -455,6 +455,9 @@
     for p in range(parts):
         fetch(2 * p).wait()
         fetch(2 * p + 1).wait()
+        if p + 1 < parts:
+            fetch(2 * p + 2).start()
+            fetch(2 * p + 3).start()
         right = held[2 * p * block : (2 * p + 2) * block]
         acc = lax.dot_general(lines[...], right, NT, preferred_element_type=F32)
         for j in (2 * p, 2 * p + 1):

time: 291 us -> 292 us (level)
  transfers between devices with their start and end apart: 57 -> 57, of which waited for: 21 -> 20; matrix products, arithmetic and copies ran while one was open for 0% -> 0% of each run, Pallas kernels for 25% -> 25%
where the time goes in v7:
time: 292 us; the launch traced here: 286 us
  Pallas kernels  99.4 us (34%)
  waiting for transfers between devices  90.3 us (31%)
  starting transfers between devices  89 us (30%)
  local copies, waits for them, and re-layouts  4.3 us (1%)
    ppermute x46, waiting for transfers between devices, swap(): return lax.ppermute(value, axis, [(i, i ^ mask) for i in range(count)])  89.2 us
    ppermute x46, starting transfers between devices, swap(): return lax.ppermute(value, axis, [(i, i ^ mask) for i in range(count)])  70.5 us
    pallas_call x3, Pallas kernels, control(): pl.pallas_call(functools.partial(second_step, band * tall + part * (tall...  30.9 us
    pallas_call x2, Pallas kernels, shards(): out = call(*operands)  22.4 us
    pallas_call x1, Pallas kernels, shards(): mu1, ef, em, ew, xr, xm, xw = call(mu, courant, limiter, directions)  21.1 us
    pallas_call x4, Pallas kernels, smooth(): outs = call(ids, *pieces, filt)  17.2 us
    ppermute x8, starting transfers between devices, neighbours(): return lax.ppermute(value, axis, pairs)  14.1 us
  transfers between devices with their start and end apart: 57, of which 20 were waited for; matrix products, arithmetic and copies ran while one was open for 0% of the time, Pallas kernels for 25%

profile of v7, /device:TPU:0, one launch (start us, length us, event | category | flops | bytes accessed | tf_op | source)
XLA Modules:
  0.0 286.0 jit_solution(18187482750045903567)
XLA Ops:
  4.1 3.1 %collective-permute-start.8 = (f32[1,32,256]{2,1,0:T(8,128)}, f32[1,32,256]{2,1,0:T(8,128)S(1)}, u32[]{:S(2)}, u32[]{:S(2)}) collective-permute-start(f32[1,32,256]{2,1,0:T(8,128)} %bitcast.16), channel_id=1, source_target_pairs={{0,2},{1,3},{2,0},{3,1},{4,6},{5,7},{6,4},{7,5},{8,10},{9,11},{10,... | collective-permute-start | bytes 98312 | tf_op jit(solution)/shard_map/ppermute | solution.py:478
  10.0 3.0 %collective-permute-start.9 = (f32[2,32,256]{2,1,0:T(8,128)S(1)}, f32[2,32,256]{2,1,0:T(8,128)S(1)}, u32[]{:S(2)}, u32[]{:S(2)}) collective-permute-start(f32[2,32,256]{2,1,0:T(8,128)S(1)} %pad_maximum_fusion.2), channel_id=1, source_target_pairs={{0,4},{1,5},{2,6},{3,7},{4,0},{5,1},{6,2},{7,3},{8,12},{9,13},{10,... | collective-permute-start | bytes 196616 | tf_op jit(solution)/shard_map/ppermute | solution.py:478
  13.0 21.1 %first_step.1 = (f32[4,8,256,256]{3,2,1,0:T(8,128)}, f32[128,128]{1,0:T(8,128)}, f32[128,128]{1,0:T(8,128)}, f32[128,128]{1,0:T(8,128)}, f32[9,8,256]{2,1,0:T(8,...) custom-call(f32[4,8,256,256]{3,2,1,0:T(8,128)} %bitcast.14, f32[2,2,8,256,256]{4,3,2,1,0:T(8,128)} %cx_high.5, ...), custom_call_target="tpu_custom_call" | custom-call | tf_op jit(solution)/shard_map/first_step/pallas_call | solution.py:607
  36.4 4.3 %collective-permute-start = (f32[128,128]{1,0:T(8,128)}, f32[128,128]{1,0:T(8,128)S(1)}, u32[]{:S(2)}, u32[]{:S(2)}) collective-permute-start(f32[128,128]{1,0:T(8,128)} %get-tuple-element.78), channel_id=1, source_target_pairs={{0,8},{8,0},{16,24},{24,16},{1,9},{9,1},{17,25},{25,17},{2,10},{10... | collective-permute-start | bytes 196616 | tf_op jit(solution)/shard_map/ppermute | solution.py:486
  41.3 3.0 %collective-permute-start.2 = (f32[9,8,256]{2,1,0:T(8,128)}, f32[9,8,256]{2,1,0:T(8,128)S(1)}, u32[]{:S(2)}, u32[]{:S(2)}) collective-permute-start(f32[9,8,256]{2,1,0:T(8,128)} %get-tuple-element.79), channel_id=1, source_target_pairs={{0,1},{1,0},{2,3},{3,2},{4,5},{5,4},{6,7},{7,6},{8,9},{9,8},{10,11... | collective-permute-start | bytes 221192 | tf_op jit(solution)/shard_map/ppermute | solution.py:486
  45.5 9.0 %collective-permute-done.11 = f32[8,32,256]{2,1,0:T(8,128)S(1)} collective-permute-done((f32[8,32,256]{2,1,0:T(8,128)S(1)}, f32[8,32,256]{2,1,0:T(8,128)S(1)}, u32[]{:S(2)}, u32[]{:S(2)}) %collective-permute-start.11) | collective-permute-done | bytes 262176 | tf_op jit(solution)/shard_map/ppermute | solution.py:478
  63.7 3.4 %arrange.1.box_ref = f32[256,1024]{1,0:T(8,128)} custom-call(s32[9]{0:T(128)} %stack.28.ids, f32[16,32,256]{2,1,0:T(8,128)} %copy-done.9, f32[16,32,256]{2,1,0:T(8,128)} %copy-done.17), custom_call_target="tpu_custom_call" | custom-call | tf_op jit(solution)/shard_map/arrange/pallas_call | solution.py:631
  67.7 13.6 %second_step.3 = (bf16[4,128,256]{2,1,0:T(8,128)(2,1)}, bf16[4,128,256]{2,1,0:T(8,128)(2,1)}, bf16[4,128,256]{2,1,0:T(8,128)(2,1)}, bf16[4,128,256]{2,1,0:T(8,12...) custom-call(s32[9]{0:T(128)} %stack.28.ids, ...), custom_call_target="tpu_custom_call" | custom-call | tf_op jit(solution)/shard_map/second_step/pallas_call | solution.py:657
  87.0 3.7 %collective-permute-done.13.refs_1_ = bf16[4,128,256]{2,1,0:T(8,128)(2,1)S(1)} collective-permute-done((bf16[4,128,256]{2,1,0:T(8,128)(2,1)}, bf16[4,128,256]{2,1,0:T(8,128)(2,1)S(1)}, u32[]{:S(2)}, u32[]{:S(2)}) %collective-permute-start.13) | collective-permute-done | bytes 262176 | tf_op jit(solution)/shard_map/ppermute | solution.py:478
  90.8 4.9 %collective-permute-done.14.refs_2_ = bf16[4,128,256]{2,1,0:T(8,128)(2,1)S(1)} collective-permute-done((bf16[4,128,256]{2,1,0:T(8,128)(2,1)}, bf16[4,128,256]{2,1,0:T(8,128)(2,1)S(1)}, u32[]{:S(2)}, u32[]{:S(2)}) %collective-permute-start.14) | collective-permute-done | bytes 262176 | tf_op jit(solution)/shard_map/ppermute | solution.py:478
  97.2 8.5 %second_step.4 = (bf16[8,128,256]{2,1,0:T(8,128)(2,1)}, bf16[8,128,256]{2,1,0:T(8,128)(2,1)}, bf16[8,128,256]{2,1,0:T(8,128)(2,1)}, bf16[8,128,256]{2,1,0:T(8,128)(2,1)}) custom-call(s32[9]{0:T(128)} %stack.28.ids, f32[4,8,256,256]{3,2,1,0:T(8,128)} %get-tuple-element.77.mu_ref.mu_low.mu_high, f32[4,8,256,256]{3,2,1,0:T(8,128)} %get-tuple-element.77.mu_ref.mu_low.mu_high, ...), custom_call_target="tpu_custom_call" | custom-call | tf_op jit(solution)/shard_map/second_step/pallas_call | solution.py:657
  105.8 8.7 %second_step.5 = (bf16[8,128,256]{2,1,0:T(8,128)(2,1)}, bf16[8,128,256]{2,1,0:T(8,128)(2,1)}, bf16[8,128,256]{2,1,0:T(8,128)(2,1)}, bf16[8,128,256]{2,1,0:T(8,128)(2,1)}) custom-call(s32[9]{0:T(128)} %stack.28.ids, ...), custom_call_target="tpu_custom_call", output_to_operand_aliasing={{0}: (22, {}), {1}: (23, {}), {2}: (24, {}), {3}: (25, {})} | custom-call | tf_op jit(solution)/shard_map/second_step/pallas_call | solution.py:657
  118.5 4.2 %lat_filter.4 = (bf16[4,128,128]{2,1,0:T(8,128)(2,1)}, bf16[4,128,128]{2,1,0:T(8,128)(2,1)}, bf16[4,128,128]{2,1,0:T(8,128)(2,1)}, bf16[4,128,128]{2,1,0:T(8,128...) custom-call(s32[9]{0:T(128)} %stack.28.ids, ...), custom_call_target="tpu_custom_call" | custom-call | tf_op jit(solution)/shard_map/lat_filter/pallas_call | solution.py:715
  122.6 4.1 %lat_filter.5 = (bf16[4,128,128]{2,1,0:T(8,128)(2,1)}, bf16[4,128,128]{2,1,0:T(8,128)(2,1)}, bf16[4,128,128]{2,1,0:T(8,128)(2,1)}, bf16[4,128,128]{2,1,0:T(8,128...) custom-call(s32[9]{0:T(128)} %stack.28.ids, ...), custom_call_target="tpu_custom_call" | custom-call | tf_op jit(solution)/shard_map/lat_filter/pallas_call | solution.py:715
  126.7 3.1 %collective-permute-done.34.refs_2_ = bf16[8,128,256]{2,1,0:T(8,128)(2,1)} collective-permute-done((bf16[8,128,256]{2,1,0:T(8,128)(2,1)}, bf16[8,128,256]{2,1,0:T(8,128)(2,1)}, u32[]{:S(2)}, u32[]{:S(2)}) %collective-permute-start.34) | collective-permute-done | bytes 524320 | tf_op jit(solution)/shard_map/ppermute | solution.py:478
  129.8 4.5 %lat_filter.6 = (bf16[8,64,128]{2,1,0:T(8,128)(2,1)}, bf16[8,64,128]{2,1,0:T(8,128)(2,1)}, bf16[8,64,128]{2,1,0:T(8,128)(2,1)}, bf16[8,64,128]{2,1,0:T(8,128)(2,...) custom-call(s32[9]{0:T(128)} %stack.28.ids, ...), custom_call_target="tpu_custom_call" | custom-call | tf_op jit(solution)/shard_map/lat_filter/pallas_call | solution.py:715
  136.4 17.7 %collective-permute-start.26 = (bf16[4,128,128]{2,1,0:T(8,128)(2,1)}, bf16[4,128,128]{2,1,0:T(8,128)(2,1)S(1)}, u32[]{:S(2)}, u32[]{:S(2)}) collective-permute-start(bf16[4,128,128]{2,1,0:T(8,128)(2,1)} %get-tuple-element.113), channel_id=1, source_target_pairs={{0,1},{1,0},{2,3},{3,2},{4,5},{5,4},{6,7},{7,6},{8,9},{9,8},{10,11... | collective-permute-start | bytes 393224 | tf_op jit(solution)/shard_map/ppermute | solution.py:478
  158.5 5.1 %collective-permute-done.27.refs_10_ = bf16[4,128,128]{2,1,0:T(8,128)(2,1)S(1)} collective-permute-done((bf16[4,128,128]{2,1,0:T(8,128)(2,1)}, bf16[4,128,128]{2,1,0:T(8,128)(2,1)S(1)}, u32[]{:S(2)}, u32[]{:S(2)}) %collective-permute-start.27) | collective-permute-done | bytes 131104 | tf_op jit(solution)/shard_map/ppermute | solution.py:478
  163.5 3.1 %collective-permute-start.31 = (bf16[4,128,128]{2,1,0:T(8,128)(2,1)}, bf16[4,128,128]{2,1,0:T(8,128)(2,1)}, u32[]{:S(2)}, u32[]{:S(2)}) collective-permute-start(bf16[4,128,128]{2,1,0:T(8,128)(2,1)} %get-tuple-element.118), channel_id=1, source_target_pairs={{0,6},{1,7},{2,4},{3,5},{4,2},{5,3},{6,0},{7,1},{8,14},{9,15},{10,... | collective-permute-start | bytes 393224 | tf_op jit(solution)/shard_map/ppermute | solution.py:478
  168.6 6.2 %collective-permute-done.29.refs_12_ = bf16[4,128,128]{2,1,0:T(8,128)(2,1)} collective-permute-done((bf16[4,128,128]{2,1,0:T(8,128)(2,1)}, bf16[4,128,128]{2,1,0:T(8,128)(2,1)}, u32[]{:S(2)}, u32[]{:S(2)}) %collective-permute-start.29) | collective-permute-done | bytes 131104 | tf_op jit(solution)/shard_map/ppermute | solution.py:478
  179.3 4.3 %collective-permute-start.19 = (bf16[4,128,128]{2,1,0:T(8,128)(2,1)}, bf16[4,128,128]{2,1,0:T(8,128)(2,1)}, u32[]{:S(2)}, u32[]{:S(2)}) collective-permute-start(bf16[4,128,128]{2,1,0:T(8,128)(2,1)} %get-tuple-element.104), channel_id=1, source_target_pairs={{0,4},{1,5},{2,6},{3,7},{4,0},{5,1},{6,2},{7,3},{8,12},{9,13},{10,... | collective-permute-start | bytes 393224 | tf_op jit(solution)/shard_map/ppermute | solution.py:478
  183.6 4.4 %lat_filter.7 = (bf16[8,64,128]{2,1,0:T(8,128)(2,1)}, bf16[8,64,128]{2,1,0:T(8,128)(2,1)}, bf16[8,64,128]{2,1,0:T(8,128)(2,1)}, bf16[8,64,128]{2,1,0:T(8,128)(2,...) custom-call(s32[9]{0:T(128)} %stack.28.ids, ...), custom_call_target="tpu_custom_call" | custom-call | tf_op jit(solution)/shard_map/lat_filter/pallas_call | solution.py:715
  191.4 8.2 %collective-permute-done.19.refs_4_ = bf16[4,128,128]{2,1,0:T(8,128)(2,1)} collective-permute-done((bf16[4,128,128]{2,1,0:T(8,128)(2,1)}, bf16[4,128,128]{2,1,0:T(8,128)(2,1)}, u32[]{:S(2)}, u32[]{:S(2)}) %collective-permute-start.19) | collective-permute-done | bytes 131104 | tf_op jit(solution)/shard_map/ppermute | solution.py:478
  205.7 3.5 %collective-permute-done.50.refs_17_ = bf16[8,64,128]{2,1,0:T(8,128)(2,1)S(1)} collective-permute-done((bf16[8,64,128]{2,1,0:T(8,128)(2,1)}, bf16[8,64,128]{2,1,0:T(8,128)(2,1)S(1)}, u32[]{:S(2)}, u32[]{:S(2)}) %collective-permute-start.50) | collective-permute-done | bytes 131104 | tf_op jit(solution)/shard_map/ppermute | solution.py:478
  211.8 4.2 %collective-permute-done.51.refs_18_ = bf16[8,64,128]{2,1,0:T(8,128)(2,1)S(1)} collective-permute-done((bf16[8,64,128]{2,1,0:T(8,128)(2,1)}, bf16[8,64,128]{2,1,0:T(8,128)(2,1)S(1)}, u32[]{:S(2)}, u32[]{:S(2)}) %collective-permute-start.51) | collective-permute-done | bytes 131104 | tf_op jit(solution)/shard_map/ppermute | solution.py:478
  216.9 4.8 %collective-permute-done.52.refs_19_ = bf16[8,64,128]{2,1,0:T(8,128)(2,1)S(1)} collective-permute-done((bf16[8,64,128]{2,1,0:T(8,128)(2,1)}, bf16[8,64,128]{2,1,0:T(8,128)(2,1)S(1)}, u32[]{:S(2)}, u32[]{:S(2)}) %collective-permute-start.52) | collective-permute-done | bytes 131104 | tf_op jit(solution)/shard_map/ppermute | solution.py:478
  223.5 7.6 %collective-permute-done.53.refs_20_ = bf16[8,64,128]{2,1,0:T(8,128)(2,1)S(1)} collective-permute-done((bf16[8,64,128]{2,1,0:T(8,128)(2,1)}, bf16[8,64,128]{2,1,0:T(8,128)(2,1)S(1)}, u32[]{:S(2)}, u32[]{:S(2)}) %collective-permute-start.53) | collective-permute-done | bytes 131104 | tf_op jit(solution)/shard_map/ppermute | solution.py:478
  231.2 8.2 %collective-permute-done.54.refs_21_ = bf16[8,64,128]{2,1,0:T(8,128)(2,1)S(1)} collective-permute-done((bf16[8,64,128]{2,1,0:T(8,128)(2,1)}, bf16[8,64,128]{2,1,0:T(8,128)(2,1)S(1)}, u32[]{:S(2)}, u32[]{:S(2)}) %collective-permute-start.54) | collective-permute-done | bytes 131104 | tf_op jit(solution)/shard_map/ppermute | solution.py:478
  241.4 5.4 %collective-permute-done.55.refs_22_ = bf16[8,64,128]{2,1,0:T(8,128)(2,1)S(1)} collective-permute-done((bf16[8,64,128]{2,1,0:T(8,128)(2,1)}, bf16[8,64,128]{2,1,0:T(8,128)(2,1)S(1)}, u32[]{:S(2)}, u32[]{:S(2)}) %collective-permute-start.55) | collective-permute-done | bytes 131104 | tf_op jit(solution)/shard_map/ppermute | solution.py:478
  247.8 6.2 %collective-permute-done.56.refs_23_ = bf16[8,64,128]{2,1,0:T(8,128)(2,1)S(1)} collective-permute-done((bf16[8,64,128]{2,1,0:T(8,128)(2,1)}, bf16[8,64,128]{2,1,0:T(8,128)(2,1)S(1)}, u32[]{:S(2)}, u32[]{:S(2)}) %collective-permute-start.56) | collective-permute-done | bytes 131104 | tf_op jit(solution)/shard_map/ppermute | solution.py:478
  261.8 11.3 %lon_filter.2.refs_32_ = f32[1024,2048]{1,0:T(8,128)} custom-call(s32[9]{0:T(128)} %stack.28.ids, bf16[4,128,128]{2,1,0:T(8,128)(2,1)} %get-tuple-element.100.refs_0_, bf16[4,128,128]{2,1,0:T(8,128)(2,1)} %collective-permute-done.16.refs_1_, bf16[4,128,128]{2,1,0:T(8,128)(2,1)} %collective-permute-done.17.refs_2_, ...), custom_call_target="tpu_custom_call" | custom-call | tf_op jit(solution)/shard_map/lon_filter/pallas_call | solution.py:787
  274.7 11.1 %lon_filter.3 = f32[1024,2048]{1,0:T(8,128)} custom-call(s32[9]{0:T(128)} %stack.28.ids, bf16[4,128,128]{2,1,0:T(8,128)(2,1)} %get-tuple-element.100.refs_0_, bf16[4,128,128]{2,1,0:T(8,128)(2,1)} %collective-permute-done.16.refs_1_, bf16[4,128,128]{2,1,0:T(8,128)(2,1)} %collective-permute-done.17.refs_2_, ...), custom_call_target="tpu_custom_call", output_to_operand_aliasing={{}: (33, {})} | custom-call | tf_op jit(solution)/shard_map/lon_filter/pallas_call | solution.py:787
  (182 shorter events, 70.2 us)
Async XLA Ops:
  10.0 24.1 %collective-permute-start.9 = (f32[2,32,256]{2,1,0:T(8,128)S(1)}, f32[2,32,256]{2,1,0:T(8,128)S(1)}, u32[]{:S(2)}, u32[]{:S(2)}) collective-permute-start(f32[2,32,256]{2,1,0:T(8,128)S(1)} %pad_maximum_fusion.2), channel_id=1, source_target_pairs={{0,4},{1,5},{2,6},{3,7},{4,0},{5,1},{6,2},{7,3},{8,12},{9,13},{10,... | collective-permute-start | bytes 196616 | tf_op jit(solution)/shard_map/ppermute | solution.py:478
  81.5 52.8 %collective-permute-start.44 = (bf16[256,2048]{1,0:T(8,128)(2,1)S(1)}, bf16[256,2048]{1,0:T(8,128)(2,1)S(1)}, u32[]{:S(2)}, u32[]{:S(2)}) collective-permute-start(bf16[256,2048]{1,0:T(8,128)(2,1)S(1)} %constant_dynamic-slice_fusion.refs_24_), channel_id=1, source_target_pairs={{0,8},{1,17},{2,10},{3,19},{4,12},{5,21},{6,14},{7,23},{8,0},{9,25... | collective-permute-start | bytes 3145736 | tf_op jit(solution)/shard_map/ppermute | solution.py:536
  83.6 12.2 %collective-permute-start.14 = (bf16[4,128,256]{2,1,0:T(8,128)(2,1)}, bf16[4,128,256]{2,1,0:T(8,128)(2,1)S(1)}, u32[]{:S(2)}, u32[]{:S(2)}) collective-permute-start(bf16[4,128,256]{2,1,0:T(8,128)(2,1)} %get-tuple-element.94), channel_id=1, source_target_pairs={{0,16},{8,24},{16,0},{24,8},{1,17},{9,25},{17,1},{25,9},{2,18},{10... | collective-permute-start | bytes 786440 | tf_op jit(solution)/shard_map/ppermute | solution.py:478
  83.7 30.9 %collective-permute-start.15 = (bf16[4,128,256]{2,1,0:T(8,128)(2,1)}, bf16[4,128,256]{2,1,0:T(8,128)(2,1)S(1)}, u32[]{:S(2)}, u32[]{:S(2)}) collective-permute-start(bf16[4,128,256]{2,1,0:T(8,128)(2,1)} %get-tuple-element.95), channel_id=1, source_target_pairs={{0,24},{8,16},{16,8},{24,0},{1,25},{9,17},{17,9},{25,1},{2,26},{10... | collective-permute-start | bytes 786440 | tf_op jit(solution)/shard_map/ppermute | solution.py:478
  85.1 29.5 %collective-permute-start.23 = (bf16[4,128,256]{2,1,0:T(8,128)(2,1)}, bf16[4,128,256]{2,1,0:T(8,128)(2,1)S(1)}, u32[]{:S(2)}, u32[]{:S(2)}) collective-permute-start(bf16[4,128,256]{2,1,0:T(8,128)(2,1)} %get-tuple-element.109), channel_id=1, source_target_pairs={{0,8},{8,0},{16,24},{24,16},{1,9},{9,1},{17,25},{25,17},{2,10},{10... | collective-permute-start | bytes 786440 | tf_op jit(solution)/shard_map/ppermute | solution.py:478
  90.8 25.9 %collective-permute-start.24 = (bf16[4,128,256]{2,1,0:T(8,128)(2,1)}, bf16[4,128,256]{2,1,0:T(8,128)(2,1)S(1)}, u32[]{:S(2)}, u32[]{:S(2)}) collective-permute-start(bf16[4,128,256]{2,1,0:T(8,128)(2,1)} %get-tuple-element.110), channel_id=1, source_target_pairs={{0,16},{8,24},{16,0},{24,8},{1,17},{9,25},{17,1},{25,9},{2,18},{10... | collective-permute-start | bytes 786440 | tf_op jit(solution)/shard_map/ppermute | solution.py:478
  95.8 22.4 %collective-permute-start.25 = (bf16[4,128,256]{2,1,0:T(8,128)(2,1)}, bf16[4,128,256]{2,1,0:T(8,128)(2,1)}, u32[]{:S(2)}, u32[]{:S(2)}) collective-permute-start(bf16[4,128,256]{2,1,0:T(8,128)(2,1)} %get-tuple-element.96), channel_id=1, source_target_pairs={{0,24},{8,16},{16,8},{24,0},{1,25},{9,17},{17,9},{25,1},{2,26},{10... | collective-permute-start | bytes 786440 | tf_op jit(solution)/shard_map/ppermute | solution.py:478
  114.6 12.2 %collective-permute-start.33 = (bf16[8,128,256]{2,1,0:T(8,128)(2,1)}, bf16[8,128,256]{2,1,0:T(8,128)(2,1)}, u32[]{:S(2)}, u32[]{:S(2)}) collective-permute-start(bf16[8,128,256]{2,1,0:T(8,128)(2,1)} %get-tuple-element.124), channel_id=1, source_target_pairs={{0,8},{8,0},{16,24},{24,16},{1,9},{9,1},{17,25},{25,17},{2,10},{10... | collective-permute-start | bytes 1572872 | tf_op jit(solution)/shard_map/ppermute | solution.py:478
  114.7 15.2 %collective-permute-start.34 = (bf16[8,128,256]{2,1,0:T(8,128)(2,1)}, bf16[8,128,256]{2,1,0:T(8,128)(2,1)}, u32[]{:S(2)}, u32[]{:S(2)}) collective-permute-start(bf16[8,128,256]{2,1,0:T(8,128)(2,1)} %get-tuple-element.125), channel_id=1, source_target_pairs={{0,16},{8,24},{16,0},{24,8},{1,17},{9,25},{17,1},{25,9},{2,18},{10... | collective-permute-start | bytes 1572872 | tf_op jit(solution)/shard_map/ppermute | solution.py:478
  116.6 13.2 %collective-permute-start.35 = (bf16[8,128,256]{2,1,0:T(8,128)(2,1)}, bf16[8,128,256]{2,1,0:T(8,128)(2,1)}, u32[]{:S(2)}, u32[]{:S(2)}) collective-permute-start(bf16[8,128,256]{2,1,0:T(8,128)(2,1)} %get-tuple-element.126), channel_id=1, source_target_pairs={{0,24},{8,16},{16,8},{24,0},{1,25},{9,17},{17,9},{25,1},{2,26},{10... | collective-permute-start | bytes 1572872 | tf_op jit(solution)/shard_map/ppermute | solution.py:478
  118.1 37.7 %collective-permute-start.46 = (bf16[256,2048]{1,0:T(8,128)(2,1)S(1)}, bf16[256,2048]{1,0:T(8,128)(2,1)S(1)}, u32[]{:S(2)}, u32[]{:S(2)}) collective-permute-start(bf16[256,2048]{1,0:T(8,128)(2,1)S(1)} %constant_dynamic-slice_fusion.refs_24_), channel_id=1, source_target_pairs={{0,16},{1,9},{2,18},{3,11},{4,20},{5,13},{6,22},{7,15},{8,24},{9,1... | collective-permute-start | bytes 3145736 | tf_op jit(solution)/shard_map/ppermute | solution.py:536
  134.4 65.2 %collective-permute-start.48 = (bf16[256,2048]{1,0:T(8,128)(2,1)S(1)}, bf16[256,2048]{1,0:T(8,128)(2,1)}, u32[]{:S(2)}, u32[]{:S(2)}) collective-permute-start(bf16[256,2048]{1,0:T(8,128)(2,1)S(1)} %collective-permute-done.44.refs_26_), channel_id=1, source_target_pairs={{0,16},{1,9},{2,18},{3,11},{4,20},{5,13},{6,22},{7,15},{8,24},{9,1... | collective-permute-start | bytes 3145736 | tf_op jit(solution)/shard_map/ppermute | solution.py:536
  136.4 20.5 %collective-permute-start.26 = (bf16[4,128,128]{2,1,0:T(8,128)(2,1)}, bf16[4,128,128]{2,1,0:T(8,128)(2,1)S(1)}, u32[]{:S(2)}, u32[]{:S(2)}) collective-permute-start(bf16[4,128,128]{2,1,0:T(8,128)(2,1)} %get-tuple-element.113), channel_id=1, source_target_pairs={{0,1},{1,0},{2,3},{3,2},{4,5},{5,4},{6,7},{7,6},{8,9},{9,8},{10,11... | collective-permute-start | bytes 393224 | tf_op jit(solution)/shard_map/ppermute | solution.py:478
  155.9 18.9 %collective-permute-start.29 = (bf16[4,128,128]{2,1,0:T(8,128)(2,1)}, bf16[4,128,128]{2,1,0:T(8,128)(2,1)}, u32[]{:S(2)}, u32[]{:S(2)}) collective-permute-start(bf16[4,128,128]{2,1,0:T(8,128)(2,1)} %get-tuple-element.116), channel_id=1, source_target_pairs={{0,4},{1,5},{2,6},{3,7},{4,0},{5,1},{6,2},{7,3},{8,12},{9,13},{10,... | collective-permute-start | bytes 393224 | tf_op jit(solution)/shard_map/ppermute | solution.py:478
  156.9 19.4 %collective-permute-start.30 = (bf16[4,128,128]{2,1,0:T(8,128)(2,1)}, bf16[4,128,128]{2,1,0:T(8,128)(2,1)}, u32[]{:S(2)}, u32[]{:S(2)}) collective-permute-start(bf16[4,128,128]{2,1,0:T(8,128)(2,1)} %get-tuple-element.117), channel_id=1, source_target_pairs={{0,5},{1,4},{2,7},{3,6},{4,1},{5,0},{6,3},{7,2},{8,13},{9,12},{10,... | collective-permute-start | bytes 393224 | tf_op jit(solution)/shard_map/ppermute | solution.py:478
  163.5 12.9 %collective-permute-start.31 = (bf16[4,128,128]{2,1,0:T(8,128)(2,1)}, bf16[4,128,128]{2,1,0:T(8,128)(2,1)}, u32[]{:S(2)}, u32[]{:S(2)}) collective-permute-start(bf16[4,128,128]{2,1,0:T(8,128)(2,1)} %get-tuple-element.118), channel_id=1, source_target_pairs={{0,6},{1,7},{2,4},{3,5},{4,2},{5,3},{6,0},{7,1},{8,14},{9,15},{10,... | collective-permute-start | bytes 393224 | tf_op jit(solution)/shard_map/ppermute | solution.py:478
  166.6 12.7 %collective-permute-start.32 = (bf16[4,128,128]{2,1,0:T(8,128)(2,1)}, bf16[4,128,128]{2,1,0:T(8,128)(2,1)}, u32[]{:S(2)}, u32[]{:S(2)}) collective-permute-start(bf16[4,128,128]{2,1,0:T(8,128)(2,1)} %get-tuple-element.119), channel_id=1, source_target_pairs={{0,7},{1,6},{2,5},{3,4},{4,3},{5,2},{6,1},{7,0},{8,15},{9,14},{10,... | collective-permute-start | bytes 393224 | tf_op jit(solution)/shard_map/ppermute | solution.py:478
  176.2 11.8 %collective-permute-start.17 = (bf16[4,128,128]{2,1,0:T(8,128)(2,1)}, bf16[4,128,128]{2,1,0:T(8,128)(2,1)}, u32[]{:S(2)}, u32[]{:S(2)}) collective-permute-start(bf16[4,128,128]{2,1,0:T(8,128)(2,1)} %get-tuple-element.102), channel_id=1, source_target_pairs={{0,2},{1,3},{2,0},{3,1},{4,6},{5,7},{6,4},{7,5},{8,10},{9,11},{10,... | collective-permute-start | bytes 393224 | tf_op jit(solution)/shard_map/ppermute | solution.py:478
  176.4 13.1 %collective-permute-start.18 = (bf16[4,128,128]{2,1,0:T(8,128)(2,1)}, bf16[4,128,128]{2,1,0:T(8,128)(2,1)}, u32[]{:S(2)}, u32[]{:S(2)}) collective-permute-start(bf16[4,128,128]{2,1,0:T(8,128)(2,1)} %get-tuple-element.103), channel_id=1, source_target_pairs={{0,3},{1,2},{2,1},{3,0},{4,7},{5,6},{6,5},{7,4},{8,11},{9,10},{10,... | collective-permute-start | bytes 393224 | tf_op jit(solution)/shard_map/ppermute | solution.py:478
  179.3 20.2 %collective-permute-start.19 = (bf16[4,128,128]{2,1,0:T(8,128)(2,1)}, bf16[4,128,128]{2,1,0:T(8,128)(2,1)}, u32[]{:S(2)}, u32[]{:S(2)}) collective-permute-start(bf16[4,128,128]{2,1,0:T(8,128)(2,1)} %get-tuple-element.104), channel_id=1, source_target_pairs={{0,4},{1,5},{2,6},{3,7},{4,0},{5,1},{6,2},{7,3},{8,12},{9,13},{10,... | collective-permute-start | bytes 393224 | tf_op jit(solution)/shard_map/ppermute | solution.py:478
  183.6 17.6 %collective-permute-start.20 = (bf16[4,128,128]{2,1,0:T(8,128)(2,1)}, bf16[4,128,128]{2,1,0:T(8,128)(2,1)}, u32[]{:S(2)}, u32[]{:S(2)}) collective-permute-start(bf16[4,128,128]{2,1,0:T(8,128)(2,1)} %get-tuple-element.105), channel_id=1, source_target_pairs={{0,5},{1,4},{2,7},{3,6},{4,1},{5,0},{6,3},{7,2},{8,13},{9,12},{10,... | collective-permute-start | bytes 393224 | tf_op jit(solution)/shard_map/ppermute | solution.py:478
  188.1 14.1 %collective-permute-start.21 = (bf16[4,128,128]{2,1,0:T(8,128)(2,1)}, bf16[4,128,128]{2,1,0:T(8,128)(2,1)}, u32[]{:S(2)}, u32[]{:S(2)}) collective-permute-start(bf16[4,128,128]{2,1,0:T(8,128)(2,1)} %get-tuple-element.106), channel_id=1, source_target_pairs={{0,6},{1,7},{2,4},{3,5},{4,2},{5,3},{6,0},{7,1},{8,14},{9,15},{10,... | collective-permute-start | bytes 393224 | tf_op jit(solution)/shard_map/ppermute | solution.py:478
  189.5 12.8 %collective-permute-start.22 = (bf16[4,128,128]{2,1,0:T(8,128)(2,1)}, bf16[4,128,128]{2,1,0:T(8,128)(2,1)}, u32[]{:S(2)}, u32[]{:S(2)}) collective-permute-start(bf16[4,128,128]{2,1,0:T(8,128)(2,1)} %get-tuple-element.107), channel_id=1, source_target_pairs={{0,7},{1,6},{2,5},{3,4},{4,3},{5,2},{6,1},{7,0},{8,15},{9,14},{10,... | collective-permute-start | bytes 393224 | tf_op jit(solution)/shard_map/ppermute | solution.py:478
  201.2 52.8 %collective-permute-start.43 = (bf16[256,2048]{1,0:T(8,128)(2,1)S(1)}, bf16[256,2048]{1,0:T(8,128)(2,1)S(1)}, u32[]{:S(2)}, u32[]{:S(2)}) collective-permute-start(bf16[256,2048]{1,0:T(8,128)(2,1)S(1)} %constant_dynamic-slice_fusion.refs_24_), channel_id=1, source_target_pairs={{0,1},{1,0},{2,3},{3,2},{4,5},{5,4},{6,7},{7,6},{8,9},{9,8},{10,11... | collective-permute-start | bytes 3145736 | tf_op jit(solution)/shard_map/ppermute | solution.py:478
  202.2 53.7 %collective-permute-start.45 = (bf16[256,2048]{1,0:T(8,128)(2,1)S(1)}, bf16[256,2048]{1,0:T(8,128)(2,1)S(1)}, u32[]{:S(2)}, u32[]{:S(2)}) collective-permute-start(bf16[256,2048]{1,0:T(8,128)(2,1)S(1)} %collective-permute-done.44.refs_26_), channel_id=1, source_target_pairs={{0,1},{1,0},{2,3},{3,2},{4,5},{5,4},{6,7},{7,6},{8,9},{9,8},{10,11... | collective-permute-start | bytes 3145736 | tf_op jit(solution)/shard_map/ppermute | solution.py:478
  202.3 54.3 %collective-permute-start.47 = (bf16[256,2048]{1,0:T(8,128)(2,1)S(1)}, bf16[256,2048]{1,0:T(8,128)(2,1)S(1)}, u32[]{:S(2)}, u32[]{:S(2)}) collective-permute-start(bf16[256,2048]{1,0:T(8,128)(2,1)S(1)} %collective-permute-done.46.refs_28_), channel_id=1, source_target_pairs={{0,1},{1,0},{2,3},{3,2},{4,5},{5,4},{6,7},{7,6},{8,9},{9,8},{10,11... | collective-permute-start | bytes 3145736 | tf_op jit(solution)/shard_map/ppermute | solution.py:478
  202.7 55.8 %collective-permute-start.49 = (bf16[256,2048]{1,0:T(8,128)(2,1)}, bf16[256,2048]{1,0:T(8,128)(2,1)S(1)}, u32[]{:S(2)}, u32[]{:S(2)}) collective-permute-start(bf16[256,2048]{1,0:T(8,128)(2,1)} %collective-permute-done.48.refs_30_), channel_id=1, source_target_pairs={{0,1},{1,0},{2,3},{3,2},{4,5},{5,4},{6,7},{7,6},{8,9},{9,8},{10,11... | collective-permute-start | bytes 3145736 | tf_op jit(solution)/shard_map/ppermute | solution.py:478
  254.1 19.1 %collective-permute-start.38 = (bf16[8,64,128]{2,1,0:T(8,128)(2,1)}, bf16[8,64,128]{2,1,0:T(8,128)(2,1)}, u32[]{:S(2)}, u32[]{:S(2)}) collective-permute-start(bf16[8,64,128]{2,1,0:T(8,128)(2,1)} %get-tuple-element.133), channel_id=1, source_target_pairs={{0,3},{1,2},{2,1},{3,0},{4,7},{5,6},{6,5},{7,4},{8,11},{9,10},{10,... | collective-permute-start | bytes 393224 | tf_op jit(solution)/shard_map/ppermute | solution.py:478
  254.1 19.1 %collective-permute-start.39 = (bf16[8,64,128]{2,1,0:T(8,128)(2,1)}, bf16[8,64,128]{2,1,0:T(8,128)(2,1)S(1)}, u32[]{:S(2)}, u32[]{:S(2)}) collective-permute-start(bf16[8,64,128]{2,1,0:T(8,128)(2,1)} %get-tuple-element.134), channel_id=1, source_target_pairs={{0,4},{1,5},{2,6},{3,7},{4,0},{5,1},{6,2},{7,3},{8,12},{9,13},{10,... | collective-permute-start | bytes 393224 | tf_op jit(solution)/shard_map/ppermute | solution.py:478
  255.9 18.1 %collective-permute-start.40 = (bf16[8,64,128]{2,1,0:T(8,128)(2,1)}, bf16[8,64,128]{2,1,0:T(8,128)(2,1)S(1)}, u32[]{:S(2)}, u32[]{:S(2)}) collective-permute-start(bf16[8,64,128]{2,1,0:T(8,128)(2,1)} %get-tuple-element.135), channel_id=1, source_target_pairs={{0,5},{1,4},{2,7},{3,6},{4,1},{5,0},{6,3},{7,2},{8,13},{9,12},{10,... | collective-permute-start | bytes 393224 | tf_op jit(solution)/shard_map/ppermute | solution.py:478
  256.8 17.1 %collective-permute-start.41 = (bf16[8,64,128]{2,1,0:T(8,128)(2,1)}, bf16[8,64,128]{2,1,0:T(8,128)(2,1)S(1)}, u32[]{:S(2)}, u32[]{:S(2)}) collective-permute-start(bf16[8,64,128]{2,1,0:T(8,128)(2,1)} %get-tuple-element.136), channel_id=1, source_target_pairs={{0,6},{1,7},{2,4},{3,5},{4,2},{5,3},{6,0},{7,1},{8,14},{9,15},{10,... | collective-permute-start | bytes 393224 | tf_op jit(solution)/shard_map/ppermute | solution.py:478
  259.5 14.5 %collective-permute-start.42 = (bf16[8,64,128]{2,1,0:T(8,128)(2,1)}, bf16[8,64,128]{2,1,0:T(8,128)(2,1)S(1)}, u32[]{:S(2)}, u32[]{:S(2)}) collective-permute-start(bf16[8,64,128]{2,1,0:T(8,128)(2,1)} %get-tuple-element.137), channel_id=1, source_target_pairs={{0,7},{1,6},{2,5},{3,4},{4,3},{5,2},{6,1},{7,0},{8,15},{9,14},{10,... | collective-permute-start | bytes 393224 | tf_op jit(solution)/shard_map/ppermute | solution.py:478
  (65 other events, 1314.8 us)
